TPU v7x, 256 devices: a whole 4x4x8 slice. The times are simulated.
256 devices in a mesh: grp: 2 (over core), dom: 64 (over y_lo, z, x), sub: 2 (over y_hi).
Axes of the slice: x: 4, y: 4 (y_hi: 2, y_lo: 2; y = y_hi * 2 + y_lo), z: 8, core: 2. Of those that a mesh axis runs over, the one named last changes fastest.
Arguments:
- positions: float32 [3, 65536], P(None, ('grp', 'dom', 'sub')), may hold values from 0 to 4
- charges: float32 [65536], P(('grp', 'dom', 'sub')), may hold values from -3 to 3
- polar: float32 [65536], P(('grp', 'dom', 'sub')), may hold values from 0.1 to 0.6
- features: bfloat16 [65536, 256], P(('grp', 'dom', 'sub')), may hold values from -6 to 6
- neighbours: int32 [65536, 32], P(('grp', 'dom', 'sub')), may hold values from 0 to 512, as said below
- send_rows: int32 [2, 32768], P(None, ('grp', 'dom', 'sub')), may hold values from 0 to 255
- blocks: int32 [1024], P(('grp', 'dom', 'sub')), may hold values from 0 to 255
- radial_in: bfloat16 [2, 8, 64], replicated, may hold values from -2 to 2
- radial_mid: bfloat16 [2, 2, 64, 64], replicated, may hold values from -0.75 to 0.75
- radial_out: bfloat16 [2, 64, 256], replicated, may hold values from -0.75 to 0.75
- node_in: bfloat16 [2, 256, 256], replicated, may hold values from -0.375 to 0.375
- node_out: bfloat16 [2, 256, 256], replicated, may hold values from -0.375 to 0.375
- field_gain: float32 [256], replicated, may hold values from -3 to 3
- readout: bfloat16 [256, 2], replicated, may hold values from -0.375 to 0.375
Outputs:
- site_result: float32 [3, 65536], P(None, ('grp', 'dom', 'sub'))
- response: float32 [3, 65536], P(None, ('grp', 'dom', 'sub'))
Inputs may be any that keep to these rules, and one draw needn't show every extreme that they name: `neighbours`: entries below 256 name the block's own sites, entries from 256 to 511 its lent sites, 512 an empty slot; empty slots follow the used ones. `blocks`: repeats may occur.
All inputs are finite; a program needn't handle non-finite values.
Results may differ from a plain program's by a relative error of at most 0.0022.
The roundings to bfloat16 on the way count: a program that leaves them out, or rounds other values in their place, can miss the bound.
Values may be sent and summed in bfloat16 or wider, within the bound.
No kernel may reach another device: no remote copies, remote signals or barrier semaphores. Data moves between devices by JAX's collectives and lax.ppermute only.
A program may use at most 64 MiB of HBM per device.

v0:
```python
import jax
import jax.numpy as jnp
from jax import lax
from jax.sharding import PartitionSpec as P

BASIS = 8
LAYERS = 2
SWEEPS = 4
BLOCK = 128


SMOOTH = 1.0
GAMMA = 1.0
SPACING = 0.75


def with_halo(block, sides, width):
    for axis, dim in sides:
        count = lax.axis_size(axis)
        forward = [(i, i + 1) for i in range(count - 1)]
        backward = [(target, source) for source, target in forward]
        low = lax.ppermute(
            lax.slice_in_dim(block, block.shape[dim] - width, None, axis=dim), axis, forward
        )
        high = lax.ppermute(lax.slice_in_dim(block, 0, width, axis=dim), axis, backward)
        block = jnp.concatenate([low, block, high], axis=dim)
    return block


def partner_2(value, axis, bit):
    mask = 2**bit
    pairs = [(source, source ^ mask) for source in range(lax.axis_size(axis))]
    return lax.ppermute(value, axis, pairs)


def field_at(target, source, charge, dipole):
    tile_count = target.shape[1] // BLOCK
    tiles = target.reshape(3, tile_count, BLOCK).transpose(1, 0, 2)

    def field_one_tile(target_tile):
        offset = target_tile[:, :, None] - source[:, None, :]
        dist_sq = jnp.sum(offset * offset, axis=0) + SMOOTH
        inverse = lax.rsqrt(dist_sq)
        inverse_cube = inverse * inverse * inverse
        inverse_fifth = inverse_cube * inverse * inverse
        projected = jnp.sum(offset * dipole[:, None, :], axis=0)
        source_scale = charge[None, :] * inverse_cube + 3.0 * projected * inverse_fifth
        return jnp.sum(
            offset * source_scale[None] - dipole[:, None, :] * inverse_cube[None], axis=2
        )

    return lax.map(field_one_tile, tiles).transpose(1, 0, 2).reshape(3, -1)


def slot_field(offset, dist_sq, source_charge, source_dipole):
    inverse = lax.rsqrt(dist_sq)
    inverse_cube = inverse * inverse * inverse
    inverse_fifth = inverse_cube * inverse * inverse
    projected = jnp.sum(offset * source_dipole, axis=0)
    source_scale = source_charge * inverse_cube + 3.0 * projected * inverse_fifth
    return jnp.sum(offset * source_scale[None] - source_dipole * inverse_cube[None], axis=1)


def message_update(
    hidden, lifted_table, radial_basis, slot_major, w_first, w_middle, w_last, w_node
):
    row_count, channel_count = hidden.shape
    slot_count = slot_major.shape[0]
    basis_width = radial_basis.shape[2]
    tile_count = row_count // BLOCK

    def message_one_tile(tile_index):
        start = tile_index * BLOCK
        basis_tile = lax.dynamic_slice_in_dim(radial_basis, start, BLOCK, 1).reshape(
            slot_count * BLOCK, basis_width
        )
        index_tile = lax.dynamic_slice_in_dim(slot_major, start, BLOCK, 1)
        first_hidden = jax.nn.silu(
            jnp.dot(basis_tile, w_first, preferred_element_type=jnp.float32)
        ).astype(jnp.bfloat16)
        second_hidden = jax.nn.silu(
            jnp.dot(first_hidden, w_middle[0], preferred_element_type=jnp.float32)
        ).astype(jnp.bfloat16)
        third_hidden = jax.nn.silu(
            jnp.dot(second_hidden, w_middle[1], preferred_element_type=jnp.float32)
        ).astype(jnp.bfloat16)
        edge_weight = jnp.dot(third_hidden, w_last, preferred_element_type=jnp.float32).reshape(
            slot_count, BLOCK, channel_count
        )
        source = lifted_table[index_tile].astype(jnp.float32)
        summed = jnp.sum(edge_weight * source, axis=0)
        return summed / slot_count

    message = (
        lax.map(message_one_tile, jnp.arange(tile_count, dtype=jnp.int32))
        .reshape(row_count, channel_count)
        .astype(jnp.bfloat16)
    )
    update = jax.nn.silu(jnp.dot(message, w_node, preferred_element_type=jnp.float32))
    return (hidden.astype(jnp.float32) + update).astype(jnp.bfloat16)


def extend_cols(values, rim_rows, rim_width):
    empty_entry = jnp.zeros(values.shape[:-1] + (1,), values.dtype)
    return jnp.concatenate(
        [values, rim_rows[..., :rim_width], rim_rows[..., 3 * rim_width :], empty_entry], axis=-1
    )


def extend_rows(values, rim_rows, rim_width):
    empty_entry = jnp.zeros((1,) + values.shape[1:], values.dtype)
    return jnp.concatenate(
        [values, rim_rows[:rim_width], rim_rows[3 * rim_width :], empty_entry], axis=0
    )


def local(
    positions,
    charges,
    polar,
    features,
    neighbours,
    send_rows,
    blocks,
    radial_in,
    radial_mid,
    radial_out,
    node_in,
    node_out,
    field_gain,
    readout,
):
    rim_width = send_rows.shape[1]
    row_count = positions.shape[1]
    block_width = BLOCK
    own_blocks = row_count // block_width
    listed_count = blocks.shape[0]
    domain_count = lax.axis_size(("dom", "sub"))
    domain_index = lax.axis_index(("dom", "sub"))
    group_blocks = own_blocks * domain_count
    learned = lax.axis_index("grp") == 0
    slot_major = neighbours.T
    local_data = jnp.concatenate([positions, charges[None], polar[None]], axis=0)
    outgoing = jnp.concatenate([local_data[:, send_rows[1]], local_data[:, send_rows[0]]], axis=1)
    rim_rows = with_halo(outgoing, ((("dom", "sub"), 1),), rim_width)
    site_table = extend_cols(local_data, rim_rows, rim_width)
    partner = partner_2(local_data, "grp", 0)
    others = lax.all_gather(partner, ("dom", "sub"), axis=1, tiled=True)
    near_sites = jnp.take(others.reshape(5, -1, block_width), blocks, axis=1).reshape(5, -1)
    outside = field_at(positions, near_sites[:3], near_sites[3], jnp.zeros_like(near_sites[:3]))
    offset = positions[:, None, :] - site_table[:3][:, slot_major]
    dist_sq = jnp.sum(offset * offset, axis=0) + SMOOTH
    strength = jnp.sqrt(1.0 + jnp.sum(outside * outside, axis=0))
    hidden = (features.astype(jnp.float32) + strength[:, None] * field_gain[None, :]).astype(
        jnp.bfloat16
    )
    centres = jnp.arange(BASIS, dtype=jnp.float32) * SPACING
    radial_basis = jnp.exp(-GAMMA * (jnp.sqrt(dist_sq)[:, :, None] - centres) ** 2).astype(
        jnp.bfloat16
    )
    for layer_index in range(LAYERS):
        lifted = lax.cond(
            learned,
            lambda h: jnp.dot(h, node_in[layer_index], preferred_element_type=jnp.float32).astype(
                jnp.bfloat16
            ),
            lambda h: jnp.zeros_like(h),
            hidden,
        )
        lent = jnp.concatenate([lifted[send_rows[1]], lifted[send_rows[0]]], axis=0)
        lifted_rims = with_halo(lent, ((("dom", "sub"), 0),), rim_width)
        lifted_table = extend_rows(lifted, lifted_rims, rim_width)
        hidden = lax.cond(
            learned,
            lambda h, t: message_update(
                h,
                t,
                radial_basis,
                slot_major,
                radial_in[layer_index],
                radial_mid[layer_index],
                radial_out[layer_index],
                node_out[layer_index],
            ),
            lambda h, t: h,
            hidden,
            lifted_table,
        )
    readouts = jnp.dot(hidden, readout, preferred_element_type=jnp.float32)
    charge = readouts[:, 0]
    energy = readouts[:, 1]
    fixed_field = outside + slot_field(
        offset, dist_sq, site_table[3][slot_major], jnp.zeros_like(offset)
    )
    dipole = jnp.where(learned, 0.0, polar[None] * fixed_field)
    for sweep_index in range(SWEEPS):
        lent_dipoles = jnp.concatenate([dipole[:, send_rows[1]], dipole[:, send_rows[0]]], axis=1)
        dipole_rims = with_halo(lent_dipoles, ((("dom", "sub"), 1),), rim_width)
        dipole_table = extend_cols(dipole, dipole_rims, rim_width)
        dipole = lax.cond(
            learned,
            lambda d, t: d,
            lambda d, t: polar[None]
            * (
                fixed_field + slot_field(offset, dist_sq, jnp.zeros_like(dist_sq), t[:, slot_major])
            ),
            dipole,
            dipole_table,
        )
    site_result = jnp.where(learned, jnp.stack([charge, energy, strength]), dipole)
    source_charge = jnp.where(learned, charge, 0.0)
    source_dipole = jnp.where(learned, 0.0, dipole)
    response_term = field_at(near_sites[:3], positions, source_charge, source_dipole)
    scattered = (
        jnp.zeros((3, group_blocks, block_width), jnp.float32)
        .at[:, blocks]
        .add(response_term.reshape(3, listed_count, block_width))
        .reshape(3, -1)
    )
    total = lax.psum(scattered, ("dom", "sub"))
    own_share = lax.dynamic_slice_in_dim(total, domain_index * row_count, row_count, 1)
    response = partner_2(own_share, "grp", 0)
    return (site_result, response)


def solution(mesh):
    in_specs = (
        P(None, ("grp", "dom", "sub")),
        P(("grp", "dom", "sub")),
        P(("grp", "dom", "sub")),
        P(("grp", "dom", "sub"), None),
        P(("grp", "dom", "sub"), None),
        P(None, ("grp", "dom", "sub")),
        P(("grp", "dom", "sub")),
        P(),
        P(),
        P(),
        P(),
        P(),
        P(),
        P(),
    )
    out_specs = (P(None, ("grp", "dom", "sub")), P(None, ("grp", "dom", "sub")))
    return jax.shard_map(local, mesh=mesh, in_specs=in_specs, out_specs=out_specs, check_vma=False)
```

profile of v0, /device:TPU:1, one launch (start us, length us, event | category | flops | bytes accessed | tf_op | source)
XLA Modules:
  0.0 878.2 jit_solution(3538958461297963734)
XLA Ops:
  7.2 0.7 pad_maximum_fusion
  8.0 3.2 collective-permute-start
  11.3 0.8 fusion.91
  12.1 0.6 gather_fusion.8
  12.8 1.3 collective-permute-start.2
  14.7 5.5 collective-permute-start.1
  20.2 0.7 compare_select_fusion.9
  20.9 0.7 compare_and_fusion
  21.5 0.8 fusion.90
  22.4 0.8 copy.119
  23.4 0.8 maximum_maximum_fusion.2
  24.2 32.9 %gather_fusion.14 = f32[8192]{0:T(1024)S(1)} fusion(f32[513]{0:T(1024)S(1)} %slice_reduce_fusion, s32[8192]{0:T(1024)S(1)} %broadcast_clamp_fusion.4), kind=kCustom, calls=%fused_computation.14 | custom fusion | bytes 98304 | tf_op jit(solution)/shard_map/gather | solution.py:193
  57.2 27.9 %gather_fusion.9 = f32[8192,3]{1,0:T(8,128)} fusion(f32[3,513]{0,1:T(8,128)S(1)} %copy.124, s32[8192]{0:T(1024)S(1)} %broadcast_clamp_fusion.4), kind=kCustom, calls=%fused_computation.9 | custom fusion | bytes 229376 | tf_op jit(solution)/shard_map/gather | solution.py:151
  85.1 4.5 multiply_reduce_fusion.4
  89.6 1.9 copy-done.1
  91.5 2.5 subtract_reduce_fusion.4
  94.0 296.4 %all_gather.3 = f32[5,32768]{1,0:T(8,128)S(1)} all-gather(f32[5,256]{1,0:T(8,128)S(1)} %collective-permute-done), channel_id=1, replica_groups=mesh['grp'=2,'dom'=64,'sub'=2] {'dom','sub'}, dimensions={1}, use_global_device_ids=true | all-gather | bytes 660480 | tf_op jit(solution)/shard_map/all_gather | solution.py:148
  391.1 1.2 while.40
  392.6 0.6 gather_fusion.16
  393.9 1.3 collective-permute-start.8
  395.2 5.5 collective-permute-start.7
  400.8 1.1 collective-permute-done.7
  402.1 36.6 %conditional.12 = (f32[3,256]{0,1:T(8,128)S(1)}) conditional(s32[]{:T(128)} %convert_element_type.76, (f32[256]{0:T(256)S(1)}, f32[32,256]{1,0:T(8,128)S(1)}, s32[32,256]{1,0:T(8,128)S(1)}, f32[3,513]{1,0:T(4,128)S(1)}, f32[3,32,256]{0,2,1:T(8,128)}, /*index=5*/f32[3,256]{0,1:T(8,128)S(1)}) %tuple.225, f32[3,256]{0,1:T(8,128)S(1)} %get-tuple-element.543), branch_computations={%region_23.26_spmd, %region_26.27_spmd} | conditional | flops 238336 | bytes 1860696 | solution.py:200
  402.3 27.9 %gather_fusion = f32[8192,3]{1,0:T(8,128)} fusion(f32[3,513]{0,1:T(8,128)S(1)} %copy.129, s32[8192]{0:T(1024)S(1)} %broadcast_clamp_fusion), kind=kCustom, calls=%fused_computation.2 | custom fusion | bytes 229376 | tf_op jit(solution)/shard_map/cond/branch_0_fun/gather | solution.py:205
  430.2 4.8 multiply_reduce_fusion
  435.0 1.1 copy-done.6
  436.1 2.5 subtract_reduce_fusion
  440.0 1.3 collective-permute-start.10
  441.3 6.1 collective-permute-start.9
  447.6 1.1 collective-permute-done.9
  448.9 36.7 %conditional.13 = (f32[3,256]{0,1:T(8,128)S(1)}) conditional(s32[]{:T(128)} %convert_element_type.76, (f32[256]{0:T(256)S(1)}, f32[32,256]{1,0:T(8,128)S(1)}, s32[32,256]{1,0:T(8,128)S(1)}, f32[3,513]{1,0:T(4,128)S(1)}, f32[3,32,256]{0,2,1:T(8,128)}, /*index=5*/f32[3,256]{0,1:T(8,128)S(1)}) %tuple.226, f32[3,256]{0,1:T(8,128)S(1)} %get-tuple-element.898), branch_computations={%region_27.30_spmd, %region_30.31_spmd} | conditional | flops 238336 | bytes 1860696 | solution.py:200
  449.1 27.9 %gather_fusion.1 = f32[8192,3]{1,0:T(8,128)} fusion(f32[3,513]{0,1:T(8,128)S(1)} %copy.133, s32[8192]{0:T(1024)S(1)} %broadcast_clamp_fusion.1), kind=kCustom, calls=%fused_computation.3 | custom fusion | bytes 229376 | tf_op jit(solution)/shard_map/cond/branch_0_fun/gather | solution.py:205
  477.0 4.8 multiply_reduce_fusion.1
  481.8 1.1 copy-done.7
  482.9 2.5 subtract_reduce_fusion.1
  486.8 1.3 collective-permute-start.12
  488.1 6.4 collective-permute-start.11
  494.9 0.8 gather_fusion.11
  495.7 0.8 gather_fusion.10
  496.6 1.3 collective-permute-start.4
  497.9 6.7 collective-permute-start.3
  504.9 36.6 %conditional.14 = (f32[3,256]{0,1:T(8,128)S(1)}) conditional(s32[]{:T(128)} %convert_element_type.76, (f32[256]{0:T(256)S(1)}, f32[32,256]{1,0:T(8,128)S(1)}, s32[32,256]{1,0:T(8,128)S(1)}, f32[3,513]{1,0:T(4,128)S(1)}, f32[3,32,256]{0,2,1:T(8,128)}, /*index=5*/f32[3,256]{0,1:T(8,128)S(1)}) %tuple.227, f32[3,256]{0,1:T(8,128)S(1)} %get-tuple-element.899), branch_computations={%region_31.34_spmd, %region_34.35_spmd} | conditional | flops 238336 | bytes 1860696 | solution.py:200
  505.1 27.9 %gather_fusion.2 = f32[8192,3]{1,0:T(8,128)} fusion(f32[3,513]{0,1:T(8,128)S(1)} %copy.137, s32[8192]{0:T(1024)S(1)} %broadcast_clamp_fusion.2), kind=kCustom, calls=%fused_computation.4 | custom fusion | bytes 229376 | tf_op jit(solution)/shard_map/cond/branch_0_fun/gather | solution.py:205
  533.0 4.8 multiply_reduce_fusion.2
  537.8 1.1 copy-done.8
  538.9 2.5 subtract_reduce_fusion.2
  542.8 1.3 collective-permute-start.14
  544.1 6.4 collective-permute-start.13
  550.8 1.0 collective-permute-done.13
  552.2 0.8 gather_fusion.13
  553.0 0.8 gather_fusion.12
  553.9 1.3 collective-permute-start.6
  555.2 6.4 collective-permute-start.5
  561.6 36.6 %conditional.15 = (f32[3,256]{0,1:T(8,128)S(1)}) conditional(s32[]{:T(128)} %convert_element_type.76, (f32[256]{0:T(256)S(1)}, f32[32,256]{1,0:T(8,128)S(1)}, s32[32,256]{1,0:T(8,128)S(1)}, f32[3,513]{1,0:T(4,128)S(1)}, f32[3,32,256]{0,2,1:T(8,128)}, /*index=5*/f32[3,256]{0,1:T(8,128)S(1)}) %tuple.228, f32[3,256]{0,1:T(8,128)S(1)} %get-tuple-element.900), branch_computations={%region_35.38_spmd, %region_38.39_spmd} | conditional | flops 238336 | bytes 1860696 | solution.py:200
  561.8 27.9 %gather_fusion.3 = f32[8192,3]{1,0:T(8,128)} fusion(f32[3,513]{0,1:T(8,128)S(1)} %copy.141, s32[8192]{0:T(1024)S(1)} %broadcast_clamp_fusion.3), kind=kCustom, calls=%fused_computation.5 | custom fusion | bytes 229376 | tf_op jit(solution)/shard_map/cond/branch_0_fun/gather | solution.py:205
  589.7 4.8 multiply_reduce_fusion.3
  594.5 1.1 copy-done.9
  595.6 2.5 subtract_reduce_fusion.3
  599.1 1.9 while.41
  601.7 0.8 copy-done.11
  602.6 261.5 %all-reduce.2.cloned.1.call-done = f32[3,32768]{1,0:T(4,128)} async-done(((f32[3,32768]{1,0:T(4,128)}), f32[3,32768]{1,0:T(4,128)}) %all-reduce.2.cloned.1.call-update) | async-done | bytes 393232 | tf_op jit(solution)/shard_map/psum | solution.py:220
  864.0 0.7 constant_dynamic-slice_fusion
  864.7 5.2 collective-permute-start.15
  869.9 0.7 copy.144
  (178 shorter events, 14.6 us)
Async XLA Ops:
  7.2 591.5 %copy-start = (bf16[256,2]{0,1:T(2,128)(2,1)S(1)}, bf16[256,2]{0,1:T(2,128)(2,1)}, u32[]{:S(2)}) copy-start(bf16[256,2]{0,1:T(2,128)(2,1)} %param.51) | copy-start | bytes 3076
  7.2 856.8 %all-reduce.2.cloned.1.call-start = ((), (), s32[]{:S(2)}) async-start(), calls=%async_computation | async-start | bytes 1048576 | tf_op jit(solution)/shard_map/psum | solution.py:220
  8.0 86.1 %collective-permute-start = (f32[5,256]{1,0:T(8,128)S(1)}, f32[5,256]{1,0:T(8,128)S(1)}, u32[]{:S(2)}, u32[]{:S(2)}) collective-permute-start(f32[5,256]{1,0:T(8,128)S(1)} %pad_maximum_fusion), channel_id=1, source_target_pairs={{0,128},{128,0},{1,129},{129,1},{2,130},{130,2},{3,131},{131,3},{4... | collective-permute-start | bytes 15368 | tf_op jit(solution)/shard_map/ppermute | solution.py:33
  12.8 10.5 %collective-permute-start.2 = (f32[5,128]{0,1:T(8,128)S(1)}, f32[5,128]{0,1:T(8,128)S(1)}, u32[]{:S(2)}, u32[]{:S(2)}) collective-permute-start(f32[5,128]{0,1:T(8,128)S(1)} %bitcast.260), channel_id=1, source_target_pairs={{1,0},{2,1},{3,2},{4,3},{5,4},{6,5},{7,6},{8,7},{9,8},{10,9},{11,1... | collective-permute-start | bytes 7688 | tf_op jit(solution)/shard_map/ppermute | solution.py:25
  14.7 8.6 collective-permute-start.1
  20.9 2.4 copy-start.20
  89.6 1.9 copy-start.1
  89.6 301.4 %copy-start.12 = (f32[3,256]{1,0:T(4,128)S(1)}, f32[3,256]{1,0:T(4,128)}, u32[]{:S(2)}) copy-start(f32[3,256]{1,0:T(4,128)} %param.38) | copy-start | bytes 9220
  391.1 1.4 copy-start.17
  391.1 11.0 %copy-start.10 = (s32[256,32]{0,1:T(8,128)S(1)}, s32[256,32]{0,1:T(8,128)}, u32[]{:S(2)}) copy-start(s32[256,32]{0,1:T(8,128)} %param.42) | copy-start | bytes 98308
  393.9 6.9 collective-permute-start.8
  395.2 6.8 collective-permute-start.7
  430.2 4.8 copy-start.2
  430.2 5.9 copy-start.6
  440.0 7.5 collective-permute-start.10
  441.3 7.4 collective-permute-start.9
  448.8 45.7 %copy-start.14 = (bf16[256,256]{1,0:T(8,128)(2,1)S(1)}, bf16[256,256]{1,0:T(8,128)(2,1)}, u32[]{:S(2)}) copy-start(bf16[256,256]{1,0:T(8,128)(2,1)} %param.41) | copy-start | bytes 393220
  448.8 45.7 %copy-start.22 = (f32[256]{0:T(256)S(1)}, f32[256]{0:T(256)}, u32[]{:S(2)}) copy-start(f32[256]{0:T(256)} %param.50) | copy-start | bytes 3076
  448.8 45.8 %copy-start.13 = (bf16[2,256,256]{2,1,0:T(8,128)(2,1)S(1)}, bf16[2,256,256]{2,1,0:T(8,128)(2,1)}, u32[]{:S(2)}) copy-start(bf16[2,256,256]{2,1,0:T(8,128)(2,1)} %param.48) | copy-start | bytes 786436
  477.0 4.8 copy-start.3
  477.0 5.9 copy-start.7
  486.8 17.9 %collective-permute-start.12 = (f32[3,128]{0,1:T(8,128)S(1)}, f32[3,128]{0,1:T(8,128)S(1)}, u32[]{:S(2)}, u32[]{:S(2)}) collective-permute-start(f32[3,128]{0,1:T(8,128)S(1)} %bitcast.263), channel_id=1, source_target_pairs={{1,0},{2,1},{3,2},{4,3},{5,4},{6,5},{7,6},{8,7},{9,8},{10,9},{11,1... | collective-permute-start | bytes 4616 | tf_op jit(solution)/shard_map/ppermute | solution.py:25
  488.1 16.7 %collective-permute-start.11 = (f32[3,128]{0,1:T(8,128)S(1)}, f32[3,128]{0,1:T(8,128)S(1)}, u32[]{:S(2)}, u32[]{:S(2)}) collective-permute-start(f32[3,128]{0,1:T(8,128)S(1)} %bitcast.262), channel_id=1, source_target_pairs={{0,1},{1,2},{2,3},{3,4},{4,5},{5,6},{6,7},{7,8},{8,9},{9,10},{10,1... | collective-permute-start | bytes 4616 | tf_op jit(solution)/shard_map/ppermute | solution.py:22
  496.6 55.3 %collective-permute-start.4 = (bf16[128,256]{1,0:T(8,128)(2,1)S(1)}, bf16[128,256]{1,0:T(8,128)(2,1)S(1)}, u32[]{:S(2)}, u32[]{:S(2)}) collective-permute-start(bf16[128,256]{1,0:T(8,128)(2,1)S(1)} %gather_fusion.11), channel_id=1, source_target_pairs={{1,0},{2,1},{3,2},{4,3},{5,4},{6,5},{7,6},{8,7},{9,8},{10,9},{11,1... | collective-permute-start | bytes 196616 | tf_op jit(solution)/shard_map/ppermute | solution.py:25
  497.9 54.0 %collective-permute-start.3 = (bf16[128,256]{1,0:T(8,128)(2,1)S(1)}, bf16[128,256]{1,0:T(8,128)(2,1)S(1)}, u32[]{:S(2)}, u32[]{:S(2)}) collective-permute-start(bf16[128,256]{1,0:T(8,128)(2,1)S(1)} %gather_fusion.10), channel_id=1, source_target_pairs={{0,1},{1,2},{2,3},{3,4},{4,5},{5,6},{6,7},{7,8},{8,9},{9,10},{10,1... | collective-permute-start | bytes 196616 | tf_op jit(solution)/shard_map/ppermute | solution.py:22
  504.9 47.2 %copy-start.15 = (bf16[2,2,64,64]{3,2,1,0:T(8,128)(2,1)S(1)}, bf16[2,2,64,64]{3,2,1,0:T(8,128)(2,1)}, u32[]{:S(2)}) copy-start(bf16[2,2,64,64]{3,2,1,0:T(8,128)(2,1)} %param.46) | copy-start | bytes 98308
  504.9 47.2 %copy-start.16 = (bf16[2,64,256]{2,1,0:T(8,128)(2,1)S(1)}, bf16[2,64,256]{2,1,0:T(8,128)(2,1)}, u32[]{:S(2)}) copy-start(bf16[2,64,256]{2,1,0:T(8,128)(2,1)} %param.47) | copy-start | bytes 196612
  504.9 47.2 %copy-start.19 = (bf16[2,8,64]{2,1,0:T(8,128)(2,1)S(1)}, bf16[2,8,64]{2,1,0:T(8,128)(2,1)}, u32[]{:S(2)}) copy-start(bf16[2,8,64]{2,1,0:T(8,128)(2,1)} %param.45) | copy-start | bytes 6148
  533.0 4.8 copy-start.4
  533.0 5.9 copy-start.8
  542.8 7.9 collective-permute-start.14
  544.1 7.7 collective-permute-start.13
  553.9 44.4 %collective-permute-start.6 = (bf16[128,256]{1,0:T(8,128)(2,1)S(1)}, bf16[128,256]{1,0:T(8,128)(2,1)S(1)}, u32[]{:S(2)}, u32[]{:S(2)}) collective-permute-start(bf16[128,256]{1,0:T(8,128)(2,1)S(1)} %gather_fusion.13), channel_id=1, source_target_pairs={{1,0},{2,1},{3,2},{4,3},{5,4},{6,5},{7,6},{8,7},{9,8},{10,9},{11,1... | collective-permute-start | bytes 196616 | tf_op jit(solution)/shard_map/ppermute | solution.py:25
  555.2 43.1 %collective-permute-start.5 = (bf16[128,256]{1,0:T(8,128)(2,1)S(1)}, bf16[128,256]{1,0:T(8,128)(2,1)S(1)}, u32[]{:S(2)}, u32[]{:S(2)}) collective-permute-start(bf16[128,256]{1,0:T(8,128)(2,1)S(1)} %gather_fusion.12), channel_id=1, source_target_pairs={{0,1},{1,2},{2,3},{3,4},{4,5},{5,6},{6,7},{7,8},{8,9},{9,10},{10,1... | collective-permute-start | bytes 196616 | tf_op jit(solution)/shard_map/ppermute | solution.py:22
  589.7 4.8 copy-start.5
  589.7 5.9 copy-start.9
  598.4 0.7 copy-start.18
  598.6 2.4 copy-start.21
  601.7 0.8 copy-start.11
  864.7 6.0 collective-permute-start.15
Sparse Core Ops, SparseCore 0:
  602.7 261.3 all-reduce.1
where the time goes:
time: 879 us; the launch traced here: 878 us
  blocking collectives  296 us (34%)
  waiting for transfers between devices  265 us (30%)
  local copies, waits for them, and re-layouts  195 us (22%)
  starting transfers between devices  60.5 us (7%)
  other arithmetic  45.1 us (5%)
  between operations  14.8 us (2%)
    all_gather x1, blocking collectives, local(): others = lax.all_gather(partner, ('dom', 'sub'), axis=1, tiled=True)  296 us
    psum x1, waiting for transfers between devices, local(): total = lax.psum(scattered, ('dom', 'sub'))  261 us
    gather x4, local copies, waits for them, and re-layouts, local(): t[:, slot_major]  112 us
    ppermute x7, starting transfers between devices, with_halo(): lax.ppermute(lax.slice_in_dim(block, block.shape[dim] - width, None, axis...  43 us
    gather x2, local copies, waits for them, and re-layouts, local(): site_table[3][slot_major]  32.9 us
    gather x1, local copies, waits for them, and re-layouts, local(): offset = positions[:, None, :] - site_table[:3][:, slot_major]  27.9 us
    reduce_sum x5, other arithmetic, slot_field(): projected = jnp.sum(offset * source_dipole, axis=0)  23.5 us
  transfers between devices with their start and end apart: 17, of which 5 were waited for; matrix products, arithmetic and copies ran while one was open for 17% of the time, Pallas kernels for 0%

commit v1 on v0

v1 whole, which is shorter than its diff:
```python
import jax
import jax.numpy as jnp
from jax import lax
from jax.experimental import pallas as pl
from jax.experimental.pallas import tpu as pltpu
from jax.sharding import PartitionSpec as P

BASIS = 8
LAYERS = 2
SMOOTH = 1.0
SPACING = 0.75
DOM = ("dom", "sub")
EVERY = ("grp", "dom", "sub")
F32 = jnp.float32
BF16 = jnp.bfloat16
VMEM = pl.BlockSpec(memory_space=pltpu.VMEM)
SMEM = pl.BlockSpec(memory_space=pltpu.SMEM)
CHUNK = 16


def call(body, outs, args, smem_count, scratch=()):
    return pl.pallas_call(
        body,
        out_shape=[jax.ShapeDtypeStruct(s, d) for s, d in outs],
        in_specs=[SMEM] * smem_count + [VMEM] * (len(args) - smem_count),
        out_specs=[VMEM] * len(outs),
        scratch_shapes=list(scratch),
        compiler_params=pltpu.CompilerParams(vmem_limit_bytes=40 * 2**20),
    )(*args)


def dot(a, b):
    return jnp.dot(a, b, preferred_element_type=F32)


def silu(x):
    return x * jax.nn.sigmoid(x)


def flip(x):
    return x.astype(F32).T


def split3(x):
    high = x.astype(BF16)
    rest = x - high.astype(F32)
    mid = rest.astype(BF16)
    low = (rest - mid.astype(F32)).astype(BF16)
    return jnp.concatenate([high, mid, low], axis=0)


def join3(x):
    return x[0:8] + x[8:16] + x[16:24]


def one_hot(row, depth):
    ids = lax.broadcasted_iota(jnp.int32, (depth, row.shape[1]), 0)
    return jnp.where(ids == row, 1.0, 0.0).astype(BF16)


def rows_kernel(meta, pos, charge, polar, neighbours, send, site, mine, lent_a, lent_b, slots, picks):
    odd = meta[1] == 1
    width = pos.shape[1]
    site[...] = jnp.zeros_like(site)
    site[0:3, :] = pos[...]
    site[3:4, :] = charge[...]
    site[4:5, :] = polar[...]
    for half in range(2):
        mine[half] = site[0:4, half * 128 : half * 128 + 128]
    first, second = send[0:1, :], send[1:2, :]
    swap = jnp.full(first.shape, meta[1], jnp.int32) == 1
    picks[0:1, :] = jnp.where(swap, second, first)
    picks[1:2, :] = jnp.where(swap, first, second)
    pieces = split3(site[...])
    lent_a[...] = join3(dot(pieces, one_hot(picks[0:1, :], width)))
    lent_b[...] = join3(dot(pieces, one_hot(picks[1:2, :], width)))
    table = flip(neighbours[...]).astype(jnp.int32)
    other = jnp.where((table >= 256) & (table < 512), jnp.bitwise_xor(table, 128), table)
    keep = jnp.full(table.shape, meta[1], jnp.int32) == 1
    slots[...] = jnp.where(keep, table, other)


def static_kernel(
    meta, site, rim_a, rim_b, slots, features, w_in, w_mid, w_out, node_in, node_out, gain,
    third, feat_t, out_t, in_t, node_t, gain_col, w3, w5, fixed, entry,
):
    learned = meta[0] == 0
    width = site.shape[1]
    depth = 2 * width
    slot_count = slots.shape[0]

    @pl.when(learned)
    def _():
        table = jnp.concatenate([site[...], rim_a[...], rim_b[...]], axis=1)
        pieces = split3(table)
        feat_t[...] = flip(features[...]).astype(BF16)
        gain_col[...] = jnp.broadcast_to(gain[...], (8, width)).T
        for layer in range(LAYERS):
            in_t[layer] = flip(node_in[layer]).astype(BF16)
            node_t[layer] = flip(node_out[layer]).astype(BF16)
            out_t[layer] = flip(w_out[layer]).astype(BF16)
        first_w = jnp.concatenate([flip(w_in[0]), flip(w_in[1])], axis=0).astype(BF16)
        zero = jnp.zeros((64, 64), F32)

        def both(depth_index):
            top = jnp.concatenate([flip(w_mid[0, depth_index]), zero], axis=1)
            bottom = jnp.concatenate([zero, flip(w_mid[1, depth_index])], axis=1)
            return jnp.concatenate([top, bottom], axis=0).astype(BF16)

        second_w, third_w = both(0), both(1)
        centres = lax.broadcasted_iota(jnp.int32, (BASIS, width), 0).astype(F32) * SPACING

        def one_slot(k, carry):
            found = join3(dot(pieces, one_hot(slots[pl.ds(k, 1), :], depth)))
            offset = site[...] - found
            squares = offset * offset
            dist_sq = squares[0:1] + squares[1:2] + squares[2:3] + SMOOTH
            gap = jnp.sqrt(dist_sq) - centres
            basis = jnp.exp(-(gap * gap)).astype(BF16)
            hidden = silu(dot(first_w, basis)).astype(BF16)
            hidden = silu(dot(second_w, hidden)).astype(BF16)
            hidden = silu(dot(third_w, hidden)).astype(BF16)
            third[k] = hidden
            return carry

        lax.fori_loop(0, slot_count, one_slot, 0, unroll=4)

    @pl.when(jnp.logical_not(learned))
    def _():
        table = jnp.concatenate([site[...], rim_a[...], rim_b[...]], axis=1)
        entry[...] = table.T
        tx, ty, tz = site[0:1, :], site[1:2, :], site[2:3, :]

        def some_rows(j, acc):
            start = pl.multiple_of(j * CHUNK, CHUNK)
            ids = lax.broadcasted_iota(jnp.int32, (CHUNK, width), 0) + start
            count = jnp.zeros((CHUNK, width), F32)
            for k in range(slot_count):
                count = count + jnp.where(ids == slots[k : k + 1, :], 1.0, 0.0)
            cols = entry[pl.ds(start, CHUNK), :]
            rx, ry, rz = tx - cols[:, 0:1], ty - cols[:, 1:2], tz - cols[:, 2:3]
            inverse = lax.rsqrt(rx * rx + ry * ry + rz * rz + SMOOTH)
            squared = inverse * inverse
            cube = count * (squared * inverse)
            w3[pl.ds(start, CHUNK), :] = cube
            w5[pl.ds(start, CHUNK), :] = 3.0 * (cube * squared)
            scale = cols[:, 3:4] * cube
            return acc[0] + rx * scale, acc[1] + ry * scale, acc[2] + rz * scale

        nil = jnp.zeros((CHUNK, width), F32)
        sums = lax.fori_loop(0, depth // CHUNK, some_rows, (nil, nil, nil))
        fixed[...] = jnp.zeros_like(fixed)
        for axis in range(3):
            fixed[axis : axis + 1, :] = jnp.sum(sums[axis], axis=0, keepdims=True)


def lend_dipoles(dipole, picks, lent_a, lent_b, whole):
    pieces = split3(dipole)
    for row, out in ((0, lent_a), (1, lent_b)):
        found = dot(pieces, one_hot(picks[row : row + 1, :], dipole.shape[1]))
        if whole:
            out[...] = join3(found)
        else:
            out[0:32, :] = jnp.concatenate([found, jnp.zeros((8, found.shape[1]), F32)], 0).astype(BF16)


def lend_lifted(lifted, picks, lent_a, lent_b):
    for row, out in ((0, lent_a), (1, lent_b)):
        out[...] = dot(lifted, one_hot(picks[row : row + 1, :], lifted.shape[1])).astype(BF16)


def sweep(site, w3, w5, fixed, dipole, side_a, side_b, entry, moment):
    width = site.shape[1]
    moment[...] = jnp.concatenate([dipole, side_a, side_b], axis=1).T
    tx, ty, tz = site[0:1, :], site[1:2, :], site[2:3, :]

    def some_rows(j, acc):
        start = pl.multiple_of(j * CHUNK, CHUNK)
        cols, d = entry[pl.ds(start, CHUNK), :], moment[pl.ds(start, CHUNK), :]
        rx, ry, rz = tx - cols[:, 0:1], ty - cols[:, 1:2], tz - cols[:, 2:3]
        dx, dy, dz = d[:, 0:1], d[:, 1:2], d[:, 2:3]
        cube = w3[pl.ds(start, CHUNK), :]
        scale = (rx * dx + ry * dy + rz * dz) * w5[pl.ds(start, CHUNK), :]
        return (
            acc[0] + (rx * scale - dx * cube),
            acc[1] + (ry * scale - dy * cube),
            acc[2] + (rz * scale - dz * cube),
        )

    nil = jnp.zeros((CHUNK, width), F32)
    sums = lax.fori_loop(0, w3.shape[0] // CHUNK, some_rows, (nil, nil, nil), unroll=2)
    induced = jnp.concatenate(
        [jnp.sum(s, axis=0, keepdims=True) for s in sums] + [jnp.zeros((5, width), F32)], axis=0
    )
    return site[4:5, :] * (fixed + induced)


def outside_kernel(
    meta, blocks, near, site, picks, feat_t, in_t, gain_col, fixed,
    outside_row, hidden, lifted, dipole, fixed_all, lent_a, lent_b, cols,
):
    learned = meta[0] == 0
    width = site.shape[1]
    listed = blocks.shape[0]
    for l in range(listed):
        tile = near[blocks[l]]
        cols[l * 128 : l * 128 + 128, :] = jnp.concatenate([tile, tile], axis=0).T
    tx, ty, tz = site[0:1, :], site[1:2, :], site[2:3, :]

    def some_rows(j, acc):
        c = cols[pl.ds(pl.multiple_of(j * CHUNK, CHUNK), CHUNK), :]
        rx, ry, rz = tx - c[:, 0:1], ty - c[:, 1:2], tz - c[:, 2:3]
        inverse = lax.rsqrt(rx * rx + ry * ry + rz * rz + SMOOTH)
        scale = c[:, 3:4] * (inverse * inverse * inverse)
        return acc[0] + rx * scale, acc[1] + ry * scale, acc[2] + rz * scale

    nil = jnp.zeros((CHUNK, width), F32)
    sums = lax.fori_loop(0, listed * 128 // CHUNK, some_rows, (nil, nil, nil), unroll=2)
    field = [jnp.sum(s, axis=0, keepdims=True) for s in sums]
    strength = jnp.sqrt(1.0 + (field[0] * field[0] + field[1] * field[1] + field[2] * field[2]))
    outside_row[...] = jnp.broadcast_to(strength, (8, width))

    @pl.when(learned)
    def _():
        start = (feat_t[...].astype(F32) + gain_col[:, 0:1] * strength).astype(BF16)
        hidden[...] = start
        raised = dot(in_t[0], start).astype(BF16)
        lifted[...] = raised
        lend_lifted(raised, picks, lent_a, lent_b)

    @pl.when(jnp.logical_not(learned))
    def _():
        total = fixed[...] + jnp.concatenate(field + [jnp.zeros((5, width), F32)], axis=0)
        fixed_all[...] = total
        moment = site[4:5, :] * total
        dipole[...] = moment
        lent_a[...] = jnp.zeros_like(lent_a)
        lent_b[...] = jnp.zeros_like(lent_b)
        lend_dipoles(moment, picks, lent_a, lent_b, False)


def message(layer, hidden, lifted, side_a, side_b, third, out_t, node_t, slots, total):
    slot_count, width = slots.shape
    table = jnp.concatenate([lifted[...], side_a[...], side_b[...]], axis=1)
    total[...] = jnp.zeros_like(total)

    def one_slot(k, carry):
        picked = dot(table, one_hot(slots[pl.ds(k, 1), :], table.shape[1]))
        weight = dot(out_t[layer], third[k, layer * 64 : layer * 64 + 64, :])
        total[...] += weight * picked
        return carry

    lax.fori_loop(0, slot_count, one_slot, 0, unroll=4)
    mean = (total[...] * (1.0 / slot_count)).astype(BF16)
    return (hidden[...].astype(F32) + silu(dot(node_t[layer], mean))).astype(BF16)


def round_one_kernel(
    meta, hidden, lifted, side_a, side_b, third, out_t, in_t, node_t, slots, picks,
    site, w3, w5, fixed, dipole, entry,
    hidden_out, lifted_out, lent_a, lent_b, dipole_out, small_a, small_b, total, moment,
):
    learned = meta[0] == 0

    @pl.when(learned)
    def _():
        new = message(0, hidden, lifted, side_a, side_b, third, out_t, node_t, slots, total)
        hidden_out[...] = new
        raised = dot(in_t[1], new).astype(BF16)
        lifted_out[...] = raised
        lend_lifted(raised, picks, lent_a, lent_b)

    @pl.when(jnp.logical_not(learned))
    def _():
        a, b = join3(side_a[0:24, :].astype(F32)), join3(side_b[0:24, :].astype(F32))
        new = sweep(site, w3, w5, fixed[...], dipole[...], a, b, entry, moment)
        dipole_out[...] = new
        lend_dipoles(new, picks, small_a, small_b, True)


def round_two_kernel(
    meta, got_a, got_b, side_a, side_b, site, w3, w5, fixed, dipole, entry, picks,
    lent_a, lent_b, dipole_out, moment,
):
    learned = meta[0] == 0

    @pl.when(learned)
    def _():
        lent_a[...] = got_a[...]
        lent_b[...] = got_b[...]

    @pl.when(jnp.logical_not(learned))
    def _():
        new = sweep(site, w3, w5, fixed[...], dipole[...], side_a[...], side_b[...], entry, moment)
        dipole_out[...] = new
        lent_a[...] = jnp.zeros_like(lent_a)
        lent_b[...] = jnp.zeros_like(lent_b)
        lend_dipoles(new, picks, lent_a, lent_b, False)


def round_three_kernel(
    meta, hidden, lifted, side_a, side_b, third, out_t, node_t, slots, picks, readout,
    site, w3, w5, fixed, dipole, entry,
    charge, dipole_out, small_a, small_b, total, moment,
):
    learned = meta[0] == 0

    @pl.when(learned)
    def _():
        new = message(1, hidden, lifted, side_a, side_b, third, out_t, node_t, slots, total)
        columns = flip(readout[...])
        padded = jnp.concatenate([columns, jnp.zeros((6, columns.shape[1]), F32)], axis=0)
        charge[...] = dot(padded.astype(BF16), new)

    @pl.when(jnp.logical_not(learned))
    def _():
        a, b = join3(side_a[0:24, :].astype(F32)), join3(side_b[0:24, :].astype(F32))
        new = sweep(site, w3, w5, fixed[...], dipole[...], a, b, entry, moment)
        dipole_out[...] = new
        lend_dipoles(new, picks, small_a, small_b, True)


def response_kernel(
    meta, blocks, near, site, charge, outside_row, side_a, side_b, w3, w5, fixed, dipole, entry,
    result, spread, cols, moment, term,
):
    learned = meta[0] == 0
    width = site.shape[1]
    listed = blocks.shape[0]
    spread[...] = jnp.zeros_like(spread)

    def terms(dipoles):
        for l in range(listed):
            tile = near[blocks[l]]
            tx, ty, tz = tile[0:1, :], tile[1:2, :], tile[2:3, :]

            def some_rows(j, acc):
                start = pl.multiple_of(j * 2 * CHUNK, 2 * CHUNK)
                c = cols[pl.ds(start, 2 * CHUNK), :]
                rx, ry, rz = tx - c[:, 0:1], ty - c[:, 1:2], tz - c[:, 2:3]
                inverse = lax.rsqrt(rx * rx + ry * ry + rz * rz + SMOOTH)
                squared = inverse * inverse
                cube = squared * inverse
                if dipoles:
                    dx, dy, dz = c[:, 4:5], c[:, 5:6], c[:, 6:7]
                    scale = (rx * dx + ry * dy + rz * dz) * (3.0 * (cube * squared))
                    return (
                        acc[0] + (rx * scale - dx * cube),
                        acc[1] + (ry * scale - dy * cube),
                        acc[2] + (rz * scale - dz * cube),
                    )
                scale = c[:, 3:4] * cube
                return acc[0] + rx * scale, acc[1] + ry * scale, acc[2] + rz * scale

            nil = jnp.zeros((2 * CHUNK, 128), F32)
            sums = lax.fori_loop(0, width // (2 * CHUNK), some_rows, (nil, nil, nil), unroll=2)
            for axis in range(3):
                term[l, axis : axis + 1, :] = jnp.sum(sums[axis], axis=0, keepdims=True)
        for l in range(listed):
            spread[blocks[l]] += term[l]

    term[...] = jnp.zeros_like(term)

    @pl.when(learned)
    def _():
        q = charge[...]
        result[...] = jnp.concatenate([q[0:2], outside_row[0:1, :], jnp.zeros((5, width), F32)], axis=0)
        cols[...] = jnp.concatenate([site[0:3, :], q[0:1], jnp.zeros((4, width), F32)], axis=0).T
        terms(False)

    @pl.when(jnp.logical_not(learned))
    def _():
        new = sweep(site, w3, w5, fixed[...], dipole[...], side_a[...], side_b[...], entry, moment)
        result[...] = new
        cols[...] = jnp.concatenate([site[0:4, :], new[0:3], jnp.zeros((1, width), F32)], axis=0).T
        terms(True)


def local(
    positions, charges, polar, features, neighbours, send_rows, blocks,
    radial_in, radial_mid, radial_out, node_in, node_out, field_gain, readout,
):
    width = positions.shape[1]
    slot_count = neighbours.shape[1]
    depth = 2 * width
    half = send_rows.shape[1]
    channels = features.shape[1]
    members = lax.axis_size(DOM)
    group = lax.axis_index("grp")
    index = lax.axis_index(DOM)
    meta = jnp.stack([group, index % 2]).astype(jnp.int32)
    near_pairs = [(i, i ^ 1) for i in range(members)]
    far_pairs = [(i, ((i - 1) ^ 1) + 1) for i in range(1, members - 1)]

    def both_groups(pairs):
        return pairs + [(a + members, b + members) for a, b in pairs]

    def trade(a, b, solvent_only=False):
        shift = [[(x + members, y + members) for x, y in pairs] for pairs in (near_pairs, far_pairs)]
        full = [both_groups(near_pairs), both_groups(far_pairs)]
        used = shift if solvent_only else full
        return lax.ppermute(a, EVERY, used[0]), lax.ppermute(b, EVERY, used[1])

    site, mine, lent_a, lent_b, slots, picks = call(
        rows_kernel,
        [((8, width), F32), ((2, 4, half), F32), ((8, half), F32), ((8, half), F32),
         ((slot_count, width), jnp.int32), ((2, half), jnp.int32)],
        (meta, positions, charges[None], polar[None], neighbours, send_rows), 1,
    )
    partner = lax.ppermute(mine, "grp", [(0, 1), (1, 0)])
    copies = jnp.broadcast_to(partner[None], (members,) + partner.shape)
    near = lax.all_to_all(copies, DOM, 0, 0, tiled=True).reshape(2 * members, 4, half)
    rim_a, rim_b = trade(lent_a, lent_b)
    third, feat_t, out_t, in_t, node_t, gain_col, w3, w5, fixed, entry = call(
        static_kernel,
        [((slot_count, 128, width), BF16), ((channels, width), BF16), ((LAYERS, channels, 64), BF16),
         ((LAYERS, channels, channels), BF16), ((LAYERS, channels, channels), BF16), ((channels, 8), F32),
         ((depth, width), F32), ((depth, width), F32), ((8, width), F32), ((depth, 8), F32)],
        (meta, site, rim_a, rim_b, slots, features, radial_in, radial_mid, radial_out, node_in, node_out,
         field_gain[None]), 1,
    )
    wide = [((channels, half), BF16)] * 2
    small = [((8, half), F32)] * 2
    outside_row, hidden, lifted, dipole, fixed_all, lent_a, lent_b = call(
        outside_kernel,
        [((8, width), F32), ((channels, width), BF16), ((channels, width), BF16), ((8, width), F32),
         ((8, width), F32)] + wide,
        (meta, blocks, near, site, picks, feat_t, in_t, gain_col, fixed), 2,
        [pltpu.VMEM((4 * half, 8), F32)],
    )
    side_a, side_b = trade(lent_a, lent_b)
    moment = pltpu.VMEM((depth, 8), F32)
    total = pltpu.VMEM((channels, width), F32)
    hidden, lifted, lent_a, lent_b, dipole, small_a, small_b = call(
        round_one_kernel,
        [((channels, width), BF16), ((channels, width), BF16)] + wide + [((8, width), F32)] + small,
        (meta, hidden, lifted, side_a, side_b, third, out_t, in_t, node_t, slots, picks,
         site, w3, w5, fixed_all, dipole, entry), 1, [total, moment],
    )
    side_a, side_b = trade(small_a, small_b, True)
    lent_a, lent_b, dipole = call(
        round_two_kernel, wide + [((8, width), F32)],
        (meta, lent_a, lent_b, side_a, side_b, site, w3, w5, fixed_all, dipole, entry, picks), 1, [moment],
    )
    side_a, side_b = trade(lent_a, lent_b)
    charge, dipole, small_a, small_b = call(
        round_three_kernel, [((8, width), F32), ((8, width), F32)] + small,
        (meta, hidden, lifted, side_a, side_b, third, out_t, node_t, slots, picks, readout,
         site, w3, w5, fixed_all, dipole, entry), 1, [total, moment],
    )
    side_a, side_b = trade(small_a, small_b, True)
    result, spread = call(
        response_kernel, [((8, width), F32), ((2 * members, 4, half), F32)],
        (meta, blocks, near, site, charge, outside_row, side_a, side_b, w3, w5, fixed_all, dipole, entry), 2,
        [pltpu.VMEM((width, 8), F32), moment, pltpu.VMEM((4, 4, half), F32)],
    )
    pieces = lax.all_to_all(spread.reshape(members, 2, 4, half), DOM, 0, 0, tiled=True)
    share = lax.ppermute(jnp.sum(pieces, axis=0), "grp", [(0, 1), (1, 0)])
    response = jnp.concatenate([share[0, :3], share[1, :3]], axis=1)
    return result[:3], response


def solution(mesh):
    sites = P(None, EVERY)
    in_specs = (sites, P(EVERY), P(EVERY), P(EVERY, None), P(EVERY, None), sites, P(EVERY)) + (P(),) * 7
    return jax.shard_map(local, mesh=mesh, in_specs=in_specs, out_specs=(sites, sites), check_vma=False)
```

time: 879 us -> 163 us (0.19)
  waiting for transfers between devices: 265 us -> 5.38 us
  blocking collectives: 296 us -> 42.8 us
  local copies, waits for them, and re-layouts: 195 us -> 33 us
  other arithmetic: 45.1 us -> 0.83 us
  Pallas kernels: 0 us -> 21.9 us
  between operations: 14.8 us -> 0.82 us
    all_gather x1 -> x0, blocking collectives: 296 us -> none  [local(): others = lax.all_gather(partner, ('dom', 'sub'), axis=1, tiled=True)]
    psum x1 -> x0, waiting for transfers between devices: 261 us -> none  [local(): total = lax.psum(scattered, ('dom', 'sub'))]
    gather x22 -> x0, local copies, waits for them, and re-layouts: 183 us -> none  [the longest x4 112 us: local(): t[:, slot_major]]
    all_to_all x0 -> x1, blocking collectives: none -> 42.8 us  [local(): lax.all_to_all(spread.reshape(members, 2, 4, half), DOM, 0, 0, tiled=True)]
    reduce_sum x23 -> x1, other arithmetic: 38.3 us -> 0.15 us  [local(): share = lax.ppermute(jnp.sum(pieces, axis=0), 'grp', [(0, 1), (1, 0)])]
    unnamed x34 -> x88, local copies, waits for them, and re-layouts: 4.89 us -> 31.6 us
    pallas_call x0 -> x7, Pallas kernels: none -> 21.9 us  [call(): pl.pallas_call(body, out_shape=[jax.ShapeDtypeStruct(s, d) for s, d in ou...]
    ppermute x16 -> x12, starting transfers between devices: 60.5 us -> 42.9 us  [the longest x10 39.6 us: trade(): return (lax.ppermute(a, EVERY, used[0]), lax.ppermute(b, EVERY, used[1]))]
  transfers between devices with their start and end apart: 17 -> 13, of which waited for: 5 -> 6; matrix products, arithmetic and copies ran while one was open for 17% -> 1% of each run, Pallas kernels for 0% -> 2%
where the time goes in v1:
time: 163 us; the launch traced here: 162 us
  starting transfers between devices  57.2 us (35%)
  blocking collectives  42.8 us (26%)
  local copies, waits for them, and re-layouts  33 us (20%)
  Pallas kernels  21.9 us (13%)
  waiting for transfers between devices  5.38 us (3%)
    all_to_all x1, blocking collectives, local(): lax.all_to_all(spread.reshape(members, 2, 4, half), DOM, 0, 0, tiled=True)  42.8 us
    ppermute x10, starting transfers between devices, trade(): return (lax.ppermute(a, EVERY, used[0]), lax.ppermute(b, EVERY, used[1]))  39.6 us
    unnamed x88, local copies, waits for them, and re-layouts  31.6 us
    pallas_call x7, Pallas kernels, call(): pl.pallas_call(body, out_shape=[jax.ShapeDtypeStruct(s, d) for s, d in ou...  21.9 us
    all_to_all x1, starting transfers between devices, local(): lax.all_to_all(copies, DOM, 0, 0, tiled=True).reshape(2 * members, 4, half)  14.3 us
    ppermute x10, waiting for transfers between devices, trade(): return (lax.ppermute(a, EVERY, used[0]), lax.ppermute(b, EVERY, used[1]))  4 us
  transfers between devices with their start and end apart: 13, of which 6 were waited for; matrix products, arithmetic and copies ran while one was open for 1% of the time, Pallas kernels for 2%

profile of v1, /device:TPU:1, one launch (start us, length us, event | category | flops | bytes accessed | tf_op | source)
XLA Modules:
  0.0 161.9 jit_solution(7793208181009628332)
XLA Ops:
  0.6 0.9 copy.16.neighbours
  1.6 0.7 copy-done.36
  2.3 0.7 copy-done.39
  3.0 0.7 copy-done.40
  3.6 0.7 copy-done.41
  4.3 0.7 shard_map.149
  5.0 0.6 copy-done.5
  6.2 3.2 %collective-permute-start = (f32[2,4,128]{2,1,0:T(4,128)S(1)}, f32[2,4,128]{2,1,0:T(4,128)S(1)}, u32[]{:S(2)}, u32[]{:S(2)}) collective-permute-start(f32[2,4,128]{2,1,0:T(4,128)S(1)} %get-tuple-element.41), channel_id=1, source_target_pairs={{0,128},{128,0},{1,129},{129,1},{2,130},{130,2},{3,131},{131,3},{4... | collective-permute-start | bytes 12296 | tf_op jit(solution)/shard_map/ppermute | solution.py:410
  9.4 0.8 collective-permute-done
  10.2 0.9 broadcast_in_dim.17
  11.1 14.3 %all-to-all-start = ((f32[128,2,4,128]{3,2,1,0:T(4,128)}), f32[128,2,4,128]{3,2,1,0:T(4,128)}, u32[]{:S(2)}, u32[]{:S(2)}) async-start(f32[128,2,4,128]{3,2,1,0:T(4,128)} %broadcast_in_dim.17), calls=%async_computation | async-start | bytes 1048576 | tf_op jit(solution)/shard_map/all_to_all | solution.py:412
  25.4 2.1 %collective-permute-start.1 = (f32[8,128]{1,0:T(8,128)S(1)}, f32[8,128]{1,0:T(8,128)S(1)}, u32[]{:S(2)}, u32[]{:S(2)}) collective-permute-start(f32[8,128]{1,0:T(8,128)S(1)} %get-tuple-element.44), channel_id=1, source_target_pairs={{0,1},{1,0},{2,3},{3,2},{4,5},{5,4},{6,7},{7,6},{8,9},{9,8},{10,11... | collective-permute-start | bytes 12296 | tf_op jit(solution)/shard_map/ppermute | solution.py:402
  27.5 0.6 collective-permute-start.2
  28.2 1.7 %collective-permute-done.1.rim_a = f32[8,128]{1,0:T(8,128)S(1)} collective-permute-done((f32[8,128]{1,0:T(8,128)S(1)}, f32[8,128]{1,0:T(8,128)S(1)}, u32[]{:S(2)}, u32[]{:S(2)}) %collective-permute-start.1) | collective-permute-done | bytes 4128 | tf_op jit(solution)/shard_map/ppermute | solution.py:402
  29.9 0.8 copy-done.6
  30.7 0.9 copy-done.10
  31.6 0.9 copy-done.11
  32.6 0.9 copy-done.16
  33.5 0.8 copy-done.21
  34.3 0.8 copy-done.22
  35.1 0.7 copy-done.35
  35.8 0.7 copy-done.42
  36.5 3.8 %shard_map.150 = (bf16[32,128,256]{2,1,0:T(8,128)(2,1)S(1)}, bf16[256,256]{1,0:T(8,128)(2,1)S(1)}, bf16[2,256,64]{2,1,0:T(8,128)(2,1)S(1)}, bf16[2,256,256]{2,1,...) custom-call(s32[2]{0:T(128)S(1)} %pad_add_fusion.meta, ...), custom_call_target="tpu_custom_call" | custom-call | tf_op jit(solution)/shard_map/pallas_call | solution.py:22
  40.3 0.7 copy-done
  41.0 0.7 copy-done.3
  41.7 0.6 copy-done.17
  42.3 0.7 copy-done.19
  43.6 0.9 copy-done.4
  44.6 0.9 copy-done.18
  45.5 0.9 copy-done.20
  46.4 0.7 copy-done.24
  47.0 0.7 copy-done.27
  47.7 0.7 copy-done.34
  48.4 0.7 copy-done.37
  49.0 3.0 %shard_map.151 = (f32[8,256]{1,0:T(8,128)S(1)}, bf16[256,256]{1,0:T(8,128)(2,1)S(1)}, bf16[256,256]{1,0:T(8,128)(2,1)S(1)}, f32[8,256]{1,0:T(8,128)S(1)}, f32[8,...) custom-call(s32[2]{0:T(128)S(1)} %copy-done.24, s32[4]{0:T(128)S(1)} %copy-done.37, ...), custom_call_target="tpu_custom_call" | custom-call | tf_op jit(solution)/shard_map/pallas_call | solution.py:22
  52.0 5.8 %collective-permute-start.3 = (bf16[256,128]{1,0:T(8,128)(2,1)S(1)}, bf16[256,128]{1,0:T(8,128)(2,1)S(1)}, u32[]{:S(2)}, u32[]{:S(2)}) collective-permute-start(bf16[256,128]{1,0:T(8,128)(2,1)S(1)} %get-tuple-element.53), channel_id=1, source_target_pairs={{0,1},{1,0},{2,3},{3,2},{4,5},{5,4},{6,7},{7,6},{8,9},{9,8},{10,11... | collective-permute-start | bytes 196616 | tf_op jit(solution)/shard_map/ppermute | solution.py:402
  57.9 0.7 collective-permute-start.4
  58.5 1.0 collective-permute-done.3.side_a
  59.5 0.9 copy-done.1
  60.5 0.8 copy-done.7
  61.2 2.6 %shard_map.152 = (bf16[256,256]{1,0:T(8,128)(2,1)S(1)}, bf16[256,256]{1,0:T(8,128)(2,1)S(1)}, bf16[256,128]{1,0:T(8,128)(2,1)S(1)}, bf16[256,128]{1,0:T(8,128)(2...) custom-call(s32[2]{0:T(128)S(1)} %copy-done.24, ...), custom_call_target="tpu_custom_call" | custom-call | tf_op jit(solution)/shard_map/pallas_call | solution.py:22
  63.9 0.6 copy-done.12
  64.5 0.7 copy-done.14
  65.2 7.7 %collective-permute-start.5 = (f32[8,128]{1,0:T(8,128)S(1)}, f32[8,128]{1,0:T(8,128)S(1)}, u32[]{:S(2)}, u32[]{:S(2)}) collective-permute-start(f32[8,128]{1,0:T(8,128)S(1)} %get-tuple-element.67), channel_id=1, source_target_pairs={{128,129},{129,128},{130,131},{131,130},{132,133},{133,132},{134,1... | collective-permute-start | bytes 12296 | tf_op jit(solution)/shard_map/ppermute | solution.py:402
  72.9 0.7 collective-permute-start.6
  73.9 3.3 %shard_map.153 = (bf16[256,128]{1,0:T(8,128)(2,1)}, bf16[256,128]{1,0:T(8,128)(2,1)}, f32[8,256]{1,0:T(8,128)S(1)}) custom-call(s32[2]{0:T(128)S(1)} %copy-done.24, bf16[256,128]{1,0:T(8,128)(2,1)S(1)} %get-tuple-element.65.got_a, bf16[256,128]{1,0:T(8,128)(2,1)S(1)} %get-tuple-element.66.got_b, f32[8,128]{1,0:T(8,128)S(1)} %collective-permute-done.5.side_a, ...), custom_call_target="tpu_custom_call" | custom-call | tf_op jit(solution)/shard_map/pallas_call | solution.py:22
  77.8 7.7 %collective-permute-start.7 = (bf16[256,128]{1,0:T(8,128)(2,1)}, bf16[256,128]{1,0:T(8,128)(2,1)}, u32[]{:S(2)}, u32[]{:S(2)}) collective-permute-start(bf16[256,128]{1,0:T(8,128)(2,1)} %get-tuple-element.70), channel_id=1, source_target_pairs={{0,1},{1,0},{2,3},{3,2},{4,5},{5,4},{6,7},{7,6},{8,9},{9,8},{10,11... | collective-permute-start | bytes 196616 | tf_op jit(solution)/shard_map/ppermute | solution.py:402
  85.5 1.3 collective-permute-start.8
  86.8 1.4 copy.17.readout
  88.2 0.9 copy-done.2
  89.2 0.8 copy-done.8
  89.9 0.8 copy-done.9
  90.8 0.9 copy-done.13
  91.7 0.9 copy-done.15
  92.6 0.7 copy-done.25
  93.2 0.7 copy-done.28
  93.9 0.7 copy-done.32
  94.6 3.0 %shard_map.154 = (f32[8,256]{1,0:T(8,128)S(1)}, f32[8,256]{1,0:T(8,128)S(1)}, f32[8,128]{1,0:T(8,128)S(1)}, f32[8,128]{1,0:T(8,128)S(1)}) custom-call(s32[2]{0:T(128)S(1)} %copy-done.25, bf16[256,256]{1,0:T(8,128)(2,1)S(1)} %copy-done.13, bf16[256,256]{1,0:T(8,128)(2,1)S(1)} %copy-done.15, bf16[256,128]{1,0:T(8,128)(2,1)} %collective-permute-done.7.side_a, ...), custom_call_target="tpu_custom_call" | custom-call | tf_op jit(solution)/shard_map/pallas_call | solution.py:22
  97.6 0.7 collective-permute-start.10
  98.3 12.3 %collective-permute-start.9 = (f32[8,128]{1,0:T(8,128)S(1)}, f32[8,128]{1,0:T(8,128)S(1)}, u32[]{:S(2)}, u32[]{:S(2)}) collective-permute-start(f32[8,128]{1,0:T(8,128)S(1)} %get-tuple-element.75), channel_id=1, source_target_pairs={{128,129},{129,128},{130,131},{131,130},{132,133},{133,132},{134,1... | collective-permute-start | bytes 12296 | tf_op jit(solution)/shard_map/ppermute | solution.py:402
  110.6 1.0 collective-permute-done.9.side_a
  111.6 5.5 %shard_map.155 = (f32[8,256]{1,0:T(8,128)S(1)}, f32[256,4,128]{2,1,0:T(4,128)S(1)}) custom-call(s32[2]{0:T(128)S(1)} %copy-done.25, s32[4]{0:T(128)S(1)} %copy-done.38, f32[256,4,128]{2,1,0:T(4,128)} %bitcast.4.near, f32[8,256]{1,0:T(8,128)S(1)} %get-tuple-element.42.site, f32[8,256]{1,0:T(8,128)S(1)} %get-tuple-element.73.charge, f32[8,256]{1,0:T(8,128)S(1)} %copy-done.30, ...), custom_call_target="tpu_custom_call" | custom-call | tf_op jit(solution)/shard_map/pallas_call | solution.py:22
  117.1 42.8 %all_to_all.10 = f32[128,2,4,128]{3,2,1,0:T(4,128)S(1)} all-to-all(f32[128,2,4,128]{3,2,1,0:T(4,128)S(1)} %bitcast.11), channel_id=1, replica_groups=mesh['grp'=2,'dom'=64,'sub'=2] {'dom','sub'}, dimensions={0} | all-to-all | bytes 1048576 | tf_op jit(solution)/shard_map/all_to_all | solution.py:457
  161.3 0.6 pad_maximum_fusion
  (64 shorter events, 3.6 us)
Async XLA Ops:
  1.6 42.0 %copy-start.23 = (s32[2]{0:T(128)}, s32[2]{0:T(128)S(1)}, u32[]{:S(2)}) copy-start(s32[2]{0:T(128)S(1)} %pad_add_fusion.meta) | copy-start | bytes 28
  1.6 0.7 copy-start.36
  2.3 0.7 copy-start.39
  3.0 0.7 copy-start.40
  3.6 0.7 copy-start.41
  5.0 0.6 copy-start.5
  5.6 0.6 copy-start.26
  6.2 4.1 %collective-permute-start = (f32[2,4,128]{2,1,0:T(4,128)S(1)}, f32[2,4,128]{2,1,0:T(4,128)S(1)}, u32[]{:S(2)}, u32[]{:S(2)}) collective-permute-start(f32[2,4,128]{2,1,0:T(4,128)S(1)} %get-tuple-element.41), channel_id=1, source_target_pairs={{0,128},{128,0},{1,129},{129,1},{2,130},{130,2},{3,131},{131,3},{4... | collective-permute-start | bytes 12296 | tf_op jit(solution)/shard_map/ppermute | solution.py:410
  11.1 32.5 %all-to-all-start = ((f32[128,2,4,128]{3,2,1,0:T(4,128)}), f32[128,2,4,128]{3,2,1,0:T(4,128)}, u32[]{:S(2)}, u32[]{:S(2)}) async-start(f32[128,2,4,128]{3,2,1,0:T(4,128)} %broadcast_in_dim.17), calls=%async_computation | async-start | bytes 1048576 | tf_op jit(solution)/shard_map/all_to_all | solution.py:412
  25.4 4.4 %collective-permute-start.1 = (f32[8,128]{1,0:T(8,128)S(1)}, f32[8,128]{1,0:T(8,128)S(1)}, u32[]{:S(2)}, u32[]{:S(2)}) collective-permute-start(f32[8,128]{1,0:T(8,128)S(1)} %get-tuple-element.44), channel_id=1, source_target_pairs={{0,1},{1,0},{2,3},{3,2},{4,5},{5,4},{6,7},{7,6},{8,9},{9,8},{10,11... | collective-permute-start | bytes 12296 | tf_op jit(solution)/shard_map/ppermute | solution.py:402
  27.5 2.4 %collective-permute-start.2 = (f32[8,128]{1,0:T(8,128)S(1)}, f32[8,128]{1,0:T(8,128)S(1)}, u32[]{:S(2)}, u32[]{:S(2)}) collective-permute-start(f32[8,128]{1,0:T(8,128)S(1)} %get-tuple-element.45), channel_id=1, source_target_pairs={{1,2},{2,1},{3,4},{4,3},{5,6},{6,5},{7,8},{8,7},{9,10},{10,9},{11,... | collective-permute-start | bytes 12296 | tf_op jit(solution)/shard_map/ppermute | solution.py:402
  29.9 0.8 copy-start.6
  30.7 0.9 copy-start.10
  31.6 0.9 copy-start.11
  32.6 0.9 copy-start.16
  33.5 0.8 copy-start.21
  34.3 0.8 copy-start.22
  35.1 0.7 copy-start.35
  35.8 0.7 copy-start.42
  40.3 0.7 copy-start
  41.0 0.7 copy-start.3
  41.7 0.6 copy-start.17
  42.3 0.7 copy-start.19
  43.0 0.6 copy-start.33
  43.6 1.0 copy-start.4
  44.6 0.9 copy-start.18
  45.5 0.9 copy-start.20
  46.4 0.7 copy-start.24
  47.0 0.7 copy-start.27
  47.7 0.7 copy-start.34
  48.4 0.7 copy-start.37
  52.0 11.9 %copy-start.29 = (f32[8,256]{1,0:T(8,128)}, f32[8,256]{1,0:T(8,128)S(1)}, u32[]{:S(2)}) copy-start(f32[8,256]{1,0:T(8,128)S(1)} %get-tuple-element.74.outside_row) | copy-start | bytes 24580
  52.0 7.5 %collective-permute-start.3 = (bf16[256,128]{1,0:T(8,128)(2,1)S(1)}, bf16[256,128]{1,0:T(8,128)(2,1)S(1)}, u32[]{:S(2)}, u32[]{:S(2)}) collective-permute-start(bf16[256,128]{1,0:T(8,128)(2,1)S(1)} %get-tuple-element.53), channel_id=1, source_target_pairs={{0,1},{1,0},{2,3},{3,2},{4,5},{5,4},{6,7},{7,6},{8,9},{9,8},{10,11... | collective-permute-start | bytes 196616 | tf_op jit(solution)/shard_map/ppermute | solution.py:402
  57.9 1.7 %collective-permute-start.4 = (bf16[256,128]{1,0:T(8,128)(2,1)S(1)}, bf16[256,128]{1,0:T(8,128)(2,1)S(1)}, u32[]{:S(2)}, u32[]{:S(2)}) collective-permute-start(bf16[256,128]{1,0:T(8,128)(2,1)S(1)} %get-tuple-element.54), channel_id=1, source_target_pairs={{1,2},{2,1},{3,4},{4,3},{5,6},{6,5},{7,8},{8,7},{9,10},{10,9},{11,... | collective-permute-start | bytes 196616 | tf_op jit(solution)/shard_map/ppermute | solution.py:402
  59.5 1.0 copy-start.1
  60.5 0.8 copy-start.7
  63.9 0.7 copy-start.12
  64.5 0.7 copy-start.14
  65.2 8.7 %collective-permute-start.5 = (f32[8,128]{1,0:T(8,128)S(1)}, f32[8,128]{1,0:T(8,128)S(1)}, u32[]{:S(2)}, u32[]{:S(2)}) collective-permute-start(f32[8,128]{1,0:T(8,128)S(1)} %get-tuple-element.67), channel_id=1, source_target_pairs={{128,129},{129,128},{130,131},{131,130},{132,133},{133,132},{134,1... | collective-permute-start | bytes 12296 | tf_op jit(solution)/shard_map/ppermute | solution.py:402
  72.9 1.0 collective-permute-start.6
  77.2 0.6 copy-start.31
  77.8 10.5 %collective-permute-start.7 = (bf16[256,128]{1,0:T(8,128)(2,1)}, bf16[256,128]{1,0:T(8,128)(2,1)}, u32[]{:S(2)}, u32[]{:S(2)}) collective-permute-start(bf16[256,128]{1,0:T(8,128)(2,1)} %get-tuple-element.70), channel_id=1, source_target_pairs={{0,1},{1,0},{2,3},{3,2},{4,5},{5,4},{6,7},{7,6},{8,9},{9,8},{10,11... | collective-permute-start | bytes 196616 | tf_op jit(solution)/shard_map/ppermute | solution.py:402
  85.5 2.7 %collective-permute-start.8 = (bf16[256,128]{1,0:T(8,128)(2,1)}, bf16[256,128]{1,0:T(8,128)(2,1)}, u32[]{:S(2)}, u32[]{:S(2)}) collective-permute-start(bf16[256,128]{1,0:T(8,128)(2,1)} %get-tuple-element.71), channel_id=1, source_target_pairs={{1,2},{2,1},{3,4},{4,3},{5,6},{6,5},{7,8},{8,7},{9,10},{10,9},{11,... | collective-permute-start | bytes 196616 | tf_op jit(solution)/shard_map/ppermute | solution.py:402
  88.2 1.0 copy-start.2
  89.2 0.8 copy-start.8
  89.9 0.8 copy-start.9
  90.8 0.9 copy-start.13
  91.7 0.9 copy-start.15
  92.6 0.7 copy-start.25
  93.2 0.7 copy-start.28
  93.9 0.7 copy-start.32
  94.6 17.0 %copy-start.30 = (f32[8,256]{1,0:T(8,128)S(1)}, f32[8,256]{1,0:T(8,128)}, u32[]{:S(2)}) copy-start(f32[8,256]{1,0:T(8,128)} %copy-done.29) | copy-start | bytes 24580
  94.6 17.0 %copy-start.38 = (s32[4]{0:T(128)S(1)}, s32[4]{0:T(128)}, u32[]{:S(2)}) copy-start(s32[4]{0:T(128)} %blocks.3) | copy-start | bytes 52
  97.6 13.0 %collective-permute-start.10 = (f32[8,128]{1,0:T(8,128)S(1)}, f32[8,128]{1,0:T(8,128)S(1)}, u32[]{:S(2)}, u32[]{:S(2)}) collective-permute-start(f32[8,128]{1,0:T(8,128)S(1)} %get-tuple-element.76), channel_id=1, source_target_pairs={{129,130},{130,129},{131,132},{132,131},{133,134},{134,133},{135,1... | collective-permute-start | bytes 12296 | tf_op jit(solution)/shard_map/ppermute | solution.py:402
  98.3 13.3 %collective-permute-start.9 = (f32[8,128]{1,0:T(8,128)S(1)}, f32[8,128]{1,0:T(8,128)S(1)}, u32[]{:S(2)}, u32[]{:S(2)}) collective-permute-start(f32[8,128]{1,0:T(8,128)S(1)} %get-tuple-element.75), channel_id=1, source_target_pairs={{128,129},{129,128},{130,131},{131,130},{132,133},{133,132},{134,1... | collective-permute-start | bytes 12296 | tf_op jit(solution)/shard_map/ppermute | solution.py:402
  160.1 1.2 collective-permute-start.11

commit v2 on v1

v2 whole, which is shorter than its diff:
```python
import jax
import jax.numpy as jnp
from jax import lax
from jax.experimental import pallas as pl
from jax.experimental.pallas import tpu as pltpu
from jax.sharding import PartitionSpec as P

BASIS = 8
LAYERS = 2
SMOOTH = 1.0
SPACING = 0.75
DOM = ("dom", "sub")
EVERY = ("grp", "dom", "sub")
F32 = jnp.float32
BF16 = jnp.bfloat16
VMEM = pl.BlockSpec(memory_space=pltpu.VMEM)
ANY = pl.BlockSpec(memory_space=pl.ANY)
CHUNK = 16


def call(body, outs, held, far=(), scratch=(), copies=0, far_outs=0, loose=0):
    return pl.pallas_call(
        body,
        out_shape=[jax.ShapeDtypeStruct(s, d) for s, d in outs[: len(outs) - far_outs]]
        + [pltpu.HBM(s, d) for s, d in outs[len(outs) - far_outs :]],
        in_specs=[VMEM] * len(held) + [ANY] * len(far),
        out_specs=[VMEM] * (len(outs) - far_outs) + [ANY] * far_outs,
        scratch_shapes=list(scratch) + ([pltpu.SemaphoreType.DMA((copies,))] if copies else []),
        compiler_params=pltpu.CompilerParams(vmem_limit_bytes=24 * 2**20),
    )(*held, *far[:loose], *[pltpu.with_memory_space_constraint(a, pltpu.HBM) for a in far[loose:]])


def fetch(pairs, done, first=0):
    copies = [pltpu.make_async_copy(a, b, done.at[first + i]) for i, (a, b) in enumerate(pairs)]
    for c in copies:
        c.start()

    def wait():
        for c in copies:
            c.wait()

    return wait


def learned():
    return lax.axis_index("grp") == 0


def dot(a, b):
    return jnp.dot(a, b, preferred_element_type=F32)


def silu(x):
    half = 0.5 * x
    return half + half * jnp.tanh(half)


def flip(x):
    return x.astype(F32).T


def split3(x):
    high = x.astype(BF16)
    rest = x - high.astype(F32)
    mid = rest.astype(BF16)
    low = (rest - mid.astype(F32)).astype(BF16)
    return jnp.concatenate([high, mid, low], axis=0)


def join3(x):
    return x[0:8] + x[8:16] + x[16:24]


def one_hot(row, depth):
    ids = lax.broadcasted_iota(jnp.int32, (depth, row.shape[1]), 0)
    return jnp.where(ids == row, 1.0, 0.0).astype(BF16)


def rows(parts, count=8):
    have = sum(p.shape[0] for p in parts)
    return jnp.concatenate(list(parts) + [jnp.zeros((count - have, parts[0].shape[1]), F32)], axis=0)


def rows_kernel(
    pos_far, charge_far, polar_far, table_far, send_far, blocks_far,
    site, mine, lent_a, lent_b, slots, picks,
    pos, charge, polar, table, send, blocks, done,
):
    pairs = ((pos_far, pos), (charge_far, charge), (polar_far, polar), (table_far, table), (send_far, send))
    wait = fetch(pairs + ((blocks_far, blocks),), done)
    odd = lax.axis_index("sub")
    width = pos.shape[1]
    wait()
    sites = rows([pos[...], charge[...], polar[...]])
    site[...] = sites
    for half in range(2):
        mine[half] = sites[0:4, half * 128 : half * 128 + 128]
    first, second = send[0:1, :], send[1:2, :]
    swap = jnp.full(first.shape, odd, jnp.int32) == 1
    picks[0:1, :] = jnp.where(swap, second, first)
    picks[1:2, :] = jnp.where(swap, first, second)
    lane = lax.broadcasted_iota(jnp.int32, (1, 128), 1)
    listed = jnp.zeros((1, 128), jnp.int32)
    for l in range(blocks.shape[0]):
        listed = jnp.where(lane == l, blocks[l], listed)
    pieces = split3(sites)
    for row, out in ((0, lent_a), (1, lent_b)):
        found = join3(dot(pieces, one_hot(picks[row : row + 1, :], width)))
        out[...] = rows([found[0:5], listed.astype(F32), jnp.ones((1, 128), F32)])
    raw = table[...]
    other = jnp.where((raw >= 256) & (raw < 512), jnp.bitwise_xor(raw, 128), raw)
    keep = jnp.full(raw.shape, odd, jnp.int32) == 1
    slots[...] = jnp.where(keep, raw, other)


def static_kernel(
    site, rim_a, rim_b, slots, picks, features_far,
    feat_t, w3, w5, fixed, entry, lent_a, lent_b, features, done,
):
    width = site.shape[1]
    depth = 2 * width
    slot_count = slots.shape[0]

    @pl.when(learned())
    def _():
        fetch(((features_far, features),), done)()
        flipped = flip(features[...]).astype(BF16)
        feat_t[...] = flipped
        lend_channels(flipped, picks, lent_a, lent_b)

    @pl.when(jnp.logical_not(learned()))
    def _():
        table = jnp.concatenate([site[...], rim_a[...], rim_b[...]], axis=1)
        entry[...] = table.T
        tx, ty, tz = site[0:1, :], site[1:2, :], site[2:3, :]

        def some_rows(j, acc):
            start = pl.multiple_of(j * CHUNK, CHUNK)
            ids = lax.broadcasted_iota(jnp.int32, (CHUNK, width), 0) + start
            count = jnp.zeros((CHUNK, width), F32)
            for k in range(slot_count):
                count = count + jnp.where(ids == slots[k : k + 1, :], 1.0, 0.0)
            cols = entry[pl.ds(start, CHUNK), :]
            rx, ry, rz = tx - cols[:, 0:1], ty - cols[:, 1:2], tz - cols[:, 2:3]
            inverse = lax.rsqrt(rx * rx + ry * ry + rz * rz + SMOOTH)
            squared = inverse * inverse
            cube = count * (squared * inverse)
            w3[pl.ds(start, CHUNK), :] = cube
            w5[pl.ds(start, CHUNK), :] = 3.0 * (cube * squared)
            scale = cols[:, 3:4] * cube
            return acc[0] + rx * scale, acc[1] + ry * scale, acc[2] + rz * scale

        nil = jnp.zeros((CHUNK, width), F32)
        sums = lax.fori_loop(0, depth // CHUNK, some_rows, (nil, nil, nil))
        total = rows([jnp.sum(s, axis=0, keepdims=True) for s in sums])
        fixed[...] = total
        lend_pieces(total, picks, lent_a, lent_b)


def radial_kernel(
    site, rim_a, rim_b, slots, w_in_far, w_mid_far,
    third_far, w_in, w_mid, third, done,
):
    width = site.shape[1]
    depth = 2 * width
    slot_count = slots.shape[0]

    @pl.when(learned())
    def _():
        wait = fetch(((w_in_far, w_in), (w_mid_far, w_mid)), done)
        pieces = split3(jnp.concatenate([site[...], rim_a[...], rim_b[...]], axis=1))
        centres = lax.broadcasted_iota(jnp.int32, (BASIS, width), 0).astype(F32) * SPACING
        wait()
        first_w = jnp.concatenate([flip(w_in[0]), flip(w_in[1])], axis=0).astype(BF16)
        zero = jnp.zeros((64, 64), F32)

        def both(level):
            top = jnp.concatenate([flip(w_mid[0, level]), zero], axis=1)
            bottom = jnp.concatenate([zero, flip(w_mid[1, level])], axis=1)
            return jnp.concatenate([top, bottom], axis=0).astype(BF16)

        second_w, third_w = both(0), both(1)

        def one_slot(k, carry):
            found = join3(dot(pieces, one_hot(slots[pl.ds(k, 1), :], depth)))
            offset = site[...] - found
            squares = offset * offset
            dist_sq = squares[0:1] + squares[1:2] + squares[2:3] + SMOOTH
            gap = jnp.sqrt(dist_sq) - centres
            basis = jnp.exp(-(gap * gap)).astype(BF16)
            hidden = silu(dot(first_w, basis)).astype(BF16)
            hidden = silu(dot(second_w, hidden)).astype(BF16)
            third[k] = silu(dot(third_w, hidden)).astype(BF16)
            return carry

        lax.fori_loop(0, slot_count, one_slot, 0, unroll=4)
        fetch(((third, third_far),), done, 2)()


def lend_pieces(values, picks, lent_a, lent_b):
    pieces = split3(values)
    for row, out in ((0, lent_a), (1, lent_b)):
        found = dot(pieces, one_hot(picks[row : row + 1, :], values.shape[1]))
        out[...] = jnp.zeros_like(out)
        out[0:32, :] = rows([found], 32).astype(BF16)


def lend_whole(values, picks, lent_a, lent_b):
    pieces = split3(values)
    for row, out in ((0, lent_a), (1, lent_b)):
        out[...] = join3(dot(pieces, one_hot(picks[row : row + 1, :], values.shape[1])))


def lend_channels(values, picks, lent_a, lent_b):
    for row, out in ((0, lent_a), (1, lent_b)):
        out[...] = dot(values, one_hot(picks[row : row + 1, :], values.shape[1])).astype(BF16)


def sweep(site, w3, w5, fixed, dipoles, entry, moment):
    width = site.shape[1]
    moment[...] = dipoles.T
    tx, ty, tz = site[0:1, :], site[1:2, :], site[2:3, :]

    def some_rows(j, acc):
        start = pl.multiple_of(j * CHUNK, CHUNK)
        cols, d = entry[pl.ds(start, CHUNK), :], moment[pl.ds(start, CHUNK), :]
        rx, ry, rz = tx - cols[:, 0:1], ty - cols[:, 1:2], tz - cols[:, 2:3]
        dx, dy, dz = d[:, 0:1], d[:, 1:2], d[:, 2:3]
        cube = w3[pl.ds(start, CHUNK), :]
        scale = (rx * dx + ry * dy + rz * dz) * w5[pl.ds(start, CHUNK), :]
        return (
            acc[0] + (rx * scale - dx * cube),
            acc[1] + (ry * scale - dy * cube),
            acc[2] + (rz * scale - dz * cube),
        )

    nil = jnp.zeros((CHUNK, width), F32)
    sums = lax.fori_loop(0, w3.shape[0] // CHUNK, some_rows, (nil, nil, nil), unroll=2)
    return site[4:5, :] * (fixed + rows([jnp.sum(s, axis=0, keepdims=True) for s in sums]))


def message(layer, hidden, table, third, out_t, node_t, slots, total):
    slot_count = slots.shape[0]
    total[...] = jnp.zeros_like(total)

    def one_slot(k, carry):
        picked = dot(table, one_hot(slots[pl.ds(k, 1), :], table.shape[1]))
        weight = dot(out_t, third[k, layer * 64 : layer * 64 + 64, :])
        total[...] += weight * picked
        return carry

    lax.fori_loop(0, slot_count, one_slot, 0, unroll=4)
    mean = (total[...] * (1.0 / slot_count)).astype(BF16)
    return (hidden.astype(F32) + silu(dot(node_t, mean))).astype(BF16)


def charge_field(target, cols, first, count):
    tx, ty, tz = target[0:1, :], target[1:2, :], target[2:3, :]

    def some_rows(j, acc):
        c = cols[pl.ds(pl.multiple_of(first + j * CHUNK, CHUNK), CHUNK), :]
        rx, ry, rz = tx - c[:, 0:1], ty - c[:, 1:2], tz - c[:, 2:3]
        inverse = lax.rsqrt(rx * rx + ry * ry + rz * rz + SMOOTH)
        scale = c[:, 3:4] * (inverse * inverse * inverse)
        return acc[0] + rx * scale, acc[1] + ry * scale, acc[2] + rz * scale

    nil = jnp.zeros((CHUNK, target.shape[1]), F32)
    sums = lax.fori_loop(0, count // CHUNK, some_rows, (nil, nil, nil), unroll=2)
    return jnp.concatenate([jnp.sum(s, axis=0, keepdims=True) for s in sums], axis=0)


def first_kernel(
    site, rim_a, rim_b, slots, picks, feat_t, side_a, side_b, w3, w5, fixed, entry,
    near_far, blocks_far, third_far, node_in_far, node_out_far, w_out_far, gain_far,
    outside_row, near_own, hidden_out, lifted_out, fixed_out, dipole_out, lent_a, lent_b,
    blocks, near, cols, third, node_in, node_out, w_out, gain, total, moment, done,
):
    width = site.shape[1]
    listed = blocks.shape[0]
    wait_blocks = fetch(((blocks_far, blocks),), done)
    weights = (
        (third_far, third), (node_in_far, node_in), (node_out_far.at[0], node_out),
        (w_out_far.at[0], w_out), (gain_far, gain),
    )

    @pl.when(learned())
    def _():
        fetch(weights, done, 1)

    lane = lax.broadcasted_iota(jnp.int32, (1, 128), 1)

    def lent_block(rim, l):
        return jnp.sum(jnp.where(lane == l, rim[5:6, :], 0.0)).astype(jnp.int32)

    numbers = [lent_block(rim, l) for rim in (rim_a, rim_b) for l in range(listed)]
    wait_blocks()
    numbers = [blocks[l] for l in range(listed)] + numbers
    fetch([(near_far.at[b], near.at[i]) for i, b in enumerate(numbers)], done, 6)()
    near_own[...] = near[0:listed]
    for i in range(3 * listed):
        tile = near[i]
        cols[i * 128 : i * 128 + 128, :] = jnp.concatenate([tile, tile], axis=0).T
    reach = listed * 128
    own_field = charge_field(site[...], cols, 0, reach)
    field = jnp.concatenate(
        [own_field, charge_field(rim_a[...], cols, reach, reach), charge_field(rim_b[...], cols, 2 * reach, reach)],
        axis=1,
    )
    strength = jnp.sqrt(1.0 + (field[0:1] * field[0:1] + field[1:2] * field[1:2] + field[2:3] * field[2:3]))
    outside_row[...] = jnp.broadcast_to(strength[:, :width], outside_row.shape)

    @pl.when(learned())
    def _():
        for i, (a, b) in enumerate(weights):
            pltpu.make_async_copy(a, b, done.at[1 + i]).wait()
        gain_col = jnp.broadcast_to(gain[...], (8, width)).T
        features = jnp.concatenate([feat_t[...], side_a[...], side_b[...]], axis=1)
        start = (features.astype(F32) + gain_col[:, 0:1] * strength).astype(BF16)
        present = jnp.concatenate([jnp.ones((1, width), F32), rim_a[6:7, :], rim_b[6:7, :]], axis=1)
        raised = dot(flip(node_in[0]).astype(BF16), start)
        table = jnp.where(present > 0.5, raised, 0.0).astype(BF16)
        out_t, node_t = flip(w_out[...]).astype(BF16), flip(node_out[...]).astype(BF16)
        new = message(0, start[:, :width], table, third, out_t, node_t, slots, total)
        hidden_out[...] = new
        raised = dot(flip(node_in[1]).astype(BF16), new).astype(BF16)
        lifted_out[...] = raised
        lend_channels(raised, picks, lent_a, lent_b)

    @pl.when(jnp.logical_not(learned()))
    def _():
        known = [fixed[...], join3(side_a[0:24, :].astype(F32)), join3(side_b[0:24, :].astype(F32))]
        whole = jnp.concatenate(known, axis=1) + rows([field])
        fixed_out[...] = whole[:, :width]
        polar = jnp.concatenate([site[4:5, :], rim_a[4:5, :], rim_b[4:5, :]], axis=1)
        new = sweep(site, w3, w5, whole[:, :width], polar * whole, entry, moment)
        dipole_out[...] = new
        lend_pieces(new, picks, lent_a, lent_b)


def second_kernel(
    hidden, lifted, side_a, side_b, slots, picks, site, w3, w5, fixed, dipole, entry,
    third_far, node_out_far, w_out_far, readout_far,
    charge, dipole_out, small_a, small_b,
    third, node_out, w_out, readout, total, moment, done,
):
    width = site.shape[1]

    @pl.when(learned())
    def _():
        fetch(
            ((third_far, third), (node_out_far.at[1], node_out), (w_out_far.at[1], w_out), (readout_far, readout)), done
        )()
        table = jnp.concatenate([lifted[...], side_a[...], side_b[...]], axis=1)
        out_t, node_t = flip(w_out[...]).astype(BF16), flip(node_out[...]).astype(BF16)
        new = message(1, hidden[...], table, third, out_t, node_t, slots, total)
        charge[...] = dot(rows([readout[...].astype(F32)]).astype(BF16), new)

    @pl.when(jnp.logical_not(learned()))
    def _():
        sides = [join3(side_a[0:24, :].astype(F32)), join3(side_b[0:24, :].astype(F32))]
        table = jnp.concatenate([dipole[...]] + sides, axis=1)
        new = sweep(site, w3, w5, fixed[...], table, entry, moment)
        dipole_out[...] = new
        lend_whole(new, picks, small_a, small_b)


def third_kernel(side_a, side_b, picks, site, w3, w5, fixed, dipole, entry, dipole_out, small_a, small_b, moment):
    @pl.when(jnp.logical_not(learned()))
    def _():
        table = jnp.concatenate([dipole[...], side_a[...], side_b[...]], axis=1)
        new = sweep(site, w3, w5, fixed[...], table, entry, moment)
        dipole_out[...] = new
        lend_whole(new, picks, small_a, small_b)


def response_kernel(
    near, site, charge, outside_row, side_a, side_b, w3, w5, fixed, dipole, entry, blocks_far,
    result, spread, blocks, cols, moment, term, done,
):
    width = site.shape[1]
    listed = blocks.shape[0]
    wait = fetch(((blocks_far, blocks),), done)
    spread[...] = jnp.zeros_like(spread)
    term[...] = jnp.zeros_like(term)

    def terms(dipoles):
        for l in range(listed):
            tile = near[l]
            tx, ty, tz = tile[0:1, :], tile[1:2, :], tile[2:3, :]

            def some_rows(j, acc):
                start = pl.multiple_of(j * 2 * CHUNK, 2 * CHUNK)
                c = cols[pl.ds(start, 2 * CHUNK), :]
                rx, ry, rz = tx - c[:, 0:1], ty - c[:, 1:2], tz - c[:, 2:3]
                inverse = lax.rsqrt(rx * rx + ry * ry + rz * rz + SMOOTH)
                squared = inverse * inverse
                cube = squared * inverse
                if dipoles:
                    dx, dy, dz = c[:, 4:5], c[:, 5:6], c[:, 6:7]
                    scale = (rx * dx + ry * dy + rz * dz) * (3.0 * (cube * squared))
                    return (
                        acc[0] + (rx * scale - dx * cube),
                        acc[1] + (ry * scale - dy * cube),
                        acc[2] + (rz * scale - dz * cube),
                    )
                scale = c[:, 3:4] * cube
                return acc[0] + rx * scale, acc[1] + ry * scale, acc[2] + rz * scale

            nil = jnp.zeros((2 * CHUNK, 128), F32)
            sums = lax.fori_loop(0, width // (2 * CHUNK), some_rows, (nil, nil, nil), unroll=2)
            for axis in range(3):
                term[l, axis : axis + 1, :] = jnp.sum(sums[axis], axis=0, keepdims=True)

    @pl.when(learned())
    def _():
        q = charge[...]
        result[...] = jnp.concatenate([q[0:2], outside_row[0:1, :]], axis=0)
        cols[...] = rows([site[0:3, :], q[0:1]]).T
        terms(False)

    @pl.when(jnp.logical_not(learned()))
    def _():
        table = jnp.concatenate([dipole[...], side_a[...], side_b[...]], axis=1)
        new = sweep(site, w3, w5, fixed[...], table, entry, moment)
        result[...] = new[0:3]
        cols[...] = rows([site[0:4, :], new[0:3]]).T
        terms(True)

    wait()
    for l in range(listed):
        spread[blocks[l]] += term[l]


def gather_kernel(pieces, share):
    total = jnp.sum(pieces[...], axis=0)
    share[...] = jnp.concatenate([total[0, 0:3], total[1, 0:3]], axis=1)


def local(
    positions, charges, polar, features, neighbours, send_rows, blocks,
    radial_in, radial_mid, radial_out, node_in, node_out, field_gain, readout,
):
    width = positions.shape[1]
    slot_count = neighbours.shape[1]
    depth = 2 * width
    half = send_rows.shape[1]
    channels = features.shape[1]
    listed = blocks.shape[0]
    members = lax.axis_size(DOM)
    near_pairs = [(i, i ^ 1) for i in range(members)]
    far_pairs = [(i, ((i - 1) ^ 1) + 1) for i in range(1, members - 1)]

    def trade(a, b, solvent_only=False):
        used = []
        for pairs in (near_pairs, far_pairs):
            shifted = [(x + members, y + members) for x, y in pairs]
            used.append(shifted if solvent_only else pairs + shifted)
        return lax.ppermute(a, EVERY, used[0]), lax.ppermute(b, EVERY, used[1])

    row8, table8 = ((8, width), F32), ((8, half), F32)
    wide = ((channels, half), BF16)
    by_site = ((channels, width), BF16)
    ints = jnp.int32
    site, mine, lent_a, lent_b, slots, picks = call(
        rows_kernel,
        [row8, ((2, 4, half), F32), table8, table8, ((slot_count, width), ints), ((2, half), ints)],
        (), (positions, charges[None], polar[None], neighbours.T, send_rows, blocks),
        [pltpu.VMEM((3, width), F32), pltpu.VMEM((1, width), F32), pltpu.VMEM((1, width), F32),
         pltpu.VMEM((slot_count, width), ints), pltpu.VMEM((2, half), ints), pltpu.SMEM((listed,), ints)], 6,
    )
    rim_a, rim_b = trade(lent_a, lent_b)
    partner = lax.ppermute(mine, "grp", [(0, 1), (1, 0)])
    partner, rim_a, rim_b = lax.optimization_barrier((partner, rim_a, rim_b))
    copies = jnp.broadcast_to(partner[None], (members,) + partner.shape)
    near = lax.all_to_all(copies, DOM, 0, 0, tiled=True).reshape(2 * members, 4, half)
    feat_t, w3, w5, fixed, entry, lent_a, lent_b = call(
        static_kernel, [by_site, ((depth, width), F32), ((depth, width), F32), row8, ((depth, 8), F32), wide, wide],
        (site, rim_a, rim_b, slots, picks), (features,), [pltpu.VMEM((width, channels), BF16)], 1,
    )
    side_a, side_b = trade(lent_a, lent_b)
    third_shape = (slot_count, LAYERS * radial_in.shape[2], width)
    (third,) = call(
        radial_kernel, [(third_shape, BF16)], (site, rim_a, rim_b, slots), (radial_in, radial_mid),
        [pltpu.VMEM(radial_in.shape, BF16), pltpu.VMEM(radial_mid.shape, BF16), pltpu.VMEM(third_shape, BF16)], 3, 1,
    )
    moment = pltpu.VMEM((depth, 8), F32)
    total = pltpu.VMEM((channels, width), F32)
    square = pltpu.VMEM(node_out.shape[1:], BF16)
    last = pltpu.VMEM(radial_out.shape[1:], BF16)
    outside_row, near_own, hidden, lifted, fixed_all, dipole, lent_a, lent_b = call(
        first_kernel, [row8, ((listed, 4, half), F32), by_site, by_site, row8, row8, wide, wide],
        (site, rim_a, rim_b, slots, picks, feat_t, side_a, side_b, w3, w5, fixed, entry),
        (near, blocks, third, node_in, node_out, radial_out, field_gain[None]),
        [pltpu.SMEM((listed,), ints), pltpu.VMEM((3 * listed, 4, half), F32), pltpu.VMEM((3 * listed * half, 8), F32),
         pltpu.VMEM(third_shape, BF16), pltpu.VMEM(node_in.shape, BF16), square, last,
         pltpu.VMEM((1, channels), F32), total, moment], 6 + 3 * listed, loose=1,
    )
    side_a, side_b = trade(lent_a, lent_b)
    charge, dipole, small_a, small_b = call(
        second_kernel, [row8, row8, table8, table8],
        (hidden, lifted, side_a, side_b, slots, picks, site, w3, w5, fixed_all, dipole, entry),
        (third, node_out, radial_out, readout.T),
        [pltpu.VMEM(third_shape, BF16), square, last, pltpu.VMEM((2, channels), BF16), total, moment], 4,
    )
    side_a, side_b = trade(small_a, small_b, True)
    dipole, small_a, small_b = call(
        third_kernel, [row8, table8, table8], (side_a, side_b, picks, site, w3, w5, fixed_all, dipole, entry),
        (), [moment],
    )
    side_a, side_b = trade(small_a, small_b, True)
    result, spread = call(
        response_kernel, [((3, width), F32), ((2 * members, 4, half), F32)],
        (near_own, site, charge, outside_row, side_a, side_b, w3, w5, fixed_all, dipole, entry), (blocks,),
        [pltpu.SMEM((listed,), ints), pltpu.VMEM((width, 8), F32), moment, pltpu.VMEM((listed, 4, half), F32)], 1,
    )
    pieces = lax.all_to_all(spread.reshape(members, 2, 4, half), DOM, 0, 0, tiled=True)
    (share,) = call(gather_kernel, [((3, width), F32)], (pieces,))
    return result, lax.ppermute(share, "grp", [(0, 1), (1, 0)])


def solution(mesh):
    sites = P(None, EVERY)
    in_specs = (sites, P(EVERY), P(EVERY), P(EVERY, None), P(EVERY, None), sites, P(EVERY)) + (P(),) * 7
    return jax.shard_map(local, mesh=mesh, in_specs=in_specs, out_specs=(sites, sites), check_vma=False)
```

time: 163 us -> 128 us (0.79)
  local copies, waits for them, and re-layouts: 33 us -> 1.46 us
  waiting for transfers between devices: 5.38 us -> 16.2 us
  starting transfers between devices: 57.2 us -> 46.4 us
  blocking collectives: 42.8 us -> 40.5 us
    unnamed x88 -> x1, local copies, waits for them, and re-layouts: 31.6 us -> 0.59 us
    ppermute x10, starting transfers between devices: 39.6 us -> 23.8 us  [trade(): return (lax.ppermute(a, EVERY, used[0]), lax.ppermute(b, EVERY, used[1]))]
    all_to_all x1, waiting for transfers between devices: 0.01 us -> 6.18 us  [local(): lax.all_to_all(copies, DOM, 0, 0, tiled=True).reshape(2 * members, 4, half)]
    all_to_all x1, starting transfers between devices: 14.3 us -> 19.2 us  [local(): lax.all_to_all(copies, DOM, 0, 0, tiled=True).reshape(2 * members, 4, half)]
    ppermute x10, waiting for transfers between devices: 4 us -> 8.85 us  [trade(): return (lax.ppermute(a, EVERY, used[0]), lax.ppermute(b, EVERY, used[1]))]
    all_to_all x1, blocking collectives: 42.8 us -> 40.5 us  [local(): lax.all_to_all(spread.reshape(members, 2, 4, half), DOM, 0, 0, tiled=True)]
    pallas_call x7 -> x8, Pallas kernels: 21.9 us -> 22.1 us  [call(): pl.pallas_call(body, out_shape=[jax.ShapeDtypeStruct(s, d) for s, d in ou...]
  transfers between devices with their start and end apart: 13 -> 13, of which waited for: 6 -> 7; matrix products, arithmetic and copies ran while one was open for 1% -> 0% of each run, Pallas kernels for 2% -> 3%
where the time goes in v2:
time: 128 us; the launch traced here: 127 us
  starting transfers between devices  46.4 us (36%)
  blocking collectives  40.5 us (32%)
  Pallas kernels  22.1 us (17%)
  waiting for transfers between devices  16.2 us (13%)
  local copies, waits for them, and re-layouts  1.46 us (1%)
    all_to_all x1, blocking collectives, local(): lax.all_to_all(spread.reshape(members, 2, 4, half), DOM, 0, 0, tiled=True)  40.5 us
    ppermute x10, starting transfers between devices, trade(): return (lax.ppermute(a, EVERY, used[0]), lax.ppermute(b, EVERY, used[1]))  23.8 us
    pallas_call x8, Pallas kernels, call(): pl.pallas_call(body, out_shape=[jax.ShapeDtypeStruct(s, d) for s, d in ou...  22.1 us
    all_to_all x1, starting transfers between devices, local(): lax.all_to_all(copies, DOM, 0, 0, tiled=True).reshape(2 * members, 4, half)  19.2 us
    ppermute x10, waiting for transfers between devices, trade(): return (lax.ppermute(a, EVERY, used[0]), lax.ppermute(b, EVERY, used[1]))  8.85 us
    all_to_all x1, waiting for transfers between devices, local(): lax.all_to_all(copies, DOM, 0, 0, tiled=True).reshape(2 * members, 4, half)  6.18 us
    ppermute x1, starting transfers between devices, local(): partner = lax.ppermute(mine, 'grp', [(0, 1), (1, 0)])  3.33 us
  transfers between devices with their start and end apart: 13, of which 7 were waited for; matrix products, arithmetic and copies ran while one was open for 0% of the time, Pallas kernels for 3%

profile of v2, /device:TPU:1, one launch (start us, length us, event | category | flops | bytes accessed | tf_op | source)
XLA Modules:
  0.0 127.4 jit_solution(3756974027043557273)
XLA Ops:
  0.6 1.0 shard_map.149
  1.7 3.3 %collective-permute-start = (f32[2,4,128]{2,1,0:T(4,128)S(1)}, f32[2,4,128]{2,1,0:T(4,128)S(1)}, u32[]{:S(2)}, u32[]{:S(2)}) collective-permute-start(f32[2,4,128]{2,1,0:T(4,128)S(1)} %get-tuple-element.36), channel_id=1, source_target_pairs={{0,128},{128,0},{1,129},{129,1},{2,130},{130,2},{3,131},{131,3},{4... | collective-permute-start | bytes 12296 | tf_op jit(solution)/shard_map/ppermute | solution.py:472
  5.0 1.2 collective-permute-start.1
  6.2 0.6 collective-permute-start.2
  6.9 0.0 collective-permute-done
  6.9 2.1 %collective-permute-done.1.rim_a = f32[8,128]{1,0:T(8,128)S(1)} collective-permute-done((f32[8,128]{1,0:T(8,128)S(1)}, f32[8,128]{1,0:T(8,128)S(1)}, u32[]{:S(2)}, u32[]{:S(2)}) %collective-permute-start.1) | collective-permute-done | bytes 4128 | tf_op jit(solution)/shard_map/ppermute | solution.py:458
  9.0 0.0 collective-permute-done.2.rim_b
  9.0 0.9 broadcast_in_dim.17
  9.8 19.2 %all-to-all-start = ((f32[128,2,4,128]{3,2,1,0:T(4,128)}), f32[128,2,4,128]{3,2,1,0:T(4,128)S(1)}, u32[]{:S(2)}, u32[]{:S(2)}) async-start(f32[128,2,4,128]{3,2,1,0:T(4,128)} %broadcast_in_dim.17), calls=%async_computation | async-start | bytes 1048576 | tf_op jit(solution)/shard_map/all_to_all | solution.py:475
  29.0 3.4 %shard_map.150 = (bf16[256,256]{1,0:T(8,128)(2,1)S(1)}, f32[512,256]{1,0:T(8,128)S(1)}, f32[512,256]{1,0:T(8,128)S(1)}, f32[8,256]{1,0:T(8,128)S(1)}, f32[512,8]...) custom-call(f32[8,256]{1,0:T(8,128)S(1)} %get-tuple-element.35.site, ...), custom_call_target="tpu_custom_call" | custom-call | tf_op jit(solution)/shard_map/pallas_call | solution.py:22
  32.5 2.2 %collective-permute-start.3 = (bf16[256,128]{1,0:T(8,128)(2,1)S(1)}, bf16[256,128]{1,0:T(8,128)(2,1)S(1)}, u32[]{:S(2)}, u32[]{:S(2)}) collective-permute-start(bf16[256,128]{1,0:T(8,128)(2,1)S(1)} %get-tuple-element.44), channel_id=1, source_target_pairs={{0,1},{1,0},{2,3},{3,2},{4,5},{5,4},{6,7},{7,6},{8,9},{9,8},{10,11... | collective-permute-start | bytes 196616 | tf_op jit(solution)/shard_map/ppermute | solution.py:458
  34.6 0.7 collective-permute-start.4
  35.3 3.9 %collective-permute-done.3.side_a = bf16[256,128]{1,0:T(8,128)(2,1)S(1)} collective-permute-done((bf16[256,128]{1,0:T(8,128)(2,1)S(1)}, bf16[256,128]{1,0:T(8,128)(2,1)S(1)}, u32[]{:S(2)}, u32[]{:S(2)}) %collective-permute-start.3) | collective-permute-done | bytes 65568 | tf_op jit(solution)/shard_map/ppermute | solution.py:458
  39.2 0.0 collective-permute-done.4.side_b
  39.2 6.2 %all-to-all-done = f32[128,2,4,128]{3,2,1,0:T(4,128)S(1)} async-done(((f32[128,2,4,128]{3,2,1,0:T(4,128)}), f32[128,2,4,128]{3,2,1,0:T(4,128)S(1)}, u32[]{:S(2)}, u32[]{:S(2)}) %all-to-all-start) | async-done | bytes 524320 | tf_op jit(solution)/shard_map/all_to_all | solution.py:475
  45.4 8.1 %shard_map.152 = (f32[8,256]{1,0:T(8,128)S(1)}, f32[4,4,128]{2,1,0:T(4,128)S(1)}, bf16[256,256]{1,0:T(8,128)(2,1)S(1)}, bf16[256,256]{1,0:T(8,128)(2,1)S(1)}, f3...) custom-call(f32[8,256]{1,0:T(8,128)S(1)} %get-tuple-element.35.site, ...), custom_call_target="tpu_custom_call" | custom-call | tf_op jit(solution)/shard_map/pallas_call | solution.py:22
  53.5 1.8 %collective-permute-start.5 = (bf16[256,128]{1,0:T(8,128)(2,1)S(1)}, bf16[256,128]{1,0:T(8,128)(2,1)S(1)}, u32[]{:S(2)}, u32[]{:S(2)}) collective-permute-start(bf16[256,128]{1,0:T(8,128)(2,1)S(1)} %get-tuple-element.54), channel_id=1, source_target_pairs={{0,1},{1,0},{2,3},{3,2},{4,5},{5,4},{6,7},{7,6},{8,9},{9,8},{10,11... | collective-permute-start | bytes 196616 | tf_op jit(solution)/shard_map/ppermute | solution.py:458
  55.4 0.7 collective-permute-start.6
  56.0 2.2 %collective-permute-done.5.side_a = bf16[256,128]{1,0:T(8,128)(2,1)S(1)} collective-permute-done((bf16[256,128]{1,0:T(8,128)(2,1)S(1)}, bf16[256,128]{1,0:T(8,128)(2,1)S(1)}, u32[]{:S(2)}, u32[]{:S(2)}) %collective-permute-start.5) | collective-permute-done | bytes 65568 | tf_op jit(solution)/shard_map/ppermute | solution.py:458
  58.2 0.0 collective-permute-done.6.side_b
  58.2 2.1 %shard_map.153 = (f32[8,256]{1,0:T(8,128)S(1)}, f32[8,256]{1,0:T(8,128)S(1)}, f32[8,128]{1,0:T(8,128)S(1)}, f32[8,128]{1,0:T(8,128)S(1)}) custom-call(bf16[256,256]{1,0:T(8,128)(2,1)S(1)} %get-tuple-element.52.hidden, bf16[256,256]{1,0:T(8,128)(2,1)S(1)} %get-tuple-element.53.lifted, bf16[256,128]{1,0:T(8,128)(2,1)S(1)} %collective-permute-done.5.side_a, ...), custom_call_target="tpu_custom_call" | custom-call | tf_op jit(solution)/shard_map/pallas_call | solution.py:22
  60.4 7.7 %collective-permute-start.7 = (f32[8,128]{1,0:T(8,128)S(1)}, f32[8,128]{1,0:T(8,128)S(1)}, u32[]{:S(2)}, u32[]{:S(2)}) collective-permute-start(f32[8,128]{1,0:T(8,128)S(1)} %get-tuple-element.60), channel_id=1, source_target_pairs={{128,129},{129,128},{130,131},{131,130},{132,133},{133,132},{134,1... | collective-permute-start | bytes 12296 | tf_op jit(solution)/shard_map/ppermute | solution.py:458
  68.1 0.7 collective-permute-start.8
  68.7 0.3 collective-permute-done.7.side_a
  69.0 0.0 collective-permute-done.8.side_b
  69.0 2.1 %shard_map.154 = (f32[8,256]{1,0:T(8,128)S(1)}, f32[8,128]{1,0:T(8,128)S(1)}, f32[8,128]{1,0:T(8,128)S(1)}) custom-call(f32[8,128]{1,0:T(8,128)S(1)} %collective-permute-done.7.side_a, f32[8,128]{1,0:T(8,128)S(1)} %collective-permute-done.8.side_b, s32[2,128]{1,0:T(2,128)S(1)} %get-tuple-element.42.picks, f32[8,256]{1,0:T(8,128)S(1)} %get-tuple-element.35.site, ...), custom_call_target="tpu_custom_call" | custom-call | tf_op jit(solution)/shard_map/pallas_call | solution.py:22
  71.1 7.7 %collective-permute-start.9 = (f32[8,128]{1,0:T(8,128)S(1)}, f32[8,128]{1,0:T(8,128)S(1)}, u32[]{:S(2)}, u32[]{:S(2)}) collective-permute-start(f32[8,128]{1,0:T(8,128)S(1)} %get-tuple-element.63), channel_id=1, source_target_pairs={{128,129},{129,128},{130,131},{131,130},{132,133},{133,132},{134,1... | collective-permute-start | bytes 12296 | tf_op jit(solution)/shard_map/ppermute | solution.py:458
  78.8 0.7 collective-permute-start.10
  79.5 0.3 collective-permute-done.9.side_a
  79.8 0.0 collective-permute-done.10.side_b
  79.8 5.1 %shard_map.155 = (f32[3,256]{1,0:T(4,128)}, f32[256,4,128]{2,1,0:T(4,128)S(1)}) custom-call(f32[4,4,128]{2,1,0:T(4,128)S(1)} %get-tuple-element.51.near, f32[8,256]{1,0:T(8,128)S(1)} %get-tuple-element.35.site, f32[8,256]{1,0:T(8,128)S(1)} %get-tuple-element.58.charge, f32[8,256]{1,0:T(8,128)S(1)} %get-tuple-element.59.outside_row, ...), custom_call_target="tpu_custom_call" | custom-call | tf_op jit(solution)/shard_map/pallas_call | solution.py:22
  84.9 40.5 %all_to_all.10.pieces = f32[128,2,4,128]{3,2,1,0:T(4,128)S(1)} all-to-all(f32[128,2,4,128]{3,2,1,0:T(4,128)S(1)} %bitcast.8), channel_id=1, replica_groups=mesh['grp'=2,'dom'=64,'sub'=2] {'dom','sub'}, dimensions={0} | all-to-all | bytes 1048576 | tf_op jit(solution)/shard_map/all_to_all | solution.py:516
  125.4 0.1 shard_map.156
  125.5 0.1 collective-permute-start.11
  125.6 1.2 collective-permute-done.11
  126.8 0.6 copy.17
  (1 shorter events, 0.0 us)
Async XLA Ops:
  1.7 5.2 %collective-permute-start = (f32[2,4,128]{2,1,0:T(4,128)S(1)}, f32[2,4,128]{2,1,0:T(4,128)S(1)}, u32[]{:S(2)}, u32[]{:S(2)}) collective-permute-start(f32[2,4,128]{2,1,0:T(4,128)S(1)} %get-tuple-element.36), channel_id=1, source_target_pairs={{0,128},{128,0},{1,129},{129,1},{2,130},{130,2},{3,131},{131,3},{4... | collective-permute-start | bytes 12296 | tf_op jit(solution)/shard_map/ppermute | solution.py:472
  5.0 4.0 %collective-permute-start.1 = (f32[8,128]{1,0:T(8,128)S(1)}, f32[8,128]{1,0:T(8,128)S(1)}, u32[]{:S(2)}, u32[]{:S(2)}) collective-permute-start(f32[8,128]{1,0:T(8,128)S(1)} %get-tuple-element.37), channel_id=1, source_target_pairs={{0,1},{1,0},{2,3},{3,2},{4,5},{5,4},{6,7},{7,6},{8,9},{9,8},{10,11... | collective-permute-start | bytes 12296 | tf_op jit(solution)/shard_map/ppermute | solution.py:458
  6.2 2.8 %collective-permute-start.2 = (f32[8,128]{1,0:T(8,128)S(1)}, f32[8,128]{1,0:T(8,128)S(1)}, u32[]{:S(2)}, u32[]{:S(2)}) collective-permute-start(f32[8,128]{1,0:T(8,128)S(1)} %get-tuple-element.38), channel_id=1, source_target_pairs={{1,2},{2,1},{3,4},{4,3},{5,6},{6,5},{7,8},{8,7},{9,10},{10,9},{11,... | collective-permute-start | bytes 12296 | tf_op jit(solution)/shard_map/ppermute | solution.py:458
  9.8 35.6 %all-to-all-start = ((f32[128,2,4,128]{3,2,1,0:T(4,128)}), f32[128,2,4,128]{3,2,1,0:T(4,128)S(1)}, u32[]{:S(2)}, u32[]{:S(2)}) async-start(f32[128,2,4,128]{3,2,1,0:T(4,128)} %broadcast_in_dim.17), calls=%async_computation | async-start | bytes 1048576 | tf_op jit(solution)/shard_map/all_to_all | solution.py:475
  32.5 6.8 %collective-permute-start.3 = (bf16[256,128]{1,0:T(8,128)(2,1)S(1)}, bf16[256,128]{1,0:T(8,128)(2,1)S(1)}, u32[]{:S(2)}, u32[]{:S(2)}) collective-permute-start(bf16[256,128]{1,0:T(8,128)(2,1)S(1)} %get-tuple-element.44), channel_id=1, source_target_pairs={{0,1},{1,0},{2,3},{3,2},{4,5},{5,4},{6,7},{7,6},{8,9},{9,8},{10,11... | collective-permute-start | bytes 196616 | tf_op jit(solution)/shard_map/ppermute | solution.py:458
  34.6 4.6 %collective-permute-start.4 = (bf16[256,128]{1,0:T(8,128)(2,1)S(1)}, bf16[256,128]{1,0:T(8,128)(2,1)S(1)}, u32[]{:S(2)}, u32[]{:S(2)}) collective-permute-start(bf16[256,128]{1,0:T(8,128)(2,1)S(1)} %get-tuple-element.45), channel_id=1, source_target_pairs={{1,2},{2,1},{3,4},{4,3},{5,6},{6,5},{7,8},{8,7},{9,10},{10,9},{11,... | collective-permute-start | bytes 196616 | tf_op jit(solution)/shard_map/ppermute | solution.py:458
  53.5 4.7 %collective-permute-start.5 = (bf16[256,128]{1,0:T(8,128)(2,1)S(1)}, bf16[256,128]{1,0:T(8,128)(2,1)S(1)}, u32[]{:S(2)}, u32[]{:S(2)}) collective-permute-start(bf16[256,128]{1,0:T(8,128)(2,1)S(1)} %get-tuple-element.54), channel_id=1, source_target_pairs={{0,1},{1,0},{2,3},{3,2},{4,5},{5,4},{6,7},{7,6},{8,9},{9,8},{10,11... | collective-permute-start | bytes 196616 | tf_op jit(solution)/shard_map/ppermute | solution.py:458
  55.4 2.9 %collective-permute-start.6 = (bf16[256,128]{1,0:T(8,128)(2,1)S(1)}, bf16[256,128]{1,0:T(8,128)(2,1)S(1)}, u32[]{:S(2)}, u32[]{:S(2)}) collective-permute-start(bf16[256,128]{1,0:T(8,128)(2,1)S(1)} %get-tuple-element.55), channel_id=1, source_target_pairs={{1,2},{2,1},{3,4},{4,3},{5,6},{6,5},{7,8},{8,7},{9,10},{10,9},{11,... | collective-permute-start | bytes 196616 | tf_op jit(solution)/shard_map/ppermute | solution.py:458
  60.4 8.6 %collective-permute-start.7 = (f32[8,128]{1,0:T(8,128)S(1)}, f32[8,128]{1,0:T(8,128)S(1)}, u32[]{:S(2)}, u32[]{:S(2)}) collective-permute-start(f32[8,128]{1,0:T(8,128)S(1)} %get-tuple-element.60), channel_id=1, source_target_pairs={{128,129},{129,128},{130,131},{131,130},{132,133},{133,132},{134,1... | collective-permute-start | bytes 12296 | tf_op jit(solution)/shard_map/ppermute | solution.py:458
  68.1 1.0 collective-permute-start.8
  71.1 8.7 %collective-permute-start.9 = (f32[8,128]{1,0:T(8,128)S(1)}, f32[8,128]{1,0:T(8,128)S(1)}, u32[]{:S(2)}, u32[]{:S(2)}) collective-permute-start(f32[8,128]{1,0:T(8,128)S(1)} %get-tuple-element.63), channel_id=1, source_target_pairs={{128,129},{129,128},{130,131},{131,130},{132,133},{133,132},{134,1... | collective-permute-start | bytes 12296 | tf_op jit(solution)/shard_map/ppermute | solution.py:458
  78.8 1.0 collective-permute-start.10
  125.5 1.2 collective-permute-start.11

commit v3 on v2

--- a/solution.py
+++ b/solution.py
@@ -15,7 +15,12 @@
 BF16 = jnp.bfloat16
 VMEM = pl.BlockSpec(memory_space=pltpu.VMEM)
 ANY = pl.BlockSpec(memory_space=pl.ANY)
-CHUNK = 16
+SWEEP_CHUNK, SWEEP_UNROLL = 32, 4
+FIELD_CHUNK, FIELD_UNROLL = 32, 4
+TERM_CHUNK, TERM_UNROLL = 64, 4
+STATIC_CHUNK = 32
+RADIAL_SLOTS = 8
+MESSAGE_SLOTS = 8
 
 
 def call(body, outs, held, far=(), scratch=(), copies=0, far_outs=0, loose=0):
@@ -74,6 +79,10 @@
 def one_hot(row, depth):
     ids = lax.broadcasted_iota(jnp.int32, (depth, row.shape[1]), 0)
     return jnp.where(ids == row, 1.0, 0.0).astype(BF16)
+
+
+def slot_row(slots, first, count):
+    return jnp.concatenate([slots[pl.ds(first + i, 1), :] for i in range(count)], axis=1)
 
 
 def rows(parts, count=8):
@@ -135,23 +144,23 @@
         tx, ty, tz = site[0:1, :], site[1:2, :], site[2:3, :]
 
         def some_rows(j, acc):
-            start = pl.multiple_of(j * CHUNK, CHUNK)
-            ids = lax.broadcasted_iota(jnp.int32, (CHUNK, width), 0) + start
-            count = jnp.zeros((CHUNK, width), F32)
+            start = pl.multiple_of(j * STATIC_CHUNK, STATIC_CHUNK)
+            ids = lax.broadcasted_iota(jnp.int32, (STATIC_CHUNK, width), 0) + start
+            count = jnp.zeros((STATIC_CHUNK, width), F32)
             for k in range(slot_count):
                 count = count + jnp.where(ids == slots[k : k + 1, :], 1.0, 0.0)
-            cols = entry[pl.ds(start, CHUNK), :]
+            cols = entry[pl.ds(start, STATIC_CHUNK), :]
             rx, ry, rz = tx - cols[:, 0:1], ty - cols[:, 1:2], tz - cols[:, 2:3]
             inverse = lax.rsqrt(rx * rx + ry * ry + rz * rz + SMOOTH)
             squared = inverse * inverse
             cube = count * (squared * inverse)
-            w3[pl.ds(start, CHUNK), :] = cube
-            w5[pl.ds(start, CHUNK), :] = 3.0 * (cube * squared)
+            w3[pl.ds(start, STATIC_CHUNK), :] = cube
+            w5[pl.ds(start, STATIC_CHUNK), :] = 3.0 * (cube * squared)
             scale = cols[:, 3:4] * cube
             return acc[0] + rx * scale, acc[1] + ry * scale, acc[2] + rz * scale
 
-        nil = jnp.zeros((CHUNK, width), F32)
-        sums = lax.fori_loop(0, depth // CHUNK, some_rows, (nil, nil, nil))
+        nil = jnp.zeros((STATIC_CHUNK, width), F32)
+        sums = lax.fori_loop(0, depth // STATIC_CHUNK, some_rows, (nil, nil, nil))
         total = rows([jnp.sum(s, axis=0, keepdims=True) for s in sums])
         fixed[...] = total
         lend_pieces(total, picks, lent_a, lent_b)
@@ -169,7 +178,9 @@
     def _():
         wait = fetch(((w_in_far, w_in), (w_mid_far, w_mid)), done)
         pieces = split3(jnp.concatenate([site[...], rim_a[...], rim_b[...]], axis=1))
-        centres = lax.broadcasted_iota(jnp.int32, (BASIS, width), 0).astype(F32) * SPACING
+        step = RADIAL_SLOTS * width
+        here = jnp.concatenate([site[...]] * RADIAL_SLOTS, axis=1)
+        centres = lax.broadcasted_iota(jnp.int32, (BASIS, step), 0).astype(F32) * SPACING
         wait()
         first_w = jnp.concatenate([flip(w_in[0]), flip(w_in[1])], axis=0).astype(BF16)
         zero = jnp.zeros((64, 64), F32)
@@ -181,19 +192,20 @@
 
         second_w, third_w = both(0), both(1)
 
-        def one_slot(k, carry):
-            found = join3(dot(pieces, one_hot(slots[pl.ds(k, 1), :], depth)))
-            offset = site[...] - found
+        def some_slots(k, carry):
+            found = join3(dot(pieces, one_hot(slot_row(slots, k * RADIAL_SLOTS, RADIAL_SLOTS), depth)))
+            offset = here - found
             squares = offset * offset
             dist_sq = squares[0:1] + squares[1:2] + squares[2:3] + SMOOTH
             gap = jnp.sqrt(dist_sq) - centres
             basis = jnp.exp(-(gap * gap)).astype(BF16)
             hidden = silu(dot(first_w, basis)).astype(BF16)
             hidden = silu(dot(second_w, hidden)).astype(BF16)
-            third[k] = silu(dot(third_w, hidden)).astype(BF16)
+            start = pl.multiple_of(k * step, step)
+            third[:, pl.ds(start, step)] = silu(dot(third_w, hidden)).astype(BF16)
             return carry
 
-        lax.fori_loop(0, slot_count, one_slot, 0, unroll=4)
+        lax.fori_loop(0, slot_count // RADIAL_SLOTS, some_slots, 0)
         fetch(((third, third_far),), done, 2)()
 
 
@@ -222,34 +234,42 @@
     tx, ty, tz = site[0:1, :], site[1:2, :], site[2:3, :]
 
     def some_rows(j, acc):
-        start = pl.multiple_of(j * CHUNK, CHUNK)
-        cols, d = entry[pl.ds(start, CHUNK), :], moment[pl.ds(start, CHUNK), :]
+        start = pl.multiple_of(j * SWEEP_CHUNK, SWEEP_CHUNK)
+        cols, d = entry[pl.ds(start, SWEEP_CHUNK), :], moment[pl.ds(start, SWEEP_CHUNK), :]
         rx, ry, rz = tx - cols[:, 0:1], ty - cols[:, 1:2], tz - cols[:, 2:3]
         dx, dy, dz = d[:, 0:1], d[:, 1:2], d[:, 2:3]
-        cube = w3[pl.ds(start, CHUNK), :]
-        scale = (rx * dx + ry * dy + rz * dz) * w5[pl.ds(start, CHUNK), :]
+        cube = w3[pl.ds(start, SWEEP_CHUNK), :]
+        scale = (rx * dx + ry * dy + rz * dz) * w5[pl.ds(start, SWEEP_CHUNK), :]
         return (
             acc[0] + (rx * scale - dx * cube),
             acc[1] + (ry * scale - dy * cube),
             acc[2] + (rz * scale - dz * cube),
         )
 
-    nil = jnp.zeros((CHUNK, width), F32)
-    sums = lax.fori_loop(0, w3.shape[0] // CHUNK, some_rows, (nil, nil, nil), unroll=2)
+    nil = jnp.zeros((SWEEP_CHUNK, width), F32)
+    sums = lax.fori_loop(0, w3.shape[0] // SWEEP_CHUNK, some_rows, (nil, nil, nil), unroll=SWEEP_UNROLL)
     return site[4:5, :] * (fixed + rows([jnp.sum(s, axis=0, keepdims=True) for s in sums]))
 
 
 def message(layer, hidden, table, third, out_t, node_t, slots, total):
     slot_count = slots.shape[0]
+    width = slots.shape[1]
+    step = MESSAGE_SLOTS * width
     total[...] = jnp.zeros_like(total)
 
-    def one_slot(k, carry):
-        picked = dot(table, one_hot(slots[pl.ds(k, 1), :], table.shape[1]))
-        weight = dot(out_t, third[k, layer * 64 : layer * 64 + 64, :])
-        total[...] += weight * picked
+    def some_slots(k, carry):
+        row = slot_row(slots, k * MESSAGE_SLOTS, MESSAGE_SLOTS)
+        picked = dot(table, one_hot(row, table.shape[1]))
+        start = pl.multiple_of(k * step, step)
+        weight = dot(out_t, third[layer * 64 : layer * 64 + 64, pl.ds(start, step)])
+        product = weight * picked
+        part = product[:, 0:width]
+        for i in range(1, MESSAGE_SLOTS):
+            part = part + product[:, i * width : (i + 1) * width]
+        total[...] += part
         return carry
 
-    lax.fori_loop(0, slot_count, one_slot, 0, unroll=4)
+    lax.fori_loop(0, slot_count // MESSAGE_SLOTS, some_slots, 0)
     mean = (total[...] * (1.0 / slot_count)).astype(BF16)
     return (hidden.astype(F32) + silu(dot(node_t, mean))).astype(BF16)
 
@@ -258,14 +278,14 @@
     tx, ty, tz = target[0:1, :], target[1:2, :], target[2:3, :]
 
     def some_rows(j, acc):
-        c = cols[pl.ds(pl.multiple_of(first + j * CHUNK, CHUNK), CHUNK), :]
+        c = cols[pl.ds(pl.multiple_of(first + j * FIELD_CHUNK, FIELD_CHUNK), FIELD_CHUNK), :]
         rx, ry, rz = tx - c[:, 0:1], ty - c[:, 1:2], tz - c[:, 2:3]
         inverse = lax.rsqrt(rx * rx + ry * ry + rz * rz + SMOOTH)
         scale = c[:, 3:4] * (inverse * inverse * inverse)
         return acc[0] + rx * scale, acc[1] + ry * scale, acc[2] + rz * scale
 
-    nil = jnp.zeros((CHUNK, target.shape[1]), F32)
-    sums = lax.fori_loop(0, count // CHUNK, some_rows, (nil, nil, nil), unroll=2)
+    nil = jnp.zeros((FIELD_CHUNK, target.shape[1]), F32)
+    sums = lax.fori_loop(0, count // FIELD_CHUNK, some_rows, (nil, nil, nil), unroll=FIELD_UNROLL)
     return jnp.concatenate([jnp.sum(s, axis=0, keepdims=True) for s in sums], axis=0)
 
 
@@ -389,8 +409,8 @@
             tx, ty, tz = tile[0:1, :], tile[1:2, :], tile[2:3, :]
 
             def some_rows(j, acc):
-                start = pl.multiple_of(j * 2 * CHUNK, 2 * CHUNK)
-                c = cols[pl.ds(start, 2 * CHUNK), :]
+                start = pl.multiple_of(j * TERM_CHUNK, TERM_CHUNK)
+                c = cols[pl.ds(start, TERM_CHUNK), :]
                 rx, ry, rz = tx - c[:, 0:1], ty - c[:, 1:2], tz - c[:, 2:3]
                 inverse = lax.rsqrt(rx * rx + ry * ry + rz * rz + SMOOTH)
                 squared = inverse * inverse
@@ -406,8 +426,8 @@
                 scale = c[:, 3:4] * cube
                 return acc[0] + rx * scale, acc[1] + ry * scale, acc[2] + rz * scale
 
-            nil = jnp.zeros((2 * CHUNK, 128), F32)
-            sums = lax.fori_loop(0, width // (2 * CHUNK), some_rows, (nil, nil, nil), unroll=2)
+            nil = jnp.zeros((TERM_CHUNK, 128), F32)
+            sums = lax.fori_loop(0, width // TERM_CHUNK, some_rows, (nil, nil, nil), unroll=TERM_UNROLL)
             for axis in range(3):
                 term[l, axis : axis + 1, :] = jnp.sum(sums[axis], axis=0, keepdims=True)
 
@@ -427,13 +447,18 @@
         terms(True)
 
     wait()
+    side = lax.broadcasted_iota(jnp.int32, (2, 128), 0)
     for l in range(listed):
-        spread[blocks[l]] += term[l]
+        owner, part = blocks[l] >> 1, blocks[l] & 1
+        for axis in range(3):
+            spread[3 * owner + axis] += jnp.where(side == part, term[l, axis : axis + 1, :], 0.0)
 
 
 def gather_kernel(pieces, share):
     total = jnp.sum(pieces[...], axis=0)
-    share[...] = jnp.concatenate([total[0, 0:3], total[1, 0:3]], axis=1)
+    share[...] = jnp.concatenate(
+        [jnp.concatenate([total[axis, 0:1], total[axis, 1:2]], axis=1) for axis in range(3)], axis=0
+    )
 
 
 def local(
@@ -478,7 +503,7 @@
         (site, rim_a, rim_b, slots, picks), (features,), [pltpu.VMEM((width, channels), BF16)], 1,
     )
     side_a, side_b = trade(lent_a, lent_b)
-    third_shape = (slot_count, LAYERS * radial_in.shape[2], width)
+    third_shape = (LAYERS * radial_in.shape[2], slot_count * width)
     (third,) = call(
         radial_kernel, [(third_shape, BF16)], (site, rim_a, rim_b, slots), (radial_in, radial_mid),
         [pltpu.VMEM(radial_in.shape, BF16), pltpu.VMEM(radial_mid.shape, BF16), pltpu.VMEM(third_shape, BF16)], 3, 1,
@@ -509,11 +534,11 @@
     )
     side_a, side_b = trade(small_a, small_b, True)
     result, spread = call(
-        response_kernel, [((3, width), F32), ((2 * members, 4, half), F32)],
+        response_kernel, [((3, width), F32), ((3 * members, 2, half), F32)],
         (near_own, site, charge, outside_row, side_a, side_b, w3, w5, fixed_all, dipole, entry), (blocks,),
         [pltpu.SMEM((listed,), ints), pltpu.VMEM((width, 8), F32), moment, pltpu.VMEM((listed, 4, half), F32)], 1,
     )
-    pieces = lax.all_to_all(spread.reshape(members, 2, 4, half), DOM, 0, 0, tiled=True)
+    pieces = lax.all_to_all(spread, DOM, 0, 0, tiled=True).reshape(members, 3, 2, half)
     (share,) = call(gather_kernel, [((3, width), F32)], (pieces,))
     return result, lax.ppermute(share, "grp", [(0, 1), (1, 0)])
 

time: 128 us -> 116 us (0.906)
  Pallas kernels: 22.1 us -> 13.9 us
  blocking collectives: 40.5 us -> 36 us
    pallas_call x8, Pallas kernels: 22.1 us -> 13.9 us  [call(): pl.pallas_call(body, out_shape=[jax.ShapeDtypeStruct(s, d) for s, d in ou...]
    all_to_all x1, blocking collectives: 40.5 us -> 36 us  [local(): lax.all_to_all(spread, DOM, 0, 0, tiled=True).reshape(members, 3, 2, half)]
  transfers between devices with their start and end apart: 13 -> 13, of which waited for: 7 -> 7; matrix products, arithmetic and copies ran while one was open for 0% -> 0% of each run, Pallas kernels for 3% -> 2%
where the time goes in v3:
time: 116 us
  starting transfers between devices  46.5 us (40%)
  blocking collectives  36 us (31%)
  waiting for transfers between devices  16.9 us (15%)
  Pallas kernels  13.9 us (12%)
  local copies, waits for them, and re-layouts  1.46 us (1%)
    all_to_all x1, blocking collectives, local(): lax.all_to_all(spread, DOM, 0, 0, tiled=True).reshape(members, 3, 2, half)  36 us
    ppermute x10, starting transfers between devices, trade(): return (lax.ppermute(a, EVERY, used[0]), lax.ppermute(b, EVERY, used[1]))  23.9 us
    all_to_all x1, starting transfers between devices, local(): lax.all_to_all(copies, DOM, 0, 0, tiled=True).reshape(2 * members, 4, half)  19.2 us
    pallas_call x8, Pallas kernels, call(): pl.pallas_call(body, out_shape=[jax.ShapeDtypeStruct(s, d) for s, d in ou...  13.9 us
    ppermute x10, waiting for transfers between devices, trade(): return (lax.ppermute(a, EVERY, used[0]), lax.ppermute(b, EVERY, used[1]))  8.37 us
    all_to_all x1, waiting for transfers between devices, local(): lax.all_to_all(copies, DOM, 0, 0, tiled=True).reshape(2 * members, 4, half)  7.4 us
    ppermute x1, starting transfers between devices, local(): partner = lax.ppermute(mine, 'grp', [(0, 1), (1, 0)])  3.33 us
  transfers between devices with their start and end apart: 13, of which 7 were waited for; matrix products, arithmetic and copies ran while one was open for 0% of the time, Pallas kernels for 2%

profile of v3, /device:TPU:1, one launch (start us, length us, event | category | flops | bytes accessed | tf_op | source)
XLA Modules:
  0.0 115.6 jit_solution(4026708722622331352)
XLA Ops:
  0.6 1.0 shard_map.149
  1.7 3.3 %collective-permute-start = (f32[2,4,128]{2,1,0:T(4,128)S(1)}, f32[2,4,128]{2,1,0:T(4,128)S(1)}, u32[]{:S(2)}, u32[]{:S(2)}) collective-permute-start(f32[2,4,128]{2,1,0:T(4,128)S(1)} %get-tuple-element.36), channel_id=1, source_target_pairs={{0,128},{128,0},{1,129},{129,1},{2,130},{130,2},{3,131},{131,3},{4... | collective-permute-start | bytes 12296 | tf_op jit(solution)/shard_map/ppermute | solution.py:497
  5.0 1.2 %collective-permute-start.1 = (f32[8,128]{1,0:T(8,128)S(1)}, f32[8,128]{1,0:T(8,128)S(1)}, u32[]{:S(2)}, u32[]{:S(2)}) collective-permute-start(f32[8,128]{1,0:T(8,128)S(1)} %get-tuple-element.37), channel_id=1, source_target_pairs={{0,1},{1,0},{2,3},{3,2},{4,5},{5,4},{6,7},{7,6},{8,9},{9,8},{10,11... | collective-permute-start | bytes 12296 | tf_op jit(solution)/shard_map/ppermute | solution.py:483
  6.2 0.6 collective-permute-start.2
  6.9 0.0 collective-permute-done
  6.9 2.1 %collective-permute-done.1.rim_a = f32[8,128]{1,0:T(8,128)S(1)} collective-permute-done((f32[8,128]{1,0:T(8,128)S(1)}, f32[8,128]{1,0:T(8,128)S(1)}, u32[]{:S(2)}, u32[]{:S(2)}) %collective-permute-start.1) | collective-permute-done | bytes 4128 | tf_op jit(solution)/shard_map/ppermute | solution.py:483
  9.0 0.0 collective-permute-done.2.rim_b
  9.0 0.9 broadcast_in_dim.17
  9.8 19.2 %all-to-all-start = ((f32[128,2,4,128]{3,2,1,0:T(4,128)}), f32[128,2,4,128]{3,2,1,0:T(4,128)S(1)}, u32[]{:S(2)}, u32[]{:S(2)}) async-start(f32[128,2,4,128]{3,2,1,0:T(4,128)} %broadcast_in_dim.17), calls=%async_computation | async-start | bytes 1048576 | tf_op jit(solution)/shard_map/all_to_all | solution.py:500
  29.0 2.7 %shard_map.150 = (bf16[256,256]{1,0:T(8,128)(2,1)S(1)}, f32[512,256]{1,0:T(8,128)S(1)}, f32[512,256]{1,0:T(8,128)S(1)}, f32[8,256]{1,0:T(8,128)S(1)}, f32[512,8]...) custom-call(f32[8,256]{1,0:T(8,128)S(1)} %get-tuple-element.35.site, ...), custom_call_target="tpu_custom_call" | custom-call | tf_op jit(solution)/shard_map/pallas_call | solution.py:27
  31.7 2.2 %collective-permute-start.3 = (bf16[256,128]{1,0:T(8,128)(2,1)S(1)}, bf16[256,128]{1,0:T(8,128)(2,1)S(1)}, u32[]{:S(2)}, u32[]{:S(2)}) collective-permute-start(bf16[256,128]{1,0:T(8,128)(2,1)S(1)} %get-tuple-element.44), channel_id=1, source_target_pairs={{0,1},{1,0},{2,3},{3,2},{4,5},{5,4},{6,7},{7,6},{8,9},{9,8},{10,11... | collective-permute-start | bytes 196616 | tf_op jit(solution)/shard_map/ppermute | solution.py:483
  33.9 0.7 collective-permute-start.4
  34.6 3.4 %collective-permute-done.3.side_a = bf16[256,128]{1,0:T(8,128)(2,1)S(1)} collective-permute-done((bf16[256,128]{1,0:T(8,128)(2,1)S(1)}, bf16[256,128]{1,0:T(8,128)(2,1)S(1)}, u32[]{:S(2)}, u32[]{:S(2)}) %collective-permute-start.3) | collective-permute-done | bytes 65568 | tf_op jit(solution)/shard_map/ppermute | solution.py:483
  38.0 0.0 collective-permute-done.4.side_b
  38.0 7.4 %all-to-all-done = f32[128,2,4,128]{3,2,1,0:T(4,128)S(1)} async-done(((f32[128,2,4,128]{3,2,1,0:T(4,128)}), f32[128,2,4,128]{3,2,1,0:T(4,128)S(1)}, u32[]{:S(2)}, u32[]{:S(2)}) %all-to-all-start) | async-done | bytes 524320 | tf_op jit(solution)/shard_map/all_to_all | solution.py:500
  45.4 4.4 %shard_map.152 = (f32[8,256]{1,0:T(8,128)S(1)}, f32[4,4,128]{2,1,0:T(4,128)S(1)}, bf16[256,256]{1,0:T(8,128)(2,1)S(1)}, bf16[256,256]{1,0:T(8,128)(2,1)S(1)}, f3...) custom-call(f32[8,256]{1,0:T(8,128)S(1)} %get-tuple-element.35.site, ...), custom_call_target="tpu_custom_call" | custom-call | tf_op jit(solution)/shard_map/pallas_call | solution.py:27
  49.8 1.8 %collective-permute-start.5 = (bf16[256,128]{1,0:T(8,128)(2,1)S(1)}, bf16[256,128]{1,0:T(8,128)(2,1)S(1)}, u32[]{:S(2)}, u32[]{:S(2)}) collective-permute-start(bf16[256,128]{1,0:T(8,128)(2,1)S(1)} %get-tuple-element.54), channel_id=1, source_target_pairs={{0,1},{1,0},{2,3},{3,2},{4,5},{5,4},{6,7},{7,6},{8,9},{9,8},{10,11... | collective-permute-start | bytes 196616 | tf_op jit(solution)/shard_map/ppermute | solution.py:483
  51.6 0.7 collective-permute-start.6
  52.3 2.2 %collective-permute-done.5.side_a = bf16[256,128]{1,0:T(8,128)(2,1)S(1)} collective-permute-done((bf16[256,128]{1,0:T(8,128)(2,1)S(1)}, bf16[256,128]{1,0:T(8,128)(2,1)S(1)}, u32[]{:S(2)}, u32[]{:S(2)}) %collective-permute-start.5) | collective-permute-done | bytes 65568 | tf_op jit(solution)/shard_map/ppermute | solution.py:483
  54.5 0.0 collective-permute-done.6.side_b
  54.5 1.2 %shard_map.153 = (f32[8,256]{1,0:T(8,128)S(1)}, f32[8,256]{1,0:T(8,128)S(1)}, f32[8,128]{1,0:T(8,128)S(1)}, f32[8,128]{1,0:T(8,128)S(1)}) custom-call(bf16[256,256]{1,0:T(8,128)(2,1)S(1)} %get-tuple-element.52.hidden, bf16[256,256]{1,0:T(8,128)(2,1)S(1)} %get-tuple-element.53.lifted, bf16[256,128]{1,0:T(8,128)(2,1)S(1)} %collective-permute-done.5.side_a, ...), custom_call_target="tpu_custom_call" | custom-call | tf_op jit(solution)/shard_map/pallas_call | solution.py:27
  55.7 7.7 %collective-permute-start.7 = (f32[8,128]{1,0:T(8,128)S(1)}, f32[8,128]{1,0:T(8,128)S(1)}, u32[]{:S(2)}, u32[]{:S(2)}) collective-permute-start(f32[8,128]{1,0:T(8,128)S(1)} %get-tuple-element.60), channel_id=1, source_target_pairs={{128,129},{129,128},{130,131},{131,130},{132,133},{133,132},{134,1... | collective-permute-start | bytes 12296 | tf_op jit(solution)/shard_map/ppermute | solution.py:483
  63.4 0.7 collective-permute-start.8
  64.0 0.3 collective-permute-done.7.side_a
  64.4 0.0 collective-permute-done.8.side_b
  64.4 1.2 shard_map.154
  65.5 7.8 %collective-permute-start.9 = (f32[8,128]{1,0:T(8,128)S(1)}, f32[8,128]{1,0:T(8,128)S(1)}, u32[]{:S(2)}, u32[]{:S(2)}) collective-permute-start(f32[8,128]{1,0:T(8,128)S(1)} %get-tuple-element.63), channel_id=1, source_target_pairs={{128,129},{129,128},{130,131},{131,130},{132,133},{133,132},{134,1... | collective-permute-start | bytes 12296 | tf_op jit(solution)/shard_map/ppermute | solution.py:483
  73.4 0.7 collective-permute-start.10
  74.0 0.3 collective-permute-done.9.side_a
  74.3 0.0 collective-permute-done.10.side_b
  74.3 3.2 %shard_map.155 = (f32[3,256]{1,0:T(4,128)}, f32[384,2,128]{2,1,0:T(2,128)S(1)}) custom-call(f32[4,4,128]{2,1,0:T(4,128)S(1)} %get-tuple-element.51.near, f32[8,256]{1,0:T(8,128)S(1)} %get-tuple-element.35.site, f32[8,256]{1,0:T(8,128)S(1)} %get-tuple-element.58.charge, f32[8,256]{1,0:T(8,128)S(1)} %get-tuple-element.59.outside_row, ...), custom_call_target="tpu_custom_call" | custom-call | tf_op jit(solution)/shard_map/pallas_call | solution.py:27
  77.6 36.0 %all_to_all.10 = f32[384,2,128]{2,1,0:T(2,128)S(1)} all-to-all(f32[384,2,128]{2,1,0:T(2,128)S(1)} %get-tuple-element.67), channel_id=1, replica_groups=mesh['grp'=2,'dom'=64,'sub'=2] {'dom','sub'}, dimensions={0} | all-to-all | bytes 786432 | tf_op jit(solution)/shard_map/all_to_all | solution.py:541
  113.6 0.2 shard_map.156
  113.8 0.1 collective-permute-start.11
  113.9 1.2 collective-permute-done.11
  115.0 0.6 copy.17
  (1 shorter events, 0.0 us)
Async XLA Ops:
  1.7 5.2 %collective-permute-start = (f32[2,4,128]{2,1,0:T(4,128)S(1)}, f32[2,4,128]{2,1,0:T(4,128)S(1)}, u32[]{:S(2)}, u32[]{:S(2)}) collective-permute-start(f32[2,4,128]{2,1,0:T(4,128)S(1)} %get-tuple-element.36), channel_id=1, source_target_pairs={{0,128},{128,0},{1,129},{129,1},{2,130},{130,2},{3,131},{131,3},{4... | collective-permute-start | bytes 12296 | tf_op jit(solution)/shard_map/ppermute | solution.py:497
  5.0 4.0 %collective-permute-start.1 = (f32[8,128]{1,0:T(8,128)S(1)}, f32[8,128]{1,0:T(8,128)S(1)}, u32[]{:S(2)}, u32[]{:S(2)}) collective-permute-start(f32[8,128]{1,0:T(8,128)S(1)} %get-tuple-element.37), channel_id=1, source_target_pairs={{0,1},{1,0},{2,3},{3,2},{4,5},{5,4},{6,7},{7,6},{8,9},{9,8},{10,11... | collective-permute-start | bytes 12296 | tf_op jit(solution)/shard_map/ppermute | solution.py:483
  6.2 2.8 %collective-permute-start.2 = (f32[8,128]{1,0:T(8,128)S(1)}, f32[8,128]{1,0:T(8,128)S(1)}, u32[]{:S(2)}, u32[]{:S(2)}) collective-permute-start(f32[8,128]{1,0:T(8,128)S(1)} %get-tuple-element.38), channel_id=1, source_target_pairs={{1,2},{2,1},{3,4},{4,3},{5,6},{6,5},{7,8},{8,7},{9,10},{10,9},{11,... | collective-permute-start | bytes 12296 | tf_op jit(solution)/shard_map/ppermute | solution.py:483
  9.8 35.6 %all-to-all-start = ((f32[128,2,4,128]{3,2,1,0:T(4,128)}), f32[128,2,4,128]{3,2,1,0:T(4,128)S(1)}, u32[]{:S(2)}, u32[]{:S(2)}) async-start(f32[128,2,4,128]{3,2,1,0:T(4,128)} %broadcast_in_dim.17), calls=%async_computation | async-start | bytes 1048576 | tf_op jit(solution)/shard_map/all_to_all | solution.py:500
  31.7 6.3 %collective-permute-start.3 = (bf16[256,128]{1,0:T(8,128)(2,1)S(1)}, bf16[256,128]{1,0:T(8,128)(2,1)S(1)}, u32[]{:S(2)}, u32[]{:S(2)}) collective-permute-start(bf16[256,128]{1,0:T(8,128)(2,1)S(1)} %get-tuple-element.44), channel_id=1, source_target_pairs={{0,1},{1,0},{2,3},{3,2},{4,5},{5,4},{6,7},{7,6},{8,9},{9,8},{10,11... | collective-permute-start | bytes 196616 | tf_op jit(solution)/shard_map/ppermute | solution.py:483
  33.9 4.1 %collective-permute-start.4 = (bf16[256,128]{1,0:T(8,128)(2,1)S(1)}, bf16[256,128]{1,0:T(8,128)(2,1)S(1)}, u32[]{:S(2)}, u32[]{:S(2)}) collective-permute-start(bf16[256,128]{1,0:T(8,128)(2,1)S(1)} %get-tuple-element.45), channel_id=1, source_target_pairs={{1,2},{2,1},{3,4},{4,3},{5,6},{6,5},{7,8},{8,7},{9,10},{10,9},{11,... | collective-permute-start | bytes 196616 | tf_op jit(solution)/shard_map/ppermute | solution.py:483
  49.8 4.7 %collective-permute-start.5 = (bf16[256,128]{1,0:T(8,128)(2,1)S(1)}, bf16[256,128]{1,0:T(8,128)(2,1)S(1)}, u32[]{:S(2)}, u32[]{:S(2)}) collective-permute-start(bf16[256,128]{1,0:T(8,128)(2,1)S(1)} %get-tuple-element.54), channel_id=1, source_target_pairs={{0,1},{1,0},{2,3},{3,2},{4,5},{5,4},{6,7},{7,6},{8,9},{9,8},{10,11... | collective-permute-start | bytes 196616 | tf_op jit(solution)/shard_map/ppermute | solution.py:483
  51.6 2.9 %collective-permute-start.6 = (bf16[256,128]{1,0:T(8,128)(2,1)S(1)}, bf16[256,128]{1,0:T(8,128)(2,1)S(1)}, u32[]{:S(2)}, u32[]{:S(2)}) collective-permute-start(bf16[256,128]{1,0:T(8,128)(2,1)S(1)} %get-tuple-element.55), channel_id=1, source_target_pairs={{1,2},{2,1},{3,4},{4,3},{5,6},{6,5},{7,8},{8,7},{9,10},{10,9},{11,... | collective-permute-start | bytes 196616 | tf_op jit(solution)/shard_map/ppermute | solution.py:483
  55.7 8.6 %collective-permute-start.7 = (f32[8,128]{1,0:T(8,128)S(1)}, f32[8,128]{1,0:T(8,128)S(1)}, u32[]{:S(2)}, u32[]{:S(2)}) collective-permute-start(f32[8,128]{1,0:T(8,128)S(1)} %get-tuple-element.60), channel_id=1, source_target_pairs={{128,129},{129,128},{130,131},{131,130},{132,133},{133,132},{134,1... | collective-permute-start | bytes 12296 | tf_op jit(solution)/shard_map/ppermute | solution.py:483
  63.4 1.0 collective-permute-start.8
  65.5 8.8 %collective-permute-start.9 = (f32[8,128]{1,0:T(8,128)S(1)}, f32[8,128]{1,0:T(8,128)S(1)}, u32[]{:S(2)}, u32[]{:S(2)}) collective-permute-start(f32[8,128]{1,0:T(8,128)S(1)} %get-tuple-element.63), channel_id=1, source_target_pairs={{128,129},{129,128},{130,131},{131,130},{132,133},{133,132},{134,1... | collective-permute-start | bytes 12296 | tf_op jit(solution)/shard_map/ppermute | solution.py:483
  73.4 1.0 collective-permute-start.10
  113.8 1.2 %collective-permute-start.11 = (f32[3,256]{1,0:T(4,128)S(1)}, f32[3,256]{1,0:T(4,128)S(1)}, u32[]{:S(2)}, u32[]{:S(2)}) collective-permute-start(f32[3,256]{1,0:T(4,128)S(1)} %shard_map.156), channel_id=1, source_target_pairs={{0,128},{128,0},{1,129},{129,1},{2,130},{130,2},{3,131},{131,3},{4... | collective-permute-start | bytes 9224 | tf_op jit(solution)/shard_map/ppermute | solution.py:543

commit v4 on v3

--- a/solution.py
+++ b/solution.py
@@ -78,7 +78,20 @@
 
 def one_hot(row, depth):
     ids = lax.broadcasted_iota(jnp.int32, (depth, row.shape[1]), 0)
-    return jnp.where(ids == row, 1.0, 0.0).astype(BF16)
+    return jnp.where(ids == row.astype(jnp.int32), 1.0, 0.0).astype(BF16)
+
+
+def views(pack):
+    return pack.at[0:8, :], pack.at[8:40, :], pack.at[40:41, :]
+
+
+def picked_row(picks, row):
+    return picks[0:1, row * 128 : row * 128 + 128]
+
+
+def listed_block(row, l):
+    lane = lax.broadcasted_iota(jnp.int32, row.shape, 1)
+    return jnp.sum(jnp.where(lane == l, row, 0.0)).astype(jnp.int32)
 
 
 def slot_row(slots, first, count):
@@ -92,7 +105,7 @@
 
 def rows_kernel(
     pos_far, charge_far, polar_far, table_far, send_far, blocks_far,
-    site, mine, lent_a, lent_b, slots, picks,
+    pack, mine, lent_a, lent_b,
     pos, charge, polar, table, send, blocks, done,
 ):
     pairs = ((pos_far, pos), (charge_far, charge), (polar_far, polar), (table_far, table), (send_far, send))
@@ -100,32 +113,34 @@
     odd = lax.axis_index("sub")
     width = pos.shape[1]
     wait()
-    sites = rows([pos[...], charge[...], polar[...]])
-    site[...] = sites
+    lane = lax.broadcasted_iota(jnp.int32, (1, width), 1)
+    listed = jnp.zeros((1, width), jnp.int32)
+    for l in range(blocks.shape[0]):
+        listed = jnp.where(lane == l, blocks[l], listed)
+    listed = listed.astype(F32)
+    sites = rows([pos[...], charge[...], polar[...], listed, jnp.ones((1, width), F32)])
     for half in range(2):
         mine[half] = sites[0:4, half * 128 : half * 128 + 128]
     first, second = send[0:1, :], send[1:2, :]
     swap = jnp.full(first.shape, odd, jnp.int32) == 1
-    picks[0:1, :] = jnp.where(swap, second, first)
-    picks[1:2, :] = jnp.where(swap, first, second)
-    lane = lax.broadcasted_iota(jnp.int32, (1, 128), 1)
-    listed = jnp.zeros((1, 128), jnp.int32)
-    for l in range(blocks.shape[0]):
-        listed = jnp.where(lane == l, blocks[l], listed)
-    pieces = split3(sites)
-    for row, out in ((0, lent_a), (1, lent_b)):
-        found = join3(dot(pieces, one_hot(picks[row : row + 1, :], width)))
-        out[...] = rows([found[0:5], listed.astype(F32), jnp.ones((1, 128), F32)])
+    picks = jnp.where(swap, second, first), jnp.where(swap, first, second)
     raw = table[...]
     other = jnp.where((raw >= 256) & (raw < 512), jnp.bitwise_xor(raw, 128), raw)
     keep = jnp.full(raw.shape, odd, jnp.int32) == 1
-    slots[...] = jnp.where(keep, raw, other)
+    pack[0:8, :] = sites
+    pack[8:40, :] = jnp.where(keep, raw, other).astype(F32)
+    pack[40:48, :] = rows([jnp.concatenate(picks, axis=1).astype(F32)])
+    pieces = split3(sites)
+    for row, out in zip(picks, (lent_a, lent_b)):
+        found = join3(dot(pieces, one_hot(row, width)))
+        out[...] = rows([found[0:5], listed[:, 0:128], jnp.ones((1, 128), F32)])
 
 
 def static_kernel(
-    site, rim_a, rim_b, slots, picks, features_far,
+    pack, rim_a, rim_b, features_far,
     feat_t, w3, w5, fixed, entry, lent_a, lent_b, features, done,
 ):
+    site, slots, picks = views(pack)
     width = site.shape[1]
     depth = 2 * width
     slot_count = slots.shape[0]
@@ -145,7 +160,7 @@
 
         def some_rows(j, acc):
             start = pl.multiple_of(j * STATIC_CHUNK, STATIC_CHUNK)
-            ids = lax.broadcasted_iota(jnp.int32, (STATIC_CHUNK, width), 0) + start
+            ids = (lax.broadcasted_iota(jnp.int32, (STATIC_CHUNK, width), 0) + start).astype(F32)
             count = jnp.zeros((STATIC_CHUNK, width), F32)
             for k in range(slot_count):
                 count = count + jnp.where(ids == slots[k : k + 1, :], 1.0, 0.0)
@@ -167,9 +182,10 @@
 
 
 def radial_kernel(
-    site, rim_a, rim_b, slots, w_in_far, w_mid_far,
+    pack, rim_a, rim_b, w_in_far, w_mid_far,
     third_far, w_in, w_mid, third, done,
 ):
+    site, slots, _ = views(pack)
     width = site.shape[1]
     depth = 2 * width
     slot_count = slots.shape[0]
@@ -212,7 +228,7 @@
 def lend_pieces(values, picks, lent_a, lent_b):
     pieces = split3(values)
     for row, out in ((0, lent_a), (1, lent_b)):
-        found = dot(pieces, one_hot(picks[row : row + 1, :], values.shape[1]))
+        found = dot(pieces, one_hot(picked_row(picks, row), values.shape[1]))
         out[...] = jnp.zeros_like(out)
         out[0:32, :] = rows([found], 32).astype(BF16)
 
@@ -220,12 +236,12 @@
 def lend_whole(values, picks, lent_a, lent_b):
     pieces = split3(values)
     for row, out in ((0, lent_a), (1, lent_b)):
-        out[...] = join3(dot(pieces, one_hot(picks[row : row + 1, :], values.shape[1])))
+        out[...] = join3(dot(pieces, one_hot(picked_row(picks, row), values.shape[1])))
 
 
 def lend_channels(values, picks, lent_a, lent_b):
     for row, out in ((0, lent_a), (1, lent_b)):
-        out[...] = dot(values, one_hot(picks[row : row + 1, :], values.shape[1])).astype(BF16)
+        out[...] = dot(values, one_hot(picked_row(picks, row), values.shape[1])).astype(BF16)
 
 
 def sweep(site, w3, w5, fixed, dipoles, entry, moment):
@@ -290,14 +306,16 @@
 
 
 def first_kernel(
-    site, rim_a, rim_b, slots, picks, feat_t, side_a, side_b, w3, w5, fixed, entry,
-    near_far, blocks_far, third_far, node_in_far, node_out_far, w_out_far, gain_far,
+    pack, rim_a, rim_b, feat_t, side_a, side_b, w3, w5, fixed, entry,
+    near_far, third_far, node_in_far, node_out_far, w_out_far, gain_far,
     outside_row, near_own, hidden_out, lifted_out, fixed_out, dipole_out, lent_a, lent_b,
-    blocks, near, cols, third, node_in, node_out, w_out, gain, total, moment, done,
-):
+    near, cols, third, node_in, node_out, w_out, gain, total, moment, done,
+):
+    site, slots, picks = views(pack)
     width = site.shape[1]
-    listed = blocks.shape[0]
-    wait_blocks = fetch(((blocks_far, blocks),), done)
+    listed = near_own.shape[0]
+    numbers = [listed_block(row[5:6, 0:128], l) for row in (site, rim_a, rim_b) for l in range(listed)]
+    fetch([(near_far.at[b], near.at[i]) for i, b in enumerate(numbers)], done, 5)
     weights = (
         (third_far, third), (node_in_far, node_in), (node_out_far.at[0], node_out),
         (w_out_far.at[0], w_out), (gain_far, gain),
@@ -305,17 +323,10 @@
 
     @pl.when(learned())
     def _():
-        fetch(weights, done, 1)
-
-    lane = lax.broadcasted_iota(jnp.int32, (1, 128), 1)
-
-    def lent_block(rim, l):
-        return jnp.sum(jnp.where(lane == l, rim[5:6, :], 0.0)).astype(jnp.int32)
-
-    numbers = [lent_block(rim, l) for rim in (rim_a, rim_b) for l in range(listed)]
-    wait_blocks()
-    numbers = [blocks[l] for l in range(listed)] + numbers
-    fetch([(near_far.at[b], near.at[i]) for i, b in enumerate(numbers)], done, 6)()
+        fetch(weights, done)
+
+    for i, b in enumerate(numbers):
+        pltpu.make_async_copy(near_far.at[b], near.at[i], done.at[5 + i]).wait()
     near_own[...] = near[0:listed]
     for i in range(3 * listed):
         tile = near[i]
@@ -332,7 +343,7 @@
     @pl.when(learned())
     def _():
         for i, (a, b) in enumerate(weights):
-            pltpu.make_async_copy(a, b, done.at[1 + i]).wait()
+            pltpu.make_async_copy(a, b, done.at[i]).wait()
         gain_col = jnp.broadcast_to(gain[...], (8, width)).T
         features = jnp.concatenate([feat_t[...], side_a[...], side_b[...]], axis=1)
         start = (features.astype(F32) + gain_col[:, 0:1] * strength).astype(BF16)
@@ -358,12 +369,12 @@
 
 
 def second_kernel(
-    hidden, lifted, side_a, side_b, slots, picks, site, w3, w5, fixed, dipole, entry,
+    hidden, lifted, side_a, side_b, pack, w3, w5, fixed, dipole, entry,
     third_far, node_out_far, w_out_far, readout_far,
     charge, dipole_out, small_a, small_b,
     third, node_out, w_out, readout, total, moment, done,
 ):
-    width = site.shape[1]
+    site, slots, picks = views(pack)
 
     @pl.when(learned())
     def _():
@@ -384,7 +395,9 @@
         lend_whole(new, picks, small_a, small_b)
 
 
-def third_kernel(side_a, side_b, picks, site, w3, w5, fixed, dipole, entry, dipole_out, small_a, small_b, moment):
+def third_kernel(side_a, side_b, pack, w3, w5, fixed, dipole, entry, dipole_out, small_a, small_b, moment):
+    site, _, picks = views(pack)
+
     @pl.when(jnp.logical_not(learned()))
     def _():
         table = jnp.concatenate([dipole[...], side_a[...], side_b[...]], axis=1)
@@ -394,12 +407,13 @@
 
 
 def response_kernel(
-    near, site, charge, outside_row, side_a, side_b, w3, w5, fixed, dipole, entry, blocks_far,
-    result, spread, blocks, cols, moment, term, done,
-):
+    near, pack, charge, outside_row, side_a, side_b, w3, w5, fixed, dipole, entry,
+    result, spread, cols, moment, term,
+):
+    site = views(pack)[0]
     width = site.shape[1]
-    listed = blocks.shape[0]
-    wait = fetch(((blocks_far, blocks),), done)
+    listed = near.shape[0]
+    blocks = [listed_block(site[5:6, 0:128], l) for l in range(listed)]
     spread[...] = jnp.zeros_like(spread)
     term[...] = jnp.zeros_like(term)
 
@@ -446,7 +460,6 @@
         cols[...] = rows([site[0:4, :], new[0:3]]).T
         terms(True)
 
-    wait()
     side = lax.broadcasted_iota(jnp.int32, (2, 128), 0)
     for l in range(listed):
         owner, part = blocks[l] >> 1, blocks[l] & 1
@@ -459,6 +472,14 @@
     share[...] = jnp.concatenate(
         [jnp.concatenate([total[axis, 0:1], total[axis, 1:2]], axis=1) for axis in range(3)], axis=0
     )
+
+
+def placed(block):
+    y_half, z, step, side = block // 64, block // 8 % 8, block // 2 % 4, block % 2
+    x = 3 - step if z % 2 else step
+    along = 1 - side if step % 2 else side
+    y = 3 - along if y_half else along
+    return ((y % 2 * 8 + z) * 4 + x) * 2 + y // 2
 
 
 def local(
@@ -474,38 +495,42 @@
     members = lax.axis_size(DOM)
     near_pairs = [(i, i ^ 1) for i in range(members)]
     far_pairs = [(i, ((i - 1) ^ 1) + 1) for i in range(1, members - 1)]
-
-    def trade(a, b, solvent_only=False):
-        used = []
-        for pairs in (near_pairs, far_pairs):
-            shifted = [(x + members, y + members) for x, y in pairs]
-            used.append(shifted if solvent_only else pairs + shifted)
-        return lax.ppermute(a, EVERY, used[0]), lax.ppermute(b, EVERY, used[1])
+    same = list(range(members))
+    place = [placed(i) for i in range(members)]
+
+    def move(value, pairs, source, target, groups=(0, 1)):
+        return lax.ppermute(
+            value, EVERY, [(source[a] + g * members, target[b] + g * members) for g in groups for a, b in pairs]
+        )
+
+    def trade(a, b, groups=(0, 1), source=place):
+        return move(a, near_pairs, source, place, groups), move(b, far_pairs, source, place, groups)
 
     row8, table8 = ((8, width), F32), ((8, half), F32)
     wide = ((channels, half), BF16)
     by_site = ((channels, width), BF16)
     ints = jnp.int32
-    site, mine, lent_a, lent_b, slots, picks = call(
-        rows_kernel,
-        [row8, ((2, 4, half), F32), table8, table8, ((slot_count, width), ints), ((2, half), ints)],
+    itself = [(i, i) for i in range(members)]
+    pack, mine, lent_a, lent_b = call(
+        rows_kernel, [((slot_count + 16, width), F32), ((2, 4, half), F32), table8, table8],
         (), (positions, charges[None], polar[None], neighbours.T, send_rows, blocks),
         [pltpu.VMEM((3, width), F32), pltpu.VMEM((1, width), F32), pltpu.VMEM((1, width), F32),
          pltpu.VMEM((slot_count, width), ints), pltpu.VMEM((2, half), ints), pltpu.SMEM((listed,), ints)], 6,
     )
-    rim_a, rim_b = trade(lent_a, lent_b)
     partner = lax.ppermute(mine, "grp", [(0, 1), (1, 0)])
-    partner, rim_a, rim_b = lax.optimization_barrier((partner, rim_a, rim_b))
     copies = jnp.broadcast_to(partner[None], (members,) + partner.shape)
     near = lax.all_to_all(copies, DOM, 0, 0, tiled=True).reshape(2 * members, 4, half)
+    pack = move(pack, itself, same, place)
+    rim_a, rim_b = trade(lent_a, lent_b, source=same)
+    features = move(features, itself, same, place, (0,))
     feat_t, w3, w5, fixed, entry, lent_a, lent_b = call(
         static_kernel, [by_site, ((depth, width), F32), ((depth, width), F32), row8, ((depth, 8), F32), wide, wide],
-        (site, rim_a, rim_b, slots, picks), (features,), [pltpu.VMEM((width, channels), BF16)], 1,
+        (pack, rim_a, rim_b), (features,), [pltpu.VMEM((width, channels), BF16)], 1, loose=1,
     )
     side_a, side_b = trade(lent_a, lent_b)
     third_shape = (LAYERS * radial_in.shape[2], slot_count * width)
     (third,) = call(
-        radial_kernel, [(third_shape, BF16)], (site, rim_a, rim_b, slots), (radial_in, radial_mid),
+        radial_kernel, [(third_shape, BF16)], (pack, rim_a, rim_b), (radial_in, radial_mid),
         [pltpu.VMEM(radial_in.shape, BF16), pltpu.VMEM(radial_mid.shape, BF16), pltpu.VMEM(third_shape, BF16)], 3, 1,
     )
     moment = pltpu.VMEM((depth, 8), F32)
@@ -514,32 +539,33 @@
     last = pltpu.VMEM(radial_out.shape[1:], BF16)
     outside_row, near_own, hidden, lifted, fixed_all, dipole, lent_a, lent_b = call(
         first_kernel, [row8, ((listed, 4, half), F32), by_site, by_site, row8, row8, wide, wide],
-        (site, rim_a, rim_b, slots, picks, feat_t, side_a, side_b, w3, w5, fixed, entry),
-        (near, blocks, third, node_in, node_out, radial_out, field_gain[None]),
-        [pltpu.SMEM((listed,), ints), pltpu.VMEM((3 * listed, 4, half), F32), pltpu.VMEM((3 * listed * half, 8), F32),
+        (pack, rim_a, rim_b, feat_t, side_a, side_b, w3, w5, fixed, entry),
+        (near, third, node_in, node_out, radial_out, field_gain[None]),
+        [pltpu.VMEM((3 * listed, 4, half), F32), pltpu.VMEM((3 * listed * half, 8), F32),
          pltpu.VMEM(third_shape, BF16), pltpu.VMEM(node_in.shape, BF16), square, last,
-         pltpu.VMEM((1, channels), F32), total, moment], 6 + 3 * listed, loose=1,
+         pltpu.VMEM((1, channels), F32), total, moment], 5 + 3 * listed, loose=1,
     )
     side_a, side_b = trade(lent_a, lent_b)
     charge, dipole, small_a, small_b = call(
         second_kernel, [row8, row8, table8, table8],
-        (hidden, lifted, side_a, side_b, slots, picks, site, w3, w5, fixed_all, dipole, entry),
+        (hidden, lifted, side_a, side_b, pack, w3, w5, fixed_all, dipole, entry),
         (third, node_out, radial_out, readout.T),
         [pltpu.VMEM(third_shape, BF16), square, last, pltpu.VMEM((2, channels), BF16), total, moment], 4,
     )
-    side_a, side_b = trade(small_a, small_b, True)
+    side_a, side_b = trade(small_a, small_b, (1,))
     dipole, small_a, small_b = call(
-        third_kernel, [row8, table8, table8], (side_a, side_b, picks, site, w3, w5, fixed_all, dipole, entry),
+        third_kernel, [row8, table8, table8], (side_a, side_b, pack, w3, w5, fixed_all, dipole, entry),
         (), [moment],
     )
-    side_a, side_b = trade(small_a, small_b, True)
+    side_a, side_b = trade(small_a, small_b, (1,))
     result, spread = call(
         response_kernel, [((3, width), F32), ((3 * members, 2, half), F32)],
-        (near_own, site, charge, outside_row, side_a, side_b, w3, w5, fixed_all, dipole, entry), (blocks,),
-        [pltpu.SMEM((listed,), ints), pltpu.VMEM((width, 8), F32), moment, pltpu.VMEM((listed, 4, half), F32)], 1,
+        (near_own, pack, charge, outside_row, side_a, side_b, w3, w5, fixed_all, dipole, entry), (),
+        [pltpu.VMEM((width, 8), F32), moment, pltpu.VMEM((listed, 4, half), F32)],
     )
     pieces = lax.all_to_all(spread, DOM, 0, 0, tiled=True).reshape(members, 3, 2, half)
     (share,) = call(gather_kernel, [((3, width), F32)], (pieces,))
+    result = move(result, itself, place, same)
     return result, lax.ppermute(share, "grp", [(0, 1), (1, 0)])
 
 

time: 116 us -> 113 us (0.974)
  blocking collectives: 36 us -> 0 us
  starting transfers between devices: 46.5 us -> 74.6 us
  waiting for transfers between devices: 16.9 us -> 21.1 us
    all_to_all x1 -> x0, blocking collectives: 36 us -> none  [local(): lax.all_to_all(spread, DOM, 0, 0, tiled=True).reshape(members, 3, 2, half)]
    all_to_all x0 -> x1, starting transfers between devices: none -> 23.1 us  [local(): lax.all_to_all(spread, DOM, 0, 0, tiled=True).reshape(members, 3, 2, half)]
    all_to_all x0 -> x1, waiting for transfers between devices: none -> 15.9 us  [local(): lax.all_to_all(spread, DOM, 0, 0, tiled=True).reshape(members, 3, 2, half)]
    ppermute x10 -> x13, starting transfers between devices: 23.9 us -> 33 us  [move(): lax.ppermute(value, EVERY, [(source[a] + g * members, target[b] + g * mem...]
    all_to_all x1, waiting for transfers between devices: 7.4 us -> 0.01 us  [local(): lax.all_to_all(copies, DOM, 0, 0, tiled=True).reshape(2 * members, 4, half)]
    all_to_all x1, starting transfers between devices: 19.2 us -> 13.8 us  [local(): lax.all_to_all(copies, DOM, 0, 0, tiled=True).reshape(2 * members, 4, half)]
    ppermute x10 -> x13, waiting for transfers between devices: 8.37 us -> 3.54 us  [move(): lax.ppermute(value, EVERY, [(source[a] + g * members, target[b] + g * mem...]
    ppermute x1, starting transfers between devices: 0.09 us -> 1.36 us  [local(): return (result, lax.ppermute(share, 'grp', [(0, 1), (1, 0)]))]
  transfers between devices with their start and end apart: 13 -> 17, of which waited for: 7 -> 8; matrix products, arithmetic and copies ran while one was open for 0% -> 0% of each run, Pallas kernels for 2% -> 3%
where the time goes in v4:
time: 113 us; the launch traced here: 112 us
  starting transfers between devices  74.6 us (66%)
  waiting for transfers between devices  21.1 us (19%)
  Pallas kernels  13.6 us (12%)
  local copies, waits for them, and re-layouts  2.05 us (2%)
    ppermute x13, starting transfers between devices, move(): lax.ppermute(value, EVERY, [(source[a] + g * members, target[b] + g * mem...  33 us
    all_to_all x1, starting transfers between devices, local(): lax.all_to_all(spread, DOM, 0, 0, tiled=True).reshape(members, 3, 2, half)  23.1 us
    all_to_all x1, waiting for transfers between devices, local(): lax.all_to_all(spread, DOM, 0, 0, tiled=True).reshape(members, 3, 2, half)  15.9 us
    all_to_all x1, starting transfers between devices, local(): lax.all_to_all(copies, DOM, 0, 0, tiled=True).reshape(2 * members, 4, half)  13.8 us
    pallas_call x8, Pallas kernels, call(): pl.pallas_call(body, out_shape=[jax.ShapeDtypeStruct(s, d) for s, d in ou...  13.6 us
    ppermute x13, waiting for transfers between devices, move(): lax.ppermute(value, EVERY, [(source[a] + g * members, target[b] + g * mem...  3.54 us
    ppermute x1, starting transfers between devices, local(): partner = lax.ppermute(mine, 'grp', [(0, 1), (1, 0)])  3.33 us
  transfers between devices with their start and end apart: 17, of which 8 were waited for; matrix products, arithmetic and copies ran while one was open for 0% of the time, Pallas kernels for 3%

profile of v4, /device:TPU:1, one launch (start us, length us, event | category | flops | bytes accessed | tf_op | source)
XLA Modules:
  0.0 112.1 jit_solution(2127484059224548102)
XLA Ops:
  0.6 1.0 shard_map.149
  1.7 3.3 %collective-permute-start.6 = (f32[2,4,128]{2,1,0:T(4,128)S(1)}, f32[2,4,128]{2,1,0:T(4,128)S(1)}, u32[]{:S(2)}, u32[]{:S(2)}) collective-permute-start(f32[2,4,128]{2,1,0:T(4,128)S(1)} %get-tuple-element.40), channel_id=1, source_target_pairs={{0,128},{128,0},{1,129},{129,1},{2,130},{130,2},{3,131},{131,3},{4... | collective-permute-start | bytes 12296 | tf_op jit(solution)/shard_map/ppermute | solution.py:520
  5.0 0.8 collective-permute-done.6
  5.8 0.9 broadcast_in_dim.17
  6.7 13.8 %all-to-all-start = ((f32[128,2,4,128]{3,2,1,0:T(4,128)}), f32[128,2,4,128]{3,2,1,0:T(4,128)S(1)}, u32[]{:S(2)}, u32[]{:S(2)}) async-start(f32[128,2,4,128]{3,2,1,0:T(4,128)} %broadcast_in_dim.17), calls=%async_computation | async-start | bytes 1048576 | tf_op jit(solution)/shard_map/all_to_all | solution.py:522
  20.5 0.7 collective-permute-start.3
  21.1 0.7 collective-permute-start
  21.8 5.8 %collective-permute-start.1 = (f32[8,128]{1,0:T(8,128)S(1)}, f32[8,128]{1,0:T(8,128)S(1)}, u32[]{:S(2)}, u32[]{:S(2)}) collective-permute-start(f32[8,128]{1,0:T(8,128)S(1)} %get-tuple-element.31), channel_id=1, source_target_pairs={{0,64},{1,0},{2,2},{3,66},{4,68},{5,4},{6,6},{7,70},{8,78},{9,14},... | collective-permute-start | bytes 12296 | tf_op jit(solution)/shard_map/ppermute | solution.py:502
  27.7 0.7 collective-permute-start.2
  28.3 0.6 collective-permute-done.1.rim_a
  28.9 0.0 collective-permute-done.2.rim_b
  28.9 0.0 collective-permute-done.pack
  28.9 0.0 collective-permute-done.3.features_far
  29.0 2.7 %shard_map.150 = (bf16[256,256]{1,0:T(8,128)(2,1)S(1)}, f32[512,256]{1,0:T(8,128)S(1)}, f32[512,256]{1,0:T(8,128)S(1)}, f32[8,256]{1,0:T(8,128)S(1)}, f32[512,8]...) custom-call(f32[48,256]{1,0:T(8,128)S(1)} %collective-permute-done.pack, ...), custom_call_target="tpu_custom_call" | custom-call | tf_op jit(solution)/shard_map/pallas_call | solution.py:27
  31.7 6.5 %collective-permute-start.4 = (bf16[256,128]{1,0:T(8,128)(2,1)S(1)}, bf16[256,128]{1,0:T(8,128)(2,1)S(1)}, u32[]{:S(2)}, u32[]{:S(2)}) collective-permute-start(bf16[256,128]{1,0:T(8,128)(2,1)S(1)} %get-tuple-element.34), channel_id=1, source_target_pairs={{0,64},{64,0},{66,2},{2,66},{4,68},{68,4},{70,6},{6,70},{14,78},{7... | collective-permute-start | bytes 196616 | tf_op jit(solution)/shard_map/ppermute | solution.py:502
  38.1 0.7 collective-permute-start.5
  38.8 1.3 %collective-permute-done.4.side_a = bf16[256,128]{1,0:T(8,128)(2,1)S(1)} collective-permute-done((bf16[256,128]{1,0:T(8,128)(2,1)S(1)}, bf16[256,128]{1,0:T(8,128)(2,1)S(1)}, u32[]{:S(2)}, u32[]{:S(2)}) %collective-permute-start.4) | collective-permute-done | bytes 65568 | tf_op jit(solution)/shard_map/ppermute | solution.py:502
  40.1 0.0 collective-permute-done.5.side_b
  40.1 0.0 all-to-all-done
  40.1 3.8 %shard_map.152 = (f32[8,256]{1,0:T(8,128)S(1)}, f32[4,4,128]{2,1,0:T(4,128)S(1)}, bf16[256,256]{1,0:T(8,128)(2,1)S(1)}, bf16[256,256]{1,0:T(8,128)(2,1)S(1)}, f3...) custom-call(f32[48,256]{1,0:T(8,128)S(1)} %collective-permute-done.pack,, ...), custom_call_target="tpu_custom_call" | custom-call | tf_op jit(solution)/shard_map/pallas_call | solution.py:27
  44.0 3.1 %collective-permute-start.7 = (bf16[256,128]{1,0:T(8,128)(2,1)S(1)}, bf16[256,128]{1,0:T(8,128)(2,1)S(1)}, u32[]{:S(2)}, u32[]{:S(2)}) collective-permute-start(bf16[256,128]{1,0:T(8,128)(2,1)S(1)} %get-tuple-element.44), channel_id=1, source_target_pairs={{0,64},{64,0},{66,2},{2,66},{4,68},{68,4},{70,6},{6,70},{14,78},{7... | collective-permute-start | bytes 196616 | tf_op jit(solution)/shard_map/ppermute | solution.py:502
  47.1 0.7 collective-permute-start.8
  47.8 1.0 collective-permute-done.7.side_a
  48.7 0.0 collective-permute-done.8.side_b
  48.7 1.2 %shard_map.153 = (f32[8,256]{1,0:T(8,128)S(1)}, f32[8,256]{1,0:T(8,128)S(1)}, f32[8,128]{1,0:T(8,128)S(1)}, f32[8,128]{1,0:T(8,128)S(1)}) custom-call(bf16[256,256]{1,0:T(8,128)(2,1)S(1)} %get-tuple-element.42.hidden, bf16[256,256]{1,0:T(8,128)(2,1)S(1)} %get-tuple-element.43.lifted, bf16[256,128]{1,0:T(8,128)(2,1)S(1)} %collective-permute-done.7.side_a, ...), custom_call_target="tpu_custom_call" | custom-call | tf_op jit(solution)/shard_map/pallas_call | solution.py:27
  50.0 5.6 %collective-permute-start.9 = (f32[8,128]{1,0:T(8,128)S(1)}, f32[8,128]{1,0:T(8,128)S(1)}, u32[]{:S(2)}, u32[]{:S(2)}) collective-permute-start(f32[8,128]{1,0:T(8,128)S(1)} %get-tuple-element.50), channel_id=1, source_target_pairs={{128,192},{192,128},{194,130},{130,194},{132,196},{196,132},{198,1... | collective-permute-start | bytes 12296 | tf_op jit(solution)/shard_map/ppermute | solution.py:502
  55.6 0.7 collective-permute-start.10
  56.2 0.3 collective-permute-done.9.side_a
  56.5 0.0 collective-permute-done.10.side_b
  56.5 1.2 %shard_map.154 = (f32[8,256]{1,0:T(8,128)S(1)}, f32[8,128]{1,0:T(8,128)S(1)}, f32[8,128]{1,0:T(8,128)S(1)}) custom-call(f32[8,128]{1,0:T(8,128)S(1)} %collective-permute-done.9.side_a, f32[8,128]{1,0:T(8,128)S(1)} %collective-permute-done.10.side_b, f32[48,256]{1,0:T(8,128)S(1)} %collective-permute-done.pack, f32[512,256]{1,0:T(8,128)S(1)} %get-tuple-element.36.w3, ...), custom_call_target="tpu_custom_call" | custom-call | tf_op jit(solution)/shard_map/pallas_call | solution.py:27
  57.7 6.7 %collective-permute-start.11 = (f32[8,128]{1,0:T(8,128)S(1)}, f32[8,128]{1,0:T(8,128)S(1)}, u32[]{:S(2)}, u32[]{:S(2)}) collective-permute-start(f32[8,128]{1,0:T(8,128)S(1)} %get-tuple-element.53), channel_id=1, source_target_pairs={{128,192},{192,128},{194,130},{130,194},{132,196},{196,132},{198,1... | collective-permute-start | bytes 12296 | tf_op jit(solution)/shard_map/ppermute | solution.py:502
  64.4 0.7 collective-permute-start.12
  65.1 0.3 collective-permute-done.11.side_a
  65.4 0.0 collective-permute-done.12.side_b
  65.4 3.4 %shard_map.155 = (f32[3,256]{1,0:T(4,128)S(1)}, f32[384,2,128]{2,1,0:T(2,128)}) custom-call(f32[4,4,128]{2,1,0:T(4,128)S(1)} %get-tuple-element.41.near, f32[48,256]{1,0:T(8,128)S(1)} %collective-permute-done.pack, f32[8,256]{1,0:T(8,128)S(1)} %get-tuple-element.48.charge, f32[8,256]{1,0:T(8,128)S(1)} %get-tuple-element.49.outside_row, ...), custom_call_target="tpu_custom_call" | custom-call | tf_op jit(solution)/shard_map/pallas_call | solution.py:27
  68.8 23.1 %all-to-all-start.1 = ((f32[384,2,128]{2,1,0:T(2,128)}), f32[384,2,128]{2,1,0:T(2,128)S(1)}, u32[]{:S(2)}, u32[]{:S(2)}) async-start(f32[384,2,128]{2,1,0:T(2,128)} %get-tuple-element.57), calls=%async_computation.1 | async-start | bytes 786432 | tf_op jit(solution)/shard_map/all_to_all | solution.py:566
  92.0 0.7 collective-permute-start.13
  92.6 15.9 %all-to-all-done.1 = f32[384,2,128]{2,1,0:T(2,128)S(1)} async-done(((f32[384,2,128]{2,1,0:T(2,128)}), f32[384,2,128]{2,1,0:T(2,128)S(1)}, u32[]{:S(2)}, u32[]{:S(2)}) %all-to-all-start.1) | async-done | bytes 393248 | tf_op jit(solution)/shard_map/all_to_all | solution.py:566
  108.6 0.2 shard_map.156
  108.7 1.4 %collective-permute-start.14 = (f32[3,256]{1,0:T(4,128)S(1)}, f32[3,256]{1,0:T(4,128)S(1)}, u32[]{:S(2)}, u32[]{:S(2)}) collective-permute-start(f32[3,256]{1,0:T(4,128)S(1)} %shard_map.156), channel_id=1, source_target_pairs={{0,128},{128,0},{1,129},{129,1},{2,130},{130,2},{3,131},{131,3},{4... | collective-permute-start | bytes 9224 | tf_op jit(solution)/shard_map/ppermute | solution.py:569
  110.1 0.0 collective-permute-done.13
  110.1 0.8 collective-permute-done.14
  110.9 0.6 copy.18
  111.5 0.6 copy.19
  (1 shorter events, 0.0 us)
Async XLA Ops:
  1.7 4.2 %collective-permute-start.6 = (f32[2,4,128]{2,1,0:T(4,128)S(1)}, f32[2,4,128]{2,1,0:T(4,128)S(1)}, u32[]{:S(2)}, u32[]{:S(2)}) collective-permute-start(f32[2,4,128]{2,1,0:T(4,128)S(1)} %get-tuple-element.40), channel_id=1, source_target_pairs={{0,128},{128,0},{1,129},{129,1},{2,130},{130,2},{3,131},{131,3},{4... | collective-permute-start | bytes 12296 | tf_op jit(solution)/shard_map/ppermute | solution.py:520
  6.7 33.4 %all-to-all-start = ((f32[128,2,4,128]{3,2,1,0:T(4,128)}), f32[128,2,4,128]{3,2,1,0:T(4,128)S(1)}, u32[]{:S(2)}, u32[]{:S(2)}) async-start(f32[128,2,4,128]{3,2,1,0:T(4,128)} %broadcast_in_dim.17), calls=%async_computation | async-start | bytes 1048576 | tf_op jit(solution)/shard_map/all_to_all | solution.py:522
  20.5 8.5 %collective-permute-start.3 = (bf16[256,256]{1,0:T(8,128)(2,1)}, bf16[256,256]{1,0:T(8,128)(2,1)S(1)}, u32[]{:S(2)}, u32[]{:S(2)}) collective-permute-start(bf16[256,256]{1,0:T(8,128)(2,1)} %param.17), channel_id=1, source_target_pairs={{0,0},{1,64},{2,66},{3,2},{4,4},{5,68},{6,70},{7,6},{8,14},{9,78},... | collective-permute-start | bytes 393224 | tf_op jit(solution)/shard_map/ppermute | solution.py:502
  21.1 7.8 %collective-permute-start = (f32[48,256]{1,0:T(8,128)S(1)}, f32[48,256]{1,0:T(8,128)S(1)}, u32[]{:S(2)}, u32[]{:S(2)}) collective-permute-start(f32[48,256]{1,0:T(8,128)S(1)} %get-tuple-element.30), channel_id=1, source_target_pairs={{0,0},{1,64},{2,66},{3,2},{4,4},{5,68},{6,70},{7,6},{8,14},{9,78},... | collective-permute-start | bytes 147464 | tf_op jit(solution)/shard_map/ppermute | solution.py:502
  21.8 7.1 %collective-permute-start.1 = (f32[8,128]{1,0:T(8,128)S(1)}, f32[8,128]{1,0:T(8,128)S(1)}, u32[]{:S(2)}, u32[]{:S(2)}) collective-permute-start(f32[8,128]{1,0:T(8,128)S(1)} %get-tuple-element.31), channel_id=1, source_target_pairs={{0,64},{1,0},{2,2},{3,66},{4,68},{5,4},{6,6},{7,70},{8,78},{9,14},... | collective-permute-start | bytes 12296 | tf_op jit(solution)/shard_map/ppermute | solution.py:502
  27.7 1.3 %collective-permute-start.2 = (f32[8,128]{1,0:T(8,128)S(1)}, f32[8,128]{1,0:T(8,128)S(1)}, u32[]{:S(2)}, u32[]{:S(2)}) collective-permute-start(f32[8,128]{1,0:T(8,128)S(1)} %get-tuple-element.32), channel_id=1, source_target_pairs={{1,66},{2,64},{3,4},{4,2},{5,70},{6,68},{7,14},{8,6},{9,76},{10,78... | collective-permute-start | bytes 12296 | tf_op jit(solution)/shard_map/ppermute | solution.py:502
  31.7 8.5 %collective-permute-start.4 = (bf16[256,128]{1,0:T(8,128)(2,1)S(1)}, bf16[256,128]{1,0:T(8,128)(2,1)S(1)}, u32[]{:S(2)}, u32[]{:S(2)}) collective-permute-start(bf16[256,128]{1,0:T(8,128)(2,1)S(1)} %get-tuple-element.34), channel_id=1, source_target_pairs={{0,64},{64,0},{66,2},{2,66},{4,68},{68,4},{70,6},{6,70},{14,78},{7... | collective-permute-start | bytes 196616 | tf_op jit(solution)/shard_map/ppermute | solution.py:502
  38.1 2.0 %collective-permute-start.5 = (bf16[256,128]{1,0:T(8,128)(2,1)S(1)}, bf16[256,128]{1,0:T(8,128)(2,1)S(1)}, u32[]{:S(2)}, u32[]{:S(2)}) collective-permute-start(bf16[256,128]{1,0:T(8,128)(2,1)S(1)} %get-tuple-element.35), channel_id=1, source_target_pairs={{64,66},{66,64},{2,4},{4,2},{68,70},{70,68},{6,14},{14,6},{78,76},... | collective-permute-start | bytes 196616 | tf_op jit(solution)/shard_map/ppermute | solution.py:502
  44.0 4.8 %collective-permute-start.7 = (bf16[256,128]{1,0:T(8,128)(2,1)S(1)}, bf16[256,128]{1,0:T(8,128)(2,1)S(1)}, u32[]{:S(2)}, u32[]{:S(2)}) collective-permute-start(bf16[256,128]{1,0:T(8,128)(2,1)S(1)} %get-tuple-element.44), channel_id=1, source_target_pairs={{0,64},{64,0},{66,2},{2,66},{4,68},{68,4},{70,6},{6,70},{14,78},{7... | collective-permute-start | bytes 196616 | tf_op jit(solution)/shard_map/ppermute | solution.py:502
  47.1 1.7 %collective-permute-start.8 = (bf16[256,128]{1,0:T(8,128)(2,1)S(1)}, bf16[256,128]{1,0:T(8,128)(2,1)S(1)}, u32[]{:S(2)}, u32[]{:S(2)}) collective-permute-start(bf16[256,128]{1,0:T(8,128)(2,1)S(1)} %get-tuple-element.45), channel_id=1, source_target_pairs={{64,66},{66,64},{2,4},{4,2},{68,70},{70,68},{6,14},{14,6},{78,76},... | collective-permute-start | bytes 196616 | tf_op jit(solution)/shard_map/ppermute | solution.py:502
  50.0 6.6 %collective-permute-start.9 = (f32[8,128]{1,0:T(8,128)S(1)}, f32[8,128]{1,0:T(8,128)S(1)}, u32[]{:S(2)}, u32[]{:S(2)}) collective-permute-start(f32[8,128]{1,0:T(8,128)S(1)} %get-tuple-element.50), channel_id=1, source_target_pairs={{128,192},{192,128},{194,130},{130,194},{132,196},{196,132},{198,1... | collective-permute-start | bytes 12296 | tf_op jit(solution)/shard_map/ppermute | solution.py:502
  55.6 1.0 collective-permute-start.10
  57.7 7.7 %collective-permute-start.11 = (f32[8,128]{1,0:T(8,128)S(1)}, f32[8,128]{1,0:T(8,128)S(1)}, u32[]{:S(2)}, u32[]{:S(2)}) collective-permute-start(f32[8,128]{1,0:T(8,128)S(1)} %get-tuple-element.53), channel_id=1, source_target_pairs={{128,192},{192,128},{194,130},{130,194},{132,196},{196,132},{198,1... | collective-permute-start | bytes 12296 | tf_op jit(solution)/shard_map/ppermute | solution.py:502
  64.4 1.0 collective-permute-start.12
  68.8 39.7 %all-to-all-start.1 = ((f32[384,2,128]{2,1,0:T(2,128)}), f32[384,2,128]{2,1,0:T(2,128)S(1)}, u32[]{:S(2)}, u32[]{:S(2)}) async-start(f32[384,2,128]{2,1,0:T(2,128)} %get-tuple-element.57), calls=%async_computation.1 | async-start | bytes 786432 | tf_op jit(solution)/shard_map/all_to_all | solution.py:566
  92.0 18.1 %collective-permute-start.13 = (f32[3,256]{1,0:T(4,128)S(1)}, f32[3,256]{1,0:T(4,128)S(1)}, u32[]{:S(2)}, u32[]{:S(2)}) collective-permute-start(f32[3,256]{1,0:T(4,128)S(1)} %get-tuple-element.56), channel_id=1, source_target_pairs={{0,0},{64,1},{66,2},{2,3},{4,4},{68,5},{70,6},{6,7},{14,8},{78,9},... | collective-permute-start | bytes 9224 | tf_op jit(solution)/shard_map/ppermute | solution.py:502
  108.7 2.2 %collective-permute-start.14 = (f32[3,256]{1,0:T(4,128)S(1)}, f32[3,256]{1,0:T(4,128)S(1)}, u32[]{:S(2)}, u32[]{:S(2)}) collective-permute-start(f32[3,256]{1,0:T(4,128)S(1)} %shard_map.156), channel_id=1, source_target_pairs={{0,128},{128,0},{1,129},{129,1},{2,130},{130,2},{3,131},{131,3},{4... | collective-permute-start | bytes 9224 | tf_op jit(solution)/shard_map/ppermute | solution.py:569

commit v5 on v4

--- a/solution.py
+++ b/solution.py
@@ -475,10 +475,11 @@
 
 
 def placed(block):
-    y_half, z, step, side = block // 64, block // 8 % 8, block // 2 % 4, block % 2
-    x = 3 - step if z % 2 else step
-    along = 1 - side if step % 2 else side
-    y = 3 - along if y_half else along
+    y_half, plane, step, side = block // 64, block // 8 % 8, block // 2 % 4, block % 2
+    x = 3 - step if plane % 2 else step
+    z = (plane - 1) % 8 if y_half else plane
+    along = 1 - side if (step + y_half) % 2 == 0 else side
+    y = 2 * y_half + along
     return ((y % 2 * 8 + z) * 4 + x) * 2 + y // 2
 
 

time: 113 us -> 111 us (0.982)
  starting transfers between devices: 74.6 us -> 69.6 us
  waiting for transfers between devices: 21.1 us -> 24.9 us
    ppermute x13, waiting for transfers between devices: 3.54 us -> 13.9 us  [move(): lax.ppermute(value, EVERY, [(source[a] + g * members, target[b] + g * mem...]
    all_to_all x1, starting transfers between devices: 23.1 us -> 15 us  [local(): lax.all_to_all(spread, DOM, 0, 0, tiled=True).reshape(members, 3, 2, half)]
    all_to_all x1, waiting for transfers between devices: 15.9 us -> 9.33 us  [local(): lax.all_to_all(spread, DOM, 0, 0, tiled=True).reshape(members, 3, 2, half)]
    ppermute x1, starting transfers between devices: 1.36 us -> 5.43 us  [local(): return (result, lax.ppermute(share, 'grp', [(0, 1), (1, 0)]))]
where the time goes in v5:
time: 111 us
  starting transfers between devices  69.6 us (63%)
  waiting for transfers between devices  24.9 us (22%)
  Pallas kernels  13.5 us (12%)
  local copies, waits for them, and re-layouts  2.05 us (2%)
    ppermute x13, starting transfers between devices, move(): lax.ppermute(value, EVERY, [(source[a] + g * members, target[b] + g * mem...  32 us
    all_to_all x1, starting transfers between devices, local(): lax.all_to_all(spread, DOM, 0, 0, tiled=True).reshape(members, 3, 2, half)  15 us
    ppermute x13, waiting for transfers between devices, move(): lax.ppermute(value, EVERY, [(source[a] + g * members, target[b] + g * mem...  13.9 us
    all_to_all x1, starting transfers between devices, local(): lax.all_to_all(copies, DOM, 0, 0, tiled=True).reshape(2 * members, 4, half)  13.8 us
    pallas_call x8, Pallas kernels, call(): pl.pallas_call(body, out_shape=[jax.ShapeDtypeStruct(s, d) for s, d in ou...  13.5 us
    all_to_all x1, waiting for transfers between devices, local(): lax.all_to_all(spread, DOM, 0, 0, tiled=True).reshape(members, 3, 2, half)  9.33 us
    ppermute x1, starting transfers between devices, local(): return (result, lax.ppermute(share, 'grp', [(0, 1), (1, 0)]))  5.43 us
    ppermute x1, starting transfers between devices, local(): partner = lax.ppermute(mine, 'grp', [(0, 1), (1, 0)])  3.33 us
  transfers between devices with their start and end apart: 17, of which 8 were waited for; matrix products, arithmetic and copies ran while one was open for 0% of the time, Pallas kernels for 3%

profile of v5, /device:TPU:1, one launch (start us, length us, event | category | flops | bytes accessed | tf_op | source)
XLA Modules:
  0.0 110.9 jit_solution(4147459336389778442)
XLA Ops:
  0.6 1.0 shard_map.149
  1.7 3.3 %collective-permute-start.6 = (f32[2,4,128]{2,1,0:T(4,128)S(1)}, f32[2,4,128]{2,1,0:T(4,128)S(1)}, u32[]{:S(2)}, u32[]{:S(2)}) collective-permute-start(f32[2,4,128]{2,1,0:T(4,128)S(1)} %get-tuple-element.40), channel_id=1, source_target_pairs={{0,128},{128,0},{1,129},{129,1},{2,130},{130,2},{3,131},{131,3},{4... | collective-permute-start | bytes 12296 | tf_op jit(solution)/shard_map/ppermute | solution.py:521
  5.0 0.8 collective-permute-done.6
  5.8 0.9 broadcast_in_dim.17
  6.7 13.8 %all-to-all-start = ((f32[128,2,4,128]{3,2,1,0:T(4,128)}), f32[128,2,4,128]{3,2,1,0:T(4,128)S(1)}, u32[]{:S(2)}, u32[]{:S(2)}) async-start(f32[128,2,4,128]{3,2,1,0:T(4,128)} %broadcast_in_dim.17), calls=%async_computation | async-start | bytes 1048576 | tf_op jit(solution)/shard_map/all_to_all | solution.py:523
  20.5 0.7 collective-permute-start.3
  21.1 2.8 %collective-permute-start = (f32[48,256]{1,0:T(8,128)S(1)}, f32[48,256]{1,0:T(8,128)S(1)}, u32[]{:S(2)}, u32[]{:S(2)}) collective-permute-start(f32[48,256]{1,0:T(8,128)S(1)} %get-tuple-element.30), channel_id=1, source_target_pairs={{0,64},{1,0},{2,2},{3,66},{4,68},{5,4},{6,6},{7,70},{8,78},{9,14},... | collective-permute-start | bytes 147464 | tf_op jit(solution)/shard_map/ppermute | solution.py:503
  23.9 0.7 collective-permute-start.1
  24.6 1.3 %collective-permute-start.2 = (f32[8,128]{1,0:T(8,128)S(1)}, f32[8,128]{1,0:T(8,128)S(1)}, u32[]{:S(2)}, u32[]{:S(2)}) collective-permute-start(f32[8,128]{1,0:T(8,128)S(1)} %get-tuple-element.32), channel_id=1, source_target_pairs={{1,2},{2,0},{3,68},{4,66},{5,6},{6,4},{7,78},{8,70},{9,12},{10,14}... | collective-permute-start | bytes 12296 | tf_op jit(solution)/shard_map/ppermute | solution.py:503
  25.9 0.0 collective-permute-done.1.rim_a
  25.9 8.6 %collective-permute-done.2.rim_b = f32[8,128]{1,0:T(8,128)S(1)} collective-permute-done((f32[8,128]{1,0:T(8,128)S(1)}, f32[8,128]{1,0:T(8,128)S(1)}, u32[]{:S(2)}, u32[]{:S(2)}) %collective-permute-start.2) | collective-permute-done | bytes 4128 | tf_op jit(solution)/shard_map/ppermute | solution.py:503
  34.6 0.0 collective-permute-done.pack
  34.6 0.0 collective-permute-done.3.features_far
  34.6 2.7 %shard_map.150 = (bf16[256,256]{1,0:T(8,128)(2,1)S(1)}, f32[512,256]{1,0:T(8,128)S(1)}, f32[512,256]{1,0:T(8,128)S(1)}, f32[8,256]{1,0:T(8,128)S(1)}, f32[512,8]...) custom-call(f32[48,256]{1,0:T(8,128)S(1)} %collective-permute-done.pack, ...), custom_call_target="tpu_custom_call" | custom-call | tf_op jit(solution)/shard_map/pallas_call | solution.py:27
  37.3 2.6 %collective-permute-start.4 = (bf16[256,128]{1,0:T(8,128)(2,1)S(1)}, bf16[256,128]{1,0:T(8,128)(2,1)S(1)}, u32[]{:S(2)}, u32[]{:S(2)}) collective-permute-start(bf16[256,128]{1,0:T(8,128)(2,1)S(1)} %get-tuple-element.34), channel_id=1, source_target_pairs={{64,0},{0,64},{2,66},{66,2},{68,4},{4,68},{6,70},{70,6},{78,14},{1... | collective-permute-start | bytes 196616 | tf_op jit(solution)/shard_map/ppermute | solution.py:503
  39.8 3.3 %collective-permute-start.5 = (bf16[256,128]{1,0:T(8,128)(2,1)S(1)}, bf16[256,128]{1,0:T(8,128)(2,1)S(1)}, u32[]{:S(2)}, u32[]{:S(2)}) collective-permute-start(bf16[256,128]{1,0:T(8,128)(2,1)S(1)} %get-tuple-element.35), channel_id=1, source_target_pairs={{0,2},{2,0},{66,68},{68,66},{4,6},{6,4},{70,78},{78,70},{14,12},{1... | collective-permute-start | bytes 196616 | tf_op jit(solution)/shard_map/ppermute | solution.py:503
  43.2 0.0 collective-permute-done.4.side_a
  43.2 1.7 %collective-permute-done.5.side_b = bf16[256,128]{1,0:T(8,128)(2,1)S(1)} collective-permute-done((bf16[256,128]{1,0:T(8,128)(2,1)S(1)}, bf16[256,128]{1,0:T(8,128)(2,1)S(1)}, u32[]{:S(2)}, u32[]{:S(2)}) %collective-permute-start.5) | collective-permute-done | bytes 65568 | tf_op jit(solution)/shard_map/ppermute | solution.py:503
  44.8 0.0 all-to-all-done
  44.8 3.8 %shard_map.152 = (f32[8,256]{1,0:T(8,128)S(1)}, f32[4,4,128]{2,1,0:T(4,128)S(1)}, bf16[256,256]{1,0:T(8,128)(2,1)S(1)}, bf16[256,256]{1,0:T(8,128)(2,1)S(1)}, f3...) custom-call(f32[48,256]{1,0:T(8,128)S(1)} %collective-permute-done.pack,, ...), custom_call_target="tpu_custom_call" | custom-call | tf_op jit(solution)/shard_map/pallas_call | solution.py:27
  48.7 0.1 collective-permute-start.7
  48.8 4.7 %collective-permute-start.8 = (bf16[256,128]{1,0:T(8,128)(2,1)S(1)}, bf16[256,128]{1,0:T(8,128)(2,1)S(1)}, u32[]{:S(2)}, u32[]{:S(2)}) collective-permute-start(bf16[256,128]{1,0:T(8,128)(2,1)S(1)} %get-tuple-element.45), channel_id=1, source_target_pairs={{0,2},{2,0},{66,68},{68,66},{4,6},{6,4},{70,78},{78,70},{14,12},{1... | collective-permute-start | bytes 196616 | tf_op jit(solution)/shard_map/ppermute | solution.py:503
  53.5 0.0 collective-permute-done.7.side_a
  53.5 1.6 %collective-permute-done.8.side_b = bf16[256,128]{1,0:T(8,128)(2,1)S(1)} collective-permute-done((bf16[256,128]{1,0:T(8,128)(2,1)S(1)}, bf16[256,128]{1,0:T(8,128)(2,1)S(1)}, u32[]{:S(2)}, u32[]{:S(2)}) %collective-permute-start.8) | collective-permute-done | bytes 65568 | tf_op jit(solution)/shard_map/ppermute | solution.py:503
  55.1 1.2 %shard_map.153 = (f32[8,256]{1,0:T(8,128)S(1)}, f32[8,256]{1,0:T(8,128)S(1)}, f32[8,128]{1,0:T(8,128)S(1)}, f32[8,128]{1,0:T(8,128)S(1)}) custom-call(bf16[256,256]{1,0:T(8,128)(2,1)S(1)} %get-tuple-element.42.hidden, bf16[256,256]{1,0:T(8,128)(2,1)S(1)} %get-tuple-element.43.lifted, bf16[256,128]{1,0:T(8,128)(2,1)S(1)} %collective-permute-done.7.side_a, ...), custom_call_target="tpu_custom_call" | custom-call | tf_op jit(solution)/shard_map/pallas_call | solution.py:27
  56.4 1.9 %collective-permute-start.9 = (f32[8,128]{1,0:T(8,128)S(1)}, f32[8,128]{1,0:T(8,128)S(1)}, u32[]{:S(2)}, u32[]{:S(2)}) collective-permute-start(f32[8,128]{1,0:T(8,128)S(1)} %get-tuple-element.50), channel_id=1, source_target_pairs={{192,128},{128,192},{130,194},{194,130},{196,132},{132,196},{134,1... | collective-permute-start | bytes 12296 | tf_op jit(solution)/shard_map/ppermute | solution.py:503
  58.3 3.4 %collective-permute-start.10 = (f32[8,128]{1,0:T(8,128)S(1)}, f32[8,128]{1,0:T(8,128)S(1)}, u32[]{:S(2)}, u32[]{:S(2)}) collective-permute-start(f32[8,128]{1,0:T(8,128)S(1)} %get-tuple-element.51), channel_id=1, source_target_pairs={{128,130},{130,128},{194,196},{196,194},{132,134},{134,132},{198,2... | collective-permute-start | bytes 12296 | tf_op jit(solution)/shard_map/ppermute | solution.py:503
  61.7 0.0 collective-permute-done.9.side_a
  61.7 1.0 collective-permute-done.10.side_b
  62.6 1.2 %shard_map.154 = (f32[8,256]{1,0:T(8,128)S(1)}, f32[8,128]{1,0:T(8,128)S(1)}, f32[8,128]{1,0:T(8,128)S(1)}) custom-call(f32[8,128]{1,0:T(8,128)S(1)} %collective-permute-done.9.side_a, f32[8,128]{1,0:T(8,128)S(1)} %collective-permute-done.10.side_b, f32[48,256]{1,0:T(8,128)S(1)} %collective-permute-done.pack, f32[512,256]{1,0:T(8,128)S(1)} %get-tuple-element.36.w3, ...), custom_call_target="tpu_custom_call" | custom-call | tf_op jit(solution)/shard_map/pallas_call | solution.py:27
  63.8 1.9 %collective-permute-start.11 = (f32[8,128]{1,0:T(8,128)S(1)}, f32[8,128]{1,0:T(8,128)S(1)}, u32[]{:S(2)}, u32[]{:S(2)}) collective-permute-start(f32[8,128]{1,0:T(8,128)S(1)} %get-tuple-element.53), channel_id=1, source_target_pairs={{192,128},{128,192},{130,194},{194,130},{196,132},{132,196},{134,1... | collective-permute-start | bytes 12296 | tf_op jit(solution)/shard_map/ppermute | solution.py:503
  65.7 4.8 %collective-permute-start.12 = (f32[8,128]{1,0:T(8,128)S(1)}, f32[8,128]{1,0:T(8,128)S(1)}, u32[]{:S(2)}, u32[]{:S(2)}) collective-permute-start(f32[8,128]{1,0:T(8,128)S(1)} %get-tuple-element.54), channel_id=1, source_target_pairs={{128,130},{130,128},{194,196},{196,194},{132,134},{134,132},{198,2... | collective-permute-start | bytes 12296 | tf_op jit(solution)/shard_map/ppermute | solution.py:503
  70.5 0.0 collective-permute-done.11.side_a
  70.5 1.0 collective-permute-done.12.side_b
  71.5 3.4 %shard_map.155 = (f32[3,256]{1,0:T(4,128)S(1)}, f32[384,2,128]{2,1,0:T(2,128)}) custom-call(f32[4,4,128]{2,1,0:T(4,128)S(1)} %get-tuple-element.41.near, f32[48,256]{1,0:T(8,128)S(1)} %collective-permute-done.pack, f32[8,256]{1,0:T(8,128)S(1)} %get-tuple-element.48.charge, f32[8,256]{1,0:T(8,128)S(1)} %get-tuple-element.49.outside_row, ...), custom_call_target="tpu_custom_call" | custom-call | tf_op jit(solution)/shard_map/pallas_call | solution.py:27
  74.9 15.0 %all-to-all-start.1 = ((f32[384,2,128]{2,1,0:T(2,128)}), f32[384,2,128]{2,1,0:T(2,128)S(1)}, u32[]{:S(2)}, u32[]{:S(2)}) async-start(f32[384,2,128]{2,1,0:T(2,128)} %get-tuple-element.57), calls=%async_computation.1 | async-start | bytes 786432 | tf_op jit(solution)/shard_map/all_to_all | solution.py:567
  89.9 4.0 %collective-permute-start.13 = (f32[3,256]{1,0:T(4,128)S(1)}, f32[3,256]{1,0:T(4,128)S(1)}, u32[]{:S(2)}, u32[]{:S(2)}) collective-permute-start(f32[3,256]{1,0:T(4,128)S(1)} %get-tuple-element.56), channel_id=1, source_target_pairs={{64,0},{0,1},{2,2},{66,3},{68,4},{4,5},{6,6},{70,7},{78,8},{14,9},... | collective-permute-start | bytes 9224 | tf_op jit(solution)/shard_map/ppermute | solution.py:503
  93.9 9.3 %all-to-all-done.1 = f32[384,2,128]{2,1,0:T(2,128)S(1)} async-done(((f32[384,2,128]{2,1,0:T(2,128)}), f32[384,2,128]{2,1,0:T(2,128)S(1)}, u32[]{:S(2)}, u32[]{:S(2)}) %all-to-all-start.1) | async-done | bytes 393248 | tf_op jit(solution)/shard_map/all_to_all | solution.py:567
  103.3 0.2 shard_map.156
  103.4 5.4 %collective-permute-start.14 = (f32[3,256]{1,0:T(4,128)S(1)}, f32[3,256]{1,0:T(4,128)S(1)}, u32[]{:S(2)}, u32[]{:S(2)}) collective-permute-start(f32[3,256]{1,0:T(4,128)S(1)} %shard_map.156), channel_id=1, source_target_pairs={{0,128},{128,0},{1,129},{129,1},{2,130},{130,2},{3,131},{131,3},{4... | collective-permute-start | bytes 9224 | tf_op jit(solution)/shard_map/ppermute | solution.py:570
  108.8 0.0 collective-permute-done.13
  108.9 0.8 collective-permute-done.14
  109.7 0.6 copy.18
  110.3 0.6 copy.19
  (1 shorter events, 0.0 us)
Async XLA Ops:
  1.7 4.2 %collective-permute-start.6 = (f32[2,4,128]{2,1,0:T(4,128)S(1)}, f32[2,4,128]{2,1,0:T(4,128)S(1)}, u32[]{:S(2)}, u32[]{:S(2)}) collective-permute-start(f32[2,4,128]{2,1,0:T(4,128)S(1)} %get-tuple-element.40), channel_id=1, source_target_pairs={{0,128},{128,0},{1,129},{129,1},{2,130},{130,2},{3,131},{131,3},{4... | collective-permute-start | bytes 12296 | tf_op jit(solution)/shard_map/ppermute | solution.py:521
  6.7 38.2 %all-to-all-start = ((f32[128,2,4,128]{3,2,1,0:T(4,128)}), f32[128,2,4,128]{3,2,1,0:T(4,128)S(1)}, u32[]{:S(2)}, u32[]{:S(2)}) async-start(f32[128,2,4,128]{3,2,1,0:T(4,128)} %broadcast_in_dim.17), calls=%async_computation | async-start | bytes 1048576 | tf_op jit(solution)/shard_map/all_to_all | solution.py:523
  20.5 14.1 %collective-permute-start.3 = (bf16[256,256]{1,0:T(8,128)(2,1)}, bf16[256,256]{1,0:T(8,128)(2,1)S(1)}, u32[]{:S(2)}, u32[]{:S(2)}) collective-permute-start(bf16[256,256]{1,0:T(8,128)(2,1)} %param.17), channel_id=1, source_target_pairs={{0,64},{1,0},{2,2},{3,66},{4,68},{5,4},{6,6},{7,70},{8,78},{9,14},... | collective-permute-start | bytes 393224 | tf_op jit(solution)/shard_map/ppermute | solution.py:503
  21.1 13.4 %collective-permute-start = (f32[48,256]{1,0:T(8,128)S(1)}, f32[48,256]{1,0:T(8,128)S(1)}, u32[]{:S(2)}, u32[]{:S(2)}) collective-permute-start(f32[48,256]{1,0:T(8,128)S(1)} %get-tuple-element.30), channel_id=1, source_target_pairs={{0,64},{1,0},{2,2},{3,66},{4,68},{5,4},{6,6},{7,70},{8,78},{9,14},... | collective-permute-start | bytes 147464 | tf_op jit(solution)/shard_map/ppermute | solution.py:503
  23.9 2.0 %collective-permute-start.1 = (f32[8,128]{1,0:T(8,128)S(1)}, f32[8,128]{1,0:T(8,128)S(1)}, u32[]{:S(2)}, u32[]{:S(2)}) collective-permute-start(f32[8,128]{1,0:T(8,128)S(1)} %get-tuple-element.31), channel_id=1, source_target_pairs={{0,0},{1,64},{2,66},{3,2},{4,4},{5,68},{6,70},{7,6},{8,14},{9,78},... | collective-permute-start | bytes 12296 | tf_op jit(solution)/shard_map/ppermute | solution.py:503
  24.6 9.9 %collective-permute-start.2 = (f32[8,128]{1,0:T(8,128)S(1)}, f32[8,128]{1,0:T(8,128)S(1)}, u32[]{:S(2)}, u32[]{:S(2)}) collective-permute-start(f32[8,128]{1,0:T(8,128)S(1)} %get-tuple-element.32), channel_id=1, source_target_pairs={{1,2},{2,0},{3,68},{4,66},{5,6},{6,4},{7,78},{8,70},{9,12},{10,14}... | collective-permute-start | bytes 12296 | tf_op jit(solution)/shard_map/ppermute | solution.py:503
  37.3 5.9 %collective-permute-start.4 = (bf16[256,128]{1,0:T(8,128)(2,1)S(1)}, bf16[256,128]{1,0:T(8,128)(2,1)S(1)}, u32[]{:S(2)}, u32[]{:S(2)}) collective-permute-start(bf16[256,128]{1,0:T(8,128)(2,1)S(1)} %get-tuple-element.34), channel_id=1, source_target_pairs={{64,0},{0,64},{2,66},{66,2},{68,4},{4,68},{6,70},{70,6},{78,14},{1... | collective-permute-start | bytes 196616 | tf_op jit(solution)/shard_map/ppermute | solution.py:503
  39.8 5.0 %collective-permute-start.5 = (bf16[256,128]{1,0:T(8,128)(2,1)S(1)}, bf16[256,128]{1,0:T(8,128)(2,1)S(1)}, u32[]{:S(2)}, u32[]{:S(2)}) collective-permute-start(bf16[256,128]{1,0:T(8,128)(2,1)S(1)} %get-tuple-element.35), channel_id=1, source_target_pairs={{0,2},{2,0},{66,68},{68,66},{4,6},{6,4},{70,78},{78,70},{14,12},{1... | collective-permute-start | bytes 196616 | tf_op jit(solution)/shard_map/ppermute | solution.py:503
  48.7 4.8 %collective-permute-start.7 = (bf16[256,128]{1,0:T(8,128)(2,1)S(1)}, bf16[256,128]{1,0:T(8,128)(2,1)S(1)}, u32[]{:S(2)}, u32[]{:S(2)}) collective-permute-start(bf16[256,128]{1,0:T(8,128)(2,1)S(1)} %get-tuple-element.44), channel_id=1, source_target_pairs={{64,0},{0,64},{2,66},{66,2},{68,4},{4,68},{6,70},{70,6},{78,14},{1... | collective-permute-start | bytes 196616 | tf_op jit(solution)/shard_map/ppermute | solution.py:503
  48.8 6.3 %collective-permute-start.8 = (bf16[256,128]{1,0:T(8,128)(2,1)S(1)}, bf16[256,128]{1,0:T(8,128)(2,1)S(1)}, u32[]{:S(2)}, u32[]{:S(2)}) collective-permute-start(bf16[256,128]{1,0:T(8,128)(2,1)S(1)} %get-tuple-element.45), channel_id=1, source_target_pairs={{0,2},{2,0},{66,68},{68,66},{4,6},{6,4},{70,78},{78,70},{14,12},{1... | collective-permute-start | bytes 196616 | tf_op jit(solution)/shard_map/ppermute | solution.py:503
  56.4 5.3 %collective-permute-start.9 = (f32[8,128]{1,0:T(8,128)S(1)}, f32[8,128]{1,0:T(8,128)S(1)}, u32[]{:S(2)}, u32[]{:S(2)}) collective-permute-start(f32[8,128]{1,0:T(8,128)S(1)} %get-tuple-element.50), channel_id=1, source_target_pairs={{192,128},{128,192},{130,194},{194,130},{196,132},{132,196},{134,1... | collective-permute-start | bytes 12296 | tf_op jit(solution)/shard_map/ppermute | solution.py:503
  58.3 4.4 %collective-permute-start.10 = (f32[8,128]{1,0:T(8,128)S(1)}, f32[8,128]{1,0:T(8,128)S(1)}, u32[]{:S(2)}, u32[]{:S(2)}) collective-permute-start(f32[8,128]{1,0:T(8,128)S(1)} %get-tuple-element.51), channel_id=1, source_target_pairs={{128,130},{130,128},{194,196},{196,194},{132,134},{134,132},{198,2... | collective-permute-start | bytes 12296 | tf_op jit(solution)/shard_map/ppermute | solution.py:503
  63.8 6.7 %collective-permute-start.11 = (f32[8,128]{1,0:T(8,128)S(1)}, f32[8,128]{1,0:T(8,128)S(1)}, u32[]{:S(2)}, u32[]{:S(2)}) collective-permute-start(f32[8,128]{1,0:T(8,128)S(1)} %get-tuple-element.53), channel_id=1, source_target_pairs={{192,128},{128,192},{130,194},{194,130},{196,132},{132,196},{134,1... | collective-permute-start | bytes 12296 | tf_op jit(solution)/shard_map/ppermute | solution.py:503
  65.7 5.8 %collective-permute-start.12 = (f32[8,128]{1,0:T(8,128)S(1)}, f32[8,128]{1,0:T(8,128)S(1)}, u32[]{:S(2)}, u32[]{:S(2)}) collective-permute-start(f32[8,128]{1,0:T(8,128)S(1)} %get-tuple-element.54), channel_id=1, source_target_pairs={{128,130},{130,128},{194,196},{196,194},{132,134},{134,132},{198,2... | collective-permute-start | bytes 12296 | tf_op jit(solution)/shard_map/ppermute | solution.py:503
  74.9 28.3 %all-to-all-start.1 = ((f32[384,2,128]{2,1,0:T(2,128)}), f32[384,2,128]{2,1,0:T(2,128)S(1)}, u32[]{:S(2)}, u32[]{:S(2)}) async-start(f32[384,2,128]{2,1,0:T(2,128)} %get-tuple-element.57), calls=%async_computation.1 | async-start | bytes 786432 | tf_op jit(solution)/shard_map/all_to_all | solution.py:567
  89.9 18.9 %collective-permute-start.13 = (f32[3,256]{1,0:T(4,128)S(1)}, f32[3,256]{1,0:T(4,128)S(1)}, u32[]{:S(2)}, u32[]{:S(2)}) collective-permute-start(f32[3,256]{1,0:T(4,128)S(1)} %get-tuple-element.56), channel_id=1, source_target_pairs={{64,0},{0,1},{2,2},{66,3},{68,4},{4,5},{6,6},{70,7},{78,8},{14,9},... | collective-permute-start | bytes 9224 | tf_op jit(solution)/shard_map/ppermute | solution.py:503
  103.4 6.3 %collective-permute-start.14 = (f32[3,256]{1,0:T(4,128)S(1)}, f32[3,256]{1,0:T(4,128)S(1)}, u32[]{:S(2)}, u32[]{:S(2)}) collective-permute-start(f32[3,256]{1,0:T(4,128)S(1)} %shard_map.156), channel_id=1, source_target_pairs={{0,128},{128,0},{1,129},{129,1},{2,130},{130,2},{3,131},{131,3},{4... | collective-permute-start | bytes 9224 | tf_op jit(solution)/shard_map/ppermute | solution.py:570

commit v6 on v5

--- a/solution.py
+++ b/solution.py
@@ -104,10 +104,14 @@
 
 
 def rows_kernel(
-    pos_far, charge_far, polar_far, table_far, send_far, blocks_far,
-    pack, mine, lent_a, lent_b,
-    pos, charge, polar, table, send, blocks, done,
+    pos_far, charge_far, polar_far, table_far, send_far, blocks_far, features_far,
+    pack, mine, lent_a, lent_b, feat_t,
+    pos, charge, polar, table, send, blocks, features, done,
 ):
+    @pl.when(learned())
+    def _():
+        fetch(((features_far, features),), done, 6)
+
     pairs = ((pos_far, pos), (charge_far, charge), (polar_far, polar), (table_far, table), (send_far, send))
     wait = fetch(pairs + ((blocks_far, blocks),), done)
     odd = lax.axis_index("sub")
@@ -131,30 +135,39 @@
     pack[8:40, :] = jnp.where(keep, raw, other).astype(F32)
     pack[40:48, :] = rows([jnp.concatenate(picks, axis=1).astype(F32)])
     pieces = split3(sites)
-    for row, out in zip(picks, (lent_a, lent_b)):
-        found = join3(dot(pieces, one_hot(row, width)))
-        out[...] = rows([found[0:5], listed[:, 0:128], jnp.ones((1, 128), F32)])
-
-
-def static_kernel(
-    pack, rim_a, rim_b, features_far,
-    feat_t, w3, w5, fixed, entry, lent_a, lent_b, features, done,
-):
+    chosen = [one_hot(row, width) for row in picks]
+    for pick, out in zip(chosen, (lent_a, lent_b)):
+        found = join3(dot(pieces, pick))
+        lent = rows([found[0:5], listed[:, 0:128], jnp.ones((1, 128), F32)])
+        out[0:32, :] = jnp.concatenate([split3(lent), jnp.zeros((8, 128), BF16)], axis=0)
+
+    @pl.when(learned())
+    def _():
+        pltpu.make_async_copy(features_far, features, done.at[6]).wait()
+        flipped = flip(features[...]).astype(BF16)
+        feat_t[...] = flipped
+        for pick, out in zip(chosen, (lent_a, lent_b)):
+            out[32:, :] = dot(flipped, pick).astype(BF16)
+
+    @pl.when(jnp.logical_not(learned()))
+    def _():
+        for out in (lent_a, lent_b):
+            out[32:, :] = jnp.zeros((feat_t.shape[0], 128), BF16)
+
+
+def rim(lent):
+    return join3(lent[0:24, :].astype(F32))
+
+
+def static_kernel(pack, from_a, from_b, w3, w5, fixed, entry, lent_a, lent_b):
     site, slots, picks = views(pack)
     width = site.shape[1]
     depth = 2 * width
     slot_count = slots.shape[0]
 
-    @pl.when(learned())
-    def _():
-        fetch(((features_far, features),), done)()
-        flipped = flip(features[...]).astype(BF16)
-        feat_t[...] = flipped
-        lend_channels(flipped, picks, lent_a, lent_b)
-
     @pl.when(jnp.logical_not(learned()))
     def _():
-        table = jnp.concatenate([site[...], rim_a[...], rim_b[...]], axis=1)
+        table = jnp.concatenate([site[...], rim(from_a), rim(from_b)], axis=1)
         entry[...] = table.T
         tx, ty, tz = site[0:1, :], site[1:2, :], site[2:3, :]
 
@@ -178,12 +191,12 @@
         sums = lax.fori_loop(0, depth // STATIC_CHUNK, some_rows, (nil, nil, nil))
         total = rows([jnp.sum(s, axis=0, keepdims=True) for s in sums])
         fixed[...] = total
-        lend_pieces(total, picks, lent_a, lent_b)
+        lend_whole(total, picks, lent_a, lent_b)
 
 
 def radial_kernel(
-    pack, rim_a, rim_b, w_in_far, w_mid_far,
-    third_far, w_in, w_mid, third, done,
+    pack, from_a, from_b, w_in_far, w_mid_far,
+    third_far, w_in, w_mid, third, entry, square, done,
 ):
     site, slots, _ = views(pack)
     width = site.shape[1]
@@ -193,10 +206,21 @@
     @pl.when(learned())
     def _():
         wait = fetch(((w_in_far, w_in), (w_mid_far, w_mid)), done)
-        pieces = split3(jnp.concatenate([site[...], rim_a[...], rim_b[...]], axis=1))
+        entry[...] = jnp.concatenate([site[...], rim(from_a), rim(from_b)], axis=1).T
+        tx, ty, tz = site[0:1, :], site[1:2, :], site[2:3, :]
+
+        def some_rows(j, carry):
+            start = pl.multiple_of(j * STATIC_CHUNK, STATIC_CHUNK)
+            cols = entry[pl.ds(start, STATIC_CHUNK), :]
+            rx, ry, rz = tx - cols[:, 0:1], ty - cols[:, 1:2], tz - cols[:, 2:3]
+            square[pl.ds(start, STATIC_CHUNK), :] = rx * rx + ry * ry + rz * rz
+            return carry
+
+        lax.fori_loop(0, depth // STATIC_CHUNK, some_rows, 0, unroll=4)
+        empty = tx * tx + ty * ty + tz * tz
         step = RADIAL_SLOTS * width
-        here = jnp.concatenate([site[...]] * RADIAL_SLOTS, axis=1)
         centres = lax.broadcasted_iota(jnp.int32, (BASIS, step), 0).astype(F32) * SPACING
+        ids = lax.broadcasted_iota(jnp.int32, (8, width), 0).astype(F32)
         wait()
         first_w = jnp.concatenate([flip(w_in[0]), flip(w_in[1])], axis=0).astype(BF16)
         zero = jnp.zeros((64, 64), F32)
@@ -209,11 +233,21 @@
         second_w, third_w = both(0), both(1)
 
         def some_slots(k, carry):
-            found = join3(dot(pieces, one_hot(slot_row(slots, k * RADIAL_SLOTS, RADIAL_SLOTS), depth)))
-            offset = here - found
-            squares = offset * offset
-            dist_sq = squares[0:1] + squares[1:2] + squares[2:3] + SMOOTH
-            gap = jnp.sqrt(dist_sq) - centres
+            named = [slots[pl.ds(k * RADIAL_SLOTS + i, 1), :] for i in range(RADIAL_SLOTS)]
+
+            def pick(j, acc):
+                start = pl.multiple_of(j * 8, 8)
+                here = square[pl.ds(start, 8), :]
+                mine = ids + start.astype(F32)
+                return tuple(a + jnp.where(mine == n, here, 0.0) for a, n in zip(acc, named))
+
+            nil = jnp.zeros((8, width), F32)
+            found = lax.fori_loop(0, depth // 8, pick, (nil,) * RADIAL_SLOTS, unroll=8)
+            far = [
+                jnp.sum(f, axis=0, keepdims=True) + jnp.where(n == float(depth), empty, 0.0)
+                for f, n in zip(found, named)
+            ]
+            gap = jnp.sqrt(jnp.concatenate(far, axis=1) + SMOOTH) - centres
             basis = jnp.exp(-(gap * gap)).astype(BF16)
             hidden = silu(dot(first_w, basis)).astype(BF16)
             hidden = silu(dot(second_w, hidden)).astype(BF16)
@@ -306,7 +340,7 @@
 
 
 def first_kernel(
-    pack, rim_a, rim_b, feat_t, side_a, side_b, w3, w5, fixed, entry,
+    pack, from_a, from_b, feat_t, side_a, side_b, w3, w5, fixed, entry,
     near_far, third_far, node_in_far, node_out_far, w_out_far, gain_far,
     outside_row, near_own, hidden_out, lifted_out, fixed_out, dipole_out, lent_a, lent_b,
     near, cols, third, node_in, node_out, w_out, gain, total, moment, done,
@@ -314,6 +348,7 @@
     site, slots, picks = views(pack)
     width = site.shape[1]
     listed = near_own.shape[0]
+    rim_a, rim_b = rim(from_a), rim(from_b)
     numbers = [listed_block(row[5:6, 0:128], l) for row in (site, rim_a, rim_b) for l in range(listed)]
     fetch([(near_far.at[b], near.at[i]) for i, b in enumerate(numbers)], done, 5)
     weights = (
@@ -334,7 +369,7 @@
     reach = listed * 128
     own_field = charge_field(site[...], cols, 0, reach)
     field = jnp.concatenate(
-        [own_field, charge_field(rim_a[...], cols, reach, reach), charge_field(rim_b[...], cols, 2 * reach, reach)],
+        [own_field, charge_field(rim_a, cols, reach, reach), charge_field(rim_b, cols, 2 * reach, reach)],
         axis=1,
     )
     strength = jnp.sqrt(1.0 + (field[0:1] * field[0:1] + field[1:2] * field[1:2] + field[2:3] * field[2:3]))
@@ -345,7 +380,7 @@
         for i, (a, b) in enumerate(weights):
             pltpu.make_async_copy(a, b, done.at[i]).wait()
         gain_col = jnp.broadcast_to(gain[...], (8, width)).T
-        features = jnp.concatenate([feat_t[...], side_a[...], side_b[...]], axis=1)
+        features = jnp.concatenate([feat_t[...], from_a[32:, :], from_b[32:, :]], axis=1)
         start = (features.astype(F32) + gain_col[:, 0:1] * strength).astype(BF16)
         present = jnp.concatenate([jnp.ones((1, width), F32), rim_a[6:7, :], rim_b[6:7, :]], axis=1)
         raised = dot(flip(node_in[0]).astype(BF16), start)
@@ -359,8 +394,7 @@
 
     @pl.when(jnp.logical_not(learned()))
     def _():
-        known = [fixed[...], join3(side_a[0:24, :].astype(F32)), join3(side_b[0:24, :].astype(F32))]
-        whole = jnp.concatenate(known, axis=1) + rows([field])
+        whole = jnp.concatenate([fixed[...], side_a[...], side_b[...]], axis=1) + rows([field])
         fixed_out[...] = whole[:, :width]
         polar = jnp.concatenate([site[4:5, :], rim_a[4:5, :], rim_b[4:5, :]], axis=1)
         new = sweep(site, w3, w5, whole[:, :width], polar * whole, entry, moment)
@@ -511,28 +545,32 @@
     wide = ((channels, half), BF16)
     by_site = ((channels, width), BF16)
     ints = jnp.int32
+    first_lent = ((32 + channels, half), BF16)
     itself = [(i, i) for i in range(members)]
-    pack, mine, lent_a, lent_b = call(
-        rows_kernel, [((slot_count + 16, width), F32), ((2, 4, half), F32), table8, table8],
-        (), (positions, charges[None], polar[None], neighbours.T, send_rows, blocks),
+    pack, mine, lent_a, lent_b, feat_t = call(
+        rows_kernel, [((slot_count + 16, width), F32), ((2, 4, half), F32), first_lent, first_lent, by_site],
+        (), (positions, charges[None], polar[None], neighbours.T, send_rows, blocks, features),
         [pltpu.VMEM((3, width), F32), pltpu.VMEM((1, width), F32), pltpu.VMEM((1, width), F32),
-         pltpu.VMEM((slot_count, width), ints), pltpu.VMEM((2, half), ints), pltpu.SMEM((listed,), ints)], 6,
+         pltpu.VMEM((slot_count, width), ints), pltpu.VMEM((2, half), ints), pltpu.SMEM((listed,), ints),
+         pltpu.VMEM((width, channels), BF16)], 7,
     )
     partner = lax.ppermute(mine, "grp", [(0, 1), (1, 0)])
     copies = jnp.broadcast_to(partner[None], (members,) + partner.shape)
     near = lax.all_to_all(copies, DOM, 0, 0, tiled=True).reshape(2 * members, 4, half)
     pack = move(pack, itself, same, place)
     rim_a, rim_b = trade(lent_a, lent_b, source=same)
-    features = move(features, itself, same, place, (0,))
-    feat_t, w3, w5, fixed, entry, lent_a, lent_b = call(
-        static_kernel, [by_site, ((depth, width), F32), ((depth, width), F32), row8, ((depth, 8), F32), wide, wide],
-        (pack, rim_a, rim_b), (features,), [pltpu.VMEM((width, channels), BF16)], 1, loose=1,
-    )
-    side_a, side_b = trade(lent_a, lent_b)
+    feat_t, rim_a, rim_b = lax.optimization_barrier((feat_t, rim_a, rim_b))
+    feat_t = move(feat_t, itself, same, place, (0,))
+    w3, w5, fixed, entry, lent_a, lent_b = call(
+        static_kernel, [((depth, width), F32), ((depth, width), F32), row8, ((depth, 8), F32), table8, table8],
+        (pack, rim_a, rim_b),
+    )
+    side_a, side_b = trade(lent_a, lent_b, (1,))
     third_shape = (LAYERS * radial_in.shape[2], slot_count * width)
     (third,) = call(
         radial_kernel, [(third_shape, BF16)], (pack, rim_a, rim_b), (radial_in, radial_mid),
-        [pltpu.VMEM(radial_in.shape, BF16), pltpu.VMEM(radial_mid.shape, BF16), pltpu.VMEM(third_shape, BF16)], 3, 1,
+        [pltpu.VMEM(radial_in.shape, BF16), pltpu.VMEM(radial_mid.shape, BF16), pltpu.VMEM(third_shape, BF16),
+         pltpu.VMEM((depth, 8), F32), pltpu.VMEM((depth, width), F32)], 3, 1,
     )
     moment = pltpu.VMEM((depth, 8), F32)
     total = pltpu.VMEM((channels, width), F32)

time: 111 us -> 122 us (1.099)
  waiting for transfers between devices: 24.9 us -> 32.4 us
  starting transfers between devices: 69.6 us -> 72.1 us
    ppermute x13, waiting for transfers between devices: 13.9 us -> 19.4 us  [move(): lax.ppermute(value, EVERY, [(source[a] + g * members, target[b] + g * mem...]
    all_to_all x1, starting transfers between devices: 15 us -> 19.1 us  [local(): lax.all_to_all(spread, DOM, 0, 0, tiled=True).reshape(members, 3, 2, half)]
    ppermute x1, starting transfers between devices: 5.43 us -> 2.91 us  [local(): return (result, lax.ppermute(share, 'grp', [(0, 1), (1, 0)]))]
    all_to_all x1, waiting for transfers between devices: 9.33 us -> 11.4 us  [local(): lax.all_to_all(spread, DOM, 0, 0, tiled=True).reshape(members, 3, 2, half)]
  transfers between devices with their start and end apart: 17 -> 17, of which waited for: 8 -> 10; matrix products, arithmetic and copies ran while one was open for 0% -> 0% of each run, Pallas kernels for 3% -> 2%
where the time goes in v6:
time: 122 us; the launch traced here: 121 us
  starting transfers between devices  72.1 us (59%)
  waiting for transfers between devices  32.4 us (27%)
  Pallas kernels  13.6 us (11%)
  local copies, waits for them, and re-layouts  2.05 us (2%)
    ppermute x13, starting transfers between devices, move(): lax.ppermute(value, EVERY, [(source[a] + g * members, target[b] + g * mem...  32.7 us
    ppermute x13, waiting for transfers between devices, move(): lax.ppermute(value, EVERY, [(source[a] + g * members, target[b] + g * mem...  19.4 us
    all_to_all x1, starting transfers between devices, local(): lax.all_to_all(spread, DOM, 0, 0, tiled=True).reshape(members, 3, 2, half)  19.1 us
    all_to_all x1, starting transfers between devices, local(): lax.all_to_all(copies, DOM, 0, 0, tiled=True).reshape(2 * members, 4, half)  13.8 us
    pallas_call x8, Pallas kernels, call(): pl.pallas_call(body, out_shape=[jax.ShapeDtypeStruct(s, d) for s, d in ou...  13.6 us
    all_to_all x1, waiting for transfers between devices, local(): lax.all_to_all(spread, DOM, 0, 0, tiled=True).reshape(members, 3, 2, half)  11.4 us
    ppermute x1, starting transfers between devices, local(): partner = lax.ppermute(mine, 'grp', [(0, 1), (1, 0)])  3.65 us
    ppermute x1, starting transfers between devices, local(): return (result, lax.ppermute(share, 'grp', [(0, 1), (1, 0)]))  2.91 us
  transfers between devices with their start and end apart: 17, of which 10 were waited for; matrix products, arithmetic and copies ran while one was open for 0% of the time, Pallas kernels for 2%

profile of v6, /device:TPU:1, one launch (start us, length us, event | category | flops | bytes accessed | tf_op | source)
XLA Modules:
  0.0 121.0 jit_solution(12898847790373237148)
XLA Ops:
  0.6 1.1 shard_map.149
  1.7 3.7 %collective-permute-start.6 = (f32[2,4,128]{2,1,0:T(4,128)S(1)}, f32[2,4,128]{2,1,0:T(4,128)S(1)}, u32[]{:S(2)}, u32[]{:S(2)}) collective-permute-start(f32[2,4,128]{2,1,0:T(4,128)S(1)} %get-tuple-element.46), channel_id=1, source_target_pairs={{0,128},{128,0},{1,129},{129,1},{2,130},{130,2},{3,131},{131,3},{4... | collective-permute-start | bytes 12296 | tf_op jit(solution)/shard_map/ppermute | solution.py:557
  5.4 0.8 collective-permute-done.6
  6.2 0.9 broadcast_in_dim.17
  7.1 13.8 %all-to-all-start = ((f32[128,2,4,128]{3,2,1,0:T(4,128)}), f32[128,2,4,128]{3,2,1,0:T(4,128)S(1)}, u32[]{:S(2)}, u32[]{:S(2)}) async-start(f32[128,2,4,128]{3,2,1,0:T(4,128)} %broadcast_in_dim.17), calls=%async_computation | async-start | bytes 1048576 | tf_op jit(solution)/shard_map/all_to_all | solution.py:559
  20.8 0.7 collective-permute-start.1
  21.5 1.3 %collective-permute-start.2 = (bf16[288,128]{1,0:T(8,128)(2,1)S(1)}, bf16[288,128]{1,0:T(8,128)(2,1)S(1)}, u32[]{:S(2)}, u32[]{:S(2)}) collective-permute-start(bf16[288,128]{1,0:T(8,128)(2,1)S(1)} %get-tuple-element.36), channel_id=1, source_target_pairs={{1,2},{2,0},{3,68},{4,66},{5,6},{6,4},{7,78},{8,70},{9,12},{10,14}... | collective-permute-start | bytes 221192 | tf_op jit(solution)/shard_map/ppermute | solution.py:537
  22.8 0.0 collective-permute-done.1.from_a
  22.8 6.7 %collective-permute-done.2.from_b = bf16[288,128]{1,0:T(8,128)(2,1)S(1)} collective-permute-done((bf16[288,128]{1,0:T(8,128)(2,1)S(1)}, bf16[288,128]{1,0:T(8,128)(2,1)S(1)}, u32[]{:S(2)}, u32[]{:S(2)}) %collective-permute-start.2) | collective-permute-done | bytes 73760 | tf_op jit(solution)/shard_map/ppermute | solution.py:537
  29.5 0.7 collective-permute-start.3
  30.2 8.3 %collective-permute-start = (f32[48,256]{1,0:T(8,128)S(1)}, f32[48,256]{1,0:T(8,128)S(1)}, u32[]{:S(2)}, u32[]{:S(2)}) collective-permute-start(f32[48,256]{1,0:T(8,128)S(1)} %get-tuple-element.33), channel_id=1, source_target_pairs={{0,64},{1,0},{2,2},{3,66},{4,68},{5,4},{6,6},{7,70},{8,78},{9,14},... | collective-permute-start | bytes 147464 | tf_op jit(solution)/shard_map/ppermute | solution.py:537
  38.4 5.6 %collective-permute-done.pack = f32[48,256]{1,0:T(8,128)S(1)} collective-permute-done((f32[48,256]{1,0:T(8,128)S(1)}, f32[48,256]{1,0:T(8,128)S(1)}, u32[]{:S(2)}, u32[]{:S(2)}) %collective-permute-start) | collective-permute-done | bytes 49184 | tf_op jit(solution)/shard_map/ppermute | solution.py:537
  44.1 2.7 %shard_map.150 = (f32[512,256]{1,0:T(8,128)S(1)}, f32[512,256]{1,0:T(8,128)S(1)}, f32[8,256]{1,0:T(8,128)S(1)}, f32[512,8]{1,0:T(8,128)S(1)}, f32[8,128]{1,0:T(8,128)S(1)}, /*index=5*/f32[8,128]{1,0:T(8,128)S(1)}) custom-call(f32[48,256]{1,0:T(8,128)S(1)} %collective-permute-done.pack, bf16[288,128]{1,0:T(8,128)(2,1)S(1)} %collective-permute-done.1.from_a, ...), custom_call_target="tpu_custom_call" | custom-call | tf_op jit(solution)/shard_map/pallas_call | solution.py:27
  46.7 2.4 %collective-permute-start.4 = (f32[8,128]{1,0:T(8,128)S(1)}, f32[8,128]{1,0:T(8,128)S(1)}, u32[]{:S(2)}, u32[]{:S(2)}) collective-permute-start(f32[8,128]{1,0:T(8,128)S(1)} %get-tuple-element.40), channel_id=1, source_target_pairs={{192,128},{128,192},{130,194},{194,130},{196,132},{132,196},{134,1... | collective-permute-start | bytes 12296 | tf_op jit(solution)/shard_map/ppermute | solution.py:537
  49.1 2.0 %collective-permute-start.5 = (f32[8,128]{1,0:T(8,128)S(1)}, f32[8,128]{1,0:T(8,128)S(1)}, u32[]{:S(2)}, u32[]{:S(2)}) collective-permute-start(f32[8,128]{1,0:T(8,128)S(1)} %get-tuple-element.41), channel_id=1, source_target_pairs={{128,130},{130,128},{194,196},{196,194},{132,134},{134,132},{198,2... | collective-permute-start | bytes 12296 | tf_op jit(solution)/shard_map/ppermute | solution.py:537
  51.2 0.0 collective-permute-done.4.side_a
  51.2 2.3 %collective-permute-done.5.side_b = f32[8,128]{1,0:T(8,128)S(1)} collective-permute-done((f32[8,128]{1,0:T(8,128)S(1)}, f32[8,128]{1,0:T(8,128)S(1)}, u32[]{:S(2)}, u32[]{:S(2)}) %collective-permute-start.5) | collective-permute-done | bytes 4128 | tf_op jit(solution)/shard_map/ppermute | solution.py:537
  53.5 0.0 collective-permute-done.3.feat_t
  53.5 0.0 all-to-all-done
  53.5 3.8 %shard_map.152 = (f32[8,256]{1,0:T(8,128)S(1)}, f32[4,4,128]{2,1,0:T(4,128)S(1)}, bf16[256,256]{1,0:T(8,128)(2,1)S(1)}, bf16[256,256]{1,0:T(8,128)(2,1)S(1)}, f3...) custom-call(f32[48,256]{1,0:T(8,128)S(1)} %collective-permute-done.pack,, ...), custom_call_target="tpu_custom_call" | custom-call | tf_op jit(solution)/shard_map/pallas_call | solution.py:27
  57.3 0.1 collective-permute-start.7
  57.4 2.2 %collective-permute-start.8 = (bf16[256,128]{1,0:T(8,128)(2,1)S(1)}, bf16[256,128]{1,0:T(8,128)(2,1)S(1)}, u32[]{:S(2)}, u32[]{:S(2)}) collective-permute-start(bf16[256,128]{1,0:T(8,128)(2,1)S(1)} %get-tuple-element.51), channel_id=1, source_target_pairs={{0,2},{2,0},{66,68},{68,66},{4,6},{6,4},{70,78},{78,70},{14,12},{1... | collective-permute-start | bytes 196616 | tf_op jit(solution)/shard_map/ppermute | solution.py:537
  59.6 0.9 collective-permute-done.7.side_a
  60.5 1.9 %collective-permute-done.8.side_b = bf16[256,128]{1,0:T(8,128)(2,1)S(1)} collective-permute-done((bf16[256,128]{1,0:T(8,128)(2,1)S(1)}, bf16[256,128]{1,0:T(8,128)(2,1)S(1)}, u32[]{:S(2)}, u32[]{:S(2)}) %collective-permute-start.8) | collective-permute-done | bytes 65568 | tf_op jit(solution)/shard_map/ppermute | solution.py:537
  62.5 1.2 shard_map.153
  63.7 1.9 %collective-permute-start.9 = (f32[8,128]{1,0:T(8,128)S(1)}, f32[8,128]{1,0:T(8,128)S(1)}, u32[]{:S(2)}, u32[]{:S(2)}) collective-permute-start(f32[8,128]{1,0:T(8,128)S(1)} %get-tuple-element.56), channel_id=1, source_target_pairs={{192,128},{128,192},{130,194},{194,130},{196,132},{132,196},{134,1... | collective-permute-start | bytes 12296 | tf_op jit(solution)/shard_map/ppermute | solution.py:537
  65.6 3.5 %collective-permute-start.10 = (f32[8,128]{1,0:T(8,128)S(1)}, f32[8,128]{1,0:T(8,128)S(1)}, u32[]{:S(2)}, u32[]{:S(2)}) collective-permute-start(f32[8,128]{1,0:T(8,128)S(1)} %get-tuple-element.57), channel_id=1, source_target_pairs={{128,130},{130,128},{194,196},{196,194},{132,134},{134,132},{198,2... | collective-permute-start | bytes 12296 | tf_op jit(solution)/shard_map/ppermute | solution.py:537
  69.1 0.0 collective-permute-done.9.side_a
  69.1 1.0 collective-permute-done.10.side_b
  70.0 1.2 shard_map.154
  71.2 1.9 %collective-permute-start.11 = (f32[8,128]{1,0:T(8,128)S(1)}, f32[8,128]{1,0:T(8,128)S(1)}, u32[]{:S(2)}, u32[]{:S(2)}) collective-permute-start(f32[8,128]{1,0:T(8,128)S(1)} %get-tuple-element.59), channel_id=1, source_target_pairs={{192,128},{128,192},{130,194},{194,130},{196,132},{132,196},{134,1... | collective-permute-start | bytes 12296 | tf_op jit(solution)/shard_map/ppermute | solution.py:537
  73.1 3.9 %collective-permute-start.12 = (f32[8,128]{1,0:T(8,128)S(1)}, f32[8,128]{1,0:T(8,128)S(1)}, u32[]{:S(2)}, u32[]{:S(2)}) collective-permute-start(f32[8,128]{1,0:T(8,128)S(1)} %get-tuple-element.60), channel_id=1, source_target_pairs={{128,130},{130,128},{194,196},{196,194},{132,134},{134,132},{198,2... | collective-permute-start | bytes 12296 | tf_op jit(solution)/shard_map/ppermute | solution.py:537
  77.0 0.0 collective-permute-done.11.side_a
  77.1 1.0 collective-permute-done.12.side_b
  78.0 3.4 %shard_map.155 = (f32[3,256]{1,0:T(4,128)S(1)}, f32[384,2,128]{2,1,0:T(2,128)}) custom-call(f32[4,4,128]{2,1,0:T(4,128)S(1)} %get-tuple-element.47.near, f32[48,256]{1,0:T(8,128)S(1)} %collective-permute-done.pack, f32[8,256]{1,0:T(8,128)S(1)} %get-tuple-element.54.charge, f32[8,256]{1,0:T(8,128)S(1)} %get-tuple-element.55.outside_row, ...), custom_call_target="tpu_custom_call" | custom-call | tf_op jit(solution)/shard_map/pallas_call | solution.py:27
  81.4 19.1 %all-to-all-start.1 = ((f32[384,2,128]{2,1,0:T(2,128)}), f32[384,2,128]{2,1,0:T(2,128)S(1)}, u32[]{:S(2)}, u32[]{:S(2)}) async-start(f32[384,2,128]{2,1,0:T(2,128)} %get-tuple-element.63), calls=%async_computation.1 | async-start | bytes 786432 | tf_op jit(solution)/shard_map/all_to_all | solution.py:605
  100.6 4.0 %collective-permute-start.13 = (f32[3,256]{1,0:T(4,128)S(1)}, f32[3,256]{1,0:T(4,128)S(1)}, u32[]{:S(2)}, u32[]{:S(2)}) collective-permute-start(f32[3,256]{1,0:T(4,128)S(1)} %get-tuple-element.62), channel_id=1, source_target_pairs={{64,0},{0,1},{2,2},{66,3},{68,4},{4,5},{6,6},{70,7},{78,8},{14,9},... | collective-permute-start | bytes 9224 | tf_op jit(solution)/shard_map/ppermute | solution.py:537
  104.5 11.4 %all-to-all-done.1 = f32[384,2,128]{2,1,0:T(2,128)S(1)} async-done(((f32[384,2,128]{2,1,0:T(2,128)}), f32[384,2,128]{2,1,0:T(2,128)S(1)}, u32[]{:S(2)}, u32[]{:S(2)}) %all-to-all-start.1) | async-done | bytes 393248 | tf_op jit(solution)/shard_map/all_to_all | solution.py:605
  116.0 0.2 shard_map.156
  116.1 2.9 %collective-permute-start.14 = (f32[3,256]{1,0:T(4,128)S(1)}, f32[3,256]{1,0:T(4,128)S(1)}, u32[]{:S(2)}, u32[]{:S(2)}) collective-permute-start(f32[3,256]{1,0:T(4,128)S(1)} %shard_map.156), channel_id=1, source_target_pairs={{0,128},{128,0},{1,129},{129,1},{2,130},{130,2},{3,131},{131,3},{4... | collective-permute-start | bytes 9224 | tf_op jit(solution)/shard_map/ppermute | solution.py:608
  119.0 0.0 collective-permute-done.13
  119.0 0.8 collective-permute-done.14
  119.9 0.6 copy.18
  120.4 0.6 copy.19
  (1 shorter events, 0.0 us)
Async XLA Ops:
  1.7 4.5 %collective-permute-start.6 = (f32[2,4,128]{2,1,0:T(4,128)S(1)}, f32[2,4,128]{2,1,0:T(4,128)S(1)}, u32[]{:S(2)}, u32[]{:S(2)}) collective-permute-start(f32[2,4,128]{2,1,0:T(4,128)S(1)} %get-tuple-element.46), channel_id=1, source_target_pairs={{0,128},{128,0},{1,129},{129,1},{2,130},{130,2},{3,131},{131,3},{4... | collective-permute-start | bytes 12296 | tf_op jit(solution)/shard_map/ppermute | solution.py:557
  7.1 46.4 %all-to-all-start = ((f32[128,2,4,128]{3,2,1,0:T(4,128)}), f32[128,2,4,128]{3,2,1,0:T(4,128)S(1)}, u32[]{:S(2)}, u32[]{:S(2)}) async-start(f32[128,2,4,128]{3,2,1,0:T(4,128)} %broadcast_in_dim.17), calls=%async_computation | async-start | bytes 1048576 | tf_op jit(solution)/shard_map/all_to_all | solution.py:559
  20.8 2.0 %collective-permute-start.1 = (bf16[288,128]{1,0:T(8,128)(2,1)S(1)}, bf16[288,128]{1,0:T(8,128)(2,1)S(1)}, u32[]{:S(2)}, u32[]{:S(2)}) collective-permute-start(bf16[288,128]{1,0:T(8,128)(2,1)S(1)} %get-tuple-element.35), channel_id=1, source_target_pairs={{0,0},{1,64},{2,66},{3,2},{4,4},{5,68},{6,70},{7,6},{8,14},{9,78},... | collective-permute-start | bytes 221192 | tf_op jit(solution)/shard_map/ppermute | solution.py:537
  21.5 8.0 %collective-permute-start.2 = (bf16[288,128]{1,0:T(8,128)(2,1)S(1)}, bf16[288,128]{1,0:T(8,128)(2,1)S(1)}, u32[]{:S(2)}, u32[]{:S(2)}) collective-permute-start(bf16[288,128]{1,0:T(8,128)(2,1)S(1)} %get-tuple-element.36), channel_id=1, source_target_pairs={{1,2},{2,0},{3,68},{4,66},{5,6},{6,4},{7,78},{8,70},{9,12},{10,14}... | collective-permute-start | bytes 221192 | tf_op jit(solution)/shard_map/ppermute | solution.py:537
  29.5 24.0 %collective-permute-start.3 = (bf16[256,256]{1,0:T(8,128)(2,1)S(1)}, bf16[256,256]{1,0:T(8,128)(2,1)S(1)}, u32[]{:S(2)}, u32[]{:S(2)}) collective-permute-start(bf16[256,256]{1,0:T(8,128)(2,1)S(1)} %get-tuple-element.39), channel_id=1, source_target_pairs={{0,64},{1,0},{2,2},{3,66},{4,68},{5,4},{6,6},{7,70},{8,78},{9,14},... | collective-permute-start | bytes 393224 | tf_op jit(solution)/shard_map/ppermute | solution.py:537
  30.2 13.9 %collective-permute-start = (f32[48,256]{1,0:T(8,128)S(1)}, f32[48,256]{1,0:T(8,128)S(1)}, u32[]{:S(2)}, u32[]{:S(2)}) collective-permute-start(f32[48,256]{1,0:T(8,128)S(1)} %get-tuple-element.33), channel_id=1, source_target_pairs={{0,64},{1,0},{2,2},{3,66},{4,68},{5,4},{6,6},{7,70},{8,78},{9,14},... | collective-permute-start | bytes 147464 | tf_op jit(solution)/shard_map/ppermute | solution.py:537
  46.7 4.5 %collective-permute-start.4 = (f32[8,128]{1,0:T(8,128)S(1)}, f32[8,128]{1,0:T(8,128)S(1)}, u32[]{:S(2)}, u32[]{:S(2)}) collective-permute-start(f32[8,128]{1,0:T(8,128)S(1)} %get-tuple-element.40), channel_id=1, source_target_pairs={{192,128},{128,192},{130,194},{194,130},{196,132},{132,196},{134,1... | collective-permute-start | bytes 12296 | tf_op jit(solution)/shard_map/ppermute | solution.py:537
  49.1 4.4 %collective-permute-start.5 = (f32[8,128]{1,0:T(8,128)S(1)}, f32[8,128]{1,0:T(8,128)S(1)}, u32[]{:S(2)}, u32[]{:S(2)}) collective-permute-start(f32[8,128]{1,0:T(8,128)S(1)} %get-tuple-element.41), channel_id=1, source_target_pairs={{128,130},{130,128},{194,196},{196,194},{132,134},{134,132},{198,2... | collective-permute-start | bytes 12296 | tf_op jit(solution)/shard_map/ppermute | solution.py:537
  57.3 3.2 %collective-permute-start.7 = (bf16[256,128]{1,0:T(8,128)(2,1)S(1)}, bf16[256,128]{1,0:T(8,128)(2,1)S(1)}, u32[]{:S(2)}, u32[]{:S(2)}) collective-permute-start(bf16[256,128]{1,0:T(8,128)(2,1)S(1)} %get-tuple-element.50), channel_id=1, source_target_pairs={{64,0},{0,64},{2,66},{66,2},{68,4},{4,68},{6,70},{70,6},{78,14},{1... | collective-permute-start | bytes 196616 | tf_op jit(solution)/shard_map/ppermute | solution.py:537
  57.4 5.0 %collective-permute-start.8 = (bf16[256,128]{1,0:T(8,128)(2,1)S(1)}, bf16[256,128]{1,0:T(8,128)(2,1)S(1)}, u32[]{:S(2)}, u32[]{:S(2)}) collective-permute-start(bf16[256,128]{1,0:T(8,128)(2,1)S(1)} %get-tuple-element.51), channel_id=1, source_target_pairs={{0,2},{2,0},{66,68},{68,66},{4,6},{6,4},{70,78},{78,70},{14,12},{1... | collective-permute-start | bytes 196616 | tf_op jit(solution)/shard_map/ppermute | solution.py:537
  63.7 5.4 %collective-permute-start.9 = (f32[8,128]{1,0:T(8,128)S(1)}, f32[8,128]{1,0:T(8,128)S(1)}, u32[]{:S(2)}, u32[]{:S(2)}) collective-permute-start(f32[8,128]{1,0:T(8,128)S(1)} %get-tuple-element.56), channel_id=1, source_target_pairs={{192,128},{128,192},{130,194},{194,130},{196,132},{132,196},{134,1... | collective-permute-start | bytes 12296 | tf_op jit(solution)/shard_map/ppermute | solution.py:537
  65.6 4.4 %collective-permute-start.10 = (f32[8,128]{1,0:T(8,128)S(1)}, f32[8,128]{1,0:T(8,128)S(1)}, u32[]{:S(2)}, u32[]{:S(2)}) collective-permute-start(f32[8,128]{1,0:T(8,128)S(1)} %get-tuple-element.57), channel_id=1, source_target_pairs={{128,130},{130,128},{194,196},{196,194},{132,134},{134,132},{198,2... | collective-permute-start | bytes 12296 | tf_op jit(solution)/shard_map/ppermute | solution.py:537
  71.2 5.8 %collective-permute-start.11 = (f32[8,128]{1,0:T(8,128)S(1)}, f32[8,128]{1,0:T(8,128)S(1)}, u32[]{:S(2)}, u32[]{:S(2)}) collective-permute-start(f32[8,128]{1,0:T(8,128)S(1)} %get-tuple-element.59), channel_id=1, source_target_pairs={{192,128},{128,192},{130,194},{194,130},{196,132},{132,196},{134,1... | collective-permute-start | bytes 12296 | tf_op jit(solution)/shard_map/ppermute | solution.py:537
  73.1 4.9 %collective-permute-start.12 = (f32[8,128]{1,0:T(8,128)S(1)}, f32[8,128]{1,0:T(8,128)S(1)}, u32[]{:S(2)}, u32[]{:S(2)}) collective-permute-start(f32[8,128]{1,0:T(8,128)S(1)} %get-tuple-element.60), channel_id=1, source_target_pairs={{128,130},{130,128},{194,196},{196,194},{132,134},{134,132},{198,2... | collective-permute-start | bytes 12296 | tf_op jit(solution)/shard_map/ppermute | solution.py:537
  81.4 34.5 %all-to-all-start.1 = ((f32[384,2,128]{2,1,0:T(2,128)}), f32[384,2,128]{2,1,0:T(2,128)S(1)}, u32[]{:S(2)}, u32[]{:S(2)}) async-start(f32[384,2,128]{2,1,0:T(2,128)} %get-tuple-element.63), calls=%async_computation.1 | async-start | bytes 786432 | tf_op jit(solution)/shard_map/all_to_all | solution.py:605
  100.6 18.5 %collective-permute-start.13 = (f32[3,256]{1,0:T(4,128)S(1)}, f32[3,256]{1,0:T(4,128)S(1)}, u32[]{:S(2)}, u32[]{:S(2)}) collective-permute-start(f32[3,256]{1,0:T(4,128)S(1)} %get-tuple-element.62), channel_id=1, source_target_pairs={{64,0},{0,1},{2,2},{66,3},{68,4},{4,5},{6,6},{70,7},{78,8},{14,9},... | collective-permute-start | bytes 9224 | tf_op jit(solution)/shard_map/ppermute | solution.py:537
  116.1 3.7 %collective-permute-start.14 = (f32[3,256]{1,0:T(4,128)S(1)}, f32[3,256]{1,0:T(4,128)S(1)}, u32[]{:S(2)}, u32[]{:S(2)}) collective-permute-start(f32[3,256]{1,0:T(4,128)S(1)} %shard_map.156), channel_id=1, source_target_pairs={{0,128},{128,0},{1,129},{129,1},{2,130},{130,2},{3,131},{131,3},{4... | collective-permute-start | bytes 9224 | tf_op jit(solution)/shard_map/ppermute | solution.py:608

commit v7 on v6

--- a/solution.py
+++ b/solution.py
@@ -196,7 +196,7 @@
 
 def radial_kernel(
     pack, from_a, from_b, w_in_far, w_mid_far,
-    third_far, w_in, w_mid, third, entry, square, done,
+    third_far, w_in, w_mid, third, done,
 ):
     site, slots, _ = views(pack)
     width = site.shape[1]
@@ -206,21 +206,10 @@
     @pl.when(learned())
     def _():
         wait = fetch(((w_in_far, w_in), (w_mid_far, w_mid)), done)
-        entry[...] = jnp.concatenate([site[...], rim(from_a), rim(from_b)], axis=1).T
-        tx, ty, tz = site[0:1, :], site[1:2, :], site[2:3, :]
-
-        def some_rows(j, carry):
-            start = pl.multiple_of(j * STATIC_CHUNK, STATIC_CHUNK)
-            cols = entry[pl.ds(start, STATIC_CHUNK), :]
-            rx, ry, rz = tx - cols[:, 0:1], ty - cols[:, 1:2], tz - cols[:, 2:3]
-            square[pl.ds(start, STATIC_CHUNK), :] = rx * rx + ry * ry + rz * rz
-            return carry
-
-        lax.fori_loop(0, depth // STATIC_CHUNK, some_rows, 0, unroll=4)
-        empty = tx * tx + ty * ty + tz * tz
+        pieces = split3(jnp.concatenate([site[...], rim(from_a), rim(from_b)], axis=1))
         step = RADIAL_SLOTS * width
+        here = jnp.concatenate([site[...]] * RADIAL_SLOTS, axis=1)
         centres = lax.broadcasted_iota(jnp.int32, (BASIS, step), 0).astype(F32) * SPACING
-        ids = lax.broadcasted_iota(jnp.int32, (8, width), 0).astype(F32)
         wait()
         first_w = jnp.concatenate([flip(w_in[0]), flip(w_in[1])], axis=0).astype(BF16)
         zero = jnp.zeros((64, 64), F32)
@@ -233,21 +222,11 @@
         second_w, third_w = both(0), both(1)
 
         def some_slots(k, carry):
-            named = [slots[pl.ds(k * RADIAL_SLOTS + i, 1), :] for i in range(RADIAL_SLOTS)]
-
-            def pick(j, acc):
-                start = pl.multiple_of(j * 8, 8)
-                here = square[pl.ds(start, 8), :]
-                mine = ids + start.astype(F32)
-                return tuple(a + jnp.where(mine == n, here, 0.0) for a, n in zip(acc, named))
-
-            nil = jnp.zeros((8, width), F32)
-            found = lax.fori_loop(0, depth // 8, pick, (nil,) * RADIAL_SLOTS, unroll=8)
-            far = [
-                jnp.sum(f, axis=0, keepdims=True) + jnp.where(n == float(depth), empty, 0.0)
-                for f, n in zip(found, named)
-            ]
-            gap = jnp.sqrt(jnp.concatenate(far, axis=1) + SMOOTH) - centres
+            found = join3(dot(pieces, one_hot(slot_row(slots, k * RADIAL_SLOTS, RADIAL_SLOTS), depth)))
+            offset = here - found
+            squares = offset * offset
+            dist_sq = squares[0:1] + squares[1:2] + squares[2:3] + SMOOTH
+            gap = jnp.sqrt(dist_sq) - centres
             basis = jnp.exp(-(gap * gap)).astype(BF16)
             hidden = silu(dot(first_w, basis)).astype(BF16)
             hidden = silu(dot(second_w, hidden)).astype(BF16)
@@ -559,7 +538,7 @@
     near = lax.all_to_all(copies, DOM, 0, 0, tiled=True).reshape(2 * members, 4, half)
     pack = move(pack, itself, same, place)
     rim_a, rim_b = trade(lent_a, lent_b, source=same)
-    feat_t, rim_a, rim_b = lax.optimization_barrier((feat_t, rim_a, rim_b))
+    feat_t, pack, rim_a, rim_b = lax.optimization_barrier((feat_t, pack, rim_a, rim_b))
     feat_t = move(feat_t, itself, same, place, (0,))
     w3, w5, fixed, entry, lent_a, lent_b = call(
         static_kernel, [((depth, width), F32), ((depth, width), F32), row8, ((depth, 8), F32), table8, table8],
@@ -569,8 +548,7 @@
     third_shape = (LAYERS * radial_in.shape[2], slot_count * width)
     (third,) = call(
         radial_kernel, [(third_shape, BF16)], (pack, rim_a, rim_b), (radial_in, radial_mid),
-        [pltpu.VMEM(radial_in.shape, BF16), pltpu.VMEM(radial_mid.shape, BF16), pltpu.VMEM(third_shape, BF16),
-         pltpu.VMEM((depth, 8), F32), pltpu.VMEM((depth, width), F32)], 3, 1,
+        [pltpu.VMEM(radial_in.shape, BF16), pltpu.VMEM(radial_mid.shape, BF16), pltpu.VMEM(third_shape, BF16)], 3, 1,
     )
     moment = pltpu.VMEM((depth, 8), F32)
     total = pltpu.VMEM((channels, width), F32)

time: 122 us -> 113 us (0.926)
  waiting for transfers between devices: 32.4 us -> 20.6 us
  starting transfers between devices: 72.1 us -> 75.8 us
    ppermute x13, waiting for transfers between devices: 19.4 us -> 6 us  [move(): lax.ppermute(value, EVERY, [(source[a] + g * members, target[b] + g * mem...]
    ppermute x13, starting transfers between devices: 32.7 us -> 41.5 us  [move(): lax.ppermute(value, EVERY, [(source[a] + g * members, target[b] + g * mem...]
    all_to_all x1, starting transfers between devices: 19.1 us -> 16.4 us  [local(): lax.all_to_all(spread, DOM, 0, 0, tiled=True).reshape(members, 3, 2, half)]
    ppermute x1, starting transfers between devices: 2.91 us -> 0.48 us  [local(): return (result, lax.ppermute(share, 'grp', [(0, 1), (1, 0)]))]
    all_to_all x1, waiting for transfers between devices: 11.4 us -> 12.9 us  [local(): lax.all_to_all(spread, DOM, 0, 0, tiled=True).reshape(members, 3, 2, half)]
  transfers between devices with their start and end apart: 17 -> 17, of which waited for: 10 -> 8; matrix products, arithmetic and copies ran while one was open for 0% -> 0% of each run, Pallas kernels for 2% -> 3%
where the time goes in v7:
time: 113 us
  starting transfers between devices  75.8 us (67%)
  waiting for transfers between devices  20.6 us (18%)
  Pallas kernels  13.6 us (12%)
  local copies, waits for them, and re-layouts  2.05 us (2%)
    ppermute x13, starting transfers between devices, move(): lax.ppermute(value, EVERY, [(source[a] + g * members, target[b] + g * mem...  41.5 us
    all_to_all x1, starting transfers between devices, local(): lax.all_to_all(spread, DOM, 0, 0, tiled=True).reshape(members, 3, 2, half)  16.4 us
    all_to_all x1, starting transfers between devices, local(): lax.all_to_all(copies, DOM, 0, 0, tiled=True).reshape(2 * members, 4, half)  13.8 us
    pallas_call x8, Pallas kernels, call(): pl.pallas_call(body, out_shape=[jax.ShapeDtypeStruct(s, d) for s, d in ou...  13.6 us
    all_to_all x1, waiting for transfers between devices, local(): lax.all_to_all(spread, DOM, 0, 0, tiled=True).reshape(members, 3, 2, half)  12.9 us
    ppermute x13, waiting for transfers between devices, move(): lax.ppermute(value, EVERY, [(source[a] + g * members, target[b] + g * mem...  6 us
    ppermute x1, starting transfers between devices, local(): partner = lax.ppermute(mine, 'grp', [(0, 1), (1, 0)])  3.65 us
  transfers between devices with their start and end apart: 17, of which 8 were waited for; matrix products, arithmetic and copies ran while one was open for 0% of the time, Pallas kernels for 3%

profile of v7, /device:TPU:1, one launch (start us, length us, event | category | flops | bytes accessed | tf_op | source)
XLA Modules:
  0.0 112.9 jit_solution(15203097387424459483)
XLA Ops:
  0.6 1.1 shard_map.149
  1.7 3.7 %collective-permute-start.6 = (f32[2,4,128]{2,1,0:T(4,128)S(1)}, f32[2,4,128]{2,1,0:T(4,128)S(1)}, u32[]{:S(2)}, u32[]{:S(2)}) collective-permute-start(f32[2,4,128]{2,1,0:T(4,128)S(1)} %get-tuple-element.48), channel_id=1, source_target_pairs={{0,128},{128,0},{1,129},{129,1},{2,130},{130,2},{3,131},{131,3},{4... | collective-permute-start | bytes 12296 | tf_op jit(solution)/shard_map/ppermute | solution.py:536
  5.4 0.8 collective-permute-done.6
  6.2 0.9 broadcast_in_dim.17
  7.1 13.8 %all-to-all-start = ((f32[128,2,4,128]{3,2,1,0:T(4,128)}), f32[128,2,4,128]{3,2,1,0:T(4,128)S(1)}, u32[]{:S(2)}, u32[]{:S(2)}) async-start(f32[128,2,4,128]{3,2,1,0:T(4,128)} %broadcast_in_dim.17), calls=%async_computation | async-start | bytes 1048576 | tf_op jit(solution)/shard_map/all_to_all | solution.py:538
  20.8 0.7 collective-permute-start.1
  21.5 1.3 %collective-permute-start.2 = (bf16[288,128]{1,0:T(8,128)(2,1)S(1)}, bf16[288,128]{1,0:T(8,128)(2,1)S(1)}, u32[]{:S(2)}, u32[]{:S(2)}) collective-permute-start(bf16[288,128]{1,0:T(8,128)(2,1)S(1)} %get-tuple-element.37), channel_id=1, source_target_pairs={{1,2},{2,0},{3,68},{4,66},{5,6},{6,4},{7,78},{8,70},{9,12},{10,14}... | collective-permute-start | bytes 221192 | tf_op jit(solution)/shard_map/ppermute | solution.py:516
  22.8 12.2 %collective-permute-start = (f32[48,256]{1,0:T(8,128)S(1)}, f32[48,256]{1,0:T(8,128)S(1)}, u32[]{:S(2)}, u32[]{:S(2)}) collective-permute-start(f32[48,256]{1,0:T(8,128)S(1)} %get-tuple-element.35), channel_id=1, source_target_pairs={{0,64},{1,0},{2,2},{3,66},{4,68},{5,4},{6,6},{7,70},{8,78},{9,14},... | collective-permute-start | bytes 147464 | tf_op jit(solution)/shard_map/ppermute | solution.py:516
  35.1 1.2 %collective-permute-done.pack = f32[48,256]{1,0:T(8,128)S(1)} collective-permute-done((f32[48,256]{1,0:T(8,128)S(1)}, f32[48,256]{1,0:T(8,128)S(1)}, u32[]{:S(2)}, u32[]{:S(2)}) %collective-permute-start) | collective-permute-done | bytes 49184 | tf_op jit(solution)/shard_map/ppermute | solution.py:516
  36.2 0.0 collective-permute-done.1.from_a
  36.2 0.0 collective-permute-done.2.from_b
  36.2 0.7 collective-permute-start.3
  36.9 2.7 %shard_map.150 = (f32[512,256]{1,0:T(8,128)S(1)}, f32[512,256]{1,0:T(8,128)S(1)}, f32[8,256]{1,0:T(8,128)S(1)}, f32[512,8]{1,0:T(8,128)S(1)}, f32[8,128]{1,0:T(8,128)S(1)}, /*index=5*/f32[8,128]{1,0:T(8,128)S(1)}) custom-call(f32[48,256]{1,0:T(8,128)S(1)} %collective-permute-done.pack, bf16[288,128]{1,0:T(8,128)(2,1)S(1)} %collective-permute-done.1.from_a, ...), custom_call_target="tpu_custom_call" | custom-call | tf_op jit(solution)/shard_map/pallas_call | solution.py:27
  39.6 4.0 %collective-permute-start.4 = (f32[8,128]{1,0:T(8,128)S(1)}, f32[8,128]{1,0:T(8,128)S(1)}, u32[]{:S(2)}, u32[]{:S(2)}) collective-permute-start(f32[8,128]{1,0:T(8,128)S(1)} %get-tuple-element.42), channel_id=1, source_target_pairs={{192,128},{128,192},{130,194},{194,130},{196,132},{132,196},{134,1... | collective-permute-start | bytes 12296 | tf_op jit(solution)/shard_map/ppermute | solution.py:516
  43.6 3.0 %collective-permute-start.5 = (f32[8,128]{1,0:T(8,128)S(1)}, f32[8,128]{1,0:T(8,128)S(1)}, u32[]{:S(2)}, u32[]{:S(2)}) collective-permute-start(f32[8,128]{1,0:T(8,128)S(1)} %get-tuple-element.43), channel_id=1, source_target_pairs={{128,130},{130,128},{194,196},{196,194},{132,134},{134,132},{198,2... | collective-permute-start | bytes 12296 | tf_op jit(solution)/shard_map/ppermute | solution.py:516
  46.7 0.0 collective-permute-done.4.side_a
  46.7 1.2 %collective-permute-done.5.side_b = f32[8,128]{1,0:T(8,128)S(1)} collective-permute-done((f32[8,128]{1,0:T(8,128)S(1)}, f32[8,128]{1,0:T(8,128)S(1)}, u32[]{:S(2)}, u32[]{:S(2)}) %collective-permute-start.5) | collective-permute-done | bytes 4128 | tf_op jit(solution)/shard_map/ppermute | solution.py:516
  47.9 0.0 collective-permute-done.3.feat_t
  47.9 0.0 all-to-all-done
  47.9 3.8 %shard_map.152 = (f32[8,256]{1,0:T(8,128)S(1)}, f32[4,4,128]{2,1,0:T(4,128)S(1)}, bf16[256,256]{1,0:T(8,128)(2,1)S(1)}, bf16[256,256]{1,0:T(8,128)(2,1)S(1)}, f3...) custom-call(f32[48,256]{1,0:T(8,128)S(1)} %collective-permute-done.pack,, ...), custom_call_target="tpu_custom_call" | custom-call | tf_op jit(solution)/shard_map/pallas_call | solution.py:27
  51.8 0.1 collective-permute-start.7
  51.9 3.4 %collective-permute-start.8 = (bf16[256,128]{1,0:T(8,128)(2,1)S(1)}, bf16[256,128]{1,0:T(8,128)(2,1)S(1)}, u32[]{:S(2)}, u32[]{:S(2)}) collective-permute-start(bf16[256,128]{1,0:T(8,128)(2,1)S(1)} %get-tuple-element.53), channel_id=1, source_target_pairs={{0,2},{2,0},{66,68},{68,66},{4,6},{6,4},{70,78},{78,70},{14,12},{1... | collective-permute-start | bytes 196616 | tf_op jit(solution)/shard_map/ppermute | solution.py:516
  55.3 0.0 collective-permute-done.7.side_a
  55.3 1.6 %collective-permute-done.8.side_b = bf16[256,128]{1,0:T(8,128)(2,1)S(1)} collective-permute-done((bf16[256,128]{1,0:T(8,128)(2,1)S(1)}, bf16[256,128]{1,0:T(8,128)(2,1)S(1)}, u32[]{:S(2)}, u32[]{:S(2)}) %collective-permute-start.8) | collective-permute-done | bytes 65568 | tf_op jit(solution)/shard_map/ppermute | solution.py:516
  57.0 1.2 %shard_map.153 = (f32[8,256]{1,0:T(8,128)S(1)}, f32[8,256]{1,0:T(8,128)S(1)}, f32[8,128]{1,0:T(8,128)S(1)}, f32[8,128]{1,0:T(8,128)S(1)}) custom-call(bf16[256,256]{1,0:T(8,128)(2,1)S(1)} %get-tuple-element.50.hidden, bf16[256,256]{1,0:T(8,128)(2,1)S(1)} %get-tuple-element.51.lifted, bf16[256,128]{1,0:T(8,128)(2,1)S(1)} %collective-permute-done.7.side_a, ...), custom_call_target="tpu_custom_call" | custom-call | tf_op jit(solution)/shard_map/pallas_call | solution.py:27
  58.2 1.9 %collective-permute-start.9 = (f32[8,128]{1,0:T(8,128)S(1)}, f32[8,128]{1,0:T(8,128)S(1)}, u32[]{:S(2)}, u32[]{:S(2)}) collective-permute-start(f32[8,128]{1,0:T(8,128)S(1)} %get-tuple-element.58), channel_id=1, source_target_pairs={{192,128},{128,192},{130,194},{194,130},{196,132},{132,196},{134,1... | collective-permute-start | bytes 12296 | tf_op jit(solution)/shard_map/ppermute | solution.py:516
  60.1 4.4 %collective-permute-start.10 = (f32[8,128]{1,0:T(8,128)S(1)}, f32[8,128]{1,0:T(8,128)S(1)}, u32[]{:S(2)}, u32[]{:S(2)}) collective-permute-start(f32[8,128]{1,0:T(8,128)S(1)} %get-tuple-element.59), channel_id=1, source_target_pairs={{128,130},{130,128},{194,196},{196,194},{132,134},{134,132},{198,2... | collective-permute-start | bytes 12296 | tf_op jit(solution)/shard_map/ppermute | solution.py:516
  64.5 0.0 collective-permute-done.9.side_a
  64.5 1.0 collective-permute-done.10.side_b
  65.5 1.2 %shard_map.154 = (f32[8,256]{1,0:T(8,128)S(1)}, f32[8,128]{1,0:T(8,128)S(1)}, f32[8,128]{1,0:T(8,128)S(1)}) custom-call(f32[8,128]{1,0:T(8,128)S(1)} %collective-permute-done.9.side_a, f32[8,128]{1,0:T(8,128)S(1)} %collective-permute-done.10.side_b, f32[48,256]{1,0:T(8,128)S(1)} %collective-permute-done.pack, f32[512,256]{1,0:T(8,128)S(1)} %get-tuple-element.44.w3, ...), custom_call_target="tpu_custom_call" | custom-call | tf_op jit(solution)/shard_map/pallas_call | solution.py:27
  66.7 1.9 %collective-permute-start.11 = (f32[8,128]{1,0:T(8,128)S(1)}, f32[8,128]{1,0:T(8,128)S(1)}, u32[]{:S(2)}, u32[]{:S(2)}) collective-permute-start(f32[8,128]{1,0:T(8,128)S(1)} %get-tuple-element.61), channel_id=1, source_target_pairs={{192,128},{128,192},{130,194},{194,130},{196,132},{132,196},{134,1... | collective-permute-start | bytes 12296 | tf_op jit(solution)/shard_map/ppermute | solution.py:516
  68.6 3.9 %collective-permute-start.12 = (f32[8,128]{1,0:T(8,128)S(1)}, f32[8,128]{1,0:T(8,128)S(1)}, u32[]{:S(2)}, u32[]{:S(2)}) collective-permute-start(f32[8,128]{1,0:T(8,128)S(1)} %get-tuple-element.62), channel_id=1, source_target_pairs={{128,130},{130,128},{194,196},{196,194},{132,134},{134,132},{198,2... | collective-permute-start | bytes 12296 | tf_op jit(solution)/shard_map/ppermute | solution.py:516
  72.4 0.0 collective-permute-done.11.side_a
  72.5 1.0 collective-permute-done.12.side_b
  73.4 3.4 %shard_map.155 = (f32[3,256]{1,0:T(4,128)S(1)}, f32[384,2,128]{2,1,0:T(2,128)}) custom-call(f32[4,4,128]{2,1,0:T(4,128)S(1)} %get-tuple-element.49.near, f32[48,256]{1,0:T(8,128)S(1)} %collective-permute-done.pack, f32[8,256]{1,0:T(8,128)S(1)} %get-tuple-element.56.charge, f32[8,256]{1,0:T(8,128)S(1)} %get-tuple-element.57.outside_row, ...), custom_call_target="tpu_custom_call" | custom-call | tf_op jit(solution)/shard_map/pallas_call | solution.py:27
  76.8 16.4 %all-to-all-start.1 = ((f32[384,2,128]{2,1,0:T(2,128)}), f32[384,2,128]{2,1,0:T(2,128)S(1)}, u32[]{:S(2)}, u32[]{:S(2)}) async-start(f32[384,2,128]{2,1,0:T(2,128)} %get-tuple-element.65), calls=%async_computation.1 | async-start | bytes 786432 | tf_op jit(solution)/shard_map/all_to_all | solution.py:583
  93.3 4.0 %collective-permute-start.13 = (f32[3,256]{1,0:T(4,128)S(1)}, f32[3,256]{1,0:T(4,128)S(1)}, u32[]{:S(2)}, u32[]{:S(2)}) collective-permute-start(f32[3,256]{1,0:T(4,128)S(1)} %get-tuple-element.64), channel_id=1, source_target_pairs={{64,0},{0,1},{2,2},{66,3},{68,4},{4,5},{6,6},{70,7},{78,8},{14,9},... | collective-permute-start | bytes 9224 | tf_op jit(solution)/shard_map/ppermute | solution.py:516
  97.3 12.9 %all-to-all-done.1 = f32[384,2,128]{2,1,0:T(2,128)S(1)} async-done(((f32[384,2,128]{2,1,0:T(2,128)}), f32[384,2,128]{2,1,0:T(2,128)S(1)}, u32[]{:S(2)}, u32[]{:S(2)}) %all-to-all-start.1) | async-done | bytes 393248 | tf_op jit(solution)/shard_map/all_to_all | solution.py:583
  110.2 0.2 shard_map.156
  110.4 0.5 collective-permute-start.14
  110.8 0.0 collective-permute-done.13
  110.8 0.8 collective-permute-done.14
  111.7 0.6 copy.18
  112.3 0.6 copy.19
  (1 shorter events, 0.0 us)
Async XLA Ops:
  1.7 4.5 %collective-permute-start.6 = (f32[2,4,128]{2,1,0:T(4,128)S(1)}, f32[2,4,128]{2,1,0:T(4,128)S(1)}, u32[]{:S(2)}, u32[]{:S(2)}) collective-permute-start(f32[2,4,128]{2,1,0:T(4,128)S(1)} %get-tuple-element.48), channel_id=1, source_target_pairs={{0,128},{128,0},{1,129},{129,1},{2,130},{130,2},{3,131},{131,3},{4... | collective-permute-start | bytes 12296 | tf_op jit(solution)/shard_map/ppermute | solution.py:536
  7.1 40.9 %all-to-all-start = ((f32[128,2,4,128]{3,2,1,0:T(4,128)}), f32[128,2,4,128]{3,2,1,0:T(4,128)S(1)}, u32[]{:S(2)}, u32[]{:S(2)}) async-start(f32[128,2,4,128]{3,2,1,0:T(4,128)} %broadcast_in_dim.17), calls=%async_computation | async-start | bytes 1048576 | tf_op jit(solution)/shard_map/all_to_all | solution.py:538
  20.8 15.4 %collective-permute-start.1 = (bf16[288,128]{1,0:T(8,128)(2,1)S(1)}, bf16[288,128]{1,0:T(8,128)(2,1)S(1)}, u32[]{:S(2)}, u32[]{:S(2)}) collective-permute-start(bf16[288,128]{1,0:T(8,128)(2,1)S(1)} %get-tuple-element.36), channel_id=1, source_target_pairs={{0,0},{1,64},{2,66},{3,2},{4,4},{5,68},{6,70},{7,6},{8,14},{9,78},... | collective-permute-start | bytes 221192 | tf_op jit(solution)/shard_map/ppermute | solution.py:516
  21.5 14.7 %collective-permute-start.2 = (bf16[288,128]{1,0:T(8,128)(2,1)S(1)}, bf16[288,128]{1,0:T(8,128)(2,1)S(1)}, u32[]{:S(2)}, u32[]{:S(2)}) collective-permute-start(bf16[288,128]{1,0:T(8,128)(2,1)S(1)} %get-tuple-element.37), channel_id=1, source_target_pairs={{1,2},{2,0},{3,68},{4,66},{5,6},{6,4},{7,78},{8,70},{9,12},{10,14}... | collective-permute-start | bytes 221192 | tf_op jit(solution)/shard_map/ppermute | solution.py:516
  22.8 13.4 %collective-permute-start = (f32[48,256]{1,0:T(8,128)S(1)}, f32[48,256]{1,0:T(8,128)S(1)}, u32[]{:S(2)}, u32[]{:S(2)}) collective-permute-start(f32[48,256]{1,0:T(8,128)S(1)} %get-tuple-element.35), channel_id=1, source_target_pairs={{0,64},{1,0},{2,2},{3,66},{4,68},{5,4},{6,6},{7,70},{8,78},{9,14},... | collective-permute-start | bytes 147464 | tf_op jit(solution)/shard_map/ppermute | solution.py:516
  36.2 11.7 %collective-permute-start.3 = (bf16[256,256]{1,0:T(8,128)(2,1)S(1)}, bf16[256,256]{1,0:T(8,128)(2,1)S(1)}, u32[]{:S(2)}, u32[]{:S(2)}) collective-permute-start(bf16[256,256]{1,0:T(8,128)(2,1)S(1)} %get-tuple-element.41), channel_id=1, source_target_pairs={{0,64},{1,0},{2,2},{3,66},{4,68},{5,4},{6,6},{7,70},{8,78},{9,14},... | collective-permute-start | bytes 393224 | tf_op jit(solution)/shard_map/ppermute | solution.py:516
  39.6 7.1 %collective-permute-start.4 = (f32[8,128]{1,0:T(8,128)S(1)}, f32[8,128]{1,0:T(8,128)S(1)}, u32[]{:S(2)}, u32[]{:S(2)}) collective-permute-start(f32[8,128]{1,0:T(8,128)S(1)} %get-tuple-element.42), channel_id=1, source_target_pairs={{192,128},{128,192},{130,194},{194,130},{196,132},{132,196},{134,1... | collective-permute-start | bytes 12296 | tf_op jit(solution)/shard_map/ppermute | solution.py:516
  43.6 4.4 %collective-permute-start.5 = (f32[8,128]{1,0:T(8,128)S(1)}, f32[8,128]{1,0:T(8,128)S(1)}, u32[]{:S(2)}, u32[]{:S(2)}) collective-permute-start(f32[8,128]{1,0:T(8,128)S(1)} %get-tuple-element.43), channel_id=1, source_target_pairs={{128,130},{130,128},{194,196},{196,194},{132,134},{134,132},{198,2... | collective-permute-start | bytes 12296 | tf_op jit(solution)/shard_map/ppermute | solution.py:516
  51.8 3.5 %collective-permute-start.7 = (bf16[256,128]{1,0:T(8,128)(2,1)S(1)}, bf16[256,128]{1,0:T(8,128)(2,1)S(1)}, u32[]{:S(2)}, u32[]{:S(2)}) collective-permute-start(bf16[256,128]{1,0:T(8,128)(2,1)S(1)} %get-tuple-element.52), channel_id=1, source_target_pairs={{64,0},{0,64},{2,66},{66,2},{68,4},{4,68},{6,70},{70,6},{78,14},{1... | collective-permute-start | bytes 196616 | tf_op jit(solution)/shard_map/ppermute | solution.py:516
  51.9 5.1 %collective-permute-start.8 = (bf16[256,128]{1,0:T(8,128)(2,1)S(1)}, bf16[256,128]{1,0:T(8,128)(2,1)S(1)}, u32[]{:S(2)}, u32[]{:S(2)}) collective-permute-start(bf16[256,128]{1,0:T(8,128)(2,1)S(1)} %get-tuple-element.53), channel_id=1, source_target_pairs={{0,2},{2,0},{66,68},{68,66},{4,6},{6,4},{70,78},{78,70},{14,12},{1... | collective-permute-start | bytes 196616 | tf_op jit(solution)/shard_map/ppermute | solution.py:516
  58.2 6.3 %collective-permute-start.9 = (f32[8,128]{1,0:T(8,128)S(1)}, f32[8,128]{1,0:T(8,128)S(1)}, u32[]{:S(2)}, u32[]{:S(2)}) collective-permute-start(f32[8,128]{1,0:T(8,128)S(1)} %get-tuple-element.58), channel_id=1, source_target_pairs={{192,128},{128,192},{130,194},{194,130},{196,132},{132,196},{134,1... | collective-permute-start | bytes 12296 | tf_op jit(solution)/shard_map/ppermute | solution.py:516
  60.1 5.4 %collective-permute-start.10 = (f32[8,128]{1,0:T(8,128)S(1)}, f32[8,128]{1,0:T(8,128)S(1)}, u32[]{:S(2)}, u32[]{:S(2)}) collective-permute-start(f32[8,128]{1,0:T(8,128)S(1)} %get-tuple-element.59), channel_id=1, source_target_pairs={{128,130},{130,128},{194,196},{196,194},{132,134},{134,132},{198,2... | collective-permute-start | bytes 12296 | tf_op jit(solution)/shard_map/ppermute | solution.py:516
  66.7 5.8 %collective-permute-start.11 = (f32[8,128]{1,0:T(8,128)S(1)}, f32[8,128]{1,0:T(8,128)S(1)}, u32[]{:S(2)}, u32[]{:S(2)}) collective-permute-start(f32[8,128]{1,0:T(8,128)S(1)} %get-tuple-element.61), channel_id=1, source_target_pairs={{192,128},{128,192},{130,194},{194,130},{196,132},{132,196},{134,1... | collective-permute-start | bytes 12296 | tf_op jit(solution)/shard_map/ppermute | solution.py:516
  68.6 4.9 %collective-permute-start.12 = (f32[8,128]{1,0:T(8,128)S(1)}, f32[8,128]{1,0:T(8,128)S(1)}, u32[]{:S(2)}, u32[]{:S(2)}) collective-permute-start(f32[8,128]{1,0:T(8,128)S(1)} %get-tuple-element.62), channel_id=1, source_target_pairs={{128,130},{130,128},{194,196},{196,194},{132,134},{134,132},{198,2... | collective-permute-start | bytes 12296 | tf_op jit(solution)/shard_map/ppermute | solution.py:516
  76.8 33.4 %all-to-all-start.1 = ((f32[384,2,128]{2,1,0:T(2,128)}), f32[384,2,128]{2,1,0:T(2,128)S(1)}, u32[]{:S(2)}, u32[]{:S(2)}) async-start(f32[384,2,128]{2,1,0:T(2,128)} %get-tuple-element.65), calls=%async_computation.1 | async-start | bytes 786432 | tf_op jit(solution)/shard_map/all_to_all | solution.py:583
  93.3 17.5 %collective-permute-start.13 = (f32[3,256]{1,0:T(4,128)S(1)}, f32[3,256]{1,0:T(4,128)S(1)}, u32[]{:S(2)}, u32[]{:S(2)}) collective-permute-start(f32[3,256]{1,0:T(4,128)S(1)} %get-tuple-element.64), channel_id=1, source_target_pairs={{64,0},{0,1},{2,2},{66,3},{68,4},{4,5},{6,6},{70,7},{78,8},{14,9},... | collective-permute-start | bytes 9224 | tf_op jit(solution)/shard_map/ppermute | solution.py:516
  110.4 1.3 %collective-permute-start.14 = (f32[3,256]{1,0:T(4,128)S(1)}, f32[3,256]{1,0:T(4,128)S(1)}, u32[]{:S(2)}, u32[]{:S(2)}) collective-permute-start(f32[3,256]{1,0:T(4,128)S(1)} %shard_map.156), channel_id=1, source_target_pairs={{0,128},{128,0},{1,129},{129,1},{2,130},{130,2},{3,131},{131,3},{4... | collective-permute-start | bytes 9224 | tf_op jit(solution)/shard_map/ppermute | solution.py:586

commit v8 on v5

--- a/solution.py
+++ b/solution.py
@@ -19,8 +19,8 @@
 FIELD_CHUNK, FIELD_UNROLL = 32, 4
 TERM_CHUNK, TERM_UNROLL = 64, 4
 STATIC_CHUNK = 32
-RADIAL_SLOTS = 8
-MESSAGE_SLOTS = 8
+RADIAL_SLOTS = 16
+MESSAGE_SLOTS = 16
 
 
 def call(body, outs, held, far=(), scratch=(), copies=0, far_outs=0, loose=0):
@@ -309,21 +309,33 @@
     pack, rim_a, rim_b, feat_t, side_a, side_b, w3, w5, fixed, entry,
     near_far, third_far, node_in_far, node_out_far, w_out_far, gain_far,
     outside_row, near_own, hidden_out, lifted_out, fixed_out, dipole_out, lent_a, lent_b,
-    near, cols, third, node_in, node_out, w_out, gain, total, moment, done,
+    near, cols, third, node_in, node_out, w_out, gain, total, moment,
+    in_first, in_second, out_t, node_t, gain_col, done,
 ):
     site, slots, picks = views(pack)
     width = site.shape[1]
     listed = near_own.shape[0]
+    weights = (
+        (node_in_far, node_in), (node_out_far.at[0], node_out), (w_out_far.at[0], w_out), (gain_far, gain),
+        (third_far, third),
+    )
+
+    @pl.when(learned())
+    def _():
+        fetch(weights, done)
+
     numbers = [listed_block(row[5:6, 0:128], l) for row in (site, rim_a, rim_b) for l in range(listed)]
     fetch([(near_far.at[b], near.at[i]) for i, b in enumerate(numbers)], done, 5)
-    weights = (
-        (third_far, third), (node_in_far, node_in), (node_out_far.at[0], node_out),
-        (w_out_far.at[0], w_out), (gain_far, gain),
-    )
-
-    @pl.when(learned())
-    def _():
-        fetch(weights, done)
+
+    @pl.when(learned())
+    def _():
+        for i, (source, target) in enumerate(weights[:4]):
+            pltpu.make_async_copy(source, target, done.at[i]).wait()
+        in_first[...] = flip(node_in[0]).astype(BF16)
+        in_second[...] = flip(node_in[1]).astype(BF16)
+        out_t[...] = flip(w_out[...]).astype(BF16)
+        node_t[...] = flip(node_out[...]).astype(BF16)
+        gain_col[...] = jnp.broadcast_to(gain[...], (8, width)).T
 
     for i, b in enumerate(numbers):
         pltpu.make_async_copy(near_far.at[b], near.at[i], done.at[5 + i]).wait()
@@ -342,18 +354,15 @@
 
     @pl.when(learned())
     def _():
-        for i, (a, b) in enumerate(weights):
-            pltpu.make_async_copy(a, b, done.at[i]).wait()
-        gain_col = jnp.broadcast_to(gain[...], (8, width)).T
         features = jnp.concatenate([feat_t[...], side_a[...], side_b[...]], axis=1)
         start = (features.astype(F32) + gain_col[:, 0:1] * strength).astype(BF16)
         present = jnp.concatenate([jnp.ones((1, width), F32), rim_a[6:7, :], rim_b[6:7, :]], axis=1)
-        raised = dot(flip(node_in[0]).astype(BF16), start)
+        raised = dot(in_first[...], start)
         table = jnp.where(present > 0.5, raised, 0.0).astype(BF16)
-        out_t, node_t = flip(w_out[...]).astype(BF16), flip(node_out[...]).astype(BF16)
-        new = message(0, start[:, :width], table, third, out_t, node_t, slots, total)
+        pltpu.make_async_copy(third_far, third, done.at[4]).wait()
+        new = message(0, start[:, :width], table, third, out_t[...], node_t[...], slots, total)
         hidden_out[...] = new
-        raised = dot(flip(node_in[1]).astype(BF16), new).astype(BF16)
+        raised = dot(in_second[...], new).astype(BF16)
         lifted_out[...] = raised
         lend_channels(raised, picks, lent_a, lent_b)
 
@@ -474,6 +483,10 @@
     )
 
 
+def finish_kernel(result, share, result_far, share_far, done):
+    fetch(((result, result_far), (share, share_far)), done)()
+
+
 def placed(block):
     y_half, plane, step, side = block // 64, block // 8 % 8, block // 2 % 4, block % 2
     x = 3 - step if plane % 2 else step
@@ -544,7 +557,9 @@
         (near, third, node_in, node_out, radial_out, field_gain[None]),
         [pltpu.VMEM((3 * listed, 4, half), F32), pltpu.VMEM((3 * listed * half, 8), F32),
          pltpu.VMEM(third_shape, BF16), pltpu.VMEM(node_in.shape, BF16), square, last,
-         pltpu.VMEM((1, channels), F32), total, moment], 5 + 3 * listed, loose=1,
+         pltpu.VMEM((1, channels), F32), total, moment, square, square,
+         pltpu.VMEM((channels, radial_out.shape[1]), BF16), square, pltpu.VMEM((channels, 8), F32)],
+        5 + 3 * listed, loose=1,
     )
     side_a, side_b = trade(lent_a, lent_b)
     charge, dipole, small_a, small_b = call(
@@ -567,7 +582,9 @@
     pieces = lax.all_to_all(spread, DOM, 0, 0, tiled=True).reshape(members, 3, 2, half)
     (share,) = call(gather_kernel, [((3, width), F32)], (pieces,))
     result = move(result, itself, place, same)
-    return result, lax.ppermute(share, "grp", [(0, 1), (1, 0)])
+    share = lax.ppermute(share, "grp", [(0, 1), (1, 0)])
+    whole = ((3, width), F32)
+    return tuple(call(finish_kernel, [whole, whole], (result, share), copies=2, far_outs=2))
 
 
 def solution(mesh):

time: 111 us -> 111 us (level)
  local copies, waits for them, and re-layouts: 2.05 us -> 0.87 us
    unnamed x2 -> x0, local copies, waits for them, and re-layouts: 1.18 us -> none
    pallas_call x8 -> x9, Pallas kernels: 13.5 us -> 14 us  [call(): pl.pallas_call(body, out_shape=[jax.ShapeDtypeStruct(s, d) for s, d in ou...]
where the time goes in v8:
time: 111 us
  starting transfers between devices  69.9 us (63%)
  waiting for transfers between devices  24.9 us (22%)
  Pallas kernels  14 us (13%)
    ppermute x13, starting transfers between devices, move(): lax.ppermute(value, EVERY, [(source[a] + g * members, target[b] + g * mem...  32 us
    all_to_all x1, starting transfers between devices, local(): lax.all_to_all(spread, DOM, 0, 0, tiled=True).reshape(members, 3, 2, half)  14.7 us
    pallas_call x9, Pallas kernels, call(): pl.pallas_call(body, out_shape=[jax.ShapeDtypeStruct(s, d) for s, d in ou...  14 us
    ppermute x13, waiting for transfers between devices, move(): lax.ppermute(value, EVERY, [(source[a] + g * members, target[b] + g * mem...  13.9 us
    all_to_all x1, starting transfers between devices, local(): lax.all_to_all(copies, DOM, 0, 0, tiled=True).reshape(2 * members, 4, half)  13.8 us
    all_to_all x1, waiting for transfers between devices, local(): lax.all_to_all(spread, DOM, 0, 0, tiled=True).reshape(members, 3, 2, half)  9.38 us
    ppermute x1, starting transfers between devices, local(): share = lax.ppermute(share, 'grp', [(0, 1), (1, 0)])  6.08 us
    ppermute x1, starting transfers between devices, local(): partner = lax.ppermute(mine, 'grp', [(0, 1), (1, 0)])  3.33 us
  transfers between devices with their start and end apart: 17, of which 8 were waited for; matrix products, arithmetic and copies ran while one was open for 0% of the time, Pallas kernels for 3%

profile of v8, /device:TPU:1, one launch (start us, length us, event | category | flops | bytes accessed | tf_op | source)
XLA Modules:
  0.0 110.7 jit_solution(1718512683432383574)
XLA Ops:
  0.6 1.0 shard_map.149
  1.7 3.3 %collective-permute-start.6 = (f32[2,4,128]{2,1,0:T(4,128)S(1)}, f32[2,4,128]{2,1,0:T(4,128)S(1)}, u32[]{:S(2)}, u32[]{:S(2)}) collective-permute-start(f32[2,4,128]{2,1,0:T(4,128)S(1)} %get-tuple-element.40), channel_id=1, source_target_pairs={{0,128},{128,0},{1,129},{129,1},{2,130},{130,2},{3,131},{131,3},{4... | collective-permute-start | bytes 12296 | tf_op jit(solution)/shard_map/ppermute | solution.py:534
  5.0 0.8 collective-permute-done.6
  5.8 0.9 broadcast_in_dim.17
  6.7 13.8 %all-to-all-start = ((f32[128,2,4,128]{3,2,1,0:T(4,128)}), f32[128,2,4,128]{3,2,1,0:T(4,128)S(1)}, u32[]{:S(2)}, u32[]{:S(2)}) async-start(f32[128,2,4,128]{3,2,1,0:T(4,128)} %broadcast_in_dim.17), calls=%async_computation | async-start | bytes 1048576 | tf_op jit(solution)/shard_map/all_to_all | solution.py:536
  20.5 0.7 collective-permute-start.3
  21.1 2.8 %collective-permute-start = (f32[48,256]{1,0:T(8,128)S(1)}, f32[48,256]{1,0:T(8,128)S(1)}, u32[]{:S(2)}, u32[]{:S(2)}) collective-permute-start(f32[48,256]{1,0:T(8,128)S(1)} %get-tuple-element.30), channel_id=1, source_target_pairs={{0,64},{1,0},{2,2},{3,66},{4,68},{5,4},{6,6},{7,70},{8,78},{9,14},... | collective-permute-start | bytes 147464 | tf_op jit(solution)/shard_map/ppermute | solution.py:516
  23.9 0.7 collective-permute-start.1
  24.6 1.3 %collective-permute-start.2 = (f32[8,128]{1,0:T(8,128)S(1)}, f32[8,128]{1,0:T(8,128)S(1)}, u32[]{:S(2)}, u32[]{:S(2)}) collective-permute-start(f32[8,128]{1,0:T(8,128)S(1)} %get-tuple-element.32), channel_id=1, source_target_pairs={{1,2},{2,0},{3,68},{4,66},{5,6},{6,4},{7,78},{8,70},{9,12},{10,14}... | collective-permute-start | bytes 12296 | tf_op jit(solution)/shard_map/ppermute | solution.py:516
  25.9 0.0 collective-permute-done.1.rim_a
  25.9 8.6 %collective-permute-done.2.rim_b = f32[8,128]{1,0:T(8,128)S(1)} collective-permute-done((f32[8,128]{1,0:T(8,128)S(1)}, f32[8,128]{1,0:T(8,128)S(1)}, u32[]{:S(2)}, u32[]{:S(2)}) %collective-permute-start.2) | collective-permute-done | bytes 4128 | tf_op jit(solution)/shard_map/ppermute | solution.py:516
  34.6 0.0 collective-permute-done.pack
  34.6 0.0 collective-permute-done.3.features_far
  34.6 2.7 %shard_map.150 = (bf16[256,256]{1,0:T(8,128)(2,1)S(1)}, f32[512,256]{1,0:T(8,128)S(1)}, f32[512,256]{1,0:T(8,128)S(1)}, f32[8,256]{1,0:T(8,128)S(1)}, f32[512,8]...) custom-call(f32[48,256]{1,0:T(8,128)S(1)} %collective-permute-done.pack, ...), custom_call_target="tpu_custom_call" | custom-call | tf_op jit(solution)/shard_map/pallas_call | solution.py:27
  37.3 2.6 %collective-permute-start.4 = (bf16[256,128]{1,0:T(8,128)(2,1)S(1)}, bf16[256,128]{1,0:T(8,128)(2,1)S(1)}, u32[]{:S(2)}, u32[]{:S(2)}) collective-permute-start(bf16[256,128]{1,0:T(8,128)(2,1)S(1)} %get-tuple-element.34), channel_id=1, source_target_pairs={{64,0},{0,64},{2,66},{66,2},{68,4},{4,68},{6,70},{70,6},{78,14},{1... | collective-permute-start | bytes 196616 | tf_op jit(solution)/shard_map/ppermute | solution.py:516
  39.8 3.3 %collective-permute-start.5 = (bf16[256,128]{1,0:T(8,128)(2,1)S(1)}, bf16[256,128]{1,0:T(8,128)(2,1)S(1)}, u32[]{:S(2)}, u32[]{:S(2)}) collective-permute-start(bf16[256,128]{1,0:T(8,128)(2,1)S(1)} %get-tuple-element.35), channel_id=1, source_target_pairs={{0,2},{2,0},{66,68},{68,66},{4,6},{6,4},{70,78},{78,70},{14,12},{1... | collective-permute-start | bytes 196616 | tf_op jit(solution)/shard_map/ppermute | solution.py:516
  43.2 0.0 collective-permute-done.4.side_a
  43.2 1.7 %collective-permute-done.5.side_b = bf16[256,128]{1,0:T(8,128)(2,1)S(1)} collective-permute-done((bf16[256,128]{1,0:T(8,128)(2,1)S(1)}, bf16[256,128]{1,0:T(8,128)(2,1)S(1)}, u32[]{:S(2)}, u32[]{:S(2)}) %collective-permute-start.5) | collective-permute-done | bytes 65568 | tf_op jit(solution)/shard_map/ppermute | solution.py:516
  44.8 0.0 all-to-all-done
  44.8 3.8 %shard_map.152 = (f32[8,256]{1,0:T(8,128)S(1)}, f32[4,4,128]{2,1,0:T(4,128)S(1)}, bf16[256,256]{1,0:T(8,128)(2,1)S(1)}, bf16[256,256]{1,0:T(8,128)(2,1)S(1)}, f3...) custom-call(f32[48,256]{1,0:T(8,128)S(1)} %collective-permute-done.pack,, ...), custom_call_target="tpu_custom_call" | custom-call | tf_op jit(solution)/shard_map/pallas_call | solution.py:27
  48.7 0.1 collective-permute-start.7
  48.8 4.7 %collective-permute-start.8 = (bf16[256,128]{1,0:T(8,128)(2,1)S(1)}, bf16[256,128]{1,0:T(8,128)(2,1)S(1)}, u32[]{:S(2)}, u32[]{:S(2)}) collective-permute-start(bf16[256,128]{1,0:T(8,128)(2,1)S(1)} %get-tuple-element.45), channel_id=1, source_target_pairs={{0,2},{2,0},{66,68},{68,66},{4,6},{6,4},{70,78},{78,70},{14,12},{1... | collective-permute-start | bytes 196616 | tf_op jit(solution)/shard_map/ppermute | solution.py:516
  53.5 0.0 collective-permute-done.7.side_a
  53.5 1.6 %collective-permute-done.8.side_b = bf16[256,128]{1,0:T(8,128)(2,1)S(1)} collective-permute-done((bf16[256,128]{1,0:T(8,128)(2,1)S(1)}, bf16[256,128]{1,0:T(8,128)(2,1)S(1)}, u32[]{:S(2)}, u32[]{:S(2)}) %collective-permute-start.8) | collective-permute-done | bytes 65568 | tf_op jit(solution)/shard_map/ppermute | solution.py:516
  55.1 1.2 %shard_map.153 = (f32[8,256]{1,0:T(8,128)S(1)}, f32[8,256]{1,0:T(8,128)S(1)}, f32[8,128]{1,0:T(8,128)S(1)}, f32[8,128]{1,0:T(8,128)S(1)}) custom-call(bf16[256,256]{1,0:T(8,128)(2,1)S(1)} %get-tuple-element.42.hidden, bf16[256,256]{1,0:T(8,128)(2,1)S(1)} %get-tuple-element.43.lifted, bf16[256,128]{1,0:T(8,128)(2,1)S(1)} %collective-permute-done.7.side_a, ...), custom_call_target="tpu_custom_call" | custom-call | tf_op jit(solution)/shard_map/pallas_call | solution.py:27
  56.3 1.9 %collective-permute-start.9 = (f32[8,128]{1,0:T(8,128)S(1)}, f32[8,128]{1,0:T(8,128)S(1)}, u32[]{:S(2)}, u32[]{:S(2)}) collective-permute-start(f32[8,128]{1,0:T(8,128)S(1)} %get-tuple-element.50), channel_id=1, source_target_pairs={{192,128},{128,192},{130,194},{194,130},{196,132},{132,196},{134,1... | collective-permute-start | bytes 12296 | tf_op jit(solution)/shard_map/ppermute | solution.py:516
  58.3 3.4 %collective-permute-start.10 = (f32[8,128]{1,0:T(8,128)S(1)}, f32[8,128]{1,0:T(8,128)S(1)}, u32[]{:S(2)}, u32[]{:S(2)}) collective-permute-start(f32[8,128]{1,0:T(8,128)S(1)} %get-tuple-element.51), channel_id=1, source_target_pairs={{128,130},{130,128},{194,196},{196,194},{132,134},{134,132},{198,2... | collective-permute-start | bytes 12296 | tf_op jit(solution)/shard_map/ppermute | solution.py:516
  61.7 0.0 collective-permute-done.9.side_a
  61.7 1.0 collective-permute-done.10.side_b
  62.6 1.2 %shard_map.154 = (f32[8,256]{1,0:T(8,128)S(1)}, f32[8,128]{1,0:T(8,128)S(1)}, f32[8,128]{1,0:T(8,128)S(1)}) custom-call(f32[8,128]{1,0:T(8,128)S(1)} %collective-permute-done.9.side_a, f32[8,128]{1,0:T(8,128)S(1)} %collective-permute-done.10.side_b, f32[48,256]{1,0:T(8,128)S(1)} %collective-permute-done.pack, f32[512,256]{1,0:T(8,128)S(1)} %get-tuple-element.36.w3, ...), custom_call_target="tpu_custom_call" | custom-call | tf_op jit(solution)/shard_map/pallas_call | solution.py:27
  63.8 1.9 %collective-permute-start.11 = (f32[8,128]{1,0:T(8,128)S(1)}, f32[8,128]{1,0:T(8,128)S(1)}, u32[]{:S(2)}, u32[]{:S(2)}) collective-permute-start(f32[8,128]{1,0:T(8,128)S(1)} %get-tuple-element.53), channel_id=1, source_target_pairs={{192,128},{128,192},{130,194},{194,130},{196,132},{132,196},{134,1... | collective-permute-start | bytes 12296 | tf_op jit(solution)/shard_map/ppermute | solution.py:516
  65.7 4.8 %collective-permute-start.12 = (f32[8,128]{1,0:T(8,128)S(1)}, f32[8,128]{1,0:T(8,128)S(1)}, u32[]{:S(2)}, u32[]{:S(2)}) collective-permute-start(f32[8,128]{1,0:T(8,128)S(1)} %get-tuple-element.54), channel_id=1, source_target_pairs={{128,130},{130,128},{194,196},{196,194},{132,134},{134,132},{198,2... | collective-permute-start | bytes 12296 | tf_op jit(solution)/shard_map/ppermute | solution.py:516
  70.5 0.0 collective-permute-done.11.side_a
  70.5 1.0 collective-permute-done.12.side_b
  71.5 3.2 %shard_map.155 = (f32[3,256]{1,0:T(4,128)S(1)}, f32[384,2,128]{2,1,0:T(2,128)}) custom-call(f32[4,4,128]{2,1,0:T(4,128)S(1)} %get-tuple-element.41.near, f32[48,256]{1,0:T(8,128)S(1)} %collective-permute-done.pack, f32[8,256]{1,0:T(8,128)S(1)} %get-tuple-element.48.charge, f32[8,256]{1,0:T(8,128)S(1)} %get-tuple-element.49.outside_row, ...), custom_call_target="tpu_custom_call" | custom-call | tf_op jit(solution)/shard_map/pallas_call | solution.py:27
  74.7 14.7 %all-to-all-start.1 = ((f32[384,2,128]{2,1,0:T(2,128)}), f32[384,2,128]{2,1,0:T(2,128)S(1)}, u32[]{:S(2)}, u32[]{:S(2)}) async-start(f32[384,2,128]{2,1,0:T(2,128)} %get-tuple-element.57), calls=%async_computation.1 | async-start | bytes 786432 | tf_op jit(solution)/shard_map/all_to_all | solution.py:582
  89.5 4.0 %collective-permute-start.13 = (f32[3,256]{1,0:T(4,128)S(1)}, f32[3,256]{1,0:T(4,128)S(1)}, u32[]{:S(2)}, u32[]{:S(2)}) collective-permute-start(f32[3,256]{1,0:T(4,128)S(1)} %get-tuple-element.56), channel_id=1, source_target_pairs={{64,0},{0,1},{2,2},{66,3},{68,4},{4,5},{6,6},{70,7},{78,8},{14,9},... | collective-permute-start | bytes 9224 | tf_op jit(solution)/shard_map/ppermute | solution.py:516
  93.4 9.4 %all-to-all-done.1 = f32[384,2,128]{2,1,0:T(2,128)S(1)} async-done(((f32[384,2,128]{2,1,0:T(2,128)}), f32[384,2,128]{2,1,0:T(2,128)S(1)}, u32[]{:S(2)}, u32[]{:S(2)}) %all-to-all-start.1) | async-done | bytes 393248 | tf_op jit(solution)/shard_map/all_to_all | solution.py:582
  102.8 0.2 shard_map.156
  103.0 6.1 %collective-permute-start.14 = (f32[3,256]{1,0:T(4,128)S(1)}, f32[3,256]{1,0:T(4,128)S(1)}, u32[]{:S(2)}, u32[]{:S(2)}) collective-permute-start(f32[3,256]{1,0:T(4,128)S(1)} %shard_map.156), channel_id=1, source_target_pairs={{0,128},{128,0},{1,129},{129,1},{2,130},{130,2},{3,131},{131,3},{4... | collective-permute-start | bytes 9224 | tf_op jit(solution)/shard_map/ppermute | solution.py:585
  109.1 0.0 collective-permute-done.13.result
  109.1 0.8 collective-permute-done.14.share
  109.9 0.6 shard_map.157
  (1 shorter events, 0.0 us)
Async XLA Ops:
  1.7 4.2 %collective-permute-start.6 = (f32[2,4,128]{2,1,0:T(4,128)S(1)}, f32[2,4,128]{2,1,0:T(4,128)S(1)}, u32[]{:S(2)}, u32[]{:S(2)}) collective-permute-start(f32[2,4,128]{2,1,0:T(4,128)S(1)} %get-tuple-element.40), channel_id=1, source_target_pairs={{0,128},{128,0},{1,129},{129,1},{2,130},{130,2},{3,131},{131,3},{4... | collective-permute-start | bytes 12296 | tf_op jit(solution)/shard_map/ppermute | solution.py:534
  6.7 38.2 %all-to-all-start = ((f32[128,2,4,128]{3,2,1,0:T(4,128)}), f32[128,2,4,128]{3,2,1,0:T(4,128)S(1)}, u32[]{:S(2)}, u32[]{:S(2)}) async-start(f32[128,2,4,128]{3,2,1,0:T(4,128)} %broadcast_in_dim.17), calls=%async_computation | async-start | bytes 1048576 | tf_op jit(solution)/shard_map/all_to_all | solution.py:536
  20.5 14.1 %collective-permute-start.3 = (bf16[256,256]{1,0:T(8,128)(2,1)}, bf16[256,256]{1,0:T(8,128)(2,1)S(1)}, u32[]{:S(2)}, u32[]{:S(2)}) collective-permute-start(bf16[256,256]{1,0:T(8,128)(2,1)} %param.17), channel_id=1, source_target_pairs={{0,64},{1,0},{2,2},{3,66},{4,68},{5,4},{6,6},{7,70},{8,78},{9,14},... | collective-permute-start | bytes 393224 | tf_op jit(solution)/shard_map/ppermute | solution.py:516
  21.1 13.4 %collective-permute-start = (f32[48,256]{1,0:T(8,128)S(1)}, f32[48,256]{1,0:T(8,128)S(1)}, u32[]{:S(2)}, u32[]{:S(2)}) collective-permute-start(f32[48,256]{1,0:T(8,128)S(1)} %get-tuple-element.30), channel_id=1, source_target_pairs={{0,64},{1,0},{2,2},{3,66},{4,68},{5,4},{6,6},{7,70},{8,78},{9,14},... | collective-permute-start | bytes 147464 | tf_op jit(solution)/shard_map/ppermute | solution.py:516
  23.9 2.0 %collective-permute-start.1 = (f32[8,128]{1,0:T(8,128)S(1)}, f32[8,128]{1,0:T(8,128)S(1)}, u32[]{:S(2)}, u32[]{:S(2)}) collective-permute-start(f32[8,128]{1,0:T(8,128)S(1)} %get-tuple-element.31), channel_id=1, source_target_pairs={{0,0},{1,64},{2,66},{3,2},{4,4},{5,68},{6,70},{7,6},{8,14},{9,78},... | collective-permute-start | bytes 12296 | tf_op jit(solution)/shard_map/ppermute | solution.py:516
  24.6 9.9 %collective-permute-start.2 = (f32[8,128]{1,0:T(8,128)S(1)}, f32[8,128]{1,0:T(8,128)S(1)}, u32[]{:S(2)}, u32[]{:S(2)}) collective-permute-start(f32[8,128]{1,0:T(8,128)S(1)} %get-tuple-element.32), channel_id=1, source_target_pairs={{1,2},{2,0},{3,68},{4,66},{5,6},{6,4},{7,78},{8,70},{9,12},{10,14}... | collective-permute-start | bytes 12296 | tf_op jit(solution)/shard_map/ppermute | solution.py:516
  37.3 5.9 %collective-permute-start.4 = (bf16[256,128]{1,0:T(8,128)(2,1)S(1)}, bf16[256,128]{1,0:T(8,128)(2,1)S(1)}, u32[]{:S(2)}, u32[]{:S(2)}) collective-permute-start(bf16[256,128]{1,0:T(8,128)(2,1)S(1)} %get-tuple-element.34), channel_id=1, source_target_pairs={{64,0},{0,64},{2,66},{66,2},{68,4},{4,68},{6,70},{70,6},{78,14},{1... | collective-permute-start | bytes 196616 | tf_op jit(solution)/shard_map/ppermute | solution.py:516
  39.8 5.0 %collective-permute-start.5 = (bf16[256,128]{1,0:T(8,128)(2,1)S(1)}, bf16[256,128]{1,0:T(8,128)(2,1)S(1)}, u32[]{:S(2)}, u32[]{:S(2)}) collective-permute-start(bf16[256,128]{1,0:T(8,128)(2,1)S(1)} %get-tuple-element.35), channel_id=1, source_target_pairs={{0,2},{2,0},{66,68},{68,66},{4,6},{6,4},{70,78},{78,70},{14,12},{1... | collective-permute-start | bytes 196616 | tf_op jit(solution)/shard_map/ppermute | solution.py:516
  48.7 4.8 %collective-permute-start.7 = (bf16[256,128]{1,0:T(8,128)(2,1)S(1)}, bf16[256,128]{1,0:T(8,128)(2,1)S(1)}, u32[]{:S(2)}, u32[]{:S(2)}) collective-permute-start(bf16[256,128]{1,0:T(8,128)(2,1)S(1)} %get-tuple-element.44), channel_id=1, source_target_pairs={{64,0},{0,64},{2,66},{66,2},{68,4},{4,68},{6,70},{70,6},{78,14},{1... | collective-permute-start | bytes 196616 | tf_op jit(solution)/shard_map/ppermute | solution.py:516
  48.8 6.3 %collective-permute-start.8 = (bf16[256,128]{1,0:T(8,128)(2,1)S(1)}, bf16[256,128]{1,0:T(8,128)(2,1)S(1)}, u32[]{:S(2)}, u32[]{:S(2)}) collective-permute-start(bf16[256,128]{1,0:T(8,128)(2,1)S(1)} %get-tuple-element.45), channel_id=1, source_target_pairs={{0,2},{2,0},{66,68},{68,66},{4,6},{6,4},{70,78},{78,70},{14,12},{1... | collective-permute-start | bytes 196616 | tf_op jit(solution)/shard_map/ppermute | solution.py:516
  56.3 5.3 %collective-permute-start.9 = (f32[8,128]{1,0:T(8,128)S(1)}, f32[8,128]{1,0:T(8,128)S(1)}, u32[]{:S(2)}, u32[]{:S(2)}) collective-permute-start(f32[8,128]{1,0:T(8,128)S(1)} %get-tuple-element.50), channel_id=1, source_target_pairs={{192,128},{128,192},{130,194},{194,130},{196,132},{132,196},{134,1... | collective-permute-start | bytes 12296 | tf_op jit(solution)/shard_map/ppermute | solution.py:516
  58.3 4.4 %collective-permute-start.10 = (f32[8,128]{1,0:T(8,128)S(1)}, f32[8,128]{1,0:T(8,128)S(1)}, u32[]{:S(2)}, u32[]{:S(2)}) collective-permute-start(f32[8,128]{1,0:T(8,128)S(1)} %get-tuple-element.51), channel_id=1, source_target_pairs={{128,130},{130,128},{194,196},{196,194},{132,134},{134,132},{198,2... | collective-permute-start | bytes 12296 | tf_op jit(solution)/shard_map/ppermute | solution.py:516
  63.8 6.7 %collective-permute-start.11 = (f32[8,128]{1,0:T(8,128)S(1)}, f32[8,128]{1,0:T(8,128)S(1)}, u32[]{:S(2)}, u32[]{:S(2)}) collective-permute-start(f32[8,128]{1,0:T(8,128)S(1)} %get-tuple-element.53), channel_id=1, source_target_pairs={{192,128},{128,192},{130,194},{194,130},{196,132},{132,196},{134,1... | collective-permute-start | bytes 12296 | tf_op jit(solution)/shard_map/ppermute | solution.py:516
  65.7 5.8 %collective-permute-start.12 = (f32[8,128]{1,0:T(8,128)S(1)}, f32[8,128]{1,0:T(8,128)S(1)}, u32[]{:S(2)}, u32[]{:S(2)}) collective-permute-start(f32[8,128]{1,0:T(8,128)S(1)} %get-tuple-element.54), channel_id=1, source_target_pairs={{128,130},{130,128},{194,196},{196,194},{132,134},{134,132},{198,2... | collective-permute-start | bytes 12296 | tf_op jit(solution)/shard_map/ppermute | solution.py:516
  74.7 28.1 %all-to-all-start.1 = ((f32[384,2,128]{2,1,0:T(2,128)}), f32[384,2,128]{2,1,0:T(2,128)S(1)}, u32[]{:S(2)}, u32[]{:S(2)}) async-start(f32[384,2,128]{2,1,0:T(2,128)} %get-tuple-element.57), calls=%async_computation.1 | async-start | bytes 786432 | tf_op jit(solution)/shard_map/all_to_all | solution.py:582
  89.5 19.6 %collective-permute-start.13 = (f32[3,256]{1,0:T(4,128)S(1)}, f32[3,256]{1,0:T(4,128)S(1)}, u32[]{:S(2)}, u32[]{:S(2)}) collective-permute-start(f32[3,256]{1,0:T(4,128)S(1)} %get-tuple-element.56), channel_id=1, source_target_pairs={{64,0},{0,1},{2,2},{66,3},{68,4},{4,5},{6,6},{70,7},{78,8},{14,9},... | collective-permute-start | bytes 9224 | tf_op jit(solution)/shard_map/ppermute | solution.py:516
  103.0 6.9 %collective-permute-start.14 = (f32[3,256]{1,0:T(4,128)S(1)}, f32[3,256]{1,0:T(4,128)S(1)}, u32[]{:S(2)}, u32[]{:S(2)}) collective-permute-start(f32[3,256]{1,0:T(4,128)S(1)} %shard_map.156), channel_id=1, source_target_pairs={{0,128},{128,0},{1,129},{129,1},{2,130},{130,2},{3,131},{131,3},{4... | collective-permute-start | bytes 9224 | tf_op jit(solution)/shard_map/ppermute | solution.py:585

commit v9 on v8

--- a/solution.py
+++ b/solution.py
@@ -19,7 +19,7 @@
 FIELD_CHUNK, FIELD_UNROLL = 32, 4
 TERM_CHUNK, TERM_UNROLL = 64, 4
 STATIC_CHUNK = 32
-RADIAL_SLOTS = 16
+RADIAL_SLOTS = 8
 MESSAGE_SLOTS = 16
 
 
@@ -208,6 +208,10 @@
 
         second_w, third_w = both(0), both(1)
 
+        def part_out(k):
+            part = pl.ds(pl.multiple_of(k * step, step), step)
+            return pltpu.make_async_copy(third.at[:, part], third_far.at[:, part], done.at[2 + k])
+
         def some_slots(k, carry):
             found = join3(dot(pieces, one_hot(slot_row(slots, k * RADIAL_SLOTS, RADIAL_SLOTS), depth)))
             offset = here - found
@@ -219,10 +223,12 @@
             hidden = silu(dot(second_w, hidden)).astype(BF16)
             start = pl.multiple_of(k * step, step)
             third[:, pl.ds(start, step)] = silu(dot(third_w, hidden)).astype(BF16)
+            part_out(k).start()
             return carry
 
         lax.fori_loop(0, slot_count // RADIAL_SLOTS, some_slots, 0)
-        fetch(((third, third_far),), done, 2)()
+        for k in range(slot_count // RADIAL_SLOTS):
+            part_out(k).wait()
 
 
 def lend_pieces(values, picks, lent_a, lent_b):
@@ -532,11 +538,12 @@
          pltpu.VMEM((slot_count, width), ints), pltpu.VMEM((2, half), ints), pltpu.SMEM((listed,), ints)], 6,
     )
     partner = lax.ppermute(mine, "grp", [(0, 1), (1, 0)])
+    features = move(features, itself, same, place, (0,))
     copies = jnp.broadcast_to(partner[None], (members,) + partner.shape)
+    copies, features = lax.optimization_barrier((copies, features))
     near = lax.all_to_all(copies, DOM, 0, 0, tiled=True).reshape(2 * members, 4, half)
     pack = move(pack, itself, same, place)
     rim_a, rim_b = trade(lent_a, lent_b, source=same)
-    features = move(features, itself, same, place, (0,))
     feat_t, w3, w5, fixed, entry, lent_a, lent_b = call(
         static_kernel, [by_site, ((depth, width), F32), ((depth, width), F32), row8, ((depth, 8), F32), wide, wide],
         (pack, rim_a, rim_b), (features,), [pltpu.VMEM((width, channels), BF16)], 1, loose=1,
@@ -545,7 +552,8 @@
     third_shape = (LAYERS * radial_in.shape[2], slot_count * width)
     (third,) = call(
         radial_kernel, [(third_shape, BF16)], (pack, rim_a, rim_b), (radial_in, radial_mid),
-        [pltpu.VMEM(radial_in.shape, BF16), pltpu.VMEM(radial_mid.shape, BF16), pltpu.VMEM(third_shape, BF16)], 3, 1,
+        [pltpu.VMEM(radial_in.shape, BF16), pltpu.VMEM(radial_mid.shape, BF16), pltpu.VMEM(third_shape, BF16)],
+        2 + slot_count // RADIAL_SLOTS, 1,
     )
     moment = pltpu.VMEM((depth, 8), F32)
     total = pltpu.VMEM((channels, width), F32)

time: 111 us -> 114 us (1.027)
  starting transfers between devices: 69.9 us -> 72.9 us
    ppermute x1, starting transfers between devices: 6.08 us -> 7.76 us  [local(): share = lax.ppermute(share, 'grp', [(0, 1), (1, 0)])]
    ppermute x1, starting transfers between devices: 3.33 us -> 4.58 us  [local(): partner = lax.ppermute(mine, 'grp', [(0, 1), (1, 0)])]
where the time goes in v9:
time: 114 us
  starting transfers between devices  72.9 us (64%)
  waiting for transfers between devices  24.8 us (22%)
  Pallas kernels  14.1 us (12%)
    ppermute x13, starting transfers between devices, move(): lax.ppermute(value, EVERY, [(source[a] + g * members, target[b] + g * mem...  32.1 us
    all_to_all x1, starting transfers between devices, local(): lax.all_to_all(spread, DOM, 0, 0, tiled=True).reshape(members, 3, 2, half)  14.3 us
    all_to_all x1, starting transfers between devices, local(): lax.all_to_all(copies, DOM, 0, 0, tiled=True).reshape(2 * members, 4, half)  14.1 us
    pallas_call x9, Pallas kernels, call(): pl.pallas_call(body, out_shape=[jax.ShapeDtypeStruct(s, d) for s, d in ou...  14.1 us
    ppermute x13, waiting for transfers between devices, move(): lax.ppermute(value, EVERY, [(source[a] + g * members, target[b] + g * mem...  13.8 us
    all_to_all x1, waiting for transfers between devices, local(): lax.all_to_all(spread, DOM, 0, 0, tiled=True).reshape(members, 3, 2, half)  9.34 us
    ppermute x1, starting transfers between devices, local(): share = lax.ppermute(share, 'grp', [(0, 1), (1, 0)])  7.76 us
    ppermute x1, starting transfers between devices, local(): partner = lax.ppermute(mine, 'grp', [(0, 1), (1, 0)])  4.58 us
  transfers between devices with their start and end apart: 17, of which 8 were waited for; matrix products, arithmetic and copies ran while one was open for 0% of the time, Pallas kernels for 3%

profile of v9, /device:TPU:1, one launch (start us, length us, event | category | flops | bytes accessed | tf_op | source)
XLA Modules:
  0.0 113.7 jit_solution(14771918583868216414)
XLA Ops:
  0.6 0.7 collective-permute-start.4
  1.3 1.0 shard_map.149
  2.3 4.6 %collective-permute-start.3 = (f32[2,4,128]{2,1,0:T(4,128)S(1)}, f32[2,4,128]{2,1,0:T(4,128)S(1)}, u32[]{:S(2)}, u32[]{:S(2)}) collective-permute-start(f32[2,4,128]{2,1,0:T(4,128)S(1)} %get-tuple-element.35), channel_id=1, source_target_pairs={{0,128},{128,0},{1,129},{129,1},{2,130},{130,2},{3,131},{131,3},{4... | collective-permute-start | bytes 12296 | tf_op jit(solution)/shard_map/ppermute | solution.py:540
  6.9 0.8 collective-permute-done.3
  7.7 0.0 collective-permute-done.4.features_far
  7.8 0.9 broadcast_in_dim.17
  8.6 14.1 %all-to-all-start = ((f32[128,2,4,128]{3,2,1,0:T(4,128)}), f32[128,2,4,128]{3,2,1,0:T(4,128)S(1)}, u32[]{:S(2)}, u32[]{:S(2)}) async-start(f32[128,2,4,128]{3,2,1,0:T(4,128)} %broadcast_in_dim.17), calls=%async_computation | async-start | bytes 1048576 | tf_op jit(solution)/shard_map/all_to_all | solution.py:544
  22.7 2.8 %collective-permute-start = (f32[48,256]{1,0:T(8,128)S(1)}, f32[48,256]{1,0:T(8,128)S(1)}, u32[]{:S(2)}, u32[]{:S(2)}) collective-permute-start(f32[48,256]{1,0:T(8,128)S(1)} %get-tuple-element.32), channel_id=1, source_target_pairs={{0,64},{1,0},{2,2},{3,66},{4,68},{5,4},{6,6},{7,70},{8,78},{9,14},... | collective-permute-start | bytes 147464 | tf_op jit(solution)/shard_map/ppermute | solution.py:522
  25.5 0.7 collective-permute-start.1
  26.2 1.3 %collective-permute-start.2 = (f32[8,128]{1,0:T(8,128)S(1)}, f32[8,128]{1,0:T(8,128)S(1)}, u32[]{:S(2)}, u32[]{:S(2)}) collective-permute-start(f32[8,128]{1,0:T(8,128)S(1)} %get-tuple-element.34), channel_id=1, source_target_pairs={{1,2},{2,0},{3,68},{4,66},{5,6},{6,4},{7,78},{8,70},{9,12},{10,14}... | collective-permute-start | bytes 12296 | tf_op jit(solution)/shard_map/ppermute | solution.py:522
  27.5 0.0 collective-permute-done.1.rim_a
  27.5 8.6 %collective-permute-done.2.rim_b = f32[8,128]{1,0:T(8,128)S(1)} collective-permute-done((f32[8,128]{1,0:T(8,128)S(1)}, f32[8,128]{1,0:T(8,128)S(1)}, u32[]{:S(2)}, u32[]{:S(2)}) %collective-permute-start.2) | collective-permute-done | bytes 4128 | tf_op jit(solution)/shard_map/ppermute | solution.py:522
  36.2 0.0 collective-permute-done.pack
  36.2 2.7 %shard_map.150 = (bf16[256,256]{1,0:T(8,128)(2,1)S(1)}, f32[512,256]{1,0:T(8,128)S(1)}, f32[512,256]{1,0:T(8,128)S(1)}, f32[8,256]{1,0:T(8,128)S(1)}, f32[512,8]...) custom-call(f32[48,256]{1,0:T(8,128)S(1)} %collective-permute-done.pack, ...), custom_call_target="tpu_custom_call" | custom-call | tf_op jit(solution)/shard_map/pallas_call | solution.py:27
  38.9 2.6 %collective-permute-start.5 = (bf16[256,128]{1,0:T(8,128)(2,1)S(1)}, bf16[256,128]{1,0:T(8,128)(2,1)S(1)}, u32[]{:S(2)}, u32[]{:S(2)}) collective-permute-start(bf16[256,128]{1,0:T(8,128)(2,1)S(1)} %get-tuple-element.38), channel_id=1, source_target_pairs={{64,0},{0,64},{2,66},{66,2},{68,4},{4,68},{6,70},{70,6},{78,14},{1... | collective-permute-start | bytes 196616 | tf_op jit(solution)/shard_map/ppermute | solution.py:522
  41.4 3.3 %collective-permute-start.6 = (bf16[256,128]{1,0:T(8,128)(2,1)S(1)}, bf16[256,128]{1,0:T(8,128)(2,1)S(1)}, u32[]{:S(2)}, u32[]{:S(2)}) collective-permute-start(bf16[256,128]{1,0:T(8,128)(2,1)S(1)} %get-tuple-element.39), channel_id=1, source_target_pairs={{0,2},{2,0},{66,68},{68,66},{4,6},{6,4},{70,78},{78,70},{14,12},{1... | collective-permute-start | bytes 196616 | tf_op jit(solution)/shard_map/ppermute | solution.py:522
  44.7 0.1 shard_map.151.third_far
  44.8 0.0 collective-permute-done.5.side_a
  44.8 1.6 %collective-permute-done.6.side_b = bf16[256,128]{1,0:T(8,128)(2,1)S(1)} collective-permute-done((bf16[256,128]{1,0:T(8,128)(2,1)S(1)}, bf16[256,128]{1,0:T(8,128)(2,1)S(1)}, u32[]{:S(2)}, u32[]{:S(2)}) %collective-permute-start.6) | collective-permute-done | bytes 65568 | tf_op jit(solution)/shard_map/ppermute | solution.py:522
  46.4 0.0 all-to-all-done
  46.4 3.8 %shard_map.152 = (f32[8,256]{1,0:T(8,128)S(1)}, f32[4,4,128]{2,1,0:T(4,128)S(1)}, bf16[256,256]{1,0:T(8,128)(2,1)S(1)}, bf16[256,256]{1,0:T(8,128)(2,1)S(1)}, f3...) custom-call(f32[48,256]{1,0:T(8,128)S(1)} %collective-permute-done.pack,, ...), custom_call_target="tpu_custom_call" | custom-call | tf_op jit(solution)/shard_map/pallas_call | solution.py:27
  50.3 0.1 collective-permute-start.7
  50.4 4.8 %collective-permute-start.8 = (bf16[256,128]{1,0:T(8,128)(2,1)S(1)}, bf16[256,128]{1,0:T(8,128)(2,1)S(1)}, u32[]{:S(2)}, u32[]{:S(2)}) collective-permute-start(bf16[256,128]{1,0:T(8,128)(2,1)S(1)} %get-tuple-element.49), channel_id=1, source_target_pairs={{0,2},{2,0},{66,68},{68,66},{4,6},{6,4},{70,78},{78,70},{14,12},{1... | collective-permute-start | bytes 196616 | tf_op jit(solution)/shard_map/ppermute | solution.py:522
  55.2 0.0 collective-permute-done.7.side_a
  55.2 1.6 %collective-permute-done.8.side_b = bf16[256,128]{1,0:T(8,128)(2,1)S(1)} collective-permute-done((bf16[256,128]{1,0:T(8,128)(2,1)S(1)}, bf16[256,128]{1,0:T(8,128)(2,1)S(1)}, u32[]{:S(2)}, u32[]{:S(2)}) %collective-permute-start.8) | collective-permute-done | bytes 65568 | tf_op jit(solution)/shard_map/ppermute | solution.py:522
  56.8 1.2 %shard_map.153 = (f32[8,256]{1,0:T(8,128)S(1)}, f32[8,256]{1,0:T(8,128)S(1)}, f32[8,128]{1,0:T(8,128)S(1)}, f32[8,128]{1,0:T(8,128)S(1)}) custom-call(bf16[256,256]{1,0:T(8,128)(2,1)S(1)} %get-tuple-element.46.hidden, bf16[256,256]{1,0:T(8,128)(2,1)S(1)} %get-tuple-element.47.lifted, bf16[256,128]{1,0:T(8,128)(2,1)S(1)} %collective-permute-done.7.side_a, ...), custom_call_target="tpu_custom_call" | custom-call | tf_op jit(solution)/shard_map/pallas_call | solution.py:27
  58.0 1.9 %collective-permute-start.9 = (f32[8,128]{1,0:T(8,128)S(1)}, f32[8,128]{1,0:T(8,128)S(1)}, u32[]{:S(2)}, u32[]{:S(2)}) collective-permute-start(f32[8,128]{1,0:T(8,128)S(1)} %get-tuple-element.54), channel_id=1, source_target_pairs={{192,128},{128,192},{130,194},{194,130},{196,132},{132,196},{134,1... | collective-permute-start | bytes 12296 | tf_op jit(solution)/shard_map/ppermute | solution.py:522
  59.9 3.4 %collective-permute-start.10 = (f32[8,128]{1,0:T(8,128)S(1)}, f32[8,128]{1,0:T(8,128)S(1)}, u32[]{:S(2)}, u32[]{:S(2)}) collective-permute-start(f32[8,128]{1,0:T(8,128)S(1)} %get-tuple-element.55), channel_id=1, source_target_pairs={{128,130},{130,128},{194,196},{196,194},{132,134},{134,132},{198,2... | collective-permute-start | bytes 12296 | tf_op jit(solution)/shard_map/ppermute | solution.py:522
  63.3 0.0 collective-permute-done.9.side_a
  63.3 1.0 collective-permute-done.10.side_b
  64.3 1.2 %shard_map.154 = (f32[8,256]{1,0:T(8,128)S(1)}, f32[8,128]{1,0:T(8,128)S(1)}, f32[8,128]{1,0:T(8,128)S(1)}) custom-call(f32[8,128]{1,0:T(8,128)S(1)} %collective-permute-done.9.side_a, f32[8,128]{1,0:T(8,128)S(1)} %collective-permute-done.10.side_b, f32[48,256]{1,0:T(8,128)S(1)} %collective-permute-done.pack, f32[512,256]{1,0:T(8,128)S(1)} %get-tuple-element.40.w3, ...), custom_call_target="tpu_custom_call" | custom-call | tf_op jit(solution)/shard_map/pallas_call | solution.py:27
  65.5 1.9 %collective-permute-start.11 = (f32[8,128]{1,0:T(8,128)S(1)}, f32[8,128]{1,0:T(8,128)S(1)}, u32[]{:S(2)}, u32[]{:S(2)}) collective-permute-start(f32[8,128]{1,0:T(8,128)S(1)} %get-tuple-element.57), channel_id=1, source_target_pairs={{192,128},{128,192},{130,194},{194,130},{196,132},{132,196},{134,1... | collective-permute-start | bytes 12296 | tf_op jit(solution)/shard_map/ppermute | solution.py:522
  67.5 4.8 %collective-permute-start.12 = (f32[8,128]{1,0:T(8,128)S(1)}, f32[8,128]{1,0:T(8,128)S(1)}, u32[]{:S(2)}, u32[]{:S(2)}) collective-permute-start(f32[8,128]{1,0:T(8,128)S(1)} %get-tuple-element.58), channel_id=1, source_target_pairs={{128,130},{130,128},{194,196},{196,194},{132,134},{134,132},{198,2... | collective-permute-start | bytes 12296 | tf_op jit(solution)/shard_map/ppermute | solution.py:522
  72.3 0.0 collective-permute-done.11.side_a
  72.3 1.0 collective-permute-done.12.side_b
  73.3 3.2 %shard_map.155 = (f32[3,256]{1,0:T(4,128)S(1)}, f32[384,2,128]{2,1,0:T(2,128)}) custom-call(f32[4,4,128]{2,1,0:T(4,128)S(1)} %get-tuple-element.45.near, f32[48,256]{1,0:T(8,128)S(1)} %collective-permute-done.pack, f32[8,256]{1,0:T(8,128)S(1)} %get-tuple-element.52.charge, f32[8,256]{1,0:T(8,128)S(1)} %get-tuple-element.53.outside_row, ...), custom_call_target="tpu_custom_call" | custom-call | tf_op jit(solution)/shard_map/pallas_call | solution.py:27
  76.5 14.3 %all-to-all-start.1 = ((f32[384,2,128]{2,1,0:T(2,128)}), f32[384,2,128]{2,1,0:T(2,128)S(1)}, u32[]{:S(2)}, u32[]{:S(2)}) async-start(f32[384,2,128]{2,1,0:T(2,128)} %get-tuple-element.61), calls=%async_computation.1 | async-start | bytes 786432 | tf_op jit(solution)/shard_map/all_to_all | solution.py:590
  90.8 4.0 %collective-permute-start.13 = (f32[3,256]{1,0:T(4,128)S(1)}, f32[3,256]{1,0:T(4,128)S(1)}, u32[]{:S(2)}, u32[]{:S(2)}) collective-permute-start(f32[3,256]{1,0:T(4,128)S(1)} %get-tuple-element.60), channel_id=1, source_target_pairs={{64,0},{0,1},{2,2},{66,3},{68,4},{4,5},{6,6},{70,7},{78,8},{14,9},... | collective-permute-start | bytes 9224 | tf_op jit(solution)/shard_map/ppermute | solution.py:522
  94.8 9.3 %all-to-all-done.1 = f32[384,2,128]{2,1,0:T(2,128)S(1)} async-done(((f32[384,2,128]{2,1,0:T(2,128)}), f32[384,2,128]{2,1,0:T(2,128)S(1)}, u32[]{:S(2)}, u32[]{:S(2)}) %all-to-all-start.1) | async-done | bytes 393248 | tf_op jit(solution)/shard_map/all_to_all | solution.py:590
  104.2 0.2 shard_map.156
  104.3 7.8 %collective-permute-start.14 = (f32[3,256]{1,0:T(4,128)S(1)}, f32[3,256]{1,0:T(4,128)S(1)}, u32[]{:S(2)}, u32[]{:S(2)}) collective-permute-start(f32[3,256]{1,0:T(4,128)S(1)} %shard_map.156), channel_id=1, source_target_pairs={{0,128},{128,0},{1,129},{129,1},{2,130},{130,2},{3,131},{131,3},{4... | collective-permute-start | bytes 9224 | tf_op jit(solution)/shard_map/ppermute | solution.py:593
  112.1 0.0 collective-permute-done.13.result
  112.1 0.8 collective-permute-done.14.share
  112.9 0.6 shard_map.157
Async XLA Ops:
  0.6 7.1 %collective-permute-start.4 = (bf16[256,256]{1,0:T(8,128)(2,1)}, bf16[256,256]{1,0:T(8,128)(2,1)S(1)}, u32[]{:S(2)}, u32[]{:S(2)}) collective-permute-start(bf16[256,256]{1,0:T(8,128)(2,1)} %param.17), channel_id=1, source_target_pairs={{0,64},{1,0},{2,2},{3,66},{4,68},{5,4},{6,6},{7,70},{8,78},{9,14},... | collective-permute-start | bytes 393224 | tf_op jit(solution)/shard_map/ppermute | solution.py:522
  2.3 5.4 %collective-permute-start.3 = (f32[2,4,128]{2,1,0:T(4,128)S(1)}, f32[2,4,128]{2,1,0:T(4,128)S(1)}, u32[]{:S(2)}, u32[]{:S(2)}) collective-permute-start(f32[2,4,128]{2,1,0:T(4,128)S(1)} %get-tuple-element.35), channel_id=1, source_target_pairs={{0,128},{128,0},{1,129},{129,1},{2,130},{130,2},{3,131},{131,3},{4... | collective-permute-start | bytes 12296 | tf_op jit(solution)/shard_map/ppermute | solution.py:540
  8.6 37.8 %all-to-all-start = ((f32[128,2,4,128]{3,2,1,0:T(4,128)}), f32[128,2,4,128]{3,2,1,0:T(4,128)S(1)}, u32[]{:S(2)}, u32[]{:S(2)}) async-start(f32[128,2,4,128]{3,2,1,0:T(4,128)} %broadcast_in_dim.17), calls=%async_computation | async-start | bytes 1048576 | tf_op jit(solution)/shard_map/all_to_all | solution.py:544
  22.7 13.4 %collective-permute-start = (f32[48,256]{1,0:T(8,128)S(1)}, f32[48,256]{1,0:T(8,128)S(1)}, u32[]{:S(2)}, u32[]{:S(2)}) collective-permute-start(f32[48,256]{1,0:T(8,128)S(1)} %get-tuple-element.32), channel_id=1, source_target_pairs={{0,64},{1,0},{2,2},{3,66},{4,68},{5,4},{6,6},{7,70},{8,78},{9,14},... | collective-permute-start | bytes 147464 | tf_op jit(solution)/shard_map/ppermute | solution.py:522
  25.5 2.0 %collective-permute-start.1 = (f32[8,128]{1,0:T(8,128)S(1)}, f32[8,128]{1,0:T(8,128)S(1)}, u32[]{:S(2)}, u32[]{:S(2)}) collective-permute-start(f32[8,128]{1,0:T(8,128)S(1)} %get-tuple-element.33), channel_id=1, source_target_pairs={{0,0},{1,64},{2,66},{3,2},{4,4},{5,68},{6,70},{7,6},{8,14},{9,78},... | collective-permute-start | bytes 12296 | tf_op jit(solution)/shard_map/ppermute | solution.py:522
  26.2 9.9 %collective-permute-start.2 = (f32[8,128]{1,0:T(8,128)S(1)}, f32[8,128]{1,0:T(8,128)S(1)}, u32[]{:S(2)}, u32[]{:S(2)}) collective-permute-start(f32[8,128]{1,0:T(8,128)S(1)} %get-tuple-element.34), channel_id=1, source_target_pairs={{1,2},{2,0},{3,68},{4,66},{5,6},{6,4},{7,78},{8,70},{9,12},{10,14}... | collective-permute-start | bytes 12296 | tf_op jit(solution)/shard_map/ppermute | solution.py:522
  38.9 6.0 %collective-permute-start.5 = (bf16[256,128]{1,0:T(8,128)(2,1)S(1)}, bf16[256,128]{1,0:T(8,128)(2,1)S(1)}, u32[]{:S(2)}, u32[]{:S(2)}) collective-permute-start(bf16[256,128]{1,0:T(8,128)(2,1)S(1)} %get-tuple-element.38), channel_id=1, source_target_pairs={{64,0},{0,64},{2,66},{66,2},{68,4},{4,68},{6,70},{70,6},{78,14},{1... | collective-permute-start | bytes 196616 | tf_op jit(solution)/shard_map/ppermute | solution.py:522
  41.4 5.0 %collective-permute-start.6 = (bf16[256,128]{1,0:T(8,128)(2,1)S(1)}, bf16[256,128]{1,0:T(8,128)(2,1)S(1)}, u32[]{:S(2)}, u32[]{:S(2)}) collective-permute-start(bf16[256,128]{1,0:T(8,128)(2,1)S(1)} %get-tuple-element.39), channel_id=1, source_target_pairs={{0,2},{2,0},{66,68},{68,66},{4,6},{6,4},{70,78},{78,70},{14,12},{1... | collective-permute-start | bytes 196616 | tf_op jit(solution)/shard_map/ppermute | solution.py:522
  50.3 4.9 %collective-permute-start.7 = (bf16[256,128]{1,0:T(8,128)(2,1)S(1)}, bf16[256,128]{1,0:T(8,128)(2,1)S(1)}, u32[]{:S(2)}, u32[]{:S(2)}) collective-permute-start(bf16[256,128]{1,0:T(8,128)(2,1)S(1)} %get-tuple-element.48), channel_id=1, source_target_pairs={{64,0},{0,64},{2,66},{66,2},{68,4},{4,68},{6,70},{70,6},{78,14},{1... | collective-permute-start | bytes 196616 | tf_op jit(solution)/shard_map/ppermute | solution.py:522
  50.4 6.4 %collective-permute-start.8 = (bf16[256,128]{1,0:T(8,128)(2,1)S(1)}, bf16[256,128]{1,0:T(8,128)(2,1)S(1)}, u32[]{:S(2)}, u32[]{:S(2)}) collective-permute-start(bf16[256,128]{1,0:T(8,128)(2,1)S(1)} %get-tuple-element.49), channel_id=1, source_target_pairs={{0,2},{2,0},{66,68},{68,66},{4,6},{6,4},{70,78},{78,70},{14,12},{1... | collective-permute-start | bytes 196616 | tf_op jit(solution)/shard_map/ppermute | solution.py:522
  58.0 5.3 %collective-permute-start.9 = (f32[8,128]{1,0:T(8,128)S(1)}, f32[8,128]{1,0:T(8,128)S(1)}, u32[]{:S(2)}, u32[]{:S(2)}) collective-permute-start(f32[8,128]{1,0:T(8,128)S(1)} %get-tuple-element.54), channel_id=1, source_target_pairs={{192,128},{128,192},{130,194},{194,130},{196,132},{132,196},{134,1... | collective-permute-start | bytes 12296 | tf_op jit(solution)/shard_map/ppermute | solution.py:522
  59.9 4.4 %collective-permute-start.10 = (f32[8,128]{1,0:T(8,128)S(1)}, f32[8,128]{1,0:T(8,128)S(1)}, u32[]{:S(2)}, u32[]{:S(2)}) collective-permute-start(f32[8,128]{1,0:T(8,128)S(1)} %get-tuple-element.55), channel_id=1, source_target_pairs={{128,130},{130,128},{194,196},{196,194},{132,134},{134,132},{198,2... | collective-permute-start | bytes 12296 | tf_op jit(solution)/shard_map/ppermute | solution.py:522
  65.5 6.7 %collective-permute-start.11 = (f32[8,128]{1,0:T(8,128)S(1)}, f32[8,128]{1,0:T(8,128)S(1)}, u32[]{:S(2)}, u32[]{:S(2)}) collective-permute-start(f32[8,128]{1,0:T(8,128)S(1)} %get-tuple-element.57), channel_id=1, source_target_pairs={{192,128},{128,192},{130,194},{194,130},{196,132},{132,196},{134,1... | collective-permute-start | bytes 12296 | tf_op jit(solution)/shard_map/ppermute | solution.py:522
  67.5 5.8 %collective-permute-start.12 = (f32[8,128]{1,0:T(8,128)S(1)}, f32[8,128]{1,0:T(8,128)S(1)}, u32[]{:S(2)}, u32[]{:S(2)}) collective-permute-start(f32[8,128]{1,0:T(8,128)S(1)} %get-tuple-element.58), channel_id=1, source_target_pairs={{128,130},{130,128},{194,196},{196,194},{132,134},{134,132},{198,2... | collective-permute-start | bytes 12296 | tf_op jit(solution)/shard_map/ppermute | solution.py:522
  76.5 27.7 %all-to-all-start.1 = ((f32[384,2,128]{2,1,0:T(2,128)}), f32[384,2,128]{2,1,0:T(2,128)S(1)}, u32[]{:S(2)}, u32[]{:S(2)}) async-start(f32[384,2,128]{2,1,0:T(2,128)} %get-tuple-element.61), calls=%async_computation.1 | async-start | bytes 786432 | tf_op jit(solution)/shard_map/all_to_all | solution.py:590
  90.8 21.3 %collective-permute-start.13 = (f32[3,256]{1,0:T(4,128)S(1)}, f32[3,256]{1,0:T(4,128)S(1)}, u32[]{:S(2)}, u32[]{:S(2)}) collective-permute-start(f32[3,256]{1,0:T(4,128)S(1)} %get-tuple-element.60), channel_id=1, source_target_pairs={{64,0},{0,1},{2,2},{66,3},{68,4},{4,5},{6,6},{70,7},{78,8},{14,9},... | collective-permute-start | bytes 9224 | tf_op jit(solution)/shard_map/ppermute | solution.py:522
  104.3 8.6 %collective-permute-start.14 = (f32[3,256]{1,0:T(4,128)S(1)}, f32[3,256]{1,0:T(4,128)S(1)}, u32[]{:S(2)}, u32[]{:S(2)}) collective-permute-start(f32[3,256]{1,0:T(4,128)S(1)} %shard_map.156), channel_id=1, source_target_pairs={{0,128},{128,0},{1,129},{129,1},{2,130},{130,2},{3,131},{131,3},{4... | collective-permute-start | bytes 9224 | tf_op jit(solution)/shard_map/ppermute | solution.py:593

commit v10 on v9

--- a/solution.py
+++ b/solution.py
@@ -20,7 +20,7 @@
 TERM_CHUNK, TERM_UNROLL = 64, 4
 STATIC_CHUNK = 32
 RADIAL_SLOTS = 8
-MESSAGE_SLOTS = 16
+MESSAGE_SLOTS = 8
 
 
 def call(body, outs, held, far=(), scratch=(), copies=0, far_outs=0, loose=0):
@@ -538,12 +538,12 @@
          pltpu.VMEM((slot_count, width), ints), pltpu.VMEM((2, half), ints), pltpu.SMEM((listed,), ints)], 6,
     )
     partner = lax.ppermute(mine, "grp", [(0, 1), (1, 0)])
-    features = move(features, itself, same, place, (0,))
     copies = jnp.broadcast_to(partner[None], (members,) + partner.shape)
-    copies, features = lax.optimization_barrier((copies, features))
     near = lax.all_to_all(copies, DOM, 0, 0, tiled=True).reshape(2 * members, 4, half)
     pack = move(pack, itself, same, place)
     rim_a, rim_b = trade(lent_a, lent_b, source=same)
+    features, pack, rim_a, rim_b = lax.optimization_barrier((features, pack, rim_a, rim_b))
+    features = move(features, itself, same, place, (0,))
     feat_t, w3, w5, fixed, entry, lent_a, lent_b = call(
         static_kernel, [by_site, ((depth, width), F32), ((depth, width), F32), row8, ((depth, 8), F32), wide, wide],
         (pack, rim_a, rim_b), (features,), [pltpu.VMEM((width, channels), BF16)], 1, loose=1,

time: 114 us -> 116 us (1.018)
  starting transfers between devices: 72.9 us -> 74.6 us
    ppermute x1, starting transfers between devices: 7.76 us -> 10.7 us  [local(): share = lax.ppermute(share, 'grp', [(0, 1), (1, 0)])]
    ppermute x1, starting transfers between devices: 4.58 us -> 3.33 us  [local(): partner = lax.ppermute(mine, 'grp', [(0, 1), (1, 0)])]
where the time goes in v10:
time: 116 us
  starting transfers between devices  74.6 us (64%)
  waiting for transfers between devices  25.1 us (22%)
  Pallas kernels  14.2 us (12%)
    ppermute x13, starting transfers between devices, move(): lax.ppermute(value, EVERY, [(source[a] + g * members, target[b] + g * mem...  31.7 us
    all_to_all x1, starting transfers between devices, local(): lax.all_to_all(spread, DOM, 0, 0, tiled=True).reshape(members, 3, 2, half)  15 us
    pallas_call x9, Pallas kernels, call(): pl.pallas_call(body, out_shape=[jax.ShapeDtypeStruct(s, d) for s, d in ou...  14.2 us
    ppermute x13, waiting for transfers between devices, move(): lax.ppermute(value, EVERY, [(source[a] + g * members, target[b] + g * mem...  14.2 us
    all_to_all x1, starting transfers between devices, local(): lax.all_to_all(copies, DOM, 0, 0, tiled=True).reshape(2 * members, 4, half)  13.8 us
    ppermute x1, starting transfers between devices, local(): share = lax.ppermute(share, 'grp', [(0, 1), (1, 0)])  10.7 us
    all_to_all x1, waiting for transfers between devices, local(): lax.all_to_all(spread, DOM, 0, 0, tiled=True).reshape(members, 3, 2, half)  9.34 us
    ppermute x1, starting transfers between devices, local(): partner = lax.ppermute(mine, 'grp', [(0, 1), (1, 0)])  3.33 us
  transfers between devices with their start and end apart: 17, of which 8 were waited for; matrix products, arithmetic and copies ran while one was open for 0% of the time, Pallas kernels for 3%

profile of v10, /device:TPU:1, one launch (start us, length us, event | category | flops | bytes accessed | tf_op | source)
XLA Modules:
  0.0 115.8 jit_solution(8767752798677570294)
XLA Ops:
  0.6 1.0 shard_map.149
  1.7 3.3 %collective-permute-start.6 = (f32[2,4,128]{2,1,0:T(4,128)S(1)}, f32[2,4,128]{2,1,0:T(4,128)S(1)}, u32[]{:S(2)}, u32[]{:S(2)}) collective-permute-start(f32[2,4,128]{2,1,0:T(4,128)S(1)} %get-tuple-element.48), channel_id=1, source_target_pairs={{0,128},{128,0},{1,129},{129,1},{2,130},{130,2},{3,131},{131,3},{4... | collective-permute-start | bytes 12296 | tf_op jit(solution)/shard_map/ppermute | solution.py:540
  5.0 0.8 collective-permute-done.6
  5.8 0.9 broadcast_in_dim.17
  6.7 13.8 %all-to-all-start = ((f32[128,2,4,128]{3,2,1,0:T(4,128)}), f32[128,2,4,128]{3,2,1,0:T(4,128)S(1)}, u32[]{:S(2)}, u32[]{:S(2)}) async-start(f32[128,2,4,128]{3,2,1,0:T(4,128)} %broadcast_in_dim.17), calls=%async_computation | async-start | bytes 1048576 | tf_op jit(solution)/shard_map/all_to_all | solution.py:542
  20.5 2.8 %collective-permute-start = (f32[48,256]{1,0:T(8,128)S(1)}, f32[48,256]{1,0:T(8,128)S(1)}, u32[]{:S(2)}, u32[]{:S(2)}) collective-permute-start(f32[48,256]{1,0:T(8,128)S(1)} %get-tuple-element.34), channel_id=1, source_target_pairs={{0,64},{1,0},{2,2},{3,66},{4,68},{5,4},{6,6},{7,70},{8,78},{9,14},... | collective-permute-start | bytes 147464 | tf_op jit(solution)/shard_map/ppermute | solution.py:522
  23.3 0.7 collective-permute-start.1
  23.9 1.3 %collective-permute-start.2 = (f32[8,128]{1,0:T(8,128)S(1)}, f32[8,128]{1,0:T(8,128)S(1)}, u32[]{:S(2)}, u32[]{:S(2)}) collective-permute-start(f32[8,128]{1,0:T(8,128)S(1)} %get-tuple-element.36), channel_id=1, source_target_pairs={{1,2},{2,0},{3,68},{4,66},{5,6},{6,4},{7,78},{8,70},{9,12},{10,14}... | collective-permute-start | bytes 12296 | tf_op jit(solution)/shard_map/ppermute | solution.py:522
  25.2 0.0 collective-permute-done.1.rim_a
  25.3 8.6 %collective-permute-done.2.rim_b = f32[8,128]{1,0:T(8,128)S(1)} collective-permute-done((f32[8,128]{1,0:T(8,128)S(1)}, f32[8,128]{1,0:T(8,128)S(1)}, u32[]{:S(2)}, u32[]{:S(2)}) %collective-permute-start.2) | collective-permute-done | bytes 4128 | tf_op jit(solution)/shard_map/ppermute | solution.py:522
  33.9 0.0 collective-permute-done.pack
  33.9 0.7 collective-permute-start.3
  34.5 0.0 collective-permute-done.3.features_far
  34.5 2.7 %shard_map.150 = (bf16[256,256]{1,0:T(8,128)(2,1)S(1)}, f32[512,256]{1,0:T(8,128)S(1)}, f32[512,256]{1,0:T(8,128)S(1)}, f32[8,256]{1,0:T(8,128)S(1)}, f32[512,8]...) custom-call(f32[48,256]{1,0:T(8,128)S(1)} %collective-permute-done.pack, ...), custom_call_target="tpu_custom_call" | custom-call | tf_op jit(solution)/shard_map/pallas_call | solution.py:27
  37.3 2.6 %collective-permute-start.4 = (bf16[256,128]{1,0:T(8,128)(2,1)S(1)}, bf16[256,128]{1,0:T(8,128)(2,1)S(1)}, u32[]{:S(2)}, u32[]{:S(2)}) collective-permute-start(bf16[256,128]{1,0:T(8,128)(2,1)S(1)} %get-tuple-element.42), channel_id=1, source_target_pairs={{64,0},{0,64},{2,66},{66,2},{68,4},{4,68},{6,70},{70,6},{78,14},{1... | collective-permute-start | bytes 196616 | tf_op jit(solution)/shard_map/ppermute | solution.py:522
  39.9 3.2 %collective-permute-start.5 = (bf16[256,128]{1,0:T(8,128)(2,1)S(1)}, bf16[256,128]{1,0:T(8,128)(2,1)S(1)}, u32[]{:S(2)}, u32[]{:S(2)}) collective-permute-start(bf16[256,128]{1,0:T(8,128)(2,1)S(1)} %get-tuple-element.43), channel_id=1, source_target_pairs={{0,2},{2,0},{66,68},{68,66},{4,6},{6,4},{70,78},{78,70},{14,12},{1... | collective-permute-start | bytes 196616 | tf_op jit(solution)/shard_map/ppermute | solution.py:522
  43.1 0.1 shard_map.151.third_far
  43.2 0.0 collective-permute-done.4.side_a
  43.2 1.9 %collective-permute-done.5.side_b = bf16[256,128]{1,0:T(8,128)(2,1)S(1)} collective-permute-done((bf16[256,128]{1,0:T(8,128)(2,1)S(1)}, bf16[256,128]{1,0:T(8,128)(2,1)S(1)}, u32[]{:S(2)}, u32[]{:S(2)}) %collective-permute-start.5) | collective-permute-done | bytes 65568 | tf_op jit(solution)/shard_map/ppermute | solution.py:522
  45.2 0.0 all-to-all-done
  45.2 3.8 %shard_map.152 = (f32[8,256]{1,0:T(8,128)S(1)}, f32[4,4,128]{2,1,0:T(4,128)S(1)}, bf16[256,256]{1,0:T(8,128)(2,1)S(1)}, bf16[256,256]{1,0:T(8,128)(2,1)S(1)}, f3...) custom-call(f32[48,256]{1,0:T(8,128)S(1)} %collective-permute-done.pack,, ...), custom_call_target="tpu_custom_call" | custom-call | tf_op jit(solution)/shard_map/pallas_call | solution.py:27
  49.0 0.1 collective-permute-start.7
  49.1 4.4 %collective-permute-start.8 = (bf16[256,128]{1,0:T(8,128)(2,1)S(1)}, bf16[256,128]{1,0:T(8,128)(2,1)S(1)}, u32[]{:S(2)}, u32[]{:S(2)}) collective-permute-start(bf16[256,128]{1,0:T(8,128)(2,1)S(1)} %get-tuple-element.53), channel_id=1, source_target_pairs={{0,2},{2,0},{66,68},{68,66},{4,6},{6,4},{70,78},{78,70},{14,12},{1... | collective-permute-start | bytes 196616 | tf_op jit(solution)/shard_map/ppermute | solution.py:522
  53.5 0.0 collective-permute-done.7.side_a
  53.5 1.6 %collective-permute-done.8.side_b = bf16[256,128]{1,0:T(8,128)(2,1)S(1)} collective-permute-done((bf16[256,128]{1,0:T(8,128)(2,1)S(1)}, bf16[256,128]{1,0:T(8,128)(2,1)S(1)}, u32[]{:S(2)}, u32[]{:S(2)}) %collective-permute-start.8) | collective-permute-done | bytes 65568 | tf_op jit(solution)/shard_map/ppermute | solution.py:522
  55.2 1.2 %shard_map.153 = (f32[8,256]{1,0:T(8,128)S(1)}, f32[8,256]{1,0:T(8,128)S(1)}, f32[8,128]{1,0:T(8,128)S(1)}, f32[8,128]{1,0:T(8,128)S(1)}) custom-call(bf16[256,256]{1,0:T(8,128)(2,1)S(1)} %get-tuple-element.50.hidden, bf16[256,256]{1,0:T(8,128)(2,1)S(1)} %get-tuple-element.51.lifted, bf16[256,128]{1,0:T(8,128)(2,1)S(1)} %collective-permute-done.7.side_a, ...), custom_call_target="tpu_custom_call" | custom-call | tf_op jit(solution)/shard_map/pallas_call | solution.py:27
  56.4 1.9 %collective-permute-start.9 = (f32[8,128]{1,0:T(8,128)S(1)}, f32[8,128]{1,0:T(8,128)S(1)}, u32[]{:S(2)}, u32[]{:S(2)}) collective-permute-start(f32[8,128]{1,0:T(8,128)S(1)} %get-tuple-element.58), channel_id=1, source_target_pairs={{192,128},{128,192},{130,194},{194,130},{196,132},{132,196},{134,1... | collective-permute-start | bytes 12296 | tf_op jit(solution)/shard_map/ppermute | solution.py:522
  58.3 3.4 %collective-permute-start.10 = (f32[8,128]{1,0:T(8,128)S(1)}, f32[8,128]{1,0:T(8,128)S(1)}, u32[]{:S(2)}, u32[]{:S(2)}) collective-permute-start(f32[8,128]{1,0:T(8,128)S(1)} %get-tuple-element.59), channel_id=1, source_target_pairs={{128,130},{130,128},{194,196},{196,194},{132,134},{134,132},{198,2... | collective-permute-start | bytes 12296 | tf_op jit(solution)/shard_map/ppermute | solution.py:522
  61.7 0.0 collective-permute-done.9.side_a
  61.7 1.0 collective-permute-done.10.side_b
  62.7 1.2 shard_map.154
  63.8 1.9 %collective-permute-start.11 = (f32[8,128]{1,0:T(8,128)S(1)}, f32[8,128]{1,0:T(8,128)S(1)}, u32[]{:S(2)}, u32[]{:S(2)}) collective-permute-start(f32[8,128]{1,0:T(8,128)S(1)} %get-tuple-element.61), channel_id=1, source_target_pairs={{192,128},{128,192},{130,194},{194,130},{196,132},{132,196},{134,1... | collective-permute-start | bytes 12296 | tf_op jit(solution)/shard_map/ppermute | solution.py:522
  65.7 4.8 %collective-permute-start.12 = (f32[8,128]{1,0:T(8,128)S(1)}, f32[8,128]{1,0:T(8,128)S(1)}, u32[]{:S(2)}, u32[]{:S(2)}) collective-permute-start(f32[8,128]{1,0:T(8,128)S(1)} %get-tuple-element.62), channel_id=1, source_target_pairs={{128,130},{130,128},{194,196},{196,194},{132,134},{134,132},{198,2... | collective-permute-start | bytes 12296 | tf_op jit(solution)/shard_map/ppermute | solution.py:522
  70.5 0.0 collective-permute-done.11.side_a
  70.6 1.0 collective-permute-done.12.side_b
  71.5 3.4 %shard_map.155 = (f32[3,256]{1,0:T(4,128)S(1)}, f32[384,2,128]{2,1,0:T(2,128)}) custom-call(f32[4,4,128]{2,1,0:T(4,128)S(1)} %get-tuple-element.49.near, f32[48,256]{1,0:T(8,128)S(1)} %collective-permute-done.pack, f32[8,256]{1,0:T(8,128)S(1)} %get-tuple-element.56.charge, f32[8,256]{1,0:T(8,128)S(1)} %get-tuple-element.57.outside_row, ...), custom_call_target="tpu_custom_call" | custom-call | tf_op jit(solution)/shard_map/pallas_call | solution.py:27
  74.9 15.0 %all-to-all-start.1 = ((f32[384,2,128]{2,1,0:T(2,128)}), f32[384,2,128]{2,1,0:T(2,128)S(1)}, u32[]{:S(2)}, u32[]{:S(2)}) async-start(f32[384,2,128]{2,1,0:T(2,128)} %get-tuple-element.65), calls=%async_computation.1 | async-start | bytes 786432 | tf_op jit(solution)/shard_map/all_to_all | solution.py:590
  90.0 4.0 %collective-permute-start.13 = (f32[3,256]{1,0:T(4,128)S(1)}, f32[3,256]{1,0:T(4,128)S(1)}, u32[]{:S(2)}, u32[]{:S(2)}) collective-permute-start(f32[3,256]{1,0:T(4,128)S(1)} %get-tuple-element.64), channel_id=1, source_target_pairs={{64,0},{0,1},{2,2},{66,3},{68,4},{4,5},{6,6},{70,7},{78,8},{14,9},... | collective-permute-start | bytes 9224 | tf_op jit(solution)/shard_map/ppermute | solution.py:522
  94.0 9.3 %all-to-all-done.1 = f32[384,2,128]{2,1,0:T(2,128)S(1)} async-done(((f32[384,2,128]{2,1,0:T(2,128)}), f32[384,2,128]{2,1,0:T(2,128)S(1)}, u32[]{:S(2)}, u32[]{:S(2)}) %all-to-all-start.1) | async-done | bytes 393248 | tf_op jit(solution)/shard_map/all_to_all | solution.py:590
  103.3 0.2 shard_map.156
  103.5 10.7 %collective-permute-start.14 = (f32[3,256]{1,0:T(4,128)S(1)}, f32[3,256]{1,0:T(4,128)S(1)}, u32[]{:S(2)}, u32[]{:S(2)}) collective-permute-start(f32[3,256]{1,0:T(4,128)S(1)} %shard_map.156), channel_id=1, source_target_pairs={{0,128},{128,0},{1,129},{129,1},{2,130},{130,2},{3,131},{131,3},{4... | collective-permute-start | bytes 9224 | tf_op jit(solution)/shard_map/ppermute | solution.py:593
  114.2 0.0 collective-permute-done.13.result
  114.2 0.8 collective-permute-done.14.share
  115.0 0.6 shard_map.157
Async XLA Ops:
  1.7 4.2 %collective-permute-start.6 = (f32[2,4,128]{2,1,0:T(4,128)S(1)}, f32[2,4,128]{2,1,0:T(4,128)S(1)}, u32[]{:S(2)}, u32[]{:S(2)}) collective-permute-start(f32[2,4,128]{2,1,0:T(4,128)S(1)} %get-tuple-element.48), channel_id=1, source_target_pairs={{0,128},{128,0},{1,129},{129,1},{2,130},{130,2},{3,131},{131,3},{4... | collective-permute-start | bytes 12296 | tf_op jit(solution)/shard_map/ppermute | solution.py:540
  6.7 38.5 %all-to-all-start = ((f32[128,2,4,128]{3,2,1,0:T(4,128)}), f32[128,2,4,128]{3,2,1,0:T(4,128)S(1)}, u32[]{:S(2)}, u32[]{:S(2)}) async-start(f32[128,2,4,128]{3,2,1,0:T(4,128)} %broadcast_in_dim.17), calls=%async_computation | async-start | bytes 1048576 | tf_op jit(solution)/shard_map/all_to_all | solution.py:542
  20.5 13.4 %collective-permute-start = (f32[48,256]{1,0:T(8,128)S(1)}, f32[48,256]{1,0:T(8,128)S(1)}, u32[]{:S(2)}, u32[]{:S(2)}) collective-permute-start(f32[48,256]{1,0:T(8,128)S(1)} %get-tuple-element.34), channel_id=1, source_target_pairs={{0,64},{1,0},{2,2},{3,66},{4,68},{5,4},{6,6},{7,70},{8,78},{9,14},... | collective-permute-start | bytes 147464 | tf_op jit(solution)/shard_map/ppermute | solution.py:522
  23.3 2.0 %collective-permute-start.1 = (f32[8,128]{1,0:T(8,128)S(1)}, f32[8,128]{1,0:T(8,128)S(1)}, u32[]{:S(2)}, u32[]{:S(2)}) collective-permute-start(f32[8,128]{1,0:T(8,128)S(1)} %get-tuple-element.35), channel_id=1, source_target_pairs={{0,0},{1,64},{2,66},{3,2},{4,4},{5,68},{6,70},{7,6},{8,14},{9,78},... | collective-permute-start | bytes 12296 | tf_op jit(solution)/shard_map/ppermute | solution.py:522
  23.9 9.9 %collective-permute-start.2 = (f32[8,128]{1,0:T(8,128)S(1)}, f32[8,128]{1,0:T(8,128)S(1)}, u32[]{:S(2)}, u32[]{:S(2)}) collective-permute-start(f32[8,128]{1,0:T(8,128)S(1)} %get-tuple-element.36), channel_id=1, source_target_pairs={{1,2},{2,0},{3,68},{4,66},{5,6},{6,4},{7,78},{8,70},{9,12},{10,14}... | collective-permute-start | bytes 12296 | tf_op jit(solution)/shard_map/ppermute | solution.py:522
  33.9 0.7 collective-permute-start.3
  37.3 6.0 %collective-permute-start.4 = (bf16[256,128]{1,0:T(8,128)(2,1)S(1)}, bf16[256,128]{1,0:T(8,128)(2,1)S(1)}, u32[]{:S(2)}, u32[]{:S(2)}) collective-permute-start(bf16[256,128]{1,0:T(8,128)(2,1)S(1)} %get-tuple-element.42), channel_id=1, source_target_pairs={{64,0},{0,64},{2,66},{66,2},{68,4},{4,68},{6,70},{70,6},{78,14},{1... | collective-permute-start | bytes 196616 | tf_op jit(solution)/shard_map/ppermute | solution.py:522
  39.9 5.3 %collective-permute-start.5 = (bf16[256,128]{1,0:T(8,128)(2,1)S(1)}, bf16[256,128]{1,0:T(8,128)(2,1)S(1)}, u32[]{:S(2)}, u32[]{:S(2)}) collective-permute-start(bf16[256,128]{1,0:T(8,128)(2,1)S(1)} %get-tuple-element.43), channel_id=1, source_target_pairs={{0,2},{2,0},{66,68},{68,66},{4,6},{6,4},{70,78},{78,70},{14,12},{1... | collective-permute-start | bytes 196616 | tf_op jit(solution)/shard_map/ppermute | solution.py:522
  49.0 4.5 %collective-permute-start.7 = (bf16[256,128]{1,0:T(8,128)(2,1)S(1)}, bf16[256,128]{1,0:T(8,128)(2,1)S(1)}, u32[]{:S(2)}, u32[]{:S(2)}) collective-permute-start(bf16[256,128]{1,0:T(8,128)(2,1)S(1)} %get-tuple-element.52), channel_id=1, source_target_pairs={{64,0},{0,64},{2,66},{66,2},{68,4},{4,68},{6,70},{70,6},{78,14},{1... | collective-permute-start | bytes 196616 | tf_op jit(solution)/shard_map/ppermute | solution.py:522
  49.1 6.0 %collective-permute-start.8 = (bf16[256,128]{1,0:T(8,128)(2,1)S(1)}, bf16[256,128]{1,0:T(8,128)(2,1)S(1)}, u32[]{:S(2)}, u32[]{:S(2)}) collective-permute-start(bf16[256,128]{1,0:T(8,128)(2,1)S(1)} %get-tuple-element.53), channel_id=1, source_target_pairs={{0,2},{2,0},{66,68},{68,66},{4,6},{6,4},{70,78},{78,70},{14,12},{1... | collective-permute-start | bytes 196616 | tf_op jit(solution)/shard_map/ppermute | solution.py:522
  56.4 5.3 %collective-permute-start.9 = (f32[8,128]{1,0:T(8,128)S(1)}, f32[8,128]{1,0:T(8,128)S(1)}, u32[]{:S(2)}, u32[]{:S(2)}) collective-permute-start(f32[8,128]{1,0:T(8,128)S(1)} %get-tuple-element.58), channel_id=1, source_target_pairs={{192,128},{128,192},{130,194},{194,130},{196,132},{132,196},{134,1... | collective-permute-start | bytes 12296 | tf_op jit(solution)/shard_map/ppermute | solution.py:522
  58.3 4.4 %collective-permute-start.10 = (f32[8,128]{1,0:T(8,128)S(1)}, f32[8,128]{1,0:T(8,128)S(1)}, u32[]{:S(2)}, u32[]{:S(2)}) collective-permute-start(f32[8,128]{1,0:T(8,128)S(1)} %get-tuple-element.59), channel_id=1, source_target_pairs={{128,130},{130,128},{194,196},{196,194},{132,134},{134,132},{198,2... | collective-permute-start | bytes 12296 | tf_op jit(solution)/shard_map/ppermute | solution.py:522
  63.8 6.7 %collective-permute-start.11 = (f32[8,128]{1,0:T(8,128)S(1)}, f32[8,128]{1,0:T(8,128)S(1)}, u32[]{:S(2)}, u32[]{:S(2)}) collective-permute-start(f32[8,128]{1,0:T(8,128)S(1)} %get-tuple-element.61), channel_id=1, source_target_pairs={{192,128},{128,192},{130,194},{194,130},{196,132},{132,196},{134,1... | collective-permute-start | bytes 12296 | tf_op jit(solution)/shard_map/ppermute | solution.py:522
  65.7 5.8 %collective-permute-start.12 = (f32[8,128]{1,0:T(8,128)S(1)}, f32[8,128]{1,0:T(8,128)S(1)}, u32[]{:S(2)}, u32[]{:S(2)}) collective-permute-start(f32[8,128]{1,0:T(8,128)S(1)} %get-tuple-element.62), channel_id=1, source_target_pairs={{128,130},{130,128},{194,196},{196,194},{132,134},{134,132},{198,2... | collective-permute-start | bytes 12296 | tf_op jit(solution)/shard_map/ppermute | solution.py:522
  74.9 28.4 %all-to-all-start.1 = ((f32[384,2,128]{2,1,0:T(2,128)}), f32[384,2,128]{2,1,0:T(2,128)S(1)}, u32[]{:S(2)}, u32[]{:S(2)}) async-start(f32[384,2,128]{2,1,0:T(2,128)} %get-tuple-element.65), calls=%async_computation.1 | async-start | bytes 786432 | tf_op jit(solution)/shard_map/all_to_all | solution.py:590
  90.0 24.2 %collective-permute-start.13 = (f32[3,256]{1,0:T(4,128)S(1)}, f32[3,256]{1,0:T(4,128)S(1)}, u32[]{:S(2)}, u32[]{:S(2)}) collective-permute-start(f32[3,256]{1,0:T(4,128)S(1)} %get-tuple-element.64), channel_id=1, source_target_pairs={{64,0},{0,1},{2,2},{66,3},{68,4},{4,5},{6,6},{70,7},{78,8},{14,9},... | collective-permute-start | bytes 9224 | tf_op jit(solution)/shard_map/ppermute | solution.py:522
  103.5 11.5 %collective-permute-start.14 = (f32[3,256]{1,0:T(4,128)S(1)}, f32[3,256]{1,0:T(4,128)S(1)}, u32[]{:S(2)}, u32[]{:S(2)}) collective-permute-start(f32[3,256]{1,0:T(4,128)S(1)} %shard_map.156), channel_id=1, source_target_pairs={{0,128},{128,0},{1,129},{129,1},{2,130},{130,2},{3,131},{131,3},{4... | collective-permute-start | bytes 9224 | tf_op jit(solution)/shard_map/ppermute | solution.py:593

commit v11 on v10

--- a/solution.py
+++ b/solution.py
@@ -20,7 +20,7 @@
 TERM_CHUNK, TERM_UNROLL = 64, 4
 STATIC_CHUNK = 32
 RADIAL_SLOTS = 8
-MESSAGE_SLOTS = 8
+MESSAGE_SLOTS = 16
 
 
 def call(body, outs, held, far=(), scratch=(), copies=0, far_outs=0, loose=0):
@@ -322,8 +322,8 @@
     width = site.shape[1]
     listed = near_own.shape[0]
     weights = (
+        (third_far, third),
         (node_in_far, node_in), (node_out_far.at[0], node_out), (w_out_far.at[0], w_out), (gain_far, gain),
-        (third_far, third),
     )
 
     @pl.when(learned())
@@ -335,8 +335,8 @@
 
     @pl.when(learned())
     def _():
-        for i, (source, target) in enumerate(weights[:4]):
-            pltpu.make_async_copy(source, target, done.at[i]).wait()
+        for i, (source, target) in enumerate(weights[1:]):
+            pltpu.make_async_copy(source, target, done.at[1 + i]).wait()
         in_first[...] = flip(node_in[0]).astype(BF16)
         in_second[...] = flip(node_in[1]).astype(BF16)
         out_t[...] = flip(w_out[...]).astype(BF16)
@@ -365,7 +365,7 @@
         present = jnp.concatenate([jnp.ones((1, width), F32), rim_a[6:7, :], rim_b[6:7, :]], axis=1)
         raised = dot(in_first[...], start)
         table = jnp.where(present > 0.5, raised, 0.0).astype(BF16)
-        pltpu.make_async_copy(third_far, third, done.at[4]).wait()
+        pltpu.make_async_copy(third_far, third, done.at[0]).wait()
         new = message(0, start[:, :width], table, third, out_t[...], node_t[...], slots, total)
         hidden_out[...] = new
         raised = dot(in_second[...], new).astype(BF16)
@@ -542,7 +542,6 @@
     near = lax.all_to_all(copies, DOM, 0, 0, tiled=True).reshape(2 * members, 4, half)
     pack = move(pack, itself, same, place)
     rim_a, rim_b = trade(lent_a, lent_b, source=same)
-    features, pack, rim_a, rim_b = lax.optimization_barrier((features, pack, rim_a, rim_b))
     features = move(features, itself, same, place, (0,))
     feat_t, w3, w5, fixed, entry, lent_a, lent_b = call(
         static_kernel, [by_site, ((depth, width), F32), ((depth, width), F32), row8, ((depth, 8), F32), wide, wide],

time: 116 us -> 111 us (0.957)
  starting transfers between devices: 74.6 us -> 70 us
    ppermute x1, starting transfers between devices: 10.7 us -> 6.17 us  [local(): share = lax.ppermute(share, 'grp', [(0, 1), (1, 0)])]
where the time goes in v11:
time: 111 us
  starting transfers between devices  70 us (63%)
  waiting for transfers between devices  24.9 us (22%)
  Pallas kernels  14.1 us (13%)
    ppermute x13, starting transfers between devices, move(): lax.ppermute(value, EVERY, [(source[a] + g * members, target[b] + g * mem...  32 us
    all_to_all x1, starting transfers between devices, local(): lax.all_to_all(spread, DOM, 0, 0, tiled=True).reshape(members, 3, 2, half)  14.7 us
    pallas_call x9, Pallas kernels, call(): pl.pallas_call(body, out_shape=[jax.ShapeDtypeStruct(s, d) for s, d in ou...  14.1 us
    ppermute x13, waiting for transfers between devices, move(): lax.ppermute(value, EVERY, [(source[a] + g * members, target[b] + g * mem...  13.9 us
    all_to_all x1, starting transfers between devices, local(): lax.all_to_all(copies, DOM, 0, 0, tiled=True).reshape(2 * members, 4, half)  13.8 us
    all_to_all x1, waiting for transfers between devices, local(): lax.all_to_all(spread, DOM, 0, 0, tiled=True).reshape(members, 3, 2, half)  9.38 us
    ppermute x1, starting transfers between devices, local(): share = lax.ppermute(share, 'grp', [(0, 1), (1, 0)])  6.17 us
    ppermute x1, starting transfers between devices, local(): partner = lax.ppermute(mine, 'grp', [(0, 1), (1, 0)])  3.33 us
  transfers between devices with their start and end apart: 17, of which 8 were waited for; matrix products, arithmetic and copies ran while one was open for 0% of the time, Pallas kernels for 3%

profile of v11, /device:TPU:1, one launch (start us, length us, event | category | flops | bytes accessed | tf_op | source)
XLA Modules:
  0.0 110.8 jit_solution(17470899150925812872)
XLA Ops:
  0.6 1.0 shard_map.149
  1.7 3.3 %collective-permute-start.6 = (f32[2,4,128]{2,1,0:T(4,128)S(1)}, f32[2,4,128]{2,1,0:T(4,128)S(1)}, u32[]{:S(2)}, u32[]{:S(2)}) collective-permute-start(f32[2,4,128]{2,1,0:T(4,128)S(1)} %get-tuple-element.40), channel_id=1, source_target_pairs={{0,128},{128,0},{1,129},{129,1},{2,130},{130,2},{3,131},{131,3},{4... | collective-permute-start | bytes 12296 | tf_op jit(solution)/shard_map/ppermute | solution.py:540
  5.0 0.8 collective-permute-done.6
  5.8 0.9 broadcast_in_dim.17
  6.7 13.8 %all-to-all-start = ((f32[128,2,4,128]{3,2,1,0:T(4,128)}), f32[128,2,4,128]{3,2,1,0:T(4,128)S(1)}, u32[]{:S(2)}, u32[]{:S(2)}) async-start(f32[128,2,4,128]{3,2,1,0:T(4,128)} %broadcast_in_dim.17), calls=%async_computation | async-start | bytes 1048576 | tf_op jit(solution)/shard_map/all_to_all | solution.py:542
  20.5 0.7 collective-permute-start.3
  21.1 2.8 %collective-permute-start = (f32[48,256]{1,0:T(8,128)S(1)}, f32[48,256]{1,0:T(8,128)S(1)}, u32[]{:S(2)}, u32[]{:S(2)}) collective-permute-start(f32[48,256]{1,0:T(8,128)S(1)} %get-tuple-element.30), channel_id=1, source_target_pairs={{0,64},{1,0},{2,2},{3,66},{4,68},{5,4},{6,6},{7,70},{8,78},{9,14},... | collective-permute-start | bytes 147464 | tf_op jit(solution)/shard_map/ppermute | solution.py:522
  23.9 0.7 collective-permute-start.1
  24.6 1.3 %collective-permute-start.2 = (f32[8,128]{1,0:T(8,128)S(1)}, f32[8,128]{1,0:T(8,128)S(1)}, u32[]{:S(2)}, u32[]{:S(2)}) collective-permute-start(f32[8,128]{1,0:T(8,128)S(1)} %get-tuple-element.32), channel_id=1, source_target_pairs={{1,2},{2,0},{3,68},{4,66},{5,6},{6,4},{7,78},{8,70},{9,12},{10,14}... | collective-permute-start | bytes 12296 | tf_op jit(solution)/shard_map/ppermute | solution.py:522
  25.9 0.0 collective-permute-done.1.rim_a
  25.9 8.6 %collective-permute-done.2.rim_b = f32[8,128]{1,0:T(8,128)S(1)} collective-permute-done((f32[8,128]{1,0:T(8,128)S(1)}, f32[8,128]{1,0:T(8,128)S(1)}, u32[]{:S(2)}, u32[]{:S(2)}) %collective-permute-start.2) | collective-permute-done | bytes 4128 | tf_op jit(solution)/shard_map/ppermute | solution.py:522
  34.6 0.0 collective-permute-done.pack
  34.6 0.0 collective-permute-done.3.features_far
  34.6 2.7 %shard_map.150 = (bf16[256,256]{1,0:T(8,128)(2,1)S(1)}, f32[512,256]{1,0:T(8,128)S(1)}, f32[512,256]{1,0:T(8,128)S(1)}, f32[8,256]{1,0:T(8,128)S(1)}, f32[512,8]...) custom-call(f32[48,256]{1,0:T(8,128)S(1)} %collective-permute-done.pack, ...), custom_call_target="tpu_custom_call" | custom-call | tf_op jit(solution)/shard_map/pallas_call | solution.py:27
  37.3 2.6 %collective-permute-start.4 = (bf16[256,128]{1,0:T(8,128)(2,1)S(1)}, bf16[256,128]{1,0:T(8,128)(2,1)S(1)}, u32[]{:S(2)}, u32[]{:S(2)}) collective-permute-start(bf16[256,128]{1,0:T(8,128)(2,1)S(1)} %get-tuple-element.34), channel_id=1, source_target_pairs={{64,0},{0,64},{2,66},{66,2},{68,4},{4,68},{6,70},{70,6},{78,14},{1... | collective-permute-start | bytes 196616 | tf_op jit(solution)/shard_map/ppermute | solution.py:522
  39.8 3.3 %collective-permute-start.5 = (bf16[256,128]{1,0:T(8,128)(2,1)S(1)}, bf16[256,128]{1,0:T(8,128)(2,1)S(1)}, u32[]{:S(2)}, u32[]{:S(2)}) collective-permute-start(bf16[256,128]{1,0:T(8,128)(2,1)S(1)} %get-tuple-element.35), channel_id=1, source_target_pairs={{0,2},{2,0},{66,68},{68,66},{4,6},{6,4},{70,78},{78,70},{14,12},{1... | collective-permute-start | bytes 196616 | tf_op jit(solution)/shard_map/ppermute | solution.py:522
  43.1 0.1 shard_map.151.third_far
  43.2 0.0 collective-permute-done.4.side_a
  43.2 1.6 %collective-permute-done.5.side_b = bf16[256,128]{1,0:T(8,128)(2,1)S(1)} collective-permute-done((bf16[256,128]{1,0:T(8,128)(2,1)S(1)}, bf16[256,128]{1,0:T(8,128)(2,1)S(1)}, u32[]{:S(2)}, u32[]{:S(2)}) %collective-permute-start.5) | collective-permute-done | bytes 65568 | tf_op jit(solution)/shard_map/ppermute | solution.py:522
  44.8 0.0 all-to-all-done
  44.8 3.8 %shard_map.152 = (f32[8,256]{1,0:T(8,128)S(1)}, f32[4,4,128]{2,1,0:T(4,128)S(1)}, bf16[256,256]{1,0:T(8,128)(2,1)S(1)}, bf16[256,256]{1,0:T(8,128)(2,1)S(1)}, f3...) custom-call(f32[48,256]{1,0:T(8,128)S(1)} %collective-permute-done.pack,, ...), custom_call_target="tpu_custom_call" | custom-call | tf_op jit(solution)/shard_map/pallas_call | solution.py:27
  48.7 0.1 collective-permute-start.7
  48.8 4.7 %collective-permute-start.8 = (bf16[256,128]{1,0:T(8,128)(2,1)S(1)}, bf16[256,128]{1,0:T(8,128)(2,1)S(1)}, u32[]{:S(2)}, u32[]{:S(2)}) collective-permute-start(bf16[256,128]{1,0:T(8,128)(2,1)S(1)} %get-tuple-element.45), channel_id=1, source_target_pairs={{0,2},{2,0},{66,68},{68,66},{4,6},{6,4},{70,78},{78,70},{14,12},{1... | collective-permute-start | bytes 196616 | tf_op jit(solution)/shard_map/ppermute | solution.py:522
  53.5 0.0 collective-permute-done.7.side_a
  53.5 1.6 %collective-permute-done.8.side_b = bf16[256,128]{1,0:T(8,128)(2,1)S(1)} collective-permute-done((bf16[256,128]{1,0:T(8,128)(2,1)S(1)}, bf16[256,128]{1,0:T(8,128)(2,1)S(1)}, u32[]{:S(2)}, u32[]{:S(2)}) %collective-permute-start.8) | collective-permute-done | bytes 65568 | tf_op jit(solution)/shard_map/ppermute | solution.py:522
  55.1 1.2 %shard_map.153 = (f32[8,256]{1,0:T(8,128)S(1)}, f32[8,256]{1,0:T(8,128)S(1)}, f32[8,128]{1,0:T(8,128)S(1)}, f32[8,128]{1,0:T(8,128)S(1)}) custom-call(bf16[256,256]{1,0:T(8,128)(2,1)S(1)} %get-tuple-element.42.hidden, bf16[256,256]{1,0:T(8,128)(2,1)S(1)} %get-tuple-element.43.lifted, bf16[256,128]{1,0:T(8,128)(2,1)S(1)} %collective-permute-done.7.side_a, ...), custom_call_target="tpu_custom_call" | custom-call | tf_op jit(solution)/shard_map/pallas_call | solution.py:27
  56.3 1.9 %collective-permute-start.9 = (f32[8,128]{1,0:T(8,128)S(1)}, f32[8,128]{1,0:T(8,128)S(1)}, u32[]{:S(2)}, u32[]{:S(2)}) collective-permute-start(f32[8,128]{1,0:T(8,128)S(1)} %get-tuple-element.50), channel_id=1, source_target_pairs={{192,128},{128,192},{130,194},{194,130},{196,132},{132,196},{134,1... | collective-permute-start | bytes 12296 | tf_op jit(solution)/shard_map/ppermute | solution.py:522
  58.3 3.4 %collective-permute-start.10 = (f32[8,128]{1,0:T(8,128)S(1)}, f32[8,128]{1,0:T(8,128)S(1)}, u32[]{:S(2)}, u32[]{:S(2)}) collective-permute-start(f32[8,128]{1,0:T(8,128)S(1)} %get-tuple-element.51), channel_id=1, source_target_pairs={{128,130},{130,128},{194,196},{196,194},{132,134},{134,132},{198,2... | collective-permute-start | bytes 12296 | tf_op jit(solution)/shard_map/ppermute | solution.py:522
  61.7 0.0 collective-permute-done.9.side_a
  61.7 1.0 collective-permute-done.10.side_b
  62.6 1.2 %shard_map.154 = (f32[8,256]{1,0:T(8,128)S(1)}, f32[8,128]{1,0:T(8,128)S(1)}, f32[8,128]{1,0:T(8,128)S(1)}) custom-call(f32[8,128]{1,0:T(8,128)S(1)} %collective-permute-done.9.side_a, f32[8,128]{1,0:T(8,128)S(1)} %collective-permute-done.10.side_b, f32[48,256]{1,0:T(8,128)S(1)} %collective-permute-done.pack, f32[512,256]{1,0:T(8,128)S(1)} %get-tuple-element.36.w3, ...), custom_call_target="tpu_custom_call" | custom-call | tf_op jit(solution)/shard_map/pallas_call | solution.py:27
  63.9 1.9 %collective-permute-start.11 = (f32[8,128]{1,0:T(8,128)S(1)}, f32[8,128]{1,0:T(8,128)S(1)}, u32[]{:S(2)}, u32[]{:S(2)}) collective-permute-start(f32[8,128]{1,0:T(8,128)S(1)} %get-tuple-element.53), channel_id=1, source_target_pairs={{192,128},{128,192},{130,194},{194,130},{196,132},{132,196},{134,1... | collective-permute-start | bytes 12296 | tf_op jit(solution)/shard_map/ppermute | solution.py:522
  65.8 4.8 %collective-permute-start.12 = (f32[8,128]{1,0:T(8,128)S(1)}, f32[8,128]{1,0:T(8,128)S(1)}, u32[]{:S(2)}, u32[]{:S(2)}) collective-permute-start(f32[8,128]{1,0:T(8,128)S(1)} %get-tuple-element.54), channel_id=1, source_target_pairs={{128,130},{130,128},{194,196},{196,194},{132,134},{134,132},{198,2... | collective-permute-start | bytes 12296 | tf_op jit(solution)/shard_map/ppermute | solution.py:522
  70.6 0.0 collective-permute-done.11.side_a
  70.6 1.0 collective-permute-done.12.side_b
  71.6 3.2 %shard_map.155 = (f32[3,256]{1,0:T(4,128)S(1)}, f32[384,2,128]{2,1,0:T(2,128)}) custom-call(f32[4,4,128]{2,1,0:T(4,128)S(1)} %get-tuple-element.41.near, f32[48,256]{1,0:T(8,128)S(1)} %collective-permute-done.pack, f32[8,256]{1,0:T(8,128)S(1)} %get-tuple-element.48.charge, f32[8,256]{1,0:T(8,128)S(1)} %get-tuple-element.49.outside_row, ...), custom_call_target="tpu_custom_call" | custom-call | tf_op jit(solution)/shard_map/pallas_call | solution.py:27
  74.8 14.7 %all-to-all-start.1 = ((f32[384,2,128]{2,1,0:T(2,128)}), f32[384,2,128]{2,1,0:T(2,128)S(1)}, u32[]{:S(2)}, u32[]{:S(2)}) async-start(f32[384,2,128]{2,1,0:T(2,128)} %get-tuple-element.57), calls=%async_computation.1 | async-start | bytes 786432 | tf_op jit(solution)/shard_map/all_to_all | solution.py:589
  89.5 4.0 %collective-permute-start.13 = (f32[3,256]{1,0:T(4,128)S(1)}, f32[3,256]{1,0:T(4,128)S(1)}, u32[]{:S(2)}, u32[]{:S(2)}) collective-permute-start(f32[3,256]{1,0:T(4,128)S(1)} %get-tuple-element.56), channel_id=1, source_target_pairs={{64,0},{0,1},{2,2},{66,3},{68,4},{4,5},{6,6},{70,7},{78,8},{14,9},... | collective-permute-start | bytes 9224 | tf_op jit(solution)/shard_map/ppermute | solution.py:522
  93.5 9.4 %all-to-all-done.1 = f32[384,2,128]{2,1,0:T(2,128)S(1)} async-done(((f32[384,2,128]{2,1,0:T(2,128)}), f32[384,2,128]{2,1,0:T(2,128)S(1)}, u32[]{:S(2)}, u32[]{:S(2)}) %all-to-all-start.1) | async-done | bytes 393248 | tf_op jit(solution)/shard_map/all_to_all | solution.py:589
  102.9 0.2 shard_map.156
  103.1 6.2 %collective-permute-start.14 = (f32[3,256]{1,0:T(4,128)S(1)}, f32[3,256]{1,0:T(4,128)S(1)}, u32[]{:S(2)}, u32[]{:S(2)}) collective-permute-start(f32[3,256]{1,0:T(4,128)S(1)} %shard_map.156), channel_id=1, source_target_pairs={{0,128},{128,0},{1,129},{129,1},{2,130},{130,2},{3,131},{131,3},{4... | collective-permute-start | bytes 9224 | tf_op jit(solution)/shard_map/ppermute | solution.py:592
  109.2 0.0 collective-permute-done.13.result
  109.2 0.8 collective-permute-done.14.share
  110.1 0.6 shard_map.157
Async XLA Ops:
  1.7 4.2 %collective-permute-start.6 = (f32[2,4,128]{2,1,0:T(4,128)S(1)}, f32[2,4,128]{2,1,0:T(4,128)S(1)}, u32[]{:S(2)}, u32[]{:S(2)}) collective-permute-start(f32[2,4,128]{2,1,0:T(4,128)S(1)} %get-tuple-element.40), channel_id=1, source_target_pairs={{0,128},{128,0},{1,129},{129,1},{2,130},{130,2},{3,131},{131,3},{4... | collective-permute-start | bytes 12296 | tf_op jit(solution)/shard_map/ppermute | solution.py:540
  6.7 38.2 %all-to-all-start = ((f32[128,2,4,128]{3,2,1,0:T(4,128)}), f32[128,2,4,128]{3,2,1,0:T(4,128)S(1)}, u32[]{:S(2)}, u32[]{:S(2)}) async-start(f32[128,2,4,128]{3,2,1,0:T(4,128)} %broadcast_in_dim.17), calls=%async_computation | async-start | bytes 1048576 | tf_op jit(solution)/shard_map/all_to_all | solution.py:542
  20.5 14.1 %collective-permute-start.3 = (bf16[256,256]{1,0:T(8,128)(2,1)}, bf16[256,256]{1,0:T(8,128)(2,1)S(1)}, u32[]{:S(2)}, u32[]{:S(2)}) collective-permute-start(bf16[256,256]{1,0:T(8,128)(2,1)} %param.17), channel_id=1, source_target_pairs={{0,64},{1,0},{2,2},{3,66},{4,68},{5,4},{6,6},{7,70},{8,78},{9,14},... | collective-permute-start | bytes 393224 | tf_op jit(solution)/shard_map/ppermute | solution.py:522
  21.1 13.4 %collective-permute-start = (f32[48,256]{1,0:T(8,128)S(1)}, f32[48,256]{1,0:T(8,128)S(1)}, u32[]{:S(2)}, u32[]{:S(2)}) collective-permute-start(f32[48,256]{1,0:T(8,128)S(1)} %get-tuple-element.30), channel_id=1, source_target_pairs={{0,64},{1,0},{2,2},{3,66},{4,68},{5,4},{6,6},{7,70},{8,78},{9,14},... | collective-permute-start | bytes 147464 | tf_op jit(solution)/shard_map/ppermute | solution.py:522
  23.9 2.0 %collective-permute-start.1 = (f32[8,128]{1,0:T(8,128)S(1)}, f32[8,128]{1,0:T(8,128)S(1)}, u32[]{:S(2)}, u32[]{:S(2)}) collective-permute-start(f32[8,128]{1,0:T(8,128)S(1)} %get-tuple-element.31), channel_id=1, source_target_pairs={{0,0},{1,64},{2,66},{3,2},{4,4},{5,68},{6,70},{7,6},{8,14},{9,78},... | collective-permute-start | bytes 12296 | tf_op jit(solution)/shard_map/ppermute | solution.py:522
  24.6 9.9 %collective-permute-start.2 = (f32[8,128]{1,0:T(8,128)S(1)}, f32[8,128]{1,0:T(8,128)S(1)}, u32[]{:S(2)}, u32[]{:S(2)}) collective-permute-start(f32[8,128]{1,0:T(8,128)S(1)} %get-tuple-element.32), channel_id=1, source_target_pairs={{1,2},{2,0},{3,68},{4,66},{5,6},{6,4},{7,78},{8,70},{9,12},{10,14}... | collective-permute-start | bytes 12296 | tf_op jit(solution)/shard_map/ppermute | solution.py:522
  37.3 5.9 %collective-permute-start.4 = (bf16[256,128]{1,0:T(8,128)(2,1)S(1)}, bf16[256,128]{1,0:T(8,128)(2,1)S(1)}, u32[]{:S(2)}, u32[]{:S(2)}) collective-permute-start(bf16[256,128]{1,0:T(8,128)(2,1)S(1)} %get-tuple-element.34), channel_id=1, source_target_pairs={{64,0},{0,64},{2,66},{66,2},{68,4},{4,68},{6,70},{70,6},{78,14},{1... | collective-permute-start | bytes 196616 | tf_op jit(solution)/shard_map/ppermute | solution.py:522
  39.8 5.0 %collective-permute-start.5 = (bf16[256,128]{1,0:T(8,128)(2,1)S(1)}, bf16[256,128]{1,0:T(8,128)(2,1)S(1)}, u32[]{:S(2)}, u32[]{:S(2)}) collective-permute-start(bf16[256,128]{1,0:T(8,128)(2,1)S(1)} %get-tuple-element.35), channel_id=1, source_target_pairs={{0,2},{2,0},{66,68},{68,66},{4,6},{6,4},{70,78},{78,70},{14,12},{1... | collective-permute-start | bytes 196616 | tf_op jit(solution)/shard_map/ppermute | solution.py:522
  48.7 4.8 %collective-permute-start.7 = (bf16[256,128]{1,0:T(8,128)(2,1)S(1)}, bf16[256,128]{1,0:T(8,128)(2,1)S(1)}, u32[]{:S(2)}, u32[]{:S(2)}) collective-permute-start(bf16[256,128]{1,0:T(8,128)(2,1)S(1)} %get-tuple-element.44), channel_id=1, source_target_pairs={{64,0},{0,64},{2,66},{66,2},{68,4},{4,68},{6,70},{70,6},{78,14},{1... | collective-permute-start | bytes 196616 | tf_op jit(solution)/shard_map/ppermute | solution.py:522
  48.8 6.3 %collective-permute-start.8 = (bf16[256,128]{1,0:T(8,128)(2,1)S(1)}, bf16[256,128]{1,0:T(8,128)(2,1)S(1)}, u32[]{:S(2)}, u32[]{:S(2)}) collective-permute-start(bf16[256,128]{1,0:T(8,128)(2,1)S(1)} %get-tuple-element.45), channel_id=1, source_target_pairs={{0,2},{2,0},{66,68},{68,66},{4,6},{6,4},{70,78},{78,70},{14,12},{1... | collective-permute-start | bytes 196616 | tf_op jit(solution)/shard_map/ppermute | solution.py:522
  56.3 5.3 %collective-permute-start.9 = (f32[8,128]{1,0:T(8,128)S(1)}, f32[8,128]{1,0:T(8,128)S(1)}, u32[]{:S(2)}, u32[]{:S(2)}) collective-permute-start(f32[8,128]{1,0:T(8,128)S(1)} %get-tuple-element.50), channel_id=1, source_target_pairs={{192,128},{128,192},{130,194},{194,130},{196,132},{132,196},{134,1... | collective-permute-start | bytes 12296 | tf_op jit(solution)/shard_map/ppermute | solution.py:522
  58.3 4.4 %collective-permute-start.10 = (f32[8,128]{1,0:T(8,128)S(1)}, f32[8,128]{1,0:T(8,128)S(1)}, u32[]{:S(2)}, u32[]{:S(2)}) collective-permute-start(f32[8,128]{1,0:T(8,128)S(1)} %get-tuple-element.51), channel_id=1, source_target_pairs={{128,130},{130,128},{194,196},{196,194},{132,134},{134,132},{198,2... | collective-permute-start | bytes 12296 | tf_op jit(solution)/shard_map/ppermute | solution.py:522
  63.9 6.7 %collective-permute-start.11 = (f32[8,128]{1,0:T(8,128)S(1)}, f32[8,128]{1,0:T(8,128)S(1)}, u32[]{:S(2)}, u32[]{:S(2)}) collective-permute-start(f32[8,128]{1,0:T(8,128)S(1)} %get-tuple-element.53), channel_id=1, source_target_pairs={{192,128},{128,192},{130,194},{194,130},{196,132},{132,196},{134,1... | collective-permute-start | bytes 12296 | tf_op jit(solution)/shard_map/ppermute | solution.py:522
  65.8 5.8 %collective-permute-start.12 = (f32[8,128]{1,0:T(8,128)S(1)}, f32[8,128]{1,0:T(8,128)S(1)}, u32[]{:S(2)}, u32[]{:S(2)}) collective-permute-start(f32[8,128]{1,0:T(8,128)S(1)} %get-tuple-element.54), channel_id=1, source_target_pairs={{128,130},{130,128},{194,196},{196,194},{132,134},{134,132},{198,2... | collective-permute-start | bytes 12296 | tf_op jit(solution)/shard_map/ppermute | solution.py:522
  74.8 28.1 %all-to-all-start.1 = ((f32[384,2,128]{2,1,0:T(2,128)}), f32[384,2,128]{2,1,0:T(2,128)S(1)}, u32[]{:S(2)}, u32[]{:S(2)}) async-start(f32[384,2,128]{2,1,0:T(2,128)} %get-tuple-element.57), calls=%async_computation.1 | async-start | bytes 786432 | tf_op jit(solution)/shard_map/all_to_all | solution.py:589
  89.5 19.7 %collective-permute-start.13 = (f32[3,256]{1,0:T(4,128)S(1)}, f32[3,256]{1,0:T(4,128)S(1)}, u32[]{:S(2)}, u32[]{:S(2)}) collective-permute-start(f32[3,256]{1,0:T(4,128)S(1)} %get-tuple-element.56), channel_id=1, source_target_pairs={{64,0},{0,1},{2,2},{66,3},{68,4},{4,5},{6,6},{70,7},{78,8},{14,9},... | collective-permute-start | bytes 9224 | tf_op jit(solution)/shard_map/ppermute | solution.py:522
  103.1 7.0 %collective-permute-start.14 = (f32[3,256]{1,0:T(4,128)S(1)}, f32[3,256]{1,0:T(4,128)S(1)}, u32[]{:S(2)}, u32[]{:S(2)}) collective-permute-start(f32[3,256]{1,0:T(4,128)S(1)} %shard_map.156), channel_id=1, source_target_pairs={{0,128},{128,0},{1,129},{129,1},{2,130},{130,2},{3,131},{131,3},{4... | collective-permute-start | bytes 9224 | tf_op jit(solution)/shard_map/ppermute | solution.py:592

commit v12 on v5

--- a/solution.py
+++ b/solution.py
@@ -20,7 +20,7 @@
 TERM_CHUNK, TERM_UNROLL = 64, 4
 STATIC_CHUNK = 32
 RADIAL_SLOTS = 8
-MESSAGE_SLOTS = 8
+MESSAGE_SLOTS = (8, 16)
 
 
 def call(body, outs, held, far=(), scratch=(), copies=0, far_outs=0, loose=0):
@@ -208,6 +208,10 @@
 
         second_w, third_w = both(0), both(1)
 
+        def part_out(k):
+            part = pl.ds(pl.multiple_of(k * step, step), step)
+            return pltpu.make_async_copy(third.at[:, part], third_far.at[:, part], done.at[2 + k])
+
         def some_slots(k, carry):
             found = join3(dot(pieces, one_hot(slot_row(slots, k * RADIAL_SLOTS, RADIAL_SLOTS), depth)))
             offset = here - found
@@ -219,10 +223,12 @@
             hidden = silu(dot(second_w, hidden)).astype(BF16)
             start = pl.multiple_of(k * step, step)
             third[:, pl.ds(start, step)] = silu(dot(third_w, hidden)).astype(BF16)
+            part_out(k).start()
             return carry
 
         lax.fori_loop(0, slot_count // RADIAL_SLOTS, some_slots, 0)
-        fetch(((third, third_far),), done, 2)()
+        for k in range(slot_count // RADIAL_SLOTS):
+            part_out(k).wait()
 
 
 def lend_pieces(values, picks, lent_a, lent_b):
@@ -270,22 +276,23 @@
 def message(layer, hidden, table, third, out_t, node_t, slots, total):
     slot_count = slots.shape[0]
     width = slots.shape[1]
-    step = MESSAGE_SLOTS * width
+    together = MESSAGE_SLOTS[layer]
+    step = together * width
     total[...] = jnp.zeros_like(total)
 
     def some_slots(k, carry):
-        row = slot_row(slots, k * MESSAGE_SLOTS, MESSAGE_SLOTS)
+        row = slot_row(slots, k * together, together)
         picked = dot(table, one_hot(row, table.shape[1]))
         start = pl.multiple_of(k * step, step)
         weight = dot(out_t, third[layer * 64 : layer * 64 + 64, pl.ds(start, step)])
         product = weight * picked
         part = product[:, 0:width]
-        for i in range(1, MESSAGE_SLOTS):
+        for i in range(1, together):
             part = part + product[:, i * width : (i + 1) * width]
         total[...] += part
         return carry
 
-    lax.fori_loop(0, slot_count // MESSAGE_SLOTS, some_slots, 0)
+    lax.fori_loop(0, slot_count // together, some_slots, 0)
     mean = (total[...] * (1.0 / slot_count)).astype(BF16)
     return (hidden.astype(F32) + silu(dot(node_t, mean))).astype(BF16)
 
@@ -474,6 +481,10 @@
     )
 
 
+def finish_kernel(result, share, result_far, share_far, done):
+    fetch(((result, result_far), (share, share_far)), done)()
+
+
 def placed(block):
     y_half, plane, step, side = block // 64, block // 8 % 8, block // 2 % 4, block % 2
     x = 3 - step if plane % 2 else step
@@ -532,7 +543,8 @@
     third_shape = (LAYERS * radial_in.shape[2], slot_count * width)
     (third,) = call(
         radial_kernel, [(third_shape, BF16)], (pack, rim_a, rim_b), (radial_in, radial_mid),
-        [pltpu.VMEM(radial_in.shape, BF16), pltpu.VMEM(radial_mid.shape, BF16), pltpu.VMEM(third_shape, BF16)], 3, 1,
+        [pltpu.VMEM(radial_in.shape, BF16), pltpu.VMEM(radial_mid.shape, BF16), pltpu.VMEM(third_shape, BF16)],
+        2 + slot_count // RADIAL_SLOTS, 1,
     )
     moment = pltpu.VMEM((depth, 8), F32)
     total = pltpu.VMEM((channels, width), F32)
@@ -567,7 +579,9 @@
     pieces = lax.all_to_all(spread, DOM, 0, 0, tiled=True).reshape(members, 3, 2, half)
     (share,) = call(gather_kernel, [((3, width), F32)], (pieces,))
     result = move(result, itself, place, same)
-    return result, lax.ppermute(share, "grp", [(0, 1), (1, 0)])
+    share = lax.ppermute(share, "grp", [(0, 1), (1, 0)])
+    whole = ((3, width), F32)
+    return tuple(call(finish_kernel, [whole, whole], (result, share), copies=2, far_outs=2))
 
 
 def solution(mesh):

time: 111 us -> 110 us (level)
  local copies, waits for them, and re-layouts: 2.05 us -> 0.87 us
    unnamed x2 -> x0, local copies, waits for them, and re-layouts: 1.18 us -> none
    pallas_call x8 -> x9, Pallas kernels: 13.5 us -> 14.2 us  [call(): pl.pallas_call(body, out_shape=[jax.ShapeDtypeStruct(s, d) for s, d in ou...]
where the time goes in v12:
time: 110 us
  starting transfers between devices  68.7 us (62%)
  waiting for transfers between devices  24.9 us (23%)
  Pallas kernels  14.2 us (13%)
    ppermute x13, starting transfers between devices, move(): lax.ppermute(value, EVERY, [(source[a] + g * members, target[b] + g * mem...  32 us
    all_to_all x1, starting transfers between devices, local(): lax.all_to_all(spread, DOM, 0, 0, tiled=True).reshape(members, 3, 2, half)  14.7 us
    pallas_call x9, Pallas kernels, call(): pl.pallas_call(body, out_shape=[jax.ShapeDtypeStruct(s, d) for s, d in ou...  14.2 us
    ppermute x13, waiting for transfers between devices, move(): lax.ppermute(value, EVERY, [(source[a] + g * members, target[b] + g * mem...  13.9 us
    all_to_all x1, starting transfers between devices, local(): lax.all_to_all(copies, DOM, 0, 0, tiled=True).reshape(2 * members, 4, half)  13.8 us
    all_to_all x1, waiting for transfers between devices, local(): lax.all_to_all(spread, DOM, 0, 0, tiled=True).reshape(members, 3, 2, half)  9.38 us
    ppermute x1, starting transfers between devices, local(): share = lax.ppermute(share, 'grp', [(0, 1), (1, 0)])  4.83 us
    ppermute x1, starting transfers between devices, local(): partner = lax.ppermute(mine, 'grp', [(0, 1), (1, 0)])  3.33 us
  transfers between devices with their start and end apart: 17, of which 8 were waited for; matrix products, arithmetic and copies ran while one was open for 0% of the time, Pallas kernels for 3%

profile of v12, /device:TPU:1, one launch (start us, length us, event | category | flops | bytes accessed | tf_op | source)
XLA Modules:
  0.0 109.6 jit_solution(13280230881700370018)
XLA Ops:
  0.6 1.0 shard_map.149
  1.7 3.3 %collective-permute-start.6 = (f32[2,4,128]{2,1,0:T(4,128)S(1)}, f32[2,4,128]{2,1,0:T(4,128)S(1)}, u32[]{:S(2)}, u32[]{:S(2)}) collective-permute-start(f32[2,4,128]{2,1,0:T(4,128)S(1)} %get-tuple-element.40), channel_id=1, source_target_pairs={{0,128},{128,0},{1,129},{129,1},{2,130},{130,2},{3,131},{131,3},{4... | collective-permute-start | bytes 12296 | tf_op jit(solution)/shard_map/ppermute | solution.py:532
  5.0 0.8 collective-permute-done.6
  5.8 0.9 broadcast_in_dim.17
  6.7 13.8 %all-to-all-start = ((f32[128,2,4,128]{3,2,1,0:T(4,128)}), f32[128,2,4,128]{3,2,1,0:T(4,128)S(1)}, u32[]{:S(2)}, u32[]{:S(2)}) async-start(f32[128,2,4,128]{3,2,1,0:T(4,128)} %broadcast_in_dim.17), calls=%async_computation | async-start | bytes 1048576 | tf_op jit(solution)/shard_map/all_to_all | solution.py:534
  20.5 0.7 collective-permute-start.3
  21.1 2.8 %collective-permute-start = (f32[48,256]{1,0:T(8,128)S(1)}, f32[48,256]{1,0:T(8,128)S(1)}, u32[]{:S(2)}, u32[]{:S(2)}) collective-permute-start(f32[48,256]{1,0:T(8,128)S(1)} %get-tuple-element.30), channel_id=1, source_target_pairs={{0,64},{1,0},{2,2},{3,66},{4,68},{5,4},{6,6},{7,70},{8,78},{9,14},... | collective-permute-start | bytes 147464 | tf_op jit(solution)/shard_map/ppermute | solution.py:514
  23.9 0.7 collective-permute-start.1
  24.6 1.3 %collective-permute-start.2 = (f32[8,128]{1,0:T(8,128)S(1)}, f32[8,128]{1,0:T(8,128)S(1)}, u32[]{:S(2)}, u32[]{:S(2)}) collective-permute-start(f32[8,128]{1,0:T(8,128)S(1)} %get-tuple-element.32), channel_id=1, source_target_pairs={{1,2},{2,0},{3,68},{4,66},{5,6},{6,4},{7,78},{8,70},{9,12},{10,14}... | collective-permute-start | bytes 12296 | tf_op jit(solution)/shard_map/ppermute | solution.py:514
  25.9 0.0 collective-permute-done.1.rim_a
  25.9 8.6 %collective-permute-done.2.rim_b = f32[8,128]{1,0:T(8,128)S(1)} collective-permute-done((f32[8,128]{1,0:T(8,128)S(1)}, f32[8,128]{1,0:T(8,128)S(1)}, u32[]{:S(2)}, u32[]{:S(2)}) %collective-permute-start.2) | collective-permute-done | bytes 4128 | tf_op jit(solution)/shard_map/ppermute | solution.py:514
  34.6 0.0 collective-permute-done.pack
  34.6 0.0 collective-permute-done.3.features_far
  34.6 2.7 %shard_map.150 = (bf16[256,256]{1,0:T(8,128)(2,1)S(1)}, f32[512,256]{1,0:T(8,128)S(1)}, f32[512,256]{1,0:T(8,128)S(1)}, f32[8,256]{1,0:T(8,128)S(1)}, f32[512,8]...) custom-call(f32[48,256]{1,0:T(8,128)S(1)} %collective-permute-done.pack, ...), custom_call_target="tpu_custom_call" | custom-call | tf_op jit(solution)/shard_map/pallas_call | solution.py:27
  37.3 2.6 %collective-permute-start.4 = (bf16[256,128]{1,0:T(8,128)(2,1)S(1)}, bf16[256,128]{1,0:T(8,128)(2,1)S(1)}, u32[]{:S(2)}, u32[]{:S(2)}) collective-permute-start(bf16[256,128]{1,0:T(8,128)(2,1)S(1)} %get-tuple-element.34), channel_id=1, source_target_pairs={{64,0},{0,64},{2,66},{66,2},{68,4},{4,68},{6,70},{70,6},{78,14},{1... | collective-permute-start | bytes 196616 | tf_op jit(solution)/shard_map/ppermute | solution.py:514
  39.8 3.3 %collective-permute-start.5 = (bf16[256,128]{1,0:T(8,128)(2,1)S(1)}, bf16[256,128]{1,0:T(8,128)(2,1)S(1)}, u32[]{:S(2)}, u32[]{:S(2)}) collective-permute-start(bf16[256,128]{1,0:T(8,128)(2,1)S(1)} %get-tuple-element.35), channel_id=1, source_target_pairs={{0,2},{2,0},{66,68},{68,66},{4,6},{6,4},{70,78},{78,70},{14,12},{1... | collective-permute-start | bytes 196616 | tf_op jit(solution)/shard_map/ppermute | solution.py:514
  43.1 0.1 shard_map.151.third_far
  43.2 0.0 collective-permute-done.4.side_a
  43.2 1.6 %collective-permute-done.5.side_b = bf16[256,128]{1,0:T(8,128)(2,1)S(1)} collective-permute-done((bf16[256,128]{1,0:T(8,128)(2,1)S(1)}, bf16[256,128]{1,0:T(8,128)(2,1)S(1)}, u32[]{:S(2)}, u32[]{:S(2)}) %collective-permute-start.5) | collective-permute-done | bytes 65568 | tf_op jit(solution)/shard_map/ppermute | solution.py:514
  44.8 0.0 all-to-all-done
  44.8 3.8 %shard_map.152 = (f32[8,256]{1,0:T(8,128)S(1)}, f32[4,4,128]{2,1,0:T(4,128)S(1)}, bf16[256,256]{1,0:T(8,128)(2,1)S(1)}, bf16[256,256]{1,0:T(8,128)(2,1)S(1)}, f3...) custom-call(f32[48,256]{1,0:T(8,128)S(1)} %collective-permute-done.pack,, ...), custom_call_target="tpu_custom_call" | custom-call | tf_op jit(solution)/shard_map/pallas_call | solution.py:27
  48.7 0.1 collective-permute-start.7
  48.8 4.7 %collective-permute-start.8 = (bf16[256,128]{1,0:T(8,128)(2,1)S(1)}, bf16[256,128]{1,0:T(8,128)(2,1)S(1)}, u32[]{:S(2)}, u32[]{:S(2)}) collective-permute-start(bf16[256,128]{1,0:T(8,128)(2,1)S(1)} %get-tuple-element.45), channel_id=1, source_target_pairs={{0,2},{2,0},{66,68},{68,66},{4,6},{6,4},{70,78},{78,70},{14,12},{1... | collective-permute-start | bytes 196616 | tf_op jit(solution)/shard_map/ppermute | solution.py:514
  53.5 0.0 collective-permute-done.7.side_a
  53.5 1.6 %collective-permute-done.8.side_b = bf16[256,128]{1,0:T(8,128)(2,1)S(1)} collective-permute-done((bf16[256,128]{1,0:T(8,128)(2,1)S(1)}, bf16[256,128]{1,0:T(8,128)(2,1)S(1)}, u32[]{:S(2)}, u32[]{:S(2)}) %collective-permute-start.8) | collective-permute-done | bytes 65568 | tf_op jit(solution)/shard_map/ppermute | solution.py:514
  55.1 1.2 %shard_map.153 = (f32[8,256]{1,0:T(8,128)S(1)}, f32[8,256]{1,0:T(8,128)S(1)}, f32[8,128]{1,0:T(8,128)S(1)}, f32[8,128]{1,0:T(8,128)S(1)}) custom-call(bf16[256,256]{1,0:T(8,128)(2,1)S(1)} %get-tuple-element.42.hidden, bf16[256,256]{1,0:T(8,128)(2,1)S(1)} %get-tuple-element.43.lifted, bf16[256,128]{1,0:T(8,128)(2,1)S(1)} %collective-permute-done.7.side_a, ...), custom_call_target="tpu_custom_call" | custom-call | tf_op jit(solution)/shard_map/pallas_call | solution.py:27
  56.4 1.9 %collective-permute-start.9 = (f32[8,128]{1,0:T(8,128)S(1)}, f32[8,128]{1,0:T(8,128)S(1)}, u32[]{:S(2)}, u32[]{:S(2)}) collective-permute-start(f32[8,128]{1,0:T(8,128)S(1)} %get-tuple-element.50), channel_id=1, source_target_pairs={{192,128},{128,192},{130,194},{194,130},{196,132},{132,196},{134,1... | collective-permute-start | bytes 12296 | tf_op jit(solution)/shard_map/ppermute | solution.py:514
  58.3 3.4 %collective-permute-start.10 = (f32[8,128]{1,0:T(8,128)S(1)}, f32[8,128]{1,0:T(8,128)S(1)}, u32[]{:S(2)}, u32[]{:S(2)}) collective-permute-start(f32[8,128]{1,0:T(8,128)S(1)} %get-tuple-element.51), channel_id=1, source_target_pairs={{128,130},{130,128},{194,196},{196,194},{132,134},{134,132},{198,2... | collective-permute-start | bytes 12296 | tf_op jit(solution)/shard_map/ppermute | solution.py:514
  61.7 0.0 collective-permute-done.9.side_a
  61.7 1.0 collective-permute-done.10.side_b
  62.6 1.2 %shard_map.154 = (f32[8,256]{1,0:T(8,128)S(1)}, f32[8,128]{1,0:T(8,128)S(1)}, f32[8,128]{1,0:T(8,128)S(1)}) custom-call(f32[8,128]{1,0:T(8,128)S(1)} %collective-permute-done.9.side_a, f32[8,128]{1,0:T(8,128)S(1)} %collective-permute-done.10.side_b, f32[48,256]{1,0:T(8,128)S(1)} %collective-permute-done.pack, f32[512,256]{1,0:T(8,128)S(1)} %get-tuple-element.36.w3, ...), custom_call_target="tpu_custom_call" | custom-call | tf_op jit(solution)/shard_map/pallas_call | solution.py:27
  63.8 1.9 %collective-permute-start.11 = (f32[8,128]{1,0:T(8,128)S(1)}, f32[8,128]{1,0:T(8,128)S(1)}, u32[]{:S(2)}, u32[]{:S(2)}) collective-permute-start(f32[8,128]{1,0:T(8,128)S(1)} %get-tuple-element.53), channel_id=1, source_target_pairs={{192,128},{128,192},{130,194},{194,130},{196,132},{132,196},{134,1... | collective-permute-start | bytes 12296 | tf_op jit(solution)/shard_map/ppermute | solution.py:514
  65.7 4.8 %collective-permute-start.12 = (f32[8,128]{1,0:T(8,128)S(1)}, f32[8,128]{1,0:T(8,128)S(1)}, u32[]{:S(2)}, u32[]{:S(2)}) collective-permute-start(f32[8,128]{1,0:T(8,128)S(1)} %get-tuple-element.54), channel_id=1, source_target_pairs={{128,130},{130,128},{194,196},{196,194},{132,134},{134,132},{198,2... | collective-permute-start | bytes 12296 | tf_op jit(solution)/shard_map/ppermute | solution.py:514
  70.5 0.0 collective-permute-done.11.side_a
  70.5 1.0 collective-permute-done.12.side_b
  71.5 3.4 %shard_map.155 = (f32[3,256]{1,0:T(4,128)S(1)}, f32[384,2,128]{2,1,0:T(2,128)}) custom-call(f32[4,4,128]{2,1,0:T(4,128)S(1)} %get-tuple-element.41.near, f32[48,256]{1,0:T(8,128)S(1)} %collective-permute-done.pack, f32[8,256]{1,0:T(8,128)S(1)} %get-tuple-element.48.charge, f32[8,256]{1,0:T(8,128)S(1)} %get-tuple-element.49.outside_row, ...), custom_call_target="tpu_custom_call" | custom-call | tf_op jit(solution)/shard_map/pallas_call | solution.py:27
  74.9 14.7 %all-to-all-start.1 = ((f32[384,2,128]{2,1,0:T(2,128)}), f32[384,2,128]{2,1,0:T(2,128)S(1)}, u32[]{:S(2)}, u32[]{:S(2)}) async-start(f32[384,2,128]{2,1,0:T(2,128)} %get-tuple-element.57), calls=%async_computation.1 | async-start | bytes 786432 | tf_op jit(solution)/shard_map/all_to_all | solution.py:579
  89.7 4.0 %collective-permute-start.13 = (f32[3,256]{1,0:T(4,128)S(1)}, f32[3,256]{1,0:T(4,128)S(1)}, u32[]{:S(2)}, u32[]{:S(2)}) collective-permute-start(f32[3,256]{1,0:T(4,128)S(1)} %get-tuple-element.56), channel_id=1, source_target_pairs={{64,0},{0,1},{2,2},{66,3},{68,4},{4,5},{6,6},{70,7},{78,8},{14,9},... | collective-permute-start | bytes 9224 | tf_op jit(solution)/shard_map/ppermute | solution.py:514
  93.7 9.4 %all-to-all-done.1 = f32[384,2,128]{2,1,0:T(2,128)S(1)} async-done(((f32[384,2,128]{2,1,0:T(2,128)}), f32[384,2,128]{2,1,0:T(2,128)S(1)}, u32[]{:S(2)}, u32[]{:S(2)}) %all-to-all-start.1) | async-done | bytes 393248 | tf_op jit(solution)/shard_map/all_to_all | solution.py:579
  103.0 0.2 shard_map.156
  103.2 4.8 %collective-permute-start.14 = (f32[3,256]{1,0:T(4,128)S(1)}, f32[3,256]{1,0:T(4,128)S(1)}, u32[]{:S(2)}, u32[]{:S(2)}) collective-permute-start(f32[3,256]{1,0:T(4,128)S(1)} %shard_map.156), channel_id=1, source_target_pairs={{0,128},{128,0},{1,129},{129,1},{2,130},{130,2},{3,131},{131,3},{4... | collective-permute-start | bytes 9224 | tf_op jit(solution)/shard_map/ppermute | solution.py:582
  108.0 0.0 collective-permute-done.13.result
  108.0 0.8 collective-permute-done.14.share
  108.9 0.6 shard_map.157
Async XLA Ops:
  1.7 4.2 %collective-permute-start.6 = (f32[2,4,128]{2,1,0:T(4,128)S(1)}, f32[2,4,128]{2,1,0:T(4,128)S(1)}, u32[]{:S(2)}, u32[]{:S(2)}) collective-permute-start(f32[2,4,128]{2,1,0:T(4,128)S(1)} %get-tuple-element.40), channel_id=1, source_target_pairs={{0,128},{128,0},{1,129},{129,1},{2,130},{130,2},{3,131},{131,3},{4... | collective-permute-start | bytes 12296 | tf_op jit(solution)/shard_map/ppermute | solution.py:532
  6.7 38.2 %all-to-all-start = ((f32[128,2,4,128]{3,2,1,0:T(4,128)}), f32[128,2,4,128]{3,2,1,0:T(4,128)S(1)}, u32[]{:S(2)}, u32[]{:S(2)}) async-start(f32[128,2,4,128]{3,2,1,0:T(4,128)} %broadcast_in_dim.17), calls=%async_computation | async-start | bytes 1048576 | tf_op jit(solution)/shard_map/all_to_all | solution.py:534
  20.5 14.1 %collective-permute-start.3 = (bf16[256,256]{1,0:T(8,128)(2,1)}, bf16[256,256]{1,0:T(8,128)(2,1)S(1)}, u32[]{:S(2)}, u32[]{:S(2)}) collective-permute-start(bf16[256,256]{1,0:T(8,128)(2,1)} %param.17), channel_id=1, source_target_pairs={{0,64},{1,0},{2,2},{3,66},{4,68},{5,4},{6,6},{7,70},{8,78},{9,14},... | collective-permute-start | bytes 393224 | tf_op jit(solution)/shard_map/ppermute | solution.py:514
  21.1 13.4 %collective-permute-start = (f32[48,256]{1,0:T(8,128)S(1)}, f32[48,256]{1,0:T(8,128)S(1)}, u32[]{:S(2)}, u32[]{:S(2)}) collective-permute-start(f32[48,256]{1,0:T(8,128)S(1)} %get-tuple-element.30), channel_id=1, source_target_pairs={{0,64},{1,0},{2,2},{3,66},{4,68},{5,4},{6,6},{7,70},{8,78},{9,14},... | collective-permute-start | bytes 147464 | tf_op jit(solution)/shard_map/ppermute | solution.py:514
  23.9 2.0 %collective-permute-start.1 = (f32[8,128]{1,0:T(8,128)S(1)}, f32[8,128]{1,0:T(8,128)S(1)}, u32[]{:S(2)}, u32[]{:S(2)}) collective-permute-start(f32[8,128]{1,0:T(8,128)S(1)} %get-tuple-element.31), channel_id=1, source_target_pairs={{0,0},{1,64},{2,66},{3,2},{4,4},{5,68},{6,70},{7,6},{8,14},{9,78},... | collective-permute-start | bytes 12296 | tf_op jit(solution)/shard_map/ppermute | solution.py:514
  24.6 9.9 %collective-permute-start.2 = (f32[8,128]{1,0:T(8,128)S(1)}, f32[8,128]{1,0:T(8,128)S(1)}, u32[]{:S(2)}, u32[]{:S(2)}) collective-permute-start(f32[8,128]{1,0:T(8,128)S(1)} %get-tuple-element.32), channel_id=1, source_target_pairs={{1,2},{2,0},{3,68},{4,66},{5,6},{6,4},{7,78},{8,70},{9,12},{10,14}... | collective-permute-start | bytes 12296 | tf_op jit(solution)/shard_map/ppermute | solution.py:514
  37.3 5.9 %collective-permute-start.4 = (bf16[256,128]{1,0:T(8,128)(2,1)S(1)}, bf16[256,128]{1,0:T(8,128)(2,1)S(1)}, u32[]{:S(2)}, u32[]{:S(2)}) collective-permute-start(bf16[256,128]{1,0:T(8,128)(2,1)S(1)} %get-tuple-element.34), channel_id=1, source_target_pairs={{64,0},{0,64},{2,66},{66,2},{68,4},{4,68},{6,70},{70,6},{78,14},{1... | collective-permute-start | bytes 196616 | tf_op jit(solution)/shard_map/ppermute | solution.py:514
  39.8 5.0 %collective-permute-start.5 = (bf16[256,128]{1,0:T(8,128)(2,1)S(1)}, bf16[256,128]{1,0:T(8,128)(2,1)S(1)}, u32[]{:S(2)}, u32[]{:S(2)}) collective-permute-start(bf16[256,128]{1,0:T(8,128)(2,1)S(1)} %get-tuple-element.35), channel_id=1, source_target_pairs={{0,2},{2,0},{66,68},{68,66},{4,6},{6,4},{70,78},{78,70},{14,12},{1... | collective-permute-start | bytes 196616 | tf_op jit(solution)/shard_map/ppermute | solution.py:514
  48.7 4.8 %collective-permute-start.7 = (bf16[256,128]{1,0:T(8,128)(2,1)S(1)}, bf16[256,128]{1,0:T(8,128)(2,1)S(1)}, u32[]{:S(2)}, u32[]{:S(2)}) collective-permute-start(bf16[256,128]{1,0:T(8,128)(2,1)S(1)} %get-tuple-element.44), channel_id=1, source_target_pairs={{64,0},{0,64},{2,66},{66,2},{68,4},{4,68},{6,70},{70,6},{78,14},{1... | collective-permute-start | bytes 196616 | tf_op jit(solution)/shard_map/ppermute | solution.py:514
  48.8 6.3 %collective-permute-start.8 = (bf16[256,128]{1,0:T(8,128)(2,1)S(1)}, bf16[256,128]{1,0:T(8,128)(2,1)S(1)}, u32[]{:S(2)}, u32[]{:S(2)}) collective-permute-start(bf16[256,128]{1,0:T(8,128)(2,1)S(1)} %get-tuple-element.45), channel_id=1, source_target_pairs={{0,2},{2,0},{66,68},{68,66},{4,6},{6,4},{70,78},{78,70},{14,12},{1... | collective-permute-start | bytes 196616 | tf_op jit(solution)/shard_map/ppermute | solution.py:514
  56.4 5.3 %collective-permute-start.9 = (f32[8,128]{1,0:T(8,128)S(1)}, f32[8,128]{1,0:T(8,128)S(1)}, u32[]{:S(2)}, u32[]{:S(2)}) collective-permute-start(f32[8,128]{1,0:T(8,128)S(1)} %get-tuple-element.50), channel_id=1, source_target_pairs={{192,128},{128,192},{130,194},{194,130},{196,132},{132,196},{134,1... | collective-permute-start | bytes 12296 | tf_op jit(solution)/shard_map/ppermute | solution.py:514
  58.3 4.4 %collective-permute-start.10 = (f32[8,128]{1,0:T(8,128)S(1)}, f32[8,128]{1,0:T(8,128)S(1)}, u32[]{:S(2)}, u32[]{:S(2)}) collective-permute-start(f32[8,128]{1,0:T(8,128)S(1)} %get-tuple-element.51), channel_id=1, source_target_pairs={{128,130},{130,128},{194,196},{196,194},{132,134},{134,132},{198,2... | collective-permute-start | bytes 12296 | tf_op jit(solution)/shard_map/ppermute | solution.py:514
  63.8 6.7 %collective-permute-start.11 = (f32[8,128]{1,0:T(8,128)S(1)}, f32[8,128]{1,0:T(8,128)S(1)}, u32[]{:S(2)}, u32[]{:S(2)}) collective-permute-start(f32[8,128]{1,0:T(8,128)S(1)} %get-tuple-element.53), channel_id=1, source_target_pairs={{192,128},{128,192},{130,194},{194,130},{196,132},{132,196},{134,1... | collective-permute-start | bytes 12296 | tf_op jit(solution)/shard_map/ppermute | solution.py:514
  65.7 5.8 %collective-permute-start.12 = (f32[8,128]{1,0:T(8,128)S(1)}, f32[8,128]{1,0:T(8,128)S(1)}, u32[]{:S(2)}, u32[]{:S(2)}) collective-permute-start(f32[8,128]{1,0:T(8,128)S(1)} %get-tuple-element.54), channel_id=1, source_target_pairs={{128,130},{130,128},{194,196},{196,194},{132,134},{134,132},{198,2... | collective-permute-start | bytes 12296 | tf_op jit(solution)/shard_map/ppermute | solution.py:514
  74.9 28.1 %all-to-all-start.1 = ((f32[384,2,128]{2,1,0:T(2,128)}), f32[384,2,128]{2,1,0:T(2,128)S(1)}, u32[]{:S(2)}, u32[]{:S(2)}) async-start(f32[384,2,128]{2,1,0:T(2,128)} %get-tuple-element.57), calls=%async_computation.1 | async-start | bytes 786432 | tf_op jit(solution)/shard_map/all_to_all | solution.py:579
  89.7 18.4 %collective-permute-start.13 = (f32[3,256]{1,0:T(4,128)S(1)}, f32[3,256]{1,0:T(4,128)S(1)}, u32[]{:S(2)}, u32[]{:S(2)}) collective-permute-start(f32[3,256]{1,0:T(4,128)S(1)} %get-tuple-element.56), channel_id=1, source_target_pairs={{64,0},{0,1},{2,2},{66,3},{68,4},{4,5},{6,6},{70,7},{78,8},{14,9},... | collective-permute-start | bytes 9224 | tf_op jit(solution)/shard_map/ppermute | solution.py:514
  103.2 5.7 %collective-permute-start.14 = (f32[3,256]{1,0:T(4,128)S(1)}, f32[3,256]{1,0:T(4,128)S(1)}, u32[]{:S(2)}, u32[]{:S(2)}) collective-permute-start(f32[3,256]{1,0:T(4,128)S(1)} %shard_map.156), channel_id=1, source_target_pairs={{0,128},{128,0},{1,129},{129,1},{2,130},{130,2},{3,131},{131,3},{4... | collective-permute-start | bytes 9224 | tf_op jit(solution)/shard_map/ppermute | solution.py:582

commit v13 on v12

--- a/solution.py
+++ b/solution.py
@@ -15,10 +15,10 @@
 BF16 = jnp.bfloat16
 VMEM = pl.BlockSpec(memory_space=pltpu.VMEM)
 ANY = pl.BlockSpec(memory_space=pl.ANY)
-SWEEP_CHUNK, SWEEP_UNROLL = 32, 4
-FIELD_CHUNK, FIELD_UNROLL = 32, 4
+SWEEP_CHUNK, SWEEP_UNROLL = 32, 16
+FIELD_CHUNK, FIELD_UNROLL = 32, 8
 TERM_CHUNK, TERM_UNROLL = 64, 4
-STATIC_CHUNK = 32
+STATIC_CHUNK = 64
 RADIAL_SLOTS = 8
 MESSAGE_SLOTS = (8, 16)
 

time: 110 us -> 110 us (level)
  Pallas kernels: 14.2 us -> 12.5 us
  starting transfers between devices: 68.7 us -> 70.1 us
    pallas_call x9, Pallas kernels: 14.2 us -> 12.5 us  [call(): pl.pallas_call(body, out_shape=[jax.ShapeDtypeStruct(s, d) for s, d in ou...]
where the time goes in v13:
time: 110 us; the launch traced here: 109 us
  starting transfers between devices  70.1 us (64%)
  waiting for transfers between devices  24.9 us (23%)
  Pallas kernels  12.5 us (11%)
    ppermute x13, starting transfers between devices, move(): lax.ppermute(value, EVERY, [(source[a] + g * members, target[b] + g * mem...  32 us
    all_to_all x1, starting transfers between devices, local(): lax.all_to_all(spread, DOM, 0, 0, tiled=True).reshape(members, 3, 2, half)  15 us
    ppermute x13, waiting for transfers between devices, move(): lax.ppermute(value, EVERY, [(source[a] + g * members, target[b] + g * mem...  13.9 us
    all_to_all x1, starting transfers between devices, local(): lax.all_to_all(copies, DOM, 0, 0, tiled=True).reshape(2 * members, 4, half)  13.8 us
    pallas_call x9, Pallas kernels, call(): pl.pallas_call(body, out_shape=[jax.ShapeDtypeStruct(s, d) for s, d in ou...  12.5 us
    all_to_all x1, waiting for transfers between devices, local(): lax.all_to_all(spread, DOM, 0, 0, tiled=True).reshape(members, 3, 2, half)  9.39 us
    ppermute x1, starting transfers between devices, local(): share = lax.ppermute(share, 'grp', [(0, 1), (1, 0)])  5.92 us
    ppermute x1, starting transfers between devices, local(): partner = lax.ppermute(mine, 'grp', [(0, 1), (1, 0)])  3.33 us
  transfers between devices with their start and end apart: 17, of which 8 were waited for; matrix products, arithmetic and copies ran while one was open for 0% of the time, Pallas kernels for 3%

profile of v13, /device:TPU:1, one launch (start us, length us, event | category | flops | bytes accessed | tf_op | source)
XLA Modules:
  0.0 109.3 jit_solution(5032684048623360161)
XLA Ops:
  0.6 1.0 shard_map.149
  1.7 3.3 %collective-permute-start.6 = (f32[2,4,128]{2,1,0:T(4,128)S(1)}, f32[2,4,128]{2,1,0:T(4,128)S(1)}, u32[]{:S(2)}, u32[]{:S(2)}) collective-permute-start(f32[2,4,128]{2,1,0:T(4,128)S(1)} %get-tuple-element.40), channel_id=1, source_target_pairs={{0,128},{128,0},{1,129},{129,1},{2,130},{130,2},{3,131},{131,3},{4... | collective-permute-start | bytes 12296 | tf_op jit(solution)/shard_map/ppermute | solution.py:532
  5.0 0.8 collective-permute-done.6
  5.8 0.9 broadcast_in_dim.17
  6.7 13.8 %all-to-all-start = ((f32[128,2,4,128]{3,2,1,0:T(4,128)}), f32[128,2,4,128]{3,2,1,0:T(4,128)S(1)}, u32[]{:S(2)}, u32[]{:S(2)}) async-start(f32[128,2,4,128]{3,2,1,0:T(4,128)} %broadcast_in_dim.17), calls=%async_computation | async-start | bytes 1048576 | tf_op jit(solution)/shard_map/all_to_all | solution.py:534
  20.5 0.7 collective-permute-start.3
  21.1 2.8 %collective-permute-start = (f32[48,256]{1,0:T(8,128)S(1)}, f32[48,256]{1,0:T(8,128)S(1)}, u32[]{:S(2)}, u32[]{:S(2)}) collective-permute-start(f32[48,256]{1,0:T(8,128)S(1)} %get-tuple-element.30), channel_id=1, source_target_pairs={{0,64},{1,0},{2,2},{3,66},{4,68},{5,4},{6,6},{7,70},{8,78},{9,14},... | collective-permute-start | bytes 147464 | tf_op jit(solution)/shard_map/ppermute | solution.py:514
  23.9 0.7 collective-permute-start.1
  24.6 1.3 %collective-permute-start.2 = (f32[8,128]{1,0:T(8,128)S(1)}, f32[8,128]{1,0:T(8,128)S(1)}, u32[]{:S(2)}, u32[]{:S(2)}) collective-permute-start(f32[8,128]{1,0:T(8,128)S(1)} %get-tuple-element.32), channel_id=1, source_target_pairs={{1,2},{2,0},{3,68},{4,66},{5,6},{6,4},{7,78},{8,70},{9,12},{10,14}... | collective-permute-start | bytes 12296 | tf_op jit(solution)/shard_map/ppermute | solution.py:514
  25.9 0.0 collective-permute-done.1.rim_a
  25.9 8.6 %collective-permute-done.2.rim_b = f32[8,128]{1,0:T(8,128)S(1)} collective-permute-done((f32[8,128]{1,0:T(8,128)S(1)}, f32[8,128]{1,0:T(8,128)S(1)}, u32[]{:S(2)}, u32[]{:S(2)}) %collective-permute-start.2) | collective-permute-done | bytes 4128 | tf_op jit(solution)/shard_map/ppermute | solution.py:514
  34.6 0.0 collective-permute-done.pack
  34.6 0.0 collective-permute-done.3.features_far
  34.6 2.5 %shard_map.150 = (bf16[256,256]{1,0:T(8,128)(2,1)S(1)}, f32[512,256]{1,0:T(8,128)S(1)}, f32[512,256]{1,0:T(8,128)S(1)}, f32[8,256]{1,0:T(8,128)S(1)}, f32[512,8]...) custom-call(f32[48,256]{1,0:T(8,128)S(1)} %collective-permute-done.pack, ...), custom_call_target="tpu_custom_call" | custom-call | tf_op jit(solution)/shard_map/pallas_call | solution.py:27
  37.1 2.6 %collective-permute-start.4 = (bf16[256,128]{1,0:T(8,128)(2,1)S(1)}, bf16[256,128]{1,0:T(8,128)(2,1)S(1)}, u32[]{:S(2)}, u32[]{:S(2)}) collective-permute-start(bf16[256,128]{1,0:T(8,128)(2,1)S(1)} %get-tuple-element.34), channel_id=1, source_target_pairs={{64,0},{0,64},{2,66},{66,2},{68,4},{4,68},{6,70},{70,6},{78,14},{1... | collective-permute-start | bytes 196616 | tf_op jit(solution)/shard_map/ppermute | solution.py:514
  39.7 3.3 %collective-permute-start.5 = (bf16[256,128]{1,0:T(8,128)(2,1)S(1)}, bf16[256,128]{1,0:T(8,128)(2,1)S(1)}, u32[]{:S(2)}, u32[]{:S(2)}) collective-permute-start(bf16[256,128]{1,0:T(8,128)(2,1)S(1)} %get-tuple-element.35), channel_id=1, source_target_pairs={{0,2},{2,0},{66,68},{68,66},{4,6},{6,4},{70,78},{78,70},{14,12},{1... | collective-permute-start | bytes 196616 | tf_op jit(solution)/shard_map/ppermute | solution.py:514
  42.9 0.1 shard_map.151.third_far
  43.0 0.0 collective-permute-done.4.side_a
  43.0 1.6 %collective-permute-done.5.side_b = bf16[256,128]{1,0:T(8,128)(2,1)S(1)} collective-permute-done((bf16[256,128]{1,0:T(8,128)(2,1)S(1)}, bf16[256,128]{1,0:T(8,128)(2,1)S(1)}, u32[]{:S(2)}, u32[]{:S(2)}) %collective-permute-start.5) | collective-permute-done | bytes 65568 | tf_op jit(solution)/shard_map/ppermute | solution.py:514
  44.7 0.0 all-to-all-done
  44.7 3.2 %shard_map.152 = (f32[8,256]{1,0:T(8,128)S(1)}, f32[4,4,128]{2,1,0:T(4,128)S(1)}, bf16[256,256]{1,0:T(8,128)(2,1)S(1)}, bf16[256,256]{1,0:T(8,128)(2,1)S(1)}, f3...) custom-call(f32[48,256]{1,0:T(8,128)S(1)} %collective-permute-done.pack,, ...), custom_call_target="tpu_custom_call" | custom-call | tf_op jit(solution)/shard_map/pallas_call | solution.py:27
  47.9 0.1 collective-permute-start.7
  48.0 4.7 %collective-permute-start.8 = (bf16[256,128]{1,0:T(8,128)(2,1)S(1)}, bf16[256,128]{1,0:T(8,128)(2,1)S(1)}, u32[]{:S(2)}, u32[]{:S(2)}) collective-permute-start(bf16[256,128]{1,0:T(8,128)(2,1)S(1)} %get-tuple-element.45), channel_id=1, source_target_pairs={{0,2},{2,0},{66,68},{68,66},{4,6},{6,4},{70,78},{78,70},{14,12},{1... | collective-permute-start | bytes 196616 | tf_op jit(solution)/shard_map/ppermute | solution.py:514
  52.7 0.0 collective-permute-done.7.side_a
  52.7 1.6 %collective-permute-done.8.side_b = bf16[256,128]{1,0:T(8,128)(2,1)S(1)} collective-permute-done((bf16[256,128]{1,0:T(8,128)(2,1)S(1)}, bf16[256,128]{1,0:T(8,128)(2,1)S(1)}, u32[]{:S(2)}, u32[]{:S(2)}) %collective-permute-start.8) | collective-permute-done | bytes 65568 | tf_op jit(solution)/shard_map/ppermute | solution.py:514
  54.3 1.0 shard_map.153
  55.3 1.9 %collective-permute-start.9 = (f32[8,128]{1,0:T(8,128)S(1)}, f32[8,128]{1,0:T(8,128)S(1)}, u32[]{:S(2)}, u32[]{:S(2)}) collective-permute-start(f32[8,128]{1,0:T(8,128)S(1)} %get-tuple-element.50), channel_id=1, source_target_pairs={{192,128},{128,192},{130,194},{194,130},{196,132},{132,196},{134,1... | collective-permute-start | bytes 12296 | tf_op jit(solution)/shard_map/ppermute | solution.py:514
  57.2 3.4 %collective-permute-start.10 = (f32[8,128]{1,0:T(8,128)S(1)}, f32[8,128]{1,0:T(8,128)S(1)}, u32[]{:S(2)}, u32[]{:S(2)}) collective-permute-start(f32[8,128]{1,0:T(8,128)S(1)} %get-tuple-element.51), channel_id=1, source_target_pairs={{128,130},{130,128},{194,196},{196,194},{132,134},{134,132},{198,2... | collective-permute-start | bytes 12296 | tf_op jit(solution)/shard_map/ppermute | solution.py:514
  60.6 0.0 collective-permute-done.9.side_a
  60.6 1.0 collective-permute-done.10.side_b
  61.6 0.9 shard_map.154
  62.5 1.9 %collective-permute-start.11 = (f32[8,128]{1,0:T(8,128)S(1)}, f32[8,128]{1,0:T(8,128)S(1)}, u32[]{:S(2)}, u32[]{:S(2)}) collective-permute-start(f32[8,128]{1,0:T(8,128)S(1)} %get-tuple-element.53), channel_id=1, source_target_pairs={{192,128},{128,192},{130,194},{194,130},{196,132},{132,196},{134,1... | collective-permute-start | bytes 12296 | tf_op jit(solution)/shard_map/ppermute | solution.py:514
  64.5 4.8 %collective-permute-start.12 = (f32[8,128]{1,0:T(8,128)S(1)}, f32[8,128]{1,0:T(8,128)S(1)}, u32[]{:S(2)}, u32[]{:S(2)}) collective-permute-start(f32[8,128]{1,0:T(8,128)S(1)} %get-tuple-element.54), channel_id=1, source_target_pairs={{128,130},{130,128},{194,196},{196,194},{132,134},{134,132},{198,2... | collective-permute-start | bytes 12296 | tf_op jit(solution)/shard_map/ppermute | solution.py:514
  69.3 0.0 collective-permute-done.11.side_a
  69.3 1.0 collective-permute-done.12.side_b
  70.2 3.0 %shard_map.155 = (f32[3,256]{1,0:T(4,128)S(1)}, f32[384,2,128]{2,1,0:T(2,128)}) custom-call(f32[4,4,128]{2,1,0:T(4,128)S(1)} %get-tuple-element.41.near, f32[48,256]{1,0:T(8,128)S(1)} %collective-permute-done.pack, f32[8,256]{1,0:T(8,128)S(1)} %get-tuple-element.48.charge, f32[8,256]{1,0:T(8,128)S(1)} %get-tuple-element.49.outside_row, ...), custom_call_target="tpu_custom_call" | custom-call | tf_op jit(solution)/shard_map/pallas_call | solution.py:27
  73.2 15.0 %all-to-all-start.1 = ((f32[384,2,128]{2,1,0:T(2,128)}), f32[384,2,128]{2,1,0:T(2,128)S(1)}, u32[]{:S(2)}, u32[]{:S(2)}) async-start(f32[384,2,128]{2,1,0:T(2,128)} %get-tuple-element.57), calls=%async_computation.1 | async-start | bytes 786432 | tf_op jit(solution)/shard_map/all_to_all | solution.py:579
  88.2 4.0 %collective-permute-start.13 = (f32[3,256]{1,0:T(4,128)S(1)}, f32[3,256]{1,0:T(4,128)S(1)}, u32[]{:S(2)}, u32[]{:S(2)}) collective-permute-start(f32[3,256]{1,0:T(4,128)S(1)} %get-tuple-element.56), channel_id=1, source_target_pairs={{64,0},{0,1},{2,2},{66,3},{68,4},{4,5},{6,6},{70,7},{78,8},{14,9},... | collective-permute-start | bytes 9224 | tf_op jit(solution)/shard_map/ppermute | solution.py:514
  92.2 9.4 %all-to-all-done.1 = f32[384,2,128]{2,1,0:T(2,128)S(1)} async-done(((f32[384,2,128]{2,1,0:T(2,128)}), f32[384,2,128]{2,1,0:T(2,128)S(1)}, u32[]{:S(2)}, u32[]{:S(2)}) %all-to-all-start.1) | async-done | bytes 393248 | tf_op jit(solution)/shard_map/all_to_all | solution.py:579
  101.6 0.2 shard_map.156
  101.8 5.9 %collective-permute-start.14 = (f32[3,256]{1,0:T(4,128)S(1)}, f32[3,256]{1,0:T(4,128)S(1)}, u32[]{:S(2)}, u32[]{:S(2)}) collective-permute-start(f32[3,256]{1,0:T(4,128)S(1)} %shard_map.156), channel_id=1, source_target_pairs={{0,128},{128,0},{1,129},{129,1},{2,130},{130,2},{3,131},{131,3},{4... | collective-permute-start | bytes 9224 | tf_op jit(solution)/shard_map/ppermute | solution.py:582
  107.7 0.0 collective-permute-done.13.result
  107.7 0.8 collective-permute-done.14.share
  108.5 0.6 shard_map.157
Async XLA Ops:
  1.7 4.2 %collective-permute-start.6 = (f32[2,4,128]{2,1,0:T(4,128)S(1)}, f32[2,4,128]{2,1,0:T(4,128)S(1)}, u32[]{:S(2)}, u32[]{:S(2)}) collective-permute-start(f32[2,4,128]{2,1,0:T(4,128)S(1)} %get-tuple-element.40), channel_id=1, source_target_pairs={{0,128},{128,0},{1,129},{129,1},{2,130},{130,2},{3,131},{131,3},{4... | collective-permute-start | bytes 12296 | tf_op jit(solution)/shard_map/ppermute | solution.py:532
  6.7 38.0 %all-to-all-start = ((f32[128,2,4,128]{3,2,1,0:T(4,128)}), f32[128,2,4,128]{3,2,1,0:T(4,128)S(1)}, u32[]{:S(2)}, u32[]{:S(2)}) async-start(f32[128,2,4,128]{3,2,1,0:T(4,128)} %broadcast_in_dim.17), calls=%async_computation | async-start | bytes 1048576 | tf_op jit(solution)/shard_map/all_to_all | solution.py:534
  20.5 14.1 %collective-permute-start.3 = (bf16[256,256]{1,0:T(8,128)(2,1)}, bf16[256,256]{1,0:T(8,128)(2,1)S(1)}, u32[]{:S(2)}, u32[]{:S(2)}) collective-permute-start(bf16[256,256]{1,0:T(8,128)(2,1)} %param.17), channel_id=1, source_target_pairs={{0,64},{1,0},{2,2},{3,66},{4,68},{5,4},{6,6},{7,70},{8,78},{9,14},... | collective-permute-start | bytes 393224 | tf_op jit(solution)/shard_map/ppermute | solution.py:514
  21.1 13.4 %collective-permute-start = (f32[48,256]{1,0:T(8,128)S(1)}, f32[48,256]{1,0:T(8,128)S(1)}, u32[]{:S(2)}, u32[]{:S(2)}) collective-permute-start(f32[48,256]{1,0:T(8,128)S(1)} %get-tuple-element.30), channel_id=1, source_target_pairs={{0,64},{1,0},{2,2},{3,66},{4,68},{5,4},{6,6},{7,70},{8,78},{9,14},... | collective-permute-start | bytes 147464 | tf_op jit(solution)/shard_map/ppermute | solution.py:514
  23.9 2.0 %collective-permute-start.1 = (f32[8,128]{1,0:T(8,128)S(1)}, f32[8,128]{1,0:T(8,128)S(1)}, u32[]{:S(2)}, u32[]{:S(2)}) collective-permute-start(f32[8,128]{1,0:T(8,128)S(1)} %get-tuple-element.31), channel_id=1, source_target_pairs={{0,0},{1,64},{2,66},{3,2},{4,4},{5,68},{6,70},{7,6},{8,14},{9,78},... | collective-permute-start | bytes 12296 | tf_op jit(solution)/shard_map/ppermute | solution.py:514
  24.6 9.9 %collective-permute-start.2 = (f32[8,128]{1,0:T(8,128)S(1)}, f32[8,128]{1,0:T(8,128)S(1)}, u32[]{:S(2)}, u32[]{:S(2)}) collective-permute-start(f32[8,128]{1,0:T(8,128)S(1)} %get-tuple-element.32), channel_id=1, source_target_pairs={{1,2},{2,0},{3,68},{4,66},{5,6},{6,4},{7,78},{8,70},{9,12},{10,14}... | collective-permute-start | bytes 12296 | tf_op jit(solution)/shard_map/ppermute | solution.py:514
  37.1 5.9 %collective-permute-start.4 = (bf16[256,128]{1,0:T(8,128)(2,1)S(1)}, bf16[256,128]{1,0:T(8,128)(2,1)S(1)}, u32[]{:S(2)}, u32[]{:S(2)}) collective-permute-start(bf16[256,128]{1,0:T(8,128)(2,1)S(1)} %get-tuple-element.34), channel_id=1, source_target_pairs={{64,0},{0,64},{2,66},{66,2},{68,4},{4,68},{6,70},{70,6},{78,14},{1... | collective-permute-start | bytes 196616 | tf_op jit(solution)/shard_map/ppermute | solution.py:514
  39.7 5.0 %collective-permute-start.5 = (bf16[256,128]{1,0:T(8,128)(2,1)S(1)}, bf16[256,128]{1,0:T(8,128)(2,1)S(1)}, u32[]{:S(2)}, u32[]{:S(2)}) collective-permute-start(bf16[256,128]{1,0:T(8,128)(2,1)S(1)} %get-tuple-element.35), channel_id=1, source_target_pairs={{0,2},{2,0},{66,68},{68,66},{4,6},{6,4},{70,78},{78,70},{14,12},{1... | collective-permute-start | bytes 196616 | tf_op jit(solution)/shard_map/ppermute | solution.py:514
  47.9 4.8 %collective-permute-start.7 = (bf16[256,128]{1,0:T(8,128)(2,1)S(1)}, bf16[256,128]{1,0:T(8,128)(2,1)S(1)}, u32[]{:S(2)}, u32[]{:S(2)}) collective-permute-start(bf16[256,128]{1,0:T(8,128)(2,1)S(1)} %get-tuple-element.44), channel_id=1, source_target_pairs={{64,0},{0,64},{2,66},{66,2},{68,4},{4,68},{6,70},{70,6},{78,14},{1... | collective-permute-start | bytes 196616 | tf_op jit(solution)/shard_map/ppermute | solution.py:514
  48.0 6.3 %collective-permute-start.8 = (bf16[256,128]{1,0:T(8,128)(2,1)S(1)}, bf16[256,128]{1,0:T(8,128)(2,1)S(1)}, u32[]{:S(2)}, u32[]{:S(2)}) collective-permute-start(bf16[256,128]{1,0:T(8,128)(2,1)S(1)} %get-tuple-element.45), channel_id=1, source_target_pairs={{0,2},{2,0},{66,68},{68,66},{4,6},{6,4},{70,78},{78,70},{14,12},{1... | collective-permute-start | bytes 196616 | tf_op jit(solution)/shard_map/ppermute | solution.py:514
  55.3 5.3 %collective-permute-start.9 = (f32[8,128]{1,0:T(8,128)S(1)}, f32[8,128]{1,0:T(8,128)S(1)}, u32[]{:S(2)}, u32[]{:S(2)}) collective-permute-start(f32[8,128]{1,0:T(8,128)S(1)} %get-tuple-element.50), channel_id=1, source_target_pairs={{192,128},{128,192},{130,194},{194,130},{196,132},{132,196},{134,1... | collective-permute-start | bytes 12296 | tf_op jit(solution)/shard_map/ppermute | solution.py:514
  57.2 4.4 %collective-permute-start.10 = (f32[8,128]{1,0:T(8,128)S(1)}, f32[8,128]{1,0:T(8,128)S(1)}, u32[]{:S(2)}, u32[]{:S(2)}) collective-permute-start(f32[8,128]{1,0:T(8,128)S(1)} %get-tuple-element.51), channel_id=1, source_target_pairs={{128,130},{130,128},{194,196},{196,194},{132,134},{134,132},{198,2... | collective-permute-start | bytes 12296 | tf_op jit(solution)/shard_map/ppermute | solution.py:514
  62.5 6.7 %collective-permute-start.11 = (f32[8,128]{1,0:T(8,128)S(1)}, f32[8,128]{1,0:T(8,128)S(1)}, u32[]{:S(2)}, u32[]{:S(2)}) collective-permute-start(f32[8,128]{1,0:T(8,128)S(1)} %get-tuple-element.53), channel_id=1, source_target_pairs={{192,128},{128,192},{130,194},{194,130},{196,132},{132,196},{134,1... | collective-permute-start | bytes 12296 | tf_op jit(solution)/shard_map/ppermute | solution.py:514
  64.5 5.8 %collective-permute-start.12 = (f32[8,128]{1,0:T(8,128)S(1)}, f32[8,128]{1,0:T(8,128)S(1)}, u32[]{:S(2)}, u32[]{:S(2)}) collective-permute-start(f32[8,128]{1,0:T(8,128)S(1)} %get-tuple-element.54), channel_id=1, source_target_pairs={{128,130},{130,128},{194,196},{196,194},{132,134},{134,132},{198,2... | collective-permute-start | bytes 12296 | tf_op jit(solution)/shard_map/ppermute | solution.py:514
  73.2 28.4 %all-to-all-start.1 = ((f32[384,2,128]{2,1,0:T(2,128)}), f32[384,2,128]{2,1,0:T(2,128)S(1)}, u32[]{:S(2)}, u32[]{:S(2)}) async-start(f32[384,2,128]{2,1,0:T(2,128)} %get-tuple-element.57), calls=%async_computation.1 | async-start | bytes 786432 | tf_op jit(solution)/shard_map/all_to_all | solution.py:579
  88.2 19.5 %collective-permute-start.13 = (f32[3,256]{1,0:T(4,128)S(1)}, f32[3,256]{1,0:T(4,128)S(1)}, u32[]{:S(2)}, u32[]{:S(2)}) collective-permute-start(f32[3,256]{1,0:T(4,128)S(1)} %get-tuple-element.56), channel_id=1, source_target_pairs={{64,0},{0,1},{2,2},{66,3},{68,4},{4,5},{6,6},{70,7},{78,8},{14,9},... | collective-permute-start | bytes 9224 | tf_op jit(solution)/shard_map/ppermute | solution.py:514
  101.8 6.7 %collective-permute-start.14 = (f32[3,256]{1,0:T(4,128)S(1)}, f32[3,256]{1,0:T(4,128)S(1)}, u32[]{:S(2)}, u32[]{:S(2)}) collective-permute-start(f32[3,256]{1,0:T(4,128)S(1)} %shard_map.156), channel_id=1, source_target_pairs={{0,128},{128,0},{1,129},{129,1},{2,130},{130,2},{3,131},{131,3},{4... | collective-permute-start | bytes 9224 | tf_op jit(solution)/shard_map/ppermute | solution.py:582

commit v14 on v13

--- a/solution.py
+++ b/solution.py
@@ -16,7 +16,7 @@
 VMEM = pl.BlockSpec(memory_space=pltpu.VMEM)
 ANY = pl.BlockSpec(memory_space=pl.ANY)
 SWEEP_CHUNK, SWEEP_UNROLL = 32, 16
-FIELD_CHUNK, FIELD_UNROLL = 32, 8
+FIELD_CHUNK, FIELD_UNROLL = 32, 16
 TERM_CHUNK, TERM_UNROLL = 64, 4
 STATIC_CHUNK = 64
 RADIAL_SLOTS = 8

time: 110 us -> 110 us (level)
  no operation moved by 1% of the time
where the time goes in v14:
time: 110 us; the launch traced here: 109 us
  starting transfers between devices  70.1 us (64%)
  waiting for transfers between devices  24.9 us (23%)
  Pallas kernels  12.1 us (11%)
    ppermute x13, starting transfers between devices, move(): lax.ppermute(value, EVERY, [(source[a] + g * members, target[b] + g * mem...  32 us
    all_to_all x1, starting transfers between devices, local(): lax.all_to_all(spread, DOM, 0, 0, tiled=True).reshape(members, 3, 2, half)  15 us
    ppermute x13, waiting for transfers between devices, move(): lax.ppermute(value, EVERY, [(source[a] + g * members, target[b] + g * mem...  13.9 us
    all_to_all x1, starting transfers between devices, local(): lax.all_to_all(copies, DOM, 0, 0, tiled=True).reshape(2 * members, 4, half)  13.8 us
    pallas_call x9, Pallas kernels, call(): pl.pallas_call(body, out_shape=[jax.ShapeDtypeStruct(s, d) for s, d in ou...  12.1 us
    all_to_all x1, waiting for transfers between devices, local(): lax.all_to_all(spread, DOM, 0, 0, tiled=True).reshape(members, 3, 2, half)  9.38 us
    ppermute x1, starting transfers between devices, local(): share = lax.ppermute(share, 'grp', [(0, 1), (1, 0)])  5.98 us
    ppermute x1, starting transfers between devices, local(): partner = lax.ppermute(mine, 'grp', [(0, 1), (1, 0)])  3.33 us
  transfers between devices with their start and end apart: 17, of which 8 were waited for; matrix products, arithmetic and copies ran while one was open for 0% of the time, Pallas kernels for 3%

profile of v14, /device:TPU:1, one launch (start us, length us, event | category | flops | bytes accessed | tf_op | source)
XLA Modules:
  0.0 109.0 jit_solution(18235993518274726352)
XLA Ops:
  0.6 1.0 shard_map.149
  1.7 3.3 %collective-permute-start.6 = (f32[2,4,128]{2,1,0:T(4,128)S(1)}, f32[2,4,128]{2,1,0:T(4,128)S(1)}, u32[]{:S(2)}, u32[]{:S(2)}) collective-permute-start(f32[2,4,128]{2,1,0:T(4,128)S(1)} %get-tuple-element.40), channel_id=1, source_target_pairs={{0,128},{128,0},{1,129},{129,1},{2,130},{130,2},{3,131},{131,3},{4... | collective-permute-start | bytes 12296 | tf_op jit(solution)/shard_map/ppermute | solution.py:532
  5.0 0.8 collective-permute-done.6
  5.8 0.9 broadcast_in_dim.17
  6.7 13.8 %all-to-all-start = ((f32[128,2,4,128]{3,2,1,0:T(4,128)}), f32[128,2,4,128]{3,2,1,0:T(4,128)S(1)}, u32[]{:S(2)}, u32[]{:S(2)}) async-start(f32[128,2,4,128]{3,2,1,0:T(4,128)} %broadcast_in_dim.17), calls=%async_computation | async-start | bytes 1048576 | tf_op jit(solution)/shard_map/all_to_all | solution.py:534
  20.5 0.7 collective-permute-start.3
  21.1 2.8 %collective-permute-start = (f32[48,256]{1,0:T(8,128)S(1)}, f32[48,256]{1,0:T(8,128)S(1)}, u32[]{:S(2)}, u32[]{:S(2)}) collective-permute-start(f32[48,256]{1,0:T(8,128)S(1)} %get-tuple-element.30), channel_id=1, source_target_pairs={{0,64},{1,0},{2,2},{3,66},{4,68},{5,4},{6,6},{7,70},{8,78},{9,14},... | collective-permute-start | bytes 147464 | tf_op jit(solution)/shard_map/ppermute | solution.py:514
  23.9 0.7 collective-permute-start.1
  24.6 1.3 %collective-permute-start.2 = (f32[8,128]{1,0:T(8,128)S(1)}, f32[8,128]{1,0:T(8,128)S(1)}, u32[]{:S(2)}, u32[]{:S(2)}) collective-permute-start(f32[8,128]{1,0:T(8,128)S(1)} %get-tuple-element.32), channel_id=1, source_target_pairs={{1,2},{2,0},{3,68},{4,66},{5,6},{6,4},{7,78},{8,70},{9,12},{10,14}... | collective-permute-start | bytes 12296 | tf_op jit(solution)/shard_map/ppermute | solution.py:514
  25.9 0.0 collective-permute-done.1.rim_a
  25.9 8.6 %collective-permute-done.2.rim_b = f32[8,128]{1,0:T(8,128)S(1)} collective-permute-done((f32[8,128]{1,0:T(8,128)S(1)}, f32[8,128]{1,0:T(8,128)S(1)}, u32[]{:S(2)}, u32[]{:S(2)}) %collective-permute-start.2) | collective-permute-done | bytes 4128 | tf_op jit(solution)/shard_map/ppermute | solution.py:514
  34.6 0.0 collective-permute-done.pack
  34.6 0.0 collective-permute-done.3.features_far
  34.6 2.5 %shard_map.150 = (bf16[256,256]{1,0:T(8,128)(2,1)S(1)}, f32[512,256]{1,0:T(8,128)S(1)}, f32[512,256]{1,0:T(8,128)S(1)}, f32[8,256]{1,0:T(8,128)S(1)}, f32[512,8]...) custom-call(f32[48,256]{1,0:T(8,128)S(1)} %collective-permute-done.pack, ...), custom_call_target="tpu_custom_call" | custom-call | tf_op jit(solution)/shard_map/pallas_call | solution.py:27
  37.1 2.6 %collective-permute-start.4 = (bf16[256,128]{1,0:T(8,128)(2,1)S(1)}, bf16[256,128]{1,0:T(8,128)(2,1)S(1)}, u32[]{:S(2)}, u32[]{:S(2)}) collective-permute-start(bf16[256,128]{1,0:T(8,128)(2,1)S(1)} %get-tuple-element.34), channel_id=1, source_target_pairs={{64,0},{0,64},{2,66},{66,2},{68,4},{4,68},{6,70},{70,6},{78,14},{1... | collective-permute-start | bytes 196616 | tf_op jit(solution)/shard_map/ppermute | solution.py:514
  39.7 3.3 %collective-permute-start.5 = (bf16[256,128]{1,0:T(8,128)(2,1)S(1)}, bf16[256,128]{1,0:T(8,128)(2,1)S(1)}, u32[]{:S(2)}, u32[]{:S(2)}) collective-permute-start(bf16[256,128]{1,0:T(8,128)(2,1)S(1)} %get-tuple-element.35), channel_id=1, source_target_pairs={{0,2},{2,0},{66,68},{68,66},{4,6},{6,4},{70,78},{78,70},{14,12},{1... | collective-permute-start | bytes 196616 | tf_op jit(solution)/shard_map/ppermute | solution.py:514
  42.9 0.1 shard_map.151.third_far
  43.0 0.0 collective-permute-done.4.side_a
  43.0 1.6 %collective-permute-done.5.side_b = bf16[256,128]{1,0:T(8,128)(2,1)S(1)} collective-permute-done((bf16[256,128]{1,0:T(8,128)(2,1)S(1)}, bf16[256,128]{1,0:T(8,128)(2,1)S(1)}, u32[]{:S(2)}, u32[]{:S(2)}) %collective-permute-start.5) | collective-permute-done | bytes 65568 | tf_op jit(solution)/shard_map/ppermute | solution.py:514
  44.7 0.0 all-to-all-done
  44.7 2.8 %shard_map.152 = (f32[8,256]{1,0:T(8,128)S(1)}, f32[4,4,128]{2,1,0:T(4,128)S(1)}, bf16[256,256]{1,0:T(8,128)(2,1)S(1)}, bf16[256,256]{1,0:T(8,128)(2,1)S(1)}, f3...) custom-call(f32[48,256]{1,0:T(8,128)S(1)} %collective-permute-done.pack,, ...), custom_call_target="tpu_custom_call" | custom-call | tf_op jit(solution)/shard_map/pallas_call | solution.py:27
  47.5 0.1 collective-permute-start.7
  47.6 4.7 %collective-permute-start.8 = (bf16[256,128]{1,0:T(8,128)(2,1)S(1)}, bf16[256,128]{1,0:T(8,128)(2,1)S(1)}, u32[]{:S(2)}, u32[]{:S(2)}) collective-permute-start(bf16[256,128]{1,0:T(8,128)(2,1)S(1)} %get-tuple-element.45), channel_id=1, source_target_pairs={{0,2},{2,0},{66,68},{68,66},{4,6},{6,4},{70,78},{78,70},{14,12},{1... | collective-permute-start | bytes 196616 | tf_op jit(solution)/shard_map/ppermute | solution.py:514
  52.3 0.0 collective-permute-done.7.side_a
  52.3 1.6 %collective-permute-done.8.side_b = bf16[256,128]{1,0:T(8,128)(2,1)S(1)} collective-permute-done((bf16[256,128]{1,0:T(8,128)(2,1)S(1)}, bf16[256,128]{1,0:T(8,128)(2,1)S(1)}, u32[]{:S(2)}, u32[]{:S(2)}) %collective-permute-start.8) | collective-permute-done | bytes 65568 | tf_op jit(solution)/shard_map/ppermute | solution.py:514
  53.9 1.0 shard_map.153
  54.9 1.9 %collective-permute-start.9 = (f32[8,128]{1,0:T(8,128)S(1)}, f32[8,128]{1,0:T(8,128)S(1)}, u32[]{:S(2)}, u32[]{:S(2)}) collective-permute-start(f32[8,128]{1,0:T(8,128)S(1)} %get-tuple-element.50), channel_id=1, source_target_pairs={{192,128},{128,192},{130,194},{194,130},{196,132},{132,196},{134,1... | collective-permute-start | bytes 12296 | tf_op jit(solution)/shard_map/ppermute | solution.py:514
  56.9 3.4 %collective-permute-start.10 = (f32[8,128]{1,0:T(8,128)S(1)}, f32[8,128]{1,0:T(8,128)S(1)}, u32[]{:S(2)}, u32[]{:S(2)}) collective-permute-start(f32[8,128]{1,0:T(8,128)S(1)} %get-tuple-element.51), channel_id=1, source_target_pairs={{128,130},{130,128},{194,196},{196,194},{132,134},{134,132},{198,2... | collective-permute-start | bytes 12296 | tf_op jit(solution)/shard_map/ppermute | solution.py:514
  60.2 0.0 collective-permute-done.9.side_a
  60.3 1.0 collective-permute-done.10.side_b
  61.2 0.9 shard_map.154
  62.2 1.9 %collective-permute-start.11 = (f32[8,128]{1,0:T(8,128)S(1)}, f32[8,128]{1,0:T(8,128)S(1)}, u32[]{:S(2)}, u32[]{:S(2)}) collective-permute-start(f32[8,128]{1,0:T(8,128)S(1)} %get-tuple-element.53), channel_id=1, source_target_pairs={{192,128},{128,192},{130,194},{194,130},{196,132},{132,196},{134,1... | collective-permute-start | bytes 12296 | tf_op jit(solution)/shard_map/ppermute | solution.py:514
  64.1 4.8 %collective-permute-start.12 = (f32[8,128]{1,0:T(8,128)S(1)}, f32[8,128]{1,0:T(8,128)S(1)}, u32[]{:S(2)}, u32[]{:S(2)}) collective-permute-start(f32[8,128]{1,0:T(8,128)S(1)} %get-tuple-element.54), channel_id=1, source_target_pairs={{128,130},{130,128},{194,196},{196,194},{132,134},{134,132},{198,2... | collective-permute-start | bytes 12296 | tf_op jit(solution)/shard_map/ppermute | solution.py:514
  68.9 0.0 collective-permute-done.11.side_a
  68.9 1.0 collective-permute-done.12.side_b
  69.9 3.0 %shard_map.155 = (f32[3,256]{1,0:T(4,128)S(1)}, f32[384,2,128]{2,1,0:T(2,128)}) custom-call(f32[4,4,128]{2,1,0:T(4,128)S(1)} %get-tuple-element.41.near, f32[48,256]{1,0:T(8,128)S(1)} %collective-permute-done.pack, f32[8,256]{1,0:T(8,128)S(1)} %get-tuple-element.48.charge, f32[8,256]{1,0:T(8,128)S(1)} %get-tuple-element.49.outside_row, ...), custom_call_target="tpu_custom_call" | custom-call | tf_op jit(solution)/shard_map/pallas_call | solution.py:27
  72.8 15.0 %all-to-all-start.1 = ((f32[384,2,128]{2,1,0:T(2,128)}), f32[384,2,128]{2,1,0:T(2,128)S(1)}, u32[]{:S(2)}, u32[]{:S(2)}) async-start(f32[384,2,128]{2,1,0:T(2,128)} %get-tuple-element.57), calls=%async_computation.1 | async-start | bytes 786432 | tf_op jit(solution)/shard_map/all_to_all | solution.py:579
  87.8 4.0 %collective-permute-start.13 = (f32[3,256]{1,0:T(4,128)S(1)}, f32[3,256]{1,0:T(4,128)S(1)}, u32[]{:S(2)}, u32[]{:S(2)}) collective-permute-start(f32[3,256]{1,0:T(4,128)S(1)} %get-tuple-element.56), channel_id=1, source_target_pairs={{64,0},{0,1},{2,2},{66,3},{68,4},{4,5},{6,6},{70,7},{78,8},{14,9},... | collective-permute-start | bytes 9224 | tf_op jit(solution)/shard_map/ppermute | solution.py:514
  91.8 9.4 %all-to-all-done.1 = f32[384,2,128]{2,1,0:T(2,128)S(1)} async-done(((f32[384,2,128]{2,1,0:T(2,128)}), f32[384,2,128]{2,1,0:T(2,128)S(1)}, u32[]{:S(2)}, u32[]{:S(2)}) %all-to-all-start.1) | async-done | bytes 393248 | tf_op jit(solution)/shard_map/all_to_all | solution.py:579
  101.2 0.2 shard_map.156
  101.4 6.0 %collective-permute-start.14 = (f32[3,256]{1,0:T(4,128)S(1)}, f32[3,256]{1,0:T(4,128)S(1)}, u32[]{:S(2)}, u32[]{:S(2)}) collective-permute-start(f32[3,256]{1,0:T(4,128)S(1)} %shard_map.156), channel_id=1, source_target_pairs={{0,128},{128,0},{1,129},{129,1},{2,130},{130,2},{3,131},{131,3},{4... | collective-permute-start | bytes 9224 | tf_op jit(solution)/shard_map/ppermute | solution.py:582
  107.4 0.0 collective-permute-done.13.result
  107.4 0.8 collective-permute-done.14.share
  108.2 0.6 shard_map.157
Async XLA Ops:
  1.7 4.2 %collective-permute-start.6 = (f32[2,4,128]{2,1,0:T(4,128)S(1)}, f32[2,4,128]{2,1,0:T(4,128)S(1)}, u32[]{:S(2)}, u32[]{:S(2)}) collective-permute-start(f32[2,4,128]{2,1,0:T(4,128)S(1)} %get-tuple-element.40), channel_id=1, source_target_pairs={{0,128},{128,0},{1,129},{129,1},{2,130},{130,2},{3,131},{131,3},{4... | collective-permute-start | bytes 12296 | tf_op jit(solution)/shard_map/ppermute | solution.py:532
  6.7 38.0 %all-to-all-start = ((f32[128,2,4,128]{3,2,1,0:T(4,128)}), f32[128,2,4,128]{3,2,1,0:T(4,128)S(1)}, u32[]{:S(2)}, u32[]{:S(2)}) async-start(f32[128,2,4,128]{3,2,1,0:T(4,128)} %broadcast_in_dim.17), calls=%async_computation | async-start | bytes 1048576 | tf_op jit(solution)/shard_map/all_to_all | solution.py:534
  20.5 14.1 %collective-permute-start.3 = (bf16[256,256]{1,0:T(8,128)(2,1)}, bf16[256,256]{1,0:T(8,128)(2,1)S(1)}, u32[]{:S(2)}, u32[]{:S(2)}) collective-permute-start(bf16[256,256]{1,0:T(8,128)(2,1)} %param.17), channel_id=1, source_target_pairs={{0,64},{1,0},{2,2},{3,66},{4,68},{5,4},{6,6},{7,70},{8,78},{9,14},... | collective-permute-start | bytes 393224 | tf_op jit(solution)/shard_map/ppermute | solution.py:514
  21.1 13.4 %collective-permute-start = (f32[48,256]{1,0:T(8,128)S(1)}, f32[48,256]{1,0:T(8,128)S(1)}, u32[]{:S(2)}, u32[]{:S(2)}) collective-permute-start(f32[48,256]{1,0:T(8,128)S(1)} %get-tuple-element.30), channel_id=1, source_target_pairs={{0,64},{1,0},{2,2},{3,66},{4,68},{5,4},{6,6},{7,70},{8,78},{9,14},... | collective-permute-start | bytes 147464 | tf_op jit(solution)/shard_map/ppermute | solution.py:514
  23.9 2.0 %collective-permute-start.1 = (f32[8,128]{1,0:T(8,128)S(1)}, f32[8,128]{1,0:T(8,128)S(1)}, u32[]{:S(2)}, u32[]{:S(2)}) collective-permute-start(f32[8,128]{1,0:T(8,128)S(1)} %get-tuple-element.31), channel_id=1, source_target_pairs={{0,0},{1,64},{2,66},{3,2},{4,4},{5,68},{6,70},{7,6},{8,14},{9,78},... | collective-permute-start | bytes 12296 | tf_op jit(solution)/shard_map/ppermute | solution.py:514
  24.6 9.9 %collective-permute-start.2 = (f32[8,128]{1,0:T(8,128)S(1)}, f32[8,128]{1,0:T(8,128)S(1)}, u32[]{:S(2)}, u32[]{:S(2)}) collective-permute-start(f32[8,128]{1,0:T(8,128)S(1)} %get-tuple-element.32), channel_id=1, source_target_pairs={{1,2},{2,0},{3,68},{4,66},{5,6},{6,4},{7,78},{8,70},{9,12},{10,14}... | collective-permute-start | bytes 12296 | tf_op jit(solution)/shard_map/ppermute | solution.py:514
  37.1 5.9 %collective-permute-start.4 = (bf16[256,128]{1,0:T(8,128)(2,1)S(1)}, bf16[256,128]{1,0:T(8,128)(2,1)S(1)}, u32[]{:S(2)}, u32[]{:S(2)}) collective-permute-start(bf16[256,128]{1,0:T(8,128)(2,1)S(1)} %get-tuple-element.34), channel_id=1, source_target_pairs={{64,0},{0,64},{2,66},{66,2},{68,4},{4,68},{6,70},{70,6},{78,14},{1... | collective-permute-start | bytes 196616 | tf_op jit(solution)/shard_map/ppermute | solution.py:514
  39.7 5.0 %collective-permute-start.5 = (bf16[256,128]{1,0:T(8,128)(2,1)S(1)}, bf16[256,128]{1,0:T(8,128)(2,1)S(1)}, u32[]{:S(2)}, u32[]{:S(2)}) collective-permute-start(bf16[256,128]{1,0:T(8,128)(2,1)S(1)} %get-tuple-element.35), channel_id=1, source_target_pairs={{0,2},{2,0},{66,68},{68,66},{4,6},{6,4},{70,78},{78,70},{14,12},{1... | collective-permute-start | bytes 196616 | tf_op jit(solution)/shard_map/ppermute | solution.py:514
  47.5 4.8 %collective-permute-start.7 = (bf16[256,128]{1,0:T(8,128)(2,1)S(1)}, bf16[256,128]{1,0:T(8,128)(2,1)S(1)}, u32[]{:S(2)}, u32[]{:S(2)}) collective-permute-start(bf16[256,128]{1,0:T(8,128)(2,1)S(1)} %get-tuple-element.44), channel_id=1, source_target_pairs={{64,0},{0,64},{2,66},{66,2},{68,4},{4,68},{6,70},{70,6},{78,14},{1... | collective-permute-start | bytes 196616 | tf_op jit(solution)/shard_map/ppermute | solution.py:514
  47.6 6.3 %collective-permute-start.8 = (bf16[256,128]{1,0:T(8,128)(2,1)S(1)}, bf16[256,128]{1,0:T(8,128)(2,1)S(1)}, u32[]{:S(2)}, u32[]{:S(2)}) collective-permute-start(bf16[256,128]{1,0:T(8,128)(2,1)S(1)} %get-tuple-element.45), channel_id=1, source_target_pairs={{0,2},{2,0},{66,68},{68,66},{4,6},{6,4},{70,78},{78,70},{14,12},{1... | collective-permute-start | bytes 196616 | tf_op jit(solution)/shard_map/ppermute | solution.py:514
  54.9 5.3 %collective-permute-start.9 = (f32[8,128]{1,0:T(8,128)S(1)}, f32[8,128]{1,0:T(8,128)S(1)}, u32[]{:S(2)}, u32[]{:S(2)}) collective-permute-start(f32[8,128]{1,0:T(8,128)S(1)} %get-tuple-element.50), channel_id=1, source_target_pairs={{192,128},{128,192},{130,194},{194,130},{196,132},{132,196},{134,1... | collective-permute-start | bytes 12296 | tf_op jit(solution)/shard_map/ppermute | solution.py:514
  56.9 4.4 %collective-permute-start.10 = (f32[8,128]{1,0:T(8,128)S(1)}, f32[8,128]{1,0:T(8,128)S(1)}, u32[]{:S(2)}, u32[]{:S(2)}) collective-permute-start(f32[8,128]{1,0:T(8,128)S(1)} %get-tuple-element.51), channel_id=1, source_target_pairs={{128,130},{130,128},{194,196},{196,194},{132,134},{134,132},{198,2... | collective-permute-start | bytes 12296 | tf_op jit(solution)/shard_map/ppermute | solution.py:514
  62.2 6.7 %collective-permute-start.11 = (f32[8,128]{1,0:T(8,128)S(1)}, f32[8,128]{1,0:T(8,128)S(1)}, u32[]{:S(2)}, u32[]{:S(2)}) collective-permute-start(f32[8,128]{1,0:T(8,128)S(1)} %get-tuple-element.53), channel_id=1, source_target_pairs={{192,128},{128,192},{130,194},{194,130},{196,132},{132,196},{134,1... | collective-permute-start | bytes 12296 | tf_op jit(solution)/shard_map/ppermute | solution.py:514
  64.1 5.8 %collective-permute-start.12 = (f32[8,128]{1,0:T(8,128)S(1)}, f32[8,128]{1,0:T(8,128)S(1)}, u32[]{:S(2)}, u32[]{:S(2)}) collective-permute-start(f32[8,128]{1,0:T(8,128)S(1)} %get-tuple-element.54), channel_id=1, source_target_pairs={{128,130},{130,128},{194,196},{196,194},{132,134},{134,132},{198,2... | collective-permute-start | bytes 12296 | tf_op jit(solution)/shard_map/ppermute | solution.py:514
  72.8 28.4 %all-to-all-start.1 = ((f32[384,2,128]{2,1,0:T(2,128)}), f32[384,2,128]{2,1,0:T(2,128)S(1)}, u32[]{:S(2)}, u32[]{:S(2)}) async-start(f32[384,2,128]{2,1,0:T(2,128)} %get-tuple-element.57), calls=%async_computation.1 | async-start | bytes 786432 | tf_op jit(solution)/shard_map/all_to_all | solution.py:579
  87.8 19.5 %collective-permute-start.13 = (f32[3,256]{1,0:T(4,128)S(1)}, f32[3,256]{1,0:T(4,128)S(1)}, u32[]{:S(2)}, u32[]{:S(2)}) collective-permute-start(f32[3,256]{1,0:T(4,128)S(1)} %get-tuple-element.56), channel_id=1, source_target_pairs={{64,0},{0,1},{2,2},{66,3},{68,4},{4,5},{6,6},{70,7},{78,8},{14,9},... | collective-permute-start | bytes 9224 | tf_op jit(solution)/shard_map/ppermute | solution.py:514
  101.4 6.8 %collective-permute-start.14 = (f32[3,256]{1,0:T(4,128)S(1)}, f32[3,256]{1,0:T(4,128)S(1)}, u32[]{:S(2)}, u32[]{:S(2)}) collective-permute-start(f32[3,256]{1,0:T(4,128)S(1)} %shard_map.156), channel_id=1, source_target_pairs={{0,128},{128,0},{1,129},{129,1},{2,130},{130,2},{3,131},{131,3},{4... | collective-permute-start | bytes 9224 | tf_op jit(solution)/shard_map/ppermute | solution.py:582
